TPU v7x, 32 devices: a whole 2x2x4 slice. The times are simulated.
32 devices in a mesh: grp: 4 (over z), blk: 8 (over y, x, core).
Axes of the slice: x: 2, y: 2, z: 4, core: 2. Of those that a mesh axis runs over, the one named last changes fastest.
Arguments:
- tokens: bfloat16 [8192, 2048], P(('grp', 'blk')), may hold values from -9 to 9
- block_group: int32 [64], replicated, may hold values from 0 to 3, as said below
- block_slot: int32 [64], replicated, may hold values from 0 to 15, as said below
- attn_gain: bfloat16 [2048], P(('grp', 'blk')), may hold values from 0.5 to 1.5
- w_query: bfloat16 [2048, 2048], P(('grp', 'blk')), may hold values from -0.5 to 0.5
- w_key: bfloat16 [2048, 512], P(('grp', 'blk')), may hold values from -0.5 to 0.5
- w_value: bfloat16 [2048, 512], P(('grp', 'blk')), may hold values from -0.125 to 0.125
- w_out: bfloat16 [2048, 2048], P(('grp', 'blk')), may hold values from -2 to 2
- mlp_gain: bfloat16 [2048], P(('grp', 'blk')), may hold values from 0.5 to 1.5
- w_gate: bfloat16 [2048, 8192], P(None, ('grp', 'blk')), may hold values from -0.125 to 0.125
- w_up: bfloat16 [2048, 8192], P(None, ('grp', 'blk')), may hold values from -0.125 to 0.125
- w_down: bfloat16 [8192, 2048], P(('grp', 'blk')), may hold values from -0.5 to 0.5
- cotangent: bfloat16 [8192, 2048], P(('grp', 'blk')), may hold values from -6 to 6
Outputs:
- output: bfloat16 [8192, 2048], P(('grp', 'blk'))
- tokens_grad: bfloat16 [8192, 2048], P(('grp', 'blk'))
- attn_gain_grad: float32 [2048], P(('grp', 'blk'))
- w_query_grad: float32 [2048, 2048], P(('grp', 'blk'))
- w_key_grad: float32 [2048, 512], P(('grp', 'blk'))
- w_value_grad: float32 [2048, 512], P(('grp', 'blk'))
- w_out_grad: float32 [2048, 2048], P(('grp', 'blk'))
- mlp_gain_grad: float32 [2048], P(('grp', 'blk'))
- w_gate_grad: float32 [2048, 8192], P(None, ('grp', 'blk'))
- w_up_grad: float32 [2048, 8192], P(None, ('grp', 'blk'))
- w_down_grad: float32 [8192, 2048], P(('grp', 'blk'))
- rms_stats: float32 [3], replicated
Inputs may be any that keep to these rules, and one draw needn't show every extreme that they name: `block_group`: each group has 16 blocks, one of each slot, and all of them lie in one aligned run of 16 blocks. `block_slot`: slots below 8 are the prompt's parts in order, the others its continuations.
All inputs are finite; a program needn't handle non-finite values.
Results may differ from a plain program's by a relative error of at most 0.019.
Values may be sent and summed in bfloat16 or wider, within the bound.
A program may use at most 448 MiB of HBM per device.

v0:
```python
import jax
import jax.numpy as jnp
from jax import lax
from jax.sharding import PartitionSpec as P

D = 2048
HEADS = 32
KV_HEADS = 8
HEAD_DIM = 64
BLOCK = 128
PROMPT_BLOCKS = 8


ATTN_MULT = 0.015625
RESID_MULT = 0.22
EPSILON = 1e-05
MASKED = -1e30


def rms_norm(values, gain):
    factor = lax.rsqrt(jnp.mean(values * values, axis=-1, keepdims=True) + EPSILON)
    return values * factor * gain


def matmul(left, right):
    return jnp.dot(left, right, preferred_element_type=jnp.float32)


def over_rows(left, right):
    return lax.dot_general(
        left, right, (((0,), (0,)), ((), ())), preferred_element_type=jnp.float32
    )


def over_cols(left, right):
    return lax.dot_general(
        left, right, (((1,), (1,)), ((), ())), preferred_element_type=jnp.float32
    )


def gated(gate_act, up_act):
    return jax.nn.silu(gate_act) * up_act


def on_device(
    tokens,
    block_group,
    block_slot,
    attn_gain,
    w_query,
    w_key,
    w_value,
    w_out,
    mlp_gain,
    w_gate,
    w_up,
    w_down,
    cotangent,
):
    gathered = (
        lax.all_gather(attn_gain, ("grp", "blk"), axis=0, tiled=True),
        lax.all_gather(w_query, ("grp", "blk"), axis=0, tiled=True),
        lax.all_gather(w_key, ("grp", "blk"), axis=0, tiled=True),
        lax.all_gather(w_value, ("grp", "blk"), axis=0, tiled=True),
        lax.all_gather(w_out, ("grp", "blk"), axis=0, tiled=True),
        lax.all_gather(mlp_gain, ("grp", "blk"), axis=0, tiled=True),
    )
    gain_one = gathered[0].astype(jnp.float32)
    query_full = gathered[1]
    key_full = gathered[2]
    value_full = gathered[3]
    out_full = gathered[4]
    gain_two = gathered[5].astype(jnp.float32)
    pair_half = key_full.shape[1]
    tok_rows = tokens.shape[0]
    blocks_here = tok_rows // BLOCK
    row_blocks = blocks_here * lax.axis_size("blk")
    prompt_len = PROMPT_BLOCKS * BLOCK
    key_count = prompt_len + BLOCK
    per_group = HEADS // KV_HEADS
    row_first = lax.axis_index("grp") * row_blocks
    own_first = row_first + lax.axis_index("blk") * blocks_here
    own_group = lax.dynamic_slice_in_dim(block_group, own_first, blocks_here)
    own_slot = lax.dynamic_slice_in_dim(block_slot, own_first, blocks_here)
    row_group = lax.dynamic_slice_in_dim(block_group, row_first, row_blocks)
    row_slot = lax.dynamic_slice_in_dim(block_slot, row_first, row_blocks)
    slot_ids = jnp.arange(PROMPT_BLOCKS, dtype=jnp.int32)
    matched = (row_group[None, None, :] == own_group[:, None, None]) & (
        row_slot[None, None, :] == slot_ids[None, :, None]
    )
    places = jnp.sum(
        jnp.where(matched, jnp.arange(row_blocks, dtype=jnp.int32)[None, None, :], 0), axis=2
    )
    starts = jnp.minimum(own_slot, PROMPT_BLOCKS) * BLOCK
    key_index = jnp.arange(key_count, dtype=jnp.int32)[None, None, :]
    row_index = jnp.arange(BLOCK, dtype=jnp.int32)[None, :, None]
    visible = jnp.where(
        key_index < prompt_len,
        key_index < starts[:, None, None],
        key_index - prompt_len <= row_index,
    )
    layer_in = tokens.astype(jnp.float32)
    normed_one = rms_norm(layer_in, gain_one).astype(jnp.bfloat16)
    queries = matmul(normed_one, query_full).astype(jnp.bfloat16)
    key_rows = matmul(normed_one, key_full).astype(jnp.bfloat16)
    value_rows = matmul(normed_one, value_full).astype(jnp.bfloat16)
    own_pairs = jnp.concatenate([key_rows, value_rows], axis=1)
    row_pairs = lax.all_gather(own_pairs, "blk", axis=0, tiled=True)
    prompt_pairs = row_pairs.reshape(row_blocks, BLOCK, 2 * pair_half)[places.reshape(-1)]
    all_pairs = jnp.concatenate(
        [
            prompt_pairs.reshape(blocks_here, prompt_len, 2 * pair_half),
            own_pairs.reshape(blocks_here, BLOCK, 2 * pair_half),
        ],
        axis=1,
    )
    all_keys = all_pairs[:, :, :pair_half].reshape(blocks_here, key_count, KV_HEADS, HEAD_DIM)
    all_values = all_pairs[:, :, pair_half:].reshape(blocks_here, key_count, KV_HEADS, HEAD_DIM)
    query_heads = queries.reshape(blocks_here, BLOCK, KV_HEADS, per_group, HEAD_DIM)

    def scores_of():
        raw_scores = (
            jnp.einsum(
                "nqkgd,nskd->nkgqs", query_heads, all_keys, preferred_element_type=jnp.float32
            )
            * ATTN_MULT
        )
        return jnp.where(visible[:, None, None, :, :], raw_scores, MASKED)

    scores = scores_of()
    row_peak = jnp.max(scores, axis=-1, keepdims=True)
    shifted = jnp.exp(scores - row_peak)
    row_total = jnp.sum(shifted, axis=-1, keepdims=True)
    log_norm = row_peak + jnp.log(row_total)
    soft_probs = (shifted / row_total).astype(jnp.bfloat16)
    attended = (
        jnp.einsum("nkgqs,nskd->nqkgd", soft_probs, all_values, preferred_element_type=jnp.float32)
        .reshape(tok_rows, D)
        .astype(jnp.bfloat16)
    )
    branch_attn = matmul(attended, out_full)
    residual = layer_in + RESID_MULT * branch_attn
    normed_two = rms_norm(residual, gain_two).astype(jnp.bfloat16)
    full_gate, full_up, full_down = (
        lax.all_gather(w_gate, ("grp", "blk"), axis=1, tiled=True),
        lax.all_gather(w_up, ("grp", "blk"), axis=1, tiled=True),
        lax.all_gather(w_down, ("grp", "blk"), axis=0, tiled=True),
    )
    gate_act = matmul(normed_two, full_gate)
    up_act = matmul(normed_two, full_up)
    hidden = gated(gate_act, up_act).astype(jnp.bfloat16)
    branch_mlp = matmul(hidden, full_down)
    layer_out = residual + RESID_MULT * branch_mlp
    upstream = cotangent.astype(jnp.float32)
    d_branch_mlp = (RESID_MULT * upstream).astype(jnp.bfloat16)
    full_gate, full_up, full_down = (
        lax.all_gather(w_gate, ("grp", "blk"), axis=1, tiled=True),
        lax.all_gather(w_up, ("grp", "blk"), axis=1, tiled=True),
        lax.all_gather(w_down, ("grp", "blk"), axis=0, tiled=True),
    )
    d_hidden = over_cols(d_branch_mlp, full_down)
    grad_down = lax.psum_scatter(
        over_rows(hidden, d_branch_mlp), ("grp", "blk"), scatter_dimension=0, tiled=True
    )
    _, gate_back = jax.vjp(gated, gate_act, up_act)
    d_gate, d_up = gate_back(d_hidden)
    d_gate = d_gate.astype(jnp.bfloat16)
    d_up = d_up.astype(jnp.bfloat16)
    d_normed_two = over_cols(d_gate, full_gate) + over_cols(d_up, full_up)
    grad_gate, grad_up = (
        lax.psum_scatter(
            over_rows(normed_two, d_gate), ("grp", "blk"), scatter_dimension=1, tiled=True
        ),
        lax.psum_scatter(
            over_rows(normed_two, d_up), ("grp", "blk"), scatter_dimension=1, tiled=True
        ),
    )
    _, norm_back_two = jax.vjp(rms_norm, residual, gain_two)
    d_residual_norm, d_gain_two = norm_back_two(d_normed_two)
    d_residual = upstream + d_residual_norm
    d_branch_attn = (RESID_MULT * d_residual).astype(jnp.bfloat16)
    grad_out = over_rows(attended, d_branch_attn)
    d_attended = over_cols(d_branch_attn, out_full).astype(jnp.bfloat16)
    d_heads = d_attended.reshape(blocks_here, BLOCK, KV_HEADS, per_group, HEAD_DIM)
    soft_exact = jnp.exp(scores_of() - log_norm)
    d_all_values = jnp.einsum(
        "nkgqs,nqkgd->nskd",
        soft_exact.astype(jnp.bfloat16),
        d_heads,
        preferred_element_type=jnp.float32,
    )
    d_soft = jnp.einsum(
        "nqkgd,nskd->nkgqs", d_heads, all_values, preferred_element_type=jnp.float32
    )
    d_scores = (
        soft_exact * (d_soft - jnp.sum(soft_exact * d_soft, axis=-1, keepdims=True))
    ).astype(jnp.bfloat16)
    d_queries = (
        (
            jnp.einsum("nkgqs,nskd->nqkgd", d_scores, all_keys, preferred_element_type=jnp.float32)
            * ATTN_MULT
        )
        .reshape(tok_rows, D)
        .astype(jnp.bfloat16)
    )
    d_all_keys = (
        jnp.einsum("nkgqs,nqkgd->nskd", d_scores, query_heads, preferred_element_type=jnp.float32)
        * ATTN_MULT
    )
    d_all_pairs = jnp.concatenate(
        [
            d_all_keys.reshape(blocks_here, key_count, pair_half),
            d_all_values.reshape(blocks_here, key_count, pair_half),
        ],
        axis=2,
    )
    prompt_terms = d_all_pairs[:, :prompt_len].reshape(
        blocks_here * PROMPT_BLOCKS, BLOCK, 2 * pair_half
    )
    row_terms = (
        jnp.zeros((row_blocks, BLOCK, 2 * pair_half), jnp.float32)
        .at[places.reshape(-1)]
        .add(prompt_terms)
    )
    returned = lax.psum_scatter(
        row_terms.reshape(row_blocks * BLOCK, 2 * pair_half).astype(jnp.bfloat16),
        "blk",
        scatter_dimension=0,
        tiled=True,
    ).astype(jnp.float32)
    d_pairs = (returned + d_all_pairs[:, prompt_len:].reshape(tok_rows, 2 * pair_half)).astype(
        jnp.bfloat16
    )
    d_key_rows = d_pairs[:, :pair_half]
    d_value_rows = d_pairs[:, pair_half:]
    grad_query = over_rows(normed_one, d_queries)
    grad_key = over_rows(normed_one, d_key_rows)
    grad_value = over_rows(normed_one, d_value_rows)
    d_normed_one = (
        over_cols(d_queries, query_full)
        + over_cols(d_key_rows, key_full)
        + over_cols(d_value_rows, value_full)
    )
    _, norm_back_one = jax.vjp(rms_norm, layer_in, gain_one)
    d_input_norm, d_gain_one = norm_back_one(d_normed_one)
    tokens_grad = (d_residual + d_input_norm).astype(jnp.bfloat16)
    grad_terms = (
        lax.psum_scatter(d_gain_one, ("grp", "blk"), scatter_dimension=0, tiled=True),
        lax.psum_scatter(grad_query, ("grp", "blk"), scatter_dimension=0, tiled=True),
        lax.psum_scatter(grad_key, ("grp", "blk"), scatter_dimension=0, tiled=True),
        lax.psum_scatter(grad_value, ("grp", "blk"), scatter_dimension=0, tiled=True),
        lax.psum_scatter(grad_out, ("grp", "blk"), scatter_dimension=0, tiled=True),
        lax.psum_scatter(d_gain_two, ("grp", "blk"), scatter_dimension=0, tiled=True),
    )
    scaled_attn = RESID_MULT * branch_attn
    scaled_mlp = RESID_MULT * branch_mlp
    squares = jnp.stack(
        [
            jnp.sum(layer_out * layer_out),
            jnp.sum(scaled_attn * scaled_attn),
            jnp.sum(scaled_mlp * scaled_mlp),
        ]
    )
    totals = lax.psum(squares, ("grp", "blk"))
    cell_count = tok_rows * lax.axis_size("grp") * lax.axis_size("blk") * D
    rms_stats = jnp.sqrt(totals / cell_count)
    return (
        layer_out.astype(jnp.bfloat16),
        tokens_grad,
        grad_terms[0],
        grad_terms[1],
        grad_terms[2],
        grad_terms[3],
        grad_terms[4],
        grad_terms[5],
        grad_gate,
        grad_up,
        grad_down,
        rms_stats,
    )


def solution(mesh):
    placed = (
        P(("grp", "blk"), None),
        P(),
        P(),
        P(("grp", "blk")),
        P(("grp", "blk"), None),
        P(("grp", "blk"), None),
        P(("grp", "blk"), None),
        P(("grp", "blk"), None),
        P(("grp", "blk")),
        P(None, ("grp", "blk")),
        P(None, ("grp", "blk")),
        P(("grp", "blk"), None),
        P(("grp", "blk"), None),
    )
    return jax.shard_map(
        on_device,
        mesh=mesh,
        in_specs=placed,
        out_specs=(
            P(("grp", "blk"), None),
            P(("grp", "blk"), None),
            P(("grp", "blk")),
            P(("grp", "blk"), None),
            P(("grp", "blk"), None),
            P(("grp", "blk"), None),
            P(("grp", "blk"), None),
            P(("grp", "blk")),
            P(None, ("grp", "blk")),
            P(None, ("grp", "blk")),
            P(("grp", "blk"), None),
            P(),
        ),
        check_vma=False,
    )
```

profile of v0, /device:TPU:0, one launch (start us, length us, event | category | flops | bytes accessed | tf_op | source)
XLA Modules:
  0.0 3983.0 jit_solution(13224011659086068885)
XLA Ops:
  10.4 42.1 %all-reduce.5 = (bf16[2048]{0:T(1024)(128)(2,1)S(1)}, bf16[2048]{0:T(1024)(128)(2,1)S(1)}) all-reduce(bf16[2048]{0:T(1024)(128)(2,1)S(1)} %dynamic-update-slice, bf16[2048]{0:T(1024)(128)(2,1)S(1)} %dynamic-update-slice.1), channel_id=1, replica_groups=mesh['grp'=4,'blk'=8] {'grp','blk'}, use_global_device_ids=true, to_apply=%add | all-reduce | flops 4096 | bytes 16384
  54.6 15.4 all-gather.11.cloned.1.call-done
  72.7 55.4 %all-gather.9.cloned.1.call-done = bf16[2048,512]{1,0:T(8,128)(2,1)} async-done(((bf16[64,512]{1,0:T(8,128)(2,1)}), bf16[2048,512]{1,0:T(8,128)(2,1)}) %all-gather.9.cloned.1.call-update) | async-done | bytes 2097168 | tf_op jit(solution)/shard_map/all_gather | solution.py:63
  139.3 27.8 all-gather.13.cloned.1.call-done
  182.1 65.2 %all-gather.15.cloned.1.call-done = bf16[2048,2048]{1,0:T(8,128)(2,1)} async-done(((bf16[64,2048]{1,0:T(8,128)(2,1)}), bf16[2048,2048]{1,0:T(8,128)(2,1)}) %all-gather.15.cloned.1.call-update) | async-done | bytes 8388624 | tf_op jit(solution)/shard_map/all_gather | solution.py:62
  263.5 15.5 fusion.62
  279.0 16.4 fusion.3
  295.4 16.9 fusion.26
  333.3 188.1 %all-gather.19.cloned.1.call-done = bf16[2048,8192]{1,0:T(8,128)(2,1)} async-done(((bf16[2048,256]{1,0:T(8,128)(2,1)}), bf16[2048,8192]{1,0:T(8,128)(2,1)}) %all-gather.19.cloned.1.call-update) | async-done | bytes 33554448 | tf_op jit(solution)/shard_map/all_gather | solution.py:145
  521.4 17.7 fusion.63
  539.0 176.4 %all-gather.21.cloned.1.call-done = bf16[2048,8192]{1,0:T(8,128)(2,1)} async-done(((bf16[2048,256]{1,0:T(8,128)(2,1)}), bf16[2048,8192]{1,0:T(8,128)(2,1)}) %all-gather.21.cloned.1.call-update) | async-done | bytes 33554448 | tf_op jit(solution)/shard_map/all_gather | solution.py:146
  715.4 17.7 fusion.64
  733.1 178.5 %all-gather.23.cloned.1.call-done = bf16[8192,2048]{1,0:T(8,128)(2,1)} async-done(((bf16[256,2048]{1,0:T(8,128)(2,1)}), bf16[8192,2048]{1,0:T(8,128)(2,1)}) %all-gather.23.cloned.1.call-update) | async-done | bytes 33554448 | tf_op jit(solution)/shard_map/all_gather | solution.py:147
  911.7 24.4 multiply_convert_fusion
  936.0 16.9 fusion.65
  952.9 17.8 convolution_add_fusion.2
  970.7 18.7 multiply_reduce_fusion.2
  1003.8 27.7 fusion
  1031.5 16.9 fusion.5
  1054.5 31.4 fusion.2
  1114.2 18.5 scatter_fusion
  1140.2 48.2 %reduce-scatter.9.cloned.1.call-done = bf16[256,1024]{1,0:T(8,128)(2,1)} async-done(((bf16[2048,1024]{1,0:T(8,128)(2,1)}), bf16[256,1024]{1,0:T(8,128)(2,1)}) %reduce-scatter.9.cloned.1.call-update) | async-done | bytes 524304 | tf_op jit(solution)/shard_map/reduce_scatter | solution.py:225
  1228.0 26.5 fusion.66
  1254.7 26.5 fusion.67
  1281.3 26.5 fusion.35
  1320.0 40.0 %all-reduce.4 = (f32[2048]{0:T(1024)S(1)}, f32[2048]{0:T(1024)S(1)}, f32[3]{0:T(128)S(1)}) all-reduce(f32[2048]{0:T(1024)S(1)} %get-tuple-element.14, f32[2048]{0:T(1024)S(1)} %copy-done.24, f32[3]{0:T(128)S(1)} %pad_maximum_fusion.3), channel_id=3, replica_groups=mesh['grp'=4,'blk'=8] {'grp','blk'}, use_global_device_ids=true, to_apply=%region_11.12.clone | all-reduce | flops 4099 | bytes 32792
  1364.9 108.9 %reduce-scatter.15.cloned.1.call-done = f32[64,512]{1,0:T(8,128)} async-done(((f32[2048,512]{1,0:T(8,128)}), f32[64,512]{1,0:T(8,128)}) %reduce-scatter.15.cloned.1.call-update) | async-done | bytes 131088 | tf_op jit(solution)/shard_map/reduce_scatter | solution.py:251
  1473.7 181.5 %reduce-scatter.11.cloned.1.call-done = f32[64,2048]{1,0:T(8,128)} async-done(((f32[2048,2048]{1,0:T(8,128)}), f32[64,2048]{1,0:T(8,128)}) %reduce-scatter.11.cloned.1.call-update) | async-done | bytes 524304 | tf_op jit(solution)/shard_map/reduce_scatter | solution.py:249
  1655.2 187.5 %reduce-scatter.17.cloned.1.call-done = f32[64,2048]{1,0:T(8,128)} async-done(((f32[2048,2048]{1,0:T(8,128)}), f32[64,2048]{1,0:T(8,128)}) %reduce-scatter.17.cloned.1.call-update) | async-done | bytes 524304 | tf_op jit(solution)/shard_map/reduce_scatter | solution.py:252
  1842.7 707.2 %reduce-scatter.19.cloned.1.call-done = f32[2048,256]{1,0:T(8,128)} async-done(((f32[2048,8192]{1,0:T(8,128)}), f32[2048,256]{1,0:T(8,128)}) %reduce-scatter.19.cloned.1.call-update) | async-done | bytes 2097168 | tf_op jit(solution)/shard_map/reduce_scatter | solution.py:171
  2549.9 713.2 %reduce-scatter.21.cloned.1.call-done = f32[2048,256]{1,0:T(8,128)} async-done(((f32[2048,8192]{1,0:T(8,128)}), f32[2048,256]{1,0:T(8,128)}) %reduce-scatter.21.cloned.1.call-update) | async-done | bytes 2097168 | tf_op jit(solution)/shard_map/reduce_scatter | solution.py:174
  3263.1 713.2 %reduce-scatter.23.cloned.1.call-done = f32[256,2048]{1,0:T(8,128)} async-done(((f32[8192,2048]{1,0:T(8,128)}), f32[256,2048]{1,0:T(8,128)}) %reduce-scatter.23.cloned.1.call-update) | async-done | bytes 2097168 | tf_op jit(solution)/shard_map/reduce_scatter | solution.py:162
  (158 shorter events, 184.1 us)
Async XLA Ops:
  7.2 121.0 %copy-start = (bf16[256,2048]{1,0:T(8,128)(2,1)S(1)}, bf16[256,2048]{1,0:T(8,128)(2,1)}, u32[]{:S(2)}) copy-start(bf16[256,2048]{1,0:T(8,128)(2,1)} %param.13) | copy-start | bytes 3145732
  7.2 62.8 %all-gather.11.cloned.1.call-start = ((), (), s32[]{:S(2)}) async-start(), calls=%async_computation.9 | async-start | bytes 2162688 | tf_op jit(solution)/shard_map/all_gather | solution.py:64
  7.9 120.2 %all-gather.9.cloned.1.call-start = ((), (), s32[]{:S(2)}) async-start(), calls=%async_computation.8 | async-start | bytes 2162688 | tf_op jit(solution)/shard_map/all_gather | solution.py:63
  8.7 158.5 %all-gather.13.cloned.1.call-start = ((), (), s32[]{:S(2)}) async-start(), calls=%async_computation.10 | async-start | bytes 4718592 | tf_op jit(solution)/shard_map/all_gather | solution.py:108
  52.6 194.8 %copy-start.18 = (f32[2048]{0:T(1024)}, f32[2048]{0:T(1024)S(1)}, u32[]{:S(2)}) copy-start(f32[2048]{0:T(1024)S(1)} %convert_element_type.91) | copy-start | bytes 24580
  54.6 192.8 %copy-start.20 = (f32[256]{0:T(256)}, f32[256]{0:T(256)S(1)}, u32[]{:S(2)}) copy-start(f32[256]{0:T(256)S(1)} %fusion.49) | copy-start | bytes 3076
  72.7 62.4 %copy-start.28 = (s32[64]{0:T(128)S(1)}, s32[64]{0:T(128)}, u32[]{:S(2)}) copy-start(s32[64]{0:T(128)} %param.15) | copy-start | bytes 772
  72.7 62.5 %copy-start.27 = (s32[64]{0:T(128)S(1)}, s32[64]{0:T(128)}, u32[]{:S(2)}) copy-start(s32[64]{0:T(128)} %param.14) | copy-start | bytes 772
  131.4 7.0 copy-start.12
  131.4 116.0 %all-gather.15.cloned.1.call-start = ((), (), s32[]{:S(2)}) async-start(), calls=%async_computation.11 | async-start | bytes 8650752 | tf_op jit(solution)/shard_map/all_gather | solution.py:62
  132.0 194.0 %all-gather.17.cloned.1.call-start = ((), (), s32[]{:S(2)}) async-start(), calls=%async_computation.12 | async-start | bytes 8650752 | tf_op jit(solution)/shard_map/all_gather | solution.py:65
  132.6 388.8 %all-gather.19.cloned.1.call-start = ((), (), s32[]{:S(2)}) async-start(), calls=%async_computation.13 | async-start | bytes 34603008 | tf_op jit(solution)/shard_map/all_gather | solution.py:145
  133.1 582.3 %all-gather.21.cloned.1.call-start = ((), (), s32[]{:S(2)}) async-start(), calls=%async_computation.14 | async-start | bytes 34603008 | tf_op jit(solution)/shard_map/all_gather | solution.py:146
  133.9 777.8 %all-gather.23.cloned.1.call-start = ((), (), s32[]{:S(2)}) async-start(), calls=%async_computation.15 | async-start | bytes 34603008 | tf_op jit(solution)/shard_map/all_gather | solution.py:147
  134.6 1053.7 %reduce-scatter.9.cloned.1.call-start = ((), (), s32[]{:S(2)}) async-start(), calls=%async_computation.16 | async-start | bytes 4718592 | tf_op jit(solution)/shard_map/reduce_scatter | solution.py:225
  182.1 81.4 %copy-start.2 = (bf16[2,1152,512]{1,2,0:T(8,128)(2,1)}, bf16[2,1152,512]{1,2,0:T(8,128)(2,1)S(1)}, u32[]{:S(2)}) copy-start(bf16[2,1152,512]{1,2,0:T(8,128)(2,1)S(1)} %get-tuple-element.30) | copy-start | bytes 7077892
  279.0 16.4 copy-start.6
  333.3 382.1 %copy-start.9 = (bf16[256,2048]{1,0:T(8,128)(2,1)}, bf16[256,2048]{1,0:T(8,128)(2,1)S(1)}, u32[]{:S(2)}) copy-start(bf16[256,2048]{1,0:T(8,128)(2,1)S(1)} %multiply_convert_fusion.4) | copy-start | bytes 3145732
  970.7 18.7 copy-start.13
  970.7 18.7 copy-start.16
  1054.5 31.4 copy-start.8
  1138.7 50.9 %copy-start.1 = (bf16[256,2048]{1,0:T(8,128)(2,1)S(1)}, bf16[256,2048]{1,0:T(8,128)(2,1)}, u32[]{:S(2)}) copy-start(bf16[256,2048]{1,0:T(8,128)(2,1)} %param.13) | copy-start | bytes 3145732
  1138.8 50.9 %copy-start.19 = (f32[2048]{0:T(1024)S(1)}, f32[2048]{0:T(1024)}, u32[]{:S(2)}) copy-start(f32[2048]{0:T(1024)} %copy-done.18) | copy-start | bytes 24580
  1138.8 50.9 %copy-start.21 = (f32[256]{0:T(256)S(1)}, f32[256]{0:T(256)}, u32[]{:S(2)}) copy-start(f32[256]{0:T(256)} %copy-done.20) | copy-start | bytes 3076
  1138.8 226.1 %reduce-scatter.13.cloned.1.call-start = ((), (), s32[]{:S(2)}) async-start(), calls=%async_computation.18 | async-start | bytes 4325376 | tf_op jit(solution)/shard_map/reduce_scatter | solution.py:250
  1192.4 281.3 %reduce-scatter.15.cloned.1.call-start = ((), (), s32[]{:S(2)}) async-start(), calls=%async_computation.19 | async-start | bytes 4325376 | tf_op jit(solution)/shard_map/reduce_scatter | solution.py:251
  1195.3 459.9 %reduce-scatter.11.cloned.1.call-start = ((), (), s32[]{:S(2)}) async-start(), calls=%async_computation.17 | async-start | bytes 17301504 | tf_op jit(solution)/shard_map/reduce_scatter | solution.py:249
  1217.0 625.7 %reduce-scatter.17.cloned.1.call-start = ((), (), s32[]{:S(2)}) async-start(), calls=%async_computation.20 | async-start | bytes 17301504 | tf_op jit(solution)/shard_map/reduce_scatter | solution.py:252
  1228.0 1321.9 %reduce-scatter.19.cloned.1.call-start = ((), (), s32[]{:S(2)}) async-start(), calls=%async_computation.21 | async-start | bytes 69206016 | tf_op jit(solution)/shard_map/reduce_scatter | solution.py:171
  1254.5 2008.6 %reduce-scatter.21.cloned.1.call-start = ((), (), s32[]{:S(2)}) async-start(), calls=%async_computation.22 | async-start | bytes 69206016 | tf_op jit(solution)/shard_map/reduce_scatter | solution.py:174
  1281.2 2695.0 %reduce-scatter.23.cloned.1.call-start = ((), (), s32[]{:S(2)}) async-start(), calls=%async_computation.23 | async-start | bytes 69206016 | tf_op jit(solution)/shard_map/reduce_scatter | solution.py:162
  1317.7 44.0 %copy-start.23 = (f32[256]{0:T(256)S(1)}, f32[256]{0:T(256)}, u32[]{:S(2)}) copy-start(f32[256]{0:T(256)} %copy-done.22) | copy-start | bytes 3076
  (13 other events, 36.9 us)
Sparse Core Ops, SparseCore 0:
  10.9 59.1 all-gather.10
  72.9 55.2 all-gather.8
  131.5 35.6 all-gather.12
  169.9 77.4 all-gather.14
  250.1 75.8 all-gather.16
  327.3 194.0 all-gather.18
  522.9 192.4 all-gather.20
  718.3 193.3 all-gather.22
  1138.9 49.4 reduce-scatter.8
  1192.6 141.0 reduce-scatter.12
  1336.6 137.0 reduce-scatter.14
  1476.5 178.5 reduce-scatter.10
  1658.2 184.4 reduce-scatter.16
  1845.6 704.2 reduce-scatter.18
  2552.8 710.2 reduce-scatter.20
  3266.0 710.2 reduce-scatter.22
where the time goes:
time: 3990 us; the launch traced here: 3980 us
  waiting for transfers between devices  3380 us (85%)
  matrix products  348 us (9%)
  other arithmetic  96 us (2%)
  blocking collectives  82.1 us (2%)
  local copies, waits for them, and re-layouts  59.2 us (1%)
    reduce_scatter x1, waiting for transfers between devices, on_device(): lax.psum_scatter(over_rows(hidden, d_branch_mlp), ('grp', 'blk'), scatter...  713 us
    reduce_scatter x1, waiting for transfers between devices, on_device(): lax.psum_scatter(over_rows(normed_two, d_up), ('grp', 'blk'), scatter_dim...  713 us
    reduce_scatter x1, waiting for transfers between devices, on_device(): lax.psum_scatter(over_rows(normed_two, d_gate), ('grp', 'blk'), scatter_d...  707 us
    all_gather x1, waiting for transfers between devices, on_device(): lax.all_gather(w_gate, ('grp', 'blk'), axis=1, tiled=True)  188 us
    reduce_scatter x1, waiting for transfers between devices, on_device(): lax.psum_scatter(grad_out, ('grp', 'blk'), scatter_dimension=0, tiled=True)  187 us
    reduce_scatter x1, waiting for transfers between devices, on_device(): lax.psum_scatter(grad_query, ('grp', 'blk'), scatter_dimension=0, tiled=T...  181 us
    all_gather x1, waiting for transfers between devices, on_device(): lax.all_gather(w_down, ('grp', 'blk'), axis=0, tiled=True)  179 us
    all_gather x1, waiting for transfers between devices, on_device(): lax.all_gather(w_up, ('grp', 'blk'), axis=1, tiled=True)  176 us
  transfers between devices with their start and end apart: 16, of which 15 were waited for; matrix products, arithmetic and copies ran while one was open for 7% of the time, Pallas kernels for 0%

commit v1 on v0

v1 whole, which is shorter than its diff:
```python
import jax
import jax.numpy as jnp
from jax import lax
from jax.sharding import Mesh
from jax.sharding import PartitionSpec as P

D = 2048
HEADS = 32
KV_HEADS = 8
HEAD_DIM = 64
BLOCK = 128
PROMPT_BLOCKS = 8
GROUP_BLOCKS = 16
PER_GROUP = HEADS // KV_HEADS

ATTN_MULT = 0.015625
RESID_MULT = 0.22
EPSILON = 1e-05
MASKED = -1e30

PLANE = ("chip", "core")
EVERY = ("grp", "chip", "core")
BF16 = jnp.bfloat16
F32 = jnp.float32


def matmul(left, right):
    return jnp.dot(left, right, preferred_element_type=F32)


def over_rows(left, right):
    return lax.dot_general(left, right, (((0,), (0,)), ((), ())), preferred_element_type=F32)


def over_cols(left, right):
    return lax.dot_general(left, right, (((1,), (1,)), ((), ())), preferred_element_type=F32)


def gather(values, axes, axis=0):
    return lax.all_gather(values, axes, axis=axis, tiled=True)


def scatter(values, axes, axis=0):
    return lax.psum_scatter(values, axes, scatter_dimension=axis, tiled=True)


def norm_parts(values):
    factor = lax.rsqrt(jnp.mean(values * values, axis=-1, keepdims=True) + EPSILON)
    return factor


def norm_back(values, factor, gain, grad):
    scaled = gain * grad
    inner = jnp.mean(values * scaled, axis=-1, keepdims=True)
    return factor * scaled - values * (factor * factor * factor * inner), jnp.sum(
        grad * values * factor, axis=0
    )


def on_device(
    tokens,
    block_group,
    block_slot,
    attn_gain,
    w_query,
    w_key,
    w_value,
    w_out,
    mlp_gain,
    w_gate,
    w_up,
    w_down,
    cotangent,
):
    tok_axes, weight_axes = TOK_AXES, WEIGHT_AXES
    grps = lax.axis_size("grp")
    devs = lax.axis_size(PLANE)
    rows = tokens.shape[0]
    w_rows = w_query.shape[0]
    q_heads = HEADS // devs
    kv_heads = max(1, KV_HEADS // devs)
    kv_copies = max(1, devs // KV_HEADS)
    q_cols, kv_cols = q_heads * HEAD_DIM, kv_heads * HEAD_DIM
    row_blocks = rows // BLOCK * devs
    row_groups = row_blocks // GROUP_BLOCKS

    row_first = lax.axis_index("grp") * row_blocks
    keys = lax.dynamic_slice_in_dim(block_group, row_first, row_blocks) * GROUP_BLOCKS
    keys = keys + lax.dynamic_slice_in_dim(block_slot, row_first, row_blocks)
    rank = jnp.sum((keys[None, :] < keys[:, None]).astype(jnp.int32), axis=1)
    ids = jnp.arange(row_blocks, dtype=jnp.int32)
    order = jnp.sum(jnp.where(rank[None, :] == ids[:, None], ids[None, :], 0), axis=1)

    def kv_split(w):
        w = w.reshape(w_rows, devs // kv_copies, kv_cols)
        return jnp.repeat(w, kv_copies, axis=1) if kv_copies > 1 else w

    gains = jnp.stack([attn_gain, mlp_gain], axis=1)
    gains = jnp.broadcast_to(
        jnp.pad(gains, ((0, 0), (0, 126)))[:, None, :], (w_rows, devs, 128)
    )
    packed = jnp.concatenate(
        [w_query.reshape(w_rows, devs, q_cols), kv_split(w_key), kv_split(w_value), gains], axis=2
    )
    packed = lax.all_to_all(packed, PLANE, split_axis=1, concat_axis=0, tiled=True)
    packed = gather(packed.reshape(devs * w_rows, q_cols + 2 * kv_cols + 128), "grp")
    w_qkv = packed[:, : q_cols + 2 * kv_cols]
    gain_one = packed[:, q_cols + 2 * kv_cols].astype(F32)
    gain_two = packed[:, q_cols + 2 * kv_cols + 1].astype(F32)

    all_tokens = gather(tokens, PLANE)
    layer_all = all_tokens.astype(F32)
    normed_one = (layer_all * norm_parts(layer_all) * gain_one).astype(BF16)
    qkv = matmul(normed_one, w_qkv).astype(BF16)
    qkv = qkv.reshape(row_blocks, BLOCK, q_cols + 2 * kv_cols)[order]
    qkv = qkv.reshape(row_groups, GROUP_BLOCKS * BLOCK, q_cols + 2 * kv_cols)
    seq = GROUP_BLOCKS * BLOCK
    per_kv = q_heads // kv_heads
    q = qkv[:, :, :q_cols].reshape(row_groups, seq, kv_heads, per_kv, HEAD_DIM)
    k = qkv[:, :, q_cols : q_cols + kv_cols].reshape(row_groups, seq, kv_heads, HEAD_DIM)
    v = qkv[:, :, q_cols + kv_cols :].reshape(row_groups, seq, kv_heads, HEAD_DIM)
    prompt = PROMPT_BLOCKS * BLOCK
    row_id = jnp.arange(seq)
    q_b = q.reshape(row_groups, GROUP_BLOCKS, BLOCK, kv_heads, per_kv, HEAD_DIM)
    k_b = k.reshape(row_groups, GROUP_BLOCKS, BLOCK, kv_heads, HEAD_DIM)
    v_b = v.reshape(row_groups, GROUP_BLOCKS, BLOCK, kv_heads, HEAD_DIM)
    k_p, v_p = k[:, :prompt], v[:, :prompt]
    starts = jnp.minimum(jnp.arange(GROUP_BLOCKS), PROMPT_BLOCKS) * BLOCK
    see_p = jnp.arange(prompt)[None, :] < starts[:, None]
    see_o = jnp.arange(BLOCK)[None, :] <= jnp.arange(BLOCK)[:, None]

    def all_scores():
        far = jnp.einsum("gbikpd,gjkd->gbkpij", q_b, k_p, preferred_element_type=F32)
        far = jnp.where(see_p[None, :, None, None, None, :], far * ATTN_MULT, MASKED)
        own = jnp.einsum("gbikpd,gbjkd->gbkpij", q_b, k_b, preferred_element_type=F32)
        own = jnp.where(see_o[None, None, None, None, :, :], own * ATTN_MULT, MASKED)
        return far, own

    far, own = all_scores()
    peak = jnp.maximum(far.max(-1, keepdims=True), own.max(-1, keepdims=True))
    far, own = jnp.exp(far - peak), jnp.exp(own - peak)
    total = far.sum(-1, keepdims=True) + own.sum(-1, keepdims=True)
    far_p, own_p = far / total, own / total
    attended = jnp.einsum(
        "gbkpij,gjkd->gbikpd", far_p.astype(BF16), v_p, preferred_element_type=F32
    ) + jnp.einsum("gbkpij,gbjkd->gbikpd", own_p.astype(BF16), v_b, preferred_element_type=F32)
    attended = attended.astype(BF16).reshape(row_blocks, BLOCK, q_cols)[rank]
    attended = lax.all_to_all(
        attended.reshape(row_blocks * BLOCK, q_cols), PLANE, split_axis=0, concat_axis=1, tiled=True
    )

    out_full = gather(w_out, EVERY)
    layer_in = tokens.astype(F32)
    branch_attn = matmul(attended, out_full)
    residual = layer_in + RESID_MULT * branch_attn
    factor_two = norm_parts(residual)
    normed_two = gather((residual * factor_two * gain_two).astype(BF16), tok_axes)
    upstream = cotangent.astype(F32)
    d_branch_mlp = gather((RESID_MULT * upstream).astype(BF16), tok_axes)

    gate_w = gather(w_gate, weight_axes, axis=1)
    up_w = gather(w_up, weight_axes, axis=1)
    down_w = gather(w_down, weight_axes)
    gate_act = matmul(normed_two, gate_w)
    up_act = matmul(normed_two, up_w)
    sig = jax.nn.sigmoid(gate_act)
    silu = gate_act * sig
    hidden = (silu * up_act).astype(BF16)
    branch_mlp = scatter(matmul(hidden, down_w).astype(BF16), tok_axes).astype(F32)
    layer_out = residual + RESID_MULT * branch_mlp

    grad_down = scatter(over_rows(hidden, d_branch_mlp).astype(BF16), weight_axes).astype(F32)
    d_hidden = over_cols(d_branch_mlp, down_w)
    d_gate = (d_hidden * up_act * (sig * (1.0 + gate_act * (1.0 - sig)))).astype(BF16)
    d_up = (d_hidden * silu).astype(BF16)
    grad_gate = scatter(over_rows(normed_two, d_gate).astype(BF16), weight_axes, axis=1).astype(F32)
    grad_up = scatter(over_rows(normed_two, d_up).astype(BF16), weight_axes, axis=1).astype(F32)
    d_normed_two = over_cols(d_gate, gate_w) + over_cols(d_up, up_w)
    d_normed_two = scatter(d_normed_two.astype(BF16), tok_axes).astype(F32)

    d_residual_norm, d_gain_two = norm_back(residual, factor_two, gain_two, d_normed_two)
    d_residual = upstream + d_residual_norm
    d_branch_attn = (RESID_MULT * d_residual).astype(BF16)
    grad_out = scatter(over_rows(attended, d_branch_attn).astype(BF16), EVERY).astype(F32)
    d_attended = over_cols(d_branch_attn, out_full).astype(BF16)
    d_attended = lax.all_to_all(d_attended, PLANE, split_axis=1, concat_axis=0, tiled=True)
    d_b = d_attended.reshape(row_blocks, BLOCK, q_cols)[order]
    d_b = d_b.reshape(row_groups, GROUP_BLOCKS, BLOCK, kv_heads, per_kv, HEAD_DIM)

    far_s = jnp.einsum("gbikpd,gjkd->gbkpij", d_b, v_p, preferred_element_type=F32)
    own_s = jnp.einsum("gbikpd,gbjkd->gbkpij", d_b, v_b, preferred_element_type=F32)
    mean_s = (far_p * far_s).sum(-1, keepdims=True) + (own_p * own_s).sum(-1, keepdims=True)
    far_d = (far_p * (far_s - mean_s)).astype(BF16)
    own_d = (own_p * (own_s - mean_s)).astype(BF16)
    far_p, own_p = far_p.astype(BF16), own_p.astype(BF16)
    d_q = ATTN_MULT * (
        jnp.einsum("gbkpij,gjkd->gbikpd", far_d, k_p, preferred_element_type=F32)
        + jnp.einsum("gbkpij,gbjkd->gbikpd", own_d, k_b, preferred_element_type=F32)
    )
    d_k = jnp.einsum("gbkpij,gbikpd->gbjkd", own_d, q_b, preferred_element_type=F32)
    d_v = jnp.einsum("gbkpij,gbikpd->gbjkd", own_p, d_b, preferred_element_type=F32)
    d_kp = jnp.einsum("gbkpij,gbikpd->gjkd", far_d, q_b, preferred_element_type=F32)
    d_vp = jnp.einsum("gbkpij,gbikpd->gjkd", far_p, d_b, preferred_element_type=F32)
    d_k = ATTN_MULT * jnp.concatenate([d_k.reshape(row_groups, seq, kv_cols)[:, :prompt] + d_kp.reshape(row_groups, prompt, kv_cols), d_k.reshape(row_groups, seq, kv_cols)[:, prompt:]], axis=1)
    d_v = jnp.concatenate([d_v.reshape(row_groups, seq, kv_cols)[:, :prompt] + d_vp.reshape(row_groups, prompt, kv_cols), d_v.reshape(row_groups, seq, kv_cols)[:, prompt:]], axis=1)
    d_qkv = jnp.concatenate([d_q.reshape(row_groups, seq, q_cols), d_k, d_v], axis=2).astype(BF16)
    d_qkv = d_qkv.reshape(row_blocks, BLOCK, q_cols + 2 * kv_cols)[rank]
    d_qkv = d_qkv.reshape(row_blocks * BLOCK, q_cols + 2 * kv_cols)

    d_normed_one = scatter(over_cols(d_qkv, w_qkv).astype(BF16), PLANE).astype(F32)
    d_input_norm, d_gain_one = norm_back(layer_in, norm_parts(layer_in), gain_one, d_normed_one)
    tokens_grad = (d_residual + d_input_norm).astype(BF16)

    grad_qkv = over_rows(normed_one, d_qkv)
    d_gains = jnp.pad(jnp.stack([d_gain_one, d_gain_two], axis=1), ((0, 0), (0, 126)))
    sent = scatter(jnp.concatenate([grad_qkv, d_gains], axis=1).astype(BF16), "grp")
    sent = sent.reshape(devs, w_rows, q_cols + 2 * kv_cols + 128)
    sent = lax.all_to_all(sent, PLANE, split_axis=0, concat_axis=0, tiled=True).astype(F32)

    def kv_join(g):
        g = g.reshape(devs // kv_copies, kv_copies, w_rows, kv_cols)
        g = jnp.sum(g, axis=1) if kv_copies > 1 else g[:, 0]
        return jnp.swapaxes(g, 0, 1).reshape(w_rows, KV_HEADS * HEAD_DIM)

    grad_query = jnp.swapaxes(sent[:, :, :q_cols], 0, 1).reshape(w_rows, D)
    grad_key = kv_join(sent[:, :, q_cols : q_cols + kv_cols])
    grad_value = kv_join(sent[:, :, q_cols + kv_cols : q_cols + 2 * kv_cols])
    gains_sum = jnp.sum(sent[:, :, q_cols + 2 * kv_cols :], axis=0)

    scaled_attn = RESID_MULT * branch_attn
    scaled_mlp = RESID_MULT * branch_mlp
    squares = jnp.stack(
        [
            jnp.sum(layer_out * layer_out),
            jnp.sum(scaled_attn * scaled_attn),
            jnp.sum(scaled_mlp * scaled_mlp),
        ]
    )
    totals = lax.psum(squares, EVERY)
    rms_stats = jnp.sqrt(totals / (rows * grps * devs * D))
    return (
        layer_out.astype(BF16),
        tokens_grad,
        gains_sum[:, 0],
        grad_query,
        grad_key,
        grad_value,
        grad_out,
        gains_sum[:, 1],
        grad_gate,
        grad_up,
        grad_down,
        rms_stats,
    )


TOK_AXES, WEIGHT_AXES = PLANE, ("grp",)


def solution(mesh):
    shape = (mesh.shape["grp"], mesh.shape["blk"] // 2, 2)
    mesh = Mesh(mesh.devices.reshape(shape), EVERY)
    row, col, vec = P(EVERY, None), P(None, EVERY), P(EVERY)
    return jax.shard_map(
        on_device,
        mesh=mesh,
        in_specs=(row, P(), P(), vec, row, row, row, row, vec, col, col, row, row),
        out_specs=(row, row, vec, row, row, row, row, vec, col, col, row, P()),
        check_vma=False,
    )
```

time: 3990 us -> 1430 us (0.36)
  waiting for transfers between devices: 3380 us -> 899 us
  matrix products: 348 us -> 285 us
    reduce_scatter x8, waiting for transfers between devices: 2660 us -> 490 us  [scatter(): return lax.psum_scatter(values, axes, scatter_dimension=axis, tiled=True)]
    all_gather x8, waiting for transfers between devices: 717 us -> 405 us  [gather(): return lax.all_gather(values, axes, axis=axis, tiled=True)]
    unnamed x2 -> x0, blocking collectives: 82.1 us -> none
    all_to_all x0 -> x3, blocking collectives: none -> 51.3 us  [the longest x1 18.6 us: on_device(): lax.all_to_all(attended.reshape(row_blocks * BLOCK, q_cols), PLANE, split...]
    psum x0 -> x1, blocking collectives: none -> 44.4 us  [on_device(): totals = lax.psum(squares, EVERY)]
    dot_general x7 -> x5, matrix products: 103 us -> 58.6 us  [over_rows(): lax.dot_general(left, right, (((0,), (0,)), ((), ())), preferred_element_...]
    dot_general x13 -> x17, matrix products: 171 us -> 156 us  [the longest x5 56.9 us: matmul(): return jnp.dot(left, right, preferred_element_type=F32)]
  transfers between devices with their start and end apart: 16 -> 17, of which waited for: 15 -> 14; matrix products, arithmetic and copies ran while one was open for 7% -> 15% of each run, Pallas kernels for 0% -> 0%
where the time goes in v1:
time: 1430 us; the launch traced here: 1420 us
  waiting for transfers between devices  899 us (63%)
  matrix products  285 us (20%)
  blocking collectives  95.7 us (7%)
  other arithmetic  87.5 us (6%)
  local copies, waits for them, and re-layouts  29.8 us (2%)
  between operations  15.2 us (1%)
    reduce_scatter x8, waiting for transfers between devices, scatter(): return lax.psum_scatter(values, axes, scatter_dimension=axis, tiled=True)  490 us
    all_gather x8, waiting for transfers between devices, gather(): return lax.all_gather(values, axes, axis=axis, tiled=True)  405 us
    dot_general x5, matrix products, over_cols(): lax.dot_general(left, right, (((1,), (1,)), ((), ())), preferred_element_...  70.8 us
    dot_general x5, matrix products, over_rows(): lax.dot_general(left, right, (((0,), (0,)), ((), ())), preferred_element_...  58.6 us
    dot_general x5, matrix products, matmul(): return jnp.dot(left, right, preferred_element_type=F32)  56.9 us
    psum x1, blocking collectives, on_device(): totals = lax.psum(squares, EVERY)  44.4 us
    another operation x3, other arithmetic  33.2 us
  transfers between devices with their start and end apart: 17, of which 14 were waited for; matrix products, arithmetic and copies ran while one was open for 15% of the time, Pallas kernels for 0%

profile of v1, /device:TPU:0, one launch (start us, length us, event | category | flops | bytes accessed | tf_op | source)
XLA Modules:
  0.0 1417.4 jit_solution(8293760625746567301)
XLA Ops:
  11.4 14.8 %all_to_all.55 = bf16[64,8,512]{2,0,1:T(8,128)(2,1)} all-to-all(bf16[64,8,512]{2,0,1:T(8,128)(2,1)S(1)} %copy.186), channel_id=1, replica_groups=mesh['grp'=4,'chip'=4,'core'=2] {'chip','core'}, dimensions={1} | all-to-all | bytes 1048576 | tf_op jit(solution)/shard_map/all_to_all | solution.py:105
  28.9 42.7 %all-gather.11.cloned.1.call-done = bf16[2048,512]{1,0:T(8,128)(2,1)} async-done(((bf16[512,512]{1,0:T(8,128)(2,1)}), bf16[2048,512]{1,0:T(8,128)(2,1)}) %all-gather.11.cloned.1.call-update) | async-done | bytes 2097168 | tf_op jit(solution)/shard_map/all_gather | solution.py:40
  73.5 53.2 %all-gather.9.cloned.1.call-done = bf16[2048,2048]{1,0:T(8,128)(2,1)} async-done(((bf16[256,2048]{1,0:T(8,128)(2,1)}), bf16[2048,2048]{1,0:T(8,128)(2,1)}) %all-gather.9.cloned.1.call-update) | async-done | bytes 8388624 | tf_op jit(solution)/shard_map/all_gather | solution.py:40
  173.9 15.7 %fusion.42 = bf16[1,16,128,1,4,64]{2,5,4,1,3,0:T(8,128)(2,1)S(1)} fusion(f32[16,64,4,128]{3,1,2,0:T(8,128)S(1)} %fusion.45, bf16[1,2048,1,64]{1,3,2,0:T(8,128)(2,1)S(1)} %bitcast.311, f32[16,4,128]{2,1,0:T(4,128)S(1)} %add.138, f32[16,4,128]{2,1,0:T(4,128)S(1)} %max.8, f32[1024,16,128,4]{2,0,3,1:T(8,128)} %copy-done, ...), kind=kOutput, calls=%fused_computation.82 | convolution fusion | flops 1116733440 | bytes 36913152 | tf_op jit(solution)/shard_map/gbkpij,gjkd->gbikpd/dot_general | solution.py:144
  190.8 18.6 %all_to_all.56 = bf16[8,256,256]{2,1,0:T(8,128)(2,1)S(1)} all-to-all(bf16[8,256,256]{2,1,0:T(8,128)(2,1)S(1)} %bitcast.291), channel_id=1, replica_groups=mesh['grp'=4,'chip'=4,'core'=2] {'chip','core'}, dimensions={0} | all-to-all | bytes 2097152 | tf_op jit(solution)/shard_map/all_to_all | solution.py:148
  222.1 65.5 %all-gather.19.cloned.1.call-done = bf16[2048,1024]{1,0:T(8,128)(2,1)} async-done(((bf16[2048,256]{1,0:T(8,128)(2,1)}), bf16[2048,1024]{1,0:T(8,128)(2,1)}) %all-gather.19.cloned.1.call-update) | async-done | bytes 4194320 | tf_op jit(solution)/shard_map/all_gather | solution.py:40
  287.7 54.9 %all-gather.15.cloned.1.call-done = bf16[2048,2048]{1,0:T(8,128)(2,1)} async-done(((bf16[256,2048]{1,0:T(8,128)(2,1)}), bf16[2048,2048]{1,0:T(8,128)(2,1)}) %all-gather.15.cloned.1.call-update) | async-done | bytes 8388624 | tf_op jit(solution)/shard_map/all_gather | solution.py:40
  342.6 14.8 %fusion.94 = f32[2048,1024]{1,0:T(8,128)} fusion(bf16[2048,2048]{1,0:T(8,128)(2,1)} %all-gather.15.cloned.1.call-done, bf16[2048,1024]{1,0:T(8,128)(2,1)} %all-gather.19.cloned.1.call-done), kind=kOutput, calls=%fused_computation.166 | convolution fusion | flops 8589934592 | bytes 20971520 | tf_op jit(solution)/shard_map/dot_general | solution.py:28
  357.4 67.2 %all-gather.17.cloned.1.call-done = bf16[2048,1024]{1,0:T(8,128)(2,1)} async-done(((bf16[2048,256]{1,0:T(8,128)(2,1)}), bf16[2048,1024]{1,0:T(8,128)(2,1)}) %all-gather.17.cloned.1.call-update) | async-done | bytes 4194320 | tf_op jit(solution)/shard_map/all_gather | solution.py:40
  424.6 14.4 %fusion.93 = f32[2048,1024]{1,0:T(8,128)} fusion(bf16[2048,2048]{1,0:T(8,128)(2,1)} %all-gather.15.cloned.1.call-done, bf16[2048,1024]{1,0:T(8,128)(2,1)} %all-gather.17.cloned.1.call-done), kind=kOutput, calls=%fused_computation.165 | convolution fusion | flops 8589934592 | bytes 20971520 | tf_op jit(solution)/shard_map/dot_general | solution.py:28
  439.0 66.2 %all-gather.21.cloned.1.call-done = bf16[1024,2048]{1,0:T(8,128)(2,1)} async-done(((bf16[256,2048]{1,0:T(8,128)(2,1)}), bf16[1024,2048]{1,0:T(8,128)(2,1)}) %all-gather.21.cloned.1.call-update) | async-done | bytes 4194320 | tf_op jit(solution)/shard_map/all_gather | solution.py:40
  505.2 55.4 %all-gather.23.cloned.1.call-done = bf16[2048,2048]{1,0:T(8,128)(2,1)} async-done(((bf16[256,2048]{1,0:T(8,128)(2,1)}), bf16[2048,2048]{1,0:T(8,128)(2,1)}) %all-gather.23.cloned.1.call-update) | async-done | bytes 8388624 | tf_op jit(solution)/shard_map/all_gather | solution.py:40
  560.6 23.2 %multiply_convert_fusion = (bf16[2048,1024]{1,0:T(8,128)(2,1)}, bf16[2048,1024]{1,0:T(8,128)(2,1)}, bf16[2048,1024]{1,0:T(8,128)(2,1)}) fusion(f32[2048,1024]{1,0:T(8,128)} %fusion.93, f32[2048,1024]{1,0:T(8,128)} %fusion.94, bf16[2048,2048]{1,0:T(8,128)(2,1)} %all-gather.23.cloned.1.call-done, bf16[1024,2048]{1,0:T(8,128)(2,1)} %all-gather.21.cloned.1.call-done), kind=kOutput, calls=%fused_computation.26 | convolution fusion | flops 8621391872 | bytes 41943040 | tf_op jit(solution)/shard_map/dot_general | solution.py:36
  583.7 13.9 convolution_convert_fusion.2
  597.8 16.3 %fusion.95 = f32[2048,2048]{1,0:T(8,128)} fusion(bf16[2048,1024]{1,0:T(8,128)(2,1)} %get-tuple-element.24, bf16[2048,1024]{1,0:T(8,128)(2,1)} %all-gather.17.cloned.1.call-done), kind=kOutput, calls=%fused_computation.167 | convolution fusion | flops 8589934592 | bytes 25165824 | tf_op jit(solution)/shard_map/dot_general | solution.py:36
  614.1 16.1 %add_convert_fusion = bf16[2048,2048]{1,0:T(8,128)(2,1)} fusion(f32[2048,2048]{1,0:T(8,128)} %fusion.95, bf16[2048,1024]{1,0:T(8,128)(2,1)} %get-tuple-element.23, bf16[2048,1024]{1,0:T(8,128)(2,1)S(1)} %copy-done.41), kind=kOutput, calls=%fused_computation.24 | convolution fusion | flops 8598323200 | bytes 33554432 | tf_op jit(solution)/shard_map/dot_general | solution.py:36
  630.5 38.7 %reduce-scatter.9.cloned.1.call-done = bf16[256,2048]{1,0:T(8,128)(2,1)} async-done(((bf16[2048,2048]{1,0:T(8,128)(2,1)}), bf16[256,2048]{1,0:T(8,128)(2,1)}) %reduce-scatter.9.cloned.1.call-update) | async-done | bytes 1048592 | tf_op jit(solution)/shard_map/reduce_scatter | solution.py:44
  669.1 75.0 %reduce-scatter.11.cloned.1.call-done = bf16[256,2048]{1,0:T(8,128)(2,1)} async-done(((bf16[2048,2048]{1,0:T(8,128)(2,1)}), bf16[256,2048]{1,0:T(8,128)(2,1)}) %reduce-scatter.11.cloned.1.call-update) | async-done | bytes 1048592 | tf_op jit(solution)/shard_map/reduce_scatter | solution.py:44
  755.8 17.9 %all_to_all.57 = bf16[256,8,256]{2,0,1:T(8,128)(2,1)S(1)} all-to-all(bf16[256,8,256]{2,0,1:T(8,128)(2,1)S(1)} %bitcast.293), channel_id=1, replica_groups=mesh['grp'=4,'chip'=4,'core'=2] {'chip','core'}, dimensions={1} | all-to-all | bytes 2097152 | tf_op jit(solution)/shard_map/all_to_all | solution.py:186
  782.6 26.2 %fusion = (f32[16,4,128]{2,1,0:T(4,128)S(1)}, f32[1024,16,128,4]{2,0,3,1:T(8,128)}) fusion(f32[16,4,128]{2,1,0:T(4,128)S(1)} %copy-done.26, f32[16,4,128]{2,1,0:T(4,128)S(1)} %copy-done.22, f32[1024,16,128,4]{2,0,3,1:T(8,128)} %copy-done, pred[16,1024]{1,0:T(8,128)(4,1)S(1)} %copy-done.24, bf16[16,128,4,64]{1,3,2,0:T(8,128)(2,1)S(1)} %bitcast.316, ...), kind=kOutput, calls=%fused_computation.7 | convolution fusion | flops 1124065280 | bytes 68403200 | tf_op jit(solution)/shard_map/gbikpd,gjkd->gbkpij/dot_general | solution.py:190
  808.8 14.7 %fusion.65 = bf16[1,1024,64]{1,2,0:T(8,128)(2,1)S(1)} fusion(bf16[16,128,4,64]{1,3,2,0:T(8,128)(2,1)S(1)} %bitcast.317, f32[1,1024,64]{1,0,2:T(1,128)S(1)} %slice.91, f32[16,4,128]{2,1,0:T(4,128)S(1)} %copy-done.26, f32[16,4,128]{2,1,0:T(4,128)S(1)} %copy-done.22, f32[1024,16,128,4]{2,0,3,1:T(8,128)} %copy-done, pred[16,1024]{1,0:T(8,128)(4,1)S(1)} %copy-done.24), kind=kOutput, calls=%fused_computation.107 | convolution fusion | flops 1115815936 | bytes 35078144 | tf_op jit(solution)/shard_map/gbkpij,gbikpd->gjkd/dot_general | solution.py:203
  823.8 28.1 %fusion.9 = bf16[16,4,128,1024]{2,3,1,0:T(8,128)(2,1)} fusion(f32[1024,16,128,4]{2,0,3,1:T(8,128)} %get-tuple-element.41, f32[16,4,128]{2,1,0:T(4,128)S(1)} %add.149, f32[16,4,128]{2,1,0:T(4,128)S(1)} %copy-done.26, f32[16,4,128]{2,1,0:T(4,128)S(1)} %copy-done.22, f32[1024,16,128,4]{2,0,3,1:T(8,128)} %copy-done, pred[16,1024]{1,0:T(8,128)(4,1)S(1)} %copy-done.24), kind=kLoop, calls=%fused_computation.19 | loop fusion | flops 58720256 | bytes 84000768 | tf_op jit(solution)/shard_map/reshape.53
  869.0 10.9 fusion.61
  897.8 14.3 %convolution_convert_fusion.3 = bf16[1024,2048]{1,0:T(8,128)(2,1)} fusion(bf16[2048,1024]{1,0:T(8,128)(2,1)} %get-tuple-element.25, bf16[2048,2048]{1,0:T(8,128)(2,1)} %all-gather.23.cloned.1.call-done), kind=kOutput, calls=%fused_computation.46 | convolution fusion | flops 8592031744 | bytes 16777216 | tf_op jit(solution)/shard_map/dot_general | solution.py:32
  912.2 14.3 %convolution_convert_fusion.4 = bf16[2048,1024]{1,0:T(8,128)(2,1)} fusion(bf16[2048,2048]{1,0:T(8,128)(2,1)} %all-gather.15.cloned.1.call-done, bf16[2048,1024]{1,0:T(8,128)(2,1)} %get-tuple-element.23), kind=kOutput, calls=%fused_computation.47 | convolution fusion | flops 8592031744 | bytes 16777216 | tf_op jit(solution)/shard_map/dot_general | solution.py:32
  926.5 14.5 %convolution_convert_fusion.5 = bf16[2048,1024]{1,0:T(8,128)(2,1)} fusion(bf16[2048,2048]{1,0:T(8,128)(2,1)} %all-gather.15.cloned.1.call-done, bf16[2048,1024]{1,0:T(8,128)(2,1)} %get-tuple-element.24), kind=kOutput, calls=%fused_computation.48 | convolution fusion | flops 8592031744 | bytes 16777216 | tf_op jit(solution)/shard_map/dot_general | solution.py:32
  951.1 17.2 %reduce-scatter.13.cloned.1.call-done = bf16[256,2048]{1,0:T(8,128)(2,1)} async-done(((bf16[2048,2048]{1,0:T(8,128)(2,1)}), bf16[256,2048]{1,0:T(8,128)(2,1)}) %reduce-scatter.13.cloned.1.call-update) | async-done | bytes 1048592 | tf_op jit(solution)/shard_map/reduce_scatter | solution.py:44
  980.5 66.9 %reduce-scatter.23.cloned.1.call-done = bf16[256,2048]{1,0:T(8,128)(2,1)} async-done(((bf16[1024,2048]{1,0:T(8,128)(2,1)}), bf16[256,2048]{1,0:T(8,128)(2,1)}) %reduce-scatter.23.cloned.1.call-update) | async-done | bytes 1048592 | tf_op jit(solution)/shard_map/reduce_scatter | solution.py:44
  1050.1 76.8 %reduce-scatter.21.cloned.1.call-done = bf16[2048,256]{1,0:T(8,128)(2,1)} async-done(((bf16[2048,1024]{1,0:T(8,128)(2,1)}), bf16[2048,256]{1,0:T(8,128)(2,1)}) %reduce-scatter.21.cloned.1.call-update) | async-done | bytes 1048592 | tf_op jit(solution)/shard_map/reduce_scatter | solution.py:44
  1131.7 74.8 %reduce-scatter.19.cloned.1.call-done = bf16[2048,256]{1,0:T(8,128)(2,1)} async-done(((bf16[2048,1024]{1,0:T(8,128)(2,1)}), bf16[2048,256]{1,0:T(8,128)(2,1)}) %reduce-scatter.19.cloned.1.call-update) | async-done | bytes 1048592 | tf_op jit(solution)/shard_map/reduce_scatter | solution.py:44
  1209.2 44.4 %psum.7 = f32[3]{0:T(128)S(1)} all-reduce(f32[3]{0:T(128)S(1)} %pad_maximum_fusion.5), channel_id=1, replica_groups=mesh['grp'=4,'chip'=4,'core'=2] {'grp','chip','core'}, use_global_device_ids=true, to_apply=%region_27.28 | all-reduce | flops 3 | bytes 24 | tf_op jit(solution)/shard_map/psum | solution.py:239
  1263.1 140.9 %reduce-scatter.17.cloned.1.call-done = bf16[64,2048]{1,0:T(8,128)(2,1)} async-done(((bf16[2048,2048]{1,0:T(8,128)(2,1)}), bf16[64,2048]{1,0:T(8,128)(2,1)}) %reduce-scatter.17.cloned.1.call-update) | async-done | bytes 262160 | tf_op jit(solution)/shard_map/reduce_scatter | solution.py:44
  (222 shorter events, 173.7 us)
Async XLA Ops:
  7.2 21.2 %copy-start.39 = (s32[64]{0:T(128)S(1)}, s32[64]{0:T(128)}, u32[]{:S(2)}) copy-start(s32[64]{0:T(128)} %param.15) | copy-start | bytes 772
  7.2 21.2 %copy-start.40 = (s32[64]{0:T(128)S(1)}, s32[64]{0:T(128)}, u32[]{:S(2)}) copy-start(s32[64]{0:T(128)} %param.14) | copy-start | bytes 772
  7.2 64.5 %all-gather.11.cloned.1.call-start = ((), (), s32[]{:S(2)}) async-start(), calls=%async_computation.13 | async-start | bytes 2621440 | tf_op jit(solution)/shard_map/all_gather | solution.py:40
  26.2 100.5 %all-gather.9.cloned.1.call-start = ((), (), s32[]{:S(2)}) async-start(), calls=%async_computation.12 | async-start | bytes 9437184 | tf_op jit(solution)/shard_map/all_gather | solution.py:40
  27.0 183.7 %all-gather.13.cloned.1.call-start = ((), (), s32[]{:S(2)}) async-start(), calls=%async_computation.14 | async-start | bytes 8650752 | tf_op jit(solution)/shard_map/all_gather | solution.py:40
  27.7 260.0 %all-gather.19.cloned.1.call-start = ((), (), s32[]{:S(2)}) async-start(), calls=%async_computation.17 | async-start | bytes 5242880 | tf_op jit(solution)/shard_map/all_gather | solution.py:40
  28.3 314.3 %all-gather.15.cloned.1.call-start = ((), (), s32[]{:S(2)}) async-start(), calls=%async_computation.15 | async-start | bytes 9437184 | tf_op jit(solution)/shard_map/all_gather | solution.py:40
  28.8 143.8 %copy-start.29 = (pred[128,128]{0,1:T(8,128)(4,1)}, pred[128,128]{0,1:T(8,128)(4,1)S(1)}, u32[]{:S(2)}) copy-start(pred[128,128]{0,1:T(8,128)(4,1)S(1)} %iota_compare_fusion.1) | copy-start | bytes 49156
  28.8 109.9 %copy-start.38 = (s32[1024]{0:T(1024)}, s32[1024]{0:T(1024)S(1)}, u32[]{:S(2)}) copy-start(s32[1024]{0:T(1024)S(1)} %pad_clamp_fusion.1) | copy-start | bytes 12292
  28.8 161.3 %copy-start.37 = (s32[1024]{0:T(1024)}, s32[1024]{0:T(1024)S(1)}, u32[]{:S(2)}) copy-start(s32[1024]{0:T(1024)S(1)} %pad_clamp_fusion) | copy-start | bytes 12292
  28.9 144.9 %copy-start.23 = (pred[16,1024]{1,0:T(8,128)(4,1)}, pred[16,1024]{1,0:T(8,128)(4,1)S(1)}, u32[]{:S(2)}) copy-start(pred[16,1024]{1,0:T(8,128)(4,1)S(1)} %iota_compare_fusion.2) | copy-start | bytes 49156
  73.5 58.5 %copy-start.31 = (f32[2048]{0:T(1024)}, f32[2048]{0:T(1024)S(1)}, u32[]{:S(2)}) copy-start(f32[2048]{0:T(1024)S(1)} %get-tuple-element.18) | copy-start | bytes 24580
  156.8 17.1 %copy-start.21 = (f32[16,4,128]{2,1,0:T(4,128)}, f32[16,4,128]{2,1,0:T(4,128)S(1)}, u32[]{:S(2)}) copy-start(f32[16,4,128]{2,1,0:T(4,128)S(1)} %max.8) | copy-start | bytes 98308
  189.6 21.1 %copy-start.7 = (bf16[256,2048]{1,0:T(8,128)(2,1)S(1)}, bf16[256,2048]{1,0:T(8,128)(2,1)}, u32[]{:S(2)}) copy-start(bf16[256,2048]{1,0:T(8,128)(2,1)} %param.13) | copy-start | bytes 3145732
  219.5 205.1 %all-gather.17.cloned.1.call-start = ((), (), s32[]{:S(2)}) async-start(), calls=%async_computation.16 | async-start | bytes 5242880 | tf_op jit(solution)/shard_map/all_gather | solution.py:40
  220.1 285.1 %all-gather.21.cloned.1.call-start = ((), (), s32[]{:S(2)}) async-start(), calls=%async_computation.18 | async-start | bytes 5242880 | tf_op jit(solution)/shard_map/all_gather | solution.py:40
  220.8 339.7 %all-gather.23.cloned.1.call-start = ((), (), s32[]{:S(2)}) async-start(), calls=%async_computation.20 | async-start | bytes 9437184 | tf_op jit(solution)/shard_map/all_gather | solution.py:40
  222.1 447.0 %reduce-scatter.9.cloned.1.call-start = ((), (), s32[]{:S(2)}) async-start(), calls=%async_computation.19 | async-start | bytes 9437184 | tf_op jit(solution)/shard_map/reduce_scatter | solution.py:44
  597.7 146.4 %reduce-scatter.11.cloned.1.call-start = ((), (), s32[]{:S(2)}) async-start(), calls=%async_computation.21 | async-start | bytes 9437184 | tf_op jit(solution)/shard_map/reduce_scatter | solution.py:44
  597.8 16.4 %copy-start.41 = (bf16[2048,1024]{1,0:T(8,128)(2,1)S(1)}, bf16[2048,1024]{1,0:T(8,128)(2,1)}, u32[]{:S(2)}) copy-start(bf16[2048,1024]{1,0:T(8,128)(2,1)} %all-gather.19.cloned.1.call-done) | copy-start | bytes 12582916
  630.2 338.1 %reduce-scatter.13.cloned.1.call-start = ((), (), s32[]{:S(2)}) async-start(), calls=%async_computation.22 | async-start | bytes 9437184 | tf_op jit(solution)/shard_map/reduce_scatter | solution.py:44
  755.7 19.4 %copy-start.22 = (f32[16,4,128]{2,1,0:T(4,128)S(1)}, f32[16,4,128]{2,1,0:T(4,128)}, u32[]{:S(2)}) copy-start(f32[16,4,128]{2,1,0:T(4,128)} %copy-done.21) | copy-start | bytes 98308
  755.7 19.4 %copy-start.26 = (f32[16,4,128]{2,1,0:T(4,128)S(1)}, f32[16,4,128]{2,1,0:T(4,128)}, u32[]{:S(2)}) copy-start(f32[16,4,128]{2,1,0:T(4,128)} %copy-done.25) | copy-start | bytes 98308
  755.7 19.4 %copy-start.30 = (pred[128,128]{0,1:T(8,128)(4,1)S(1)}, pred[128,128]{0,1:T(8,128)(4,1)}, u32[]{:S(2)}) copy-start(pred[128,128]{0,1:T(8,128)(4,1)} %copy-done.29) | copy-start | bytes 49156
  897.8 149.6 %reduce-scatter.23.cloned.1.call-start = ((), (), s32[]{:S(2)}) async-start(), calls=%async_computation.27 | async-start | bytes 5242880 | tf_op jit(solution)/shard_map/reduce_scatter | solution.py:44
  912.1 214.8 %reduce-scatter.21.cloned.1.call-start = ((), (), s32[]{:S(2)}) async-start(), calls=%async_computation.26 | async-start | bytes 5242880 | tf_op jit(solution)/shard_map/reduce_scatter | solution.py:44
  926.5 280.0 %reduce-scatter.19.cloned.1.call-start = ((), (), s32[]{:S(2)}) async-start(), calls=%async_computation.25 | async-start | bytes 5242880 | tf_op jit(solution)/shard_map/reduce_scatter | solution.py:44
  941.1 313.0 %reduce-scatter.15.cloned.1.call-start = ((), (), s32[]{:S(2)}) async-start(), calls=%async_computation.23 | async-start | bytes 2621440 | tf_op jit(solution)/shard_map/reduce_scatter | solution.py:44
  942.5 25.9 %copy-start.8 = (bf16[256,2048]{1,0:T(8,128)(2,1)S(1)}, bf16[256,2048]{1,0:T(8,128)(2,1)}, u32[]{:S(2)}) copy-start(bf16[256,2048]{1,0:T(8,128)(2,1)} %param.13) | copy-start | bytes 3145732
  951.1 22.5 %copy-start.6 = (f32[256,2048]{1,0:T(8,128)S(1)}, f32[256,2048]{1,0:T(8,128)}, u32[]{:S(2)}) copy-start(f32[256,2048]{1,0:T(8,128)} %copy-done.5) | copy-start | bytes 6291460
  973.3 430.7 %reduce-scatter.17.cloned.1.call-start = ((), (), s32[]{:S(2)}) async-start(), calls=%async_computation.24 | async-start | bytes 8650752 | tf_op jit(solution)/shard_map/reduce_scatter | solution.py:44
  1256.1 149.7 %all-to-all-start.3 = ((bf16[8,64,512]{2,1,0:T(8,128)(2,1)}), bf16[8,64,512]{2,1,0:T(8,128)(2,1)}, u32[]{:S(2)}, u32[]{:S(2)}) async-start(bf16[8,64,512]{2,1,0:T(8,128)(2,1)} %bitcast.303), calls=%async_computation.7 | async-start | bytes 1048576 | tf_op jit(solution)/shard_map/all_to_all | solution.py:218
  (27 other events, 126.8 us)
Sparse Core Ops, SparseCore 0:
  26.3 45.2 all-gather.10
  73.5 53.1 all-gather.8
  129.6 77.4 all-gather.12
  208.5 79.1 all-gather.18
  290.0 52.5 all-gather.14
  344.0 80.5 all-gather.16
  426.2 78.9 all-gather.20
  507.6 52.9 all-gather.22
  597.8 71.2 reduce-scatter.8
  672.8 71.2 reduce-scatter.10
  897.9 70.3 reduce-scatter.12
  970.6 76.7 reduce-scatter.22
  1049.6 77.2 reduce-scatter.20
  1129.2 77.2 reduce-scatter.18
  1208.6 45.3 reduce-scatter.14
  1256.3 147.6 reduce-scatter.16

commit v2 on v1

--- a/solution.py
+++ b/solution.py
@@ -1,6 +1,10 @@
+import functools
+
 import jax
 import jax.numpy as jnp
 from jax import lax
+from jax.experimental import pallas as pl
+from jax.experimental.pallas import tpu as pltpu
 from jax.sharding import Mesh
 from jax.sharding import PartitionSpec as P
 
@@ -22,6 +26,298 @@
 EVERY = ("grp", "chip", "core")
 BF16 = jnp.bfloat16
 F32 = jnp.float32
+
+
+MESH = pl.DeviceIdType.MESH
+ANY = pl.BlockSpec(memory_space=pl.ANY)
+VMEM = pl.BlockSpec(memory_space=pltpu.VMEM)
+
+
+def place():
+    return lax.axis_index("chip"), lax.axis_index("core")
+
+
+def flip(chip, step, chips):
+    return jnp.bitwise_xor(chip, step) if chips == 4 else lax.rem(chip + step, chips)
+
+
+def unflip(chip, step, chips):
+    return jnp.bitwise_xor(chip, step) if chips == 4 else lax.rem(chip + chips - step, chips)
+
+
+def greet(peers):
+    barrier = pltpu.get_barrier_semaphore()
+    for chip, core in peers:
+        pl.semaphore_signal(
+            barrier, inc=1, device_id={"chip": chip, "core": core}, device_id_type=MESH
+        )
+    pl.semaphore_wait(barrier, len(peers))
+
+
+def remote(src, dst, send, recv, chip, core):
+    return pltpu.make_async_remote_copy(
+        src_ref=src,
+        dst_ref=dst,
+        send_sem=send,
+        recv_sem=recv,
+        device_id={"chip": chip, "core": core},
+        device_id_type=MESH,
+    )
+
+
+class Gather:
+    def __init__(self, chips, inner, x_ref, o_ref, send, recv, local):
+        self.chips, self.inner, self.x, self.o = chips, inner, x_ref, o_ref
+        self.send, self.recv, self.local = send, recv, local
+        self.chip, self.core = place()
+        self.half = x_ref.shape[0] // 2
+        self.started = []
+
+    def greet(self):
+        steps = (1, 2) if self.chips == 4 else range(1, self.chips)
+        peers = [(flip(self.chip, s, self.chips), self.core) for s in steps]
+        greet(peers + [(self.chip, 1 - self.core)])
+
+    def piece(self, slot, h):
+        at = pl.ds(h * self.half, self.half)
+        return self.o.at[at, slot] if self.inner else self.o.at[slot, at]
+
+    def own(self, h):
+        return self.x.at[pl.ds(h * self.half, self.half)]
+
+    def slot(self, chip, core):
+        return chip * 2 + core
+
+    def push(self, src, slot, h, chip, core):
+        i = len(self.started)
+        copy = remote(src, self.piece(slot, h), self.send.at[i], self.recv.at[slot, h], chip, core)
+        copy.start()
+        self.started.append(copy)
+
+    def wait_for(self, slot, h):
+        remote(
+            self.own(h), self.piece(slot, h), self.send.at[0], self.recv.at[slot, h],
+            self.chip, 1 - self.core,
+        ).wait_recv()
+
+    def start(self):
+        me = self.slot(self.chip, self.core)
+        if self.chips == 4:
+            for h, s in ((0, 1), (1, 2), (1, 1), (0, 2)):
+                self.push(self.own(h), me, h, flip(self.chip, s, 4), self.core)
+        else:
+            for s in range(1, self.chips):
+                for h in range(2):
+                    self.push(self.own(h), me, h, flip(self.chip, s, self.chips), self.core)
+        for h in range(2):
+            self.push(self.own(h), me, h, self.chip, 1 - self.core)
+        whole = self.o.at[:, me] if self.inner else self.o.at[me]
+        self.mine = pltpu.make_async_copy(self.x, whole, self.local)
+        self.mine.start()
+
+    def relay(self):
+        if self.chips == 4:
+            plan = ((1, 0, 2), (2, 1, 1), (1, 1, 0), (2, 0, 0), (3, 0, 0), (3, 1, 0))
+        else:
+            plan = tuple((s, h, 0) for s in range(1, self.chips) for h in range(2))
+        for s, h, onward in plan:
+            slot = self.slot(unflip(self.chip, s, self.chips), self.core)
+            self.wait_for(slot, h)
+            if onward:
+                self.push(self.piece(slot, h), slot, h, flip(self.chip, onward, 4), self.core)
+            self.push(self.piece(slot, h), slot, h, self.chip, 1 - self.core)
+
+    def finish(self):
+        for s in range(self.chips):
+            slot = self.slot(unflip(self.chip, s, self.chips), 1 - self.core)
+            for h in range(2):
+                self.wait_for(slot, h)
+        for copy in self.started:
+            copy.wait_send()
+        self.mine.wait()
+
+
+def gather_sems(chips):
+    return [
+        pltpu.SemaphoreType.DMA((4 * chips + 4,)),
+        pltpu.SemaphoreType.DMA((2 * chips, 2)),
+        pltpu.SemaphoreType.DMA,
+    ]
+
+
+def gather_kernel(chips, inner, x_ref, o_ref, *sems):
+    run = Gather(chips, inner, x_ref, o_ref, *sems)
+    run.greet()
+    run.start()
+    run.relay()
+    run.finish()
+
+
+def plane_gather(x, chips, call_id, inner=False):
+    devs = 2 * chips
+    shape = (x.shape[0], devs) + x.shape[1:] if inner else (devs,) + x.shape
+    return pl.pallas_call(
+        functools.partial(gather_kernel, chips, inner),
+        out_shape=jax.ShapeDtypeStruct(shape, x.dtype),
+        in_specs=[ANY],
+        out_specs=ANY,
+        scratch_shapes=gather_sems(chips),
+        compiler_params=pltpu.CompilerParams(collective_id=call_id, has_side_effects=True),
+    )(x)
+
+
+def reduce_kernel(chips, inner, p_ref, o_ref, total, mine, twin, moved, corner, landed, lsem, tsend, trecv, msend, mrecv, csend, crecv):
+    chip, core = place()
+    sib = 1 - core
+    half = (p_ref.shape[0] if inner else p_ref.shape[1]) // 2
+    block = (lambda slot: p_ref.at[:, slot]) if inner else (lambda slot: p_ref.at[slot])
+    steps = (1, 2) if chips == 4 else tuple(range(1, chips))
+    peers = [(flip(chip, s, chips), core) for s in steps]
+    greet(peers + [(chip, sib)])
+    order = (3, 1, 2, 0) if chips == 4 else tuple(range(1, chips)) + (0,)
+    loads, twins = {}, {}
+    for s in order:
+        to = flip(chip, s, chips) * 2
+        twins[s] = remote(block(to + sib), twin.at[s], tsend.at[s], trecv.at[s], chip, sib)
+        twins[s].start()
+        loads[s] = pltpu.make_async_copy(block(to + core), mine.at[s], lsem.at[s])
+        loads[s].start()
+
+    def part(s, h):
+        at = pl.ds(h * half, half)
+        return mine[s, at].astype(F32) + twin[s, at].astype(F32)
+
+    def ready(s):
+        loads[s].wait()
+        twins[s].wait_recv()
+
+    sent = []
+    if chips == 4:
+        corners = []
+        ready(3)
+        for h, s in ((0, 1), (1, 2)):
+            moved[3, pl.ds(h * half, half)] = part(3, h).astype(BF16)
+            copy = remote(moved.at[3, pl.ds(h * half, half)], corner.at[h], csend.at[h], crecv.at[h], flip(chip, s, 4), core)
+            copy.start()
+            corners.append(copy)
+
+        def send(s, h):
+            at = pl.ds(h * half, half)
+            copy = remote(moved.at[s, at], landed.at[s - 1, at], msend.at[s - 1, h], mrecv.at[s - 1, h], flip(chip, s, 4), core)
+            copy.start()
+            sent.append(copy)
+
+        for s, h in ((1, 0), (2, 1)):
+            ready(s)
+            moved[s, pl.ds(h * half, half)] = part(s, h).astype(BF16)
+            send(s, h)
+        for s, h in ((2, 0), (1, 1)):
+            corners[h].wait_recv()
+            moved[s, pl.ds(h * half, half)] = (part(s, h) + corner[h].astype(F32)).astype(BF16)
+            send(s, h)
+        for copy in corners:
+            copy.wait_send()
+    else:
+        for s in steps:
+            ready(s)
+            for h in range(2):
+                at = pl.ds(h * half, half)
+                moved[s, at] = part(s, h).astype(BF16)
+                copy = remote(moved.at[s, at], landed.at[s - 1, at], msend.at[s - 1, h], mrecv.at[s - 1, h], flip(chip, s, chips), core)
+                copy.start()
+                sent.append(copy)
+    ready(0)
+    for h in range(2):
+        total[pl.ds(h * half, half)] = part(0, h)
+    for copy in sent:
+        copy.wait()
+    for s in steps[:-1]:
+        total[...] += landed[s - 1].astype(F32)
+    o_ref[...] = (total[...] + landed[steps[-1] - 1].astype(F32)).astype(o_ref.dtype)
+    for s in order:
+        twins[s].wait_send()
+
+
+def plane_reduce(p, chips, call_id, dtype=F32, inner=False):
+    block = (p.shape[0],) + p.shape[2:] if inner else p.shape[1:]
+    steps = 2 if chips == 4 else chips - 1
+    return pl.pallas_call(
+        functools.partial(reduce_kernel, chips, inner),
+        out_shape=jax.ShapeDtypeStruct(block, dtype),
+        in_specs=[ANY],
+        out_specs=VMEM,
+        scratch_shapes=[
+            pltpu.VMEM(block, F32),
+            pltpu.VMEM((chips,) + block, BF16),
+            pltpu.VMEM((chips,) + block, BF16),
+            pltpu.VMEM((chips,) + block, BF16),
+            pltpu.VMEM((2, block[0] // 2) + block[1:], BF16),
+            pltpu.VMEM((steps,) + block, BF16),
+            pltpu.SemaphoreType.DMA((chips,)),
+            pltpu.SemaphoreType.DMA((chips,)),
+            pltpu.SemaphoreType.DMA((chips,)),
+            pltpu.SemaphoreType.DMA((steps, 2)),
+            pltpu.SemaphoreType.DMA((steps, 2)),
+            pltpu.SemaphoreType.DMA((2,)),
+            pltpu.SemaphoreType.DMA((2,)),
+        ],
+        compiler_params=pltpu.CompilerParams(
+            collective_id=call_id, has_side_effects=True, vmem_limit_bytes=56 << 20
+        ),
+    )(p)
+
+
+def exchange_kernel(chips, cut, paste, x_ref, o_ref, send, recv, local):
+    chip, core = place()
+    me = chip * 2 + core
+    peers = [(flip(chip, s, chips), c) for s in range(1, chips) for c in (core, 1 - core)]
+    peers = peers + [(chip, 1 - core)]
+    greet(peers)
+    far = [p for p in ([3, 1, 2] if chips == 4 else range(1, chips))]
+    order = [(flip(chip, s, chips), c) for s in far for c in (core, 1 - core)] + [(chip, 1 - core)]
+    copies = []
+    for i, (to, c) in enumerate(order):
+        copy = remote(cut(x_ref, to * 2 + c), paste(o_ref, me), send.at[i], recv.at[me], to, c)
+        copy.start()
+        copies.append(copy)
+    mine = pltpu.make_async_copy(cut(x_ref, me), paste(o_ref, me), local)
+    mine.start()
+    for s in far:
+        for c in (core, 1 - core):
+            slot = unflip(chip, s, chips) * 2 + c
+            remote(cut(x_ref, me), paste(o_ref, slot), send.at[0], recv.at[slot], chip, 1 - core).wait_recv()
+    slot = chip * 2 + 1 - core
+    remote(cut(x_ref, me), paste(o_ref, slot), send.at[0], recv.at[slot], chip, 1 - core).wait_recv()
+    for copy in copies:
+        copy.wait_send()
+    mine.wait()
+
+
+def plane_exchange(x, shape, cut, paste, chips, call_id):
+    return pl.pallas_call(
+        functools.partial(exchange_kernel, chips, cut, paste),
+        out_shape=jax.ShapeDtypeStruct(shape, x.dtype),
+        in_specs=[ANY],
+        out_specs=ANY,
+        scratch_shapes=[
+            pltpu.SemaphoreType.DMA((2 * chips,)),
+            pltpu.SemaphoreType.DMA((2 * chips,)),
+            pltpu.SemaphoreType.DMA,
+        ],
+        compiler_params=pltpu.CompilerParams(collective_id=call_id, has_side_effects=True),
+    )(x)
+
+
+def by_slot(ref, dev):
+    return ref.at[dev]
+
+
+def by_rows(rows):
+    return lambda ref, dev: ref.at[pl.ds(pl.multiple_of(dev * rows, rows), rows)]
+
+
+def by_cols(cols):
+    return lambda ref, dev: ref.at[:, pl.ds(pl.multiple_of(dev * cols, cols), cols)]
 
 
 def matmul(left, right):
@@ -72,9 +368,9 @@
     w_down,
     cotangent,
 ):
-    tok_axes, weight_axes = TOK_AXES, WEIGHT_AXES
     grps = lax.axis_size("grp")
     devs = lax.axis_size(PLANE)
+    chips = devs // 2
     rows = tokens.shape[0]
     w_rows = w_query.shape[0]
     q_heads = HEADS // devs
@@ -102,13 +398,15 @@
     packed = jnp.concatenate(
         [w_query.reshape(w_rows, devs, q_cols), kv_split(w_key), kv_split(w_value), gains], axis=2
     )
-    packed = lax.all_to_all(packed, PLANE, split_axis=1, concat_axis=0, tiled=True)
+    packed = jnp.swapaxes(packed, 0, 1)
+    packed = plane_exchange(packed, packed.shape, by_slot, by_slot, chips, 1)
+    packed, w_out = lax.optimization_barrier((packed, w_out))
     packed = gather(packed.reshape(devs * w_rows, q_cols + 2 * kv_cols + 128), "grp")
     w_qkv = packed[:, : q_cols + 2 * kv_cols]
     gain_one = packed[:, q_cols + 2 * kv_cols].astype(F32)
     gain_two = packed[:, q_cols + 2 * kv_cols + 1].astype(F32)
 
-    all_tokens = gather(tokens, PLANE)
+    all_tokens = plane_gather(tokens, chips, 2).reshape(devs * rows, D)
     layer_all = all_tokens.astype(F32)
     normed_one = (layer_all * norm_parts(layer_all) * gain_one).astype(BF16)
     qkv = matmul(normed_one, w_qkv).astype(BF16)
@@ -145,45 +443,56 @@
         "gbkpij,gjkd->gbikpd", far_p.astype(BF16), v_p, preferred_element_type=F32
     ) + jnp.einsum("gbkpij,gbjkd->gbikpd", own_p.astype(BF16), v_b, preferred_element_type=F32)
     attended = attended.astype(BF16).reshape(row_blocks, BLOCK, q_cols)[rank]
-    attended = lax.all_to_all(
-        attended.reshape(row_blocks * BLOCK, q_cols), PLANE, split_axis=0, concat_axis=1, tiled=True
-    )
-
-    out_full = gather(w_out, EVERY)
+    attended = plane_exchange(
+        attended.reshape(row_blocks * BLOCK, q_cols), (rows, D), by_rows(rows), by_cols(q_cols), chips, 3
+    )
+
+    out_full = gather(w_out[None], "grp")
+    out_full = plane_gather(out_full, chips, 4, inner=True).reshape(D, D)
     layer_in = tokens.astype(F32)
     branch_attn = matmul(attended, out_full)
     residual = layer_in + RESID_MULT * branch_attn
     factor_two = norm_parts(residual)
-    normed_two = gather((residual * factor_two * gain_two).astype(BF16), tok_axes)
+    normed_two = (residual * factor_two * gain_two).astype(BF16)
+    normed_two = plane_gather(normed_two, chips, 2).reshape(devs * rows, D)
     upstream = cotangent.astype(F32)
-    d_branch_mlp = gather((RESID_MULT * upstream).astype(BF16), tok_axes)
-
-    gate_w = gather(w_gate, weight_axes, axis=1)
-    up_w = gather(w_up, weight_axes, axis=1)
-    down_w = gather(w_down, weight_axes)
+    d_branch_mlp = plane_gather((RESID_MULT * upstream).astype(BF16), chips, 2)
+    d_branch_mlp = d_branch_mlp.reshape(devs * rows, D)
+
+    gate_w = gather(w_gate, "grp", axis=1)
+    up_w = gather(w_up, "grp", axis=1)
+    down_w = gather(w_down, "grp")
     gate_act = matmul(normed_two, gate_w)
     up_act = matmul(normed_two, up_w)
     sig = jax.nn.sigmoid(gate_act)
     silu = gate_act * sig
     hidden = (silu * up_act).astype(BF16)
-    branch_mlp = scatter(matmul(hidden, down_w).astype(BF16), tok_axes).astype(F32)
-    layer_out = residual + RESID_MULT * branch_mlp
-
-    grad_down = scatter(over_rows(hidden, d_branch_mlp).astype(BF16), weight_axes).astype(F32)
+    part_down = over_rows(hidden, d_branch_mlp).astype(BF16)
     d_hidden = over_cols(d_branch_mlp, down_w)
     d_gate = (d_hidden * up_act * (sig * (1.0 + gate_act * (1.0 - sig)))).astype(BF16)
     d_up = (d_hidden * silu).astype(BF16)
-    grad_gate = scatter(over_rows(normed_two, d_gate).astype(BF16), weight_axes, axis=1).astype(F32)
-    grad_up = scatter(over_rows(normed_two, d_up).astype(BF16), weight_axes, axis=1).astype(F32)
+    part_gate = over_rows(normed_two, d_gate).astype(BF16)
+    part_up = over_rows(normed_two, d_up).astype(BF16)
+    d_gate, d_up, part_down, part_gate, part_up = lax.optimization_barrier(
+        (d_gate, d_up, part_down, part_gate, part_up)
+    )
+    grad_down = scatter(part_down, "grp")
+    grad_gate = scatter(part_gate, "grp", axis=1)
+    grad_up = scatter(part_up, "grp", axis=1)
     d_normed_two = over_cols(d_gate, gate_w) + over_cols(d_up, up_w)
-    d_normed_two = scatter(d_normed_two.astype(BF16), tok_axes).astype(F32)
+    d_normed_two = plane_reduce(d_normed_two.astype(BF16).reshape(devs, rows, D), chips, 5)
 
     d_residual_norm, d_gain_two = norm_back(residual, factor_two, gain_two, d_normed_two)
     d_residual = upstream + d_residual_norm
     d_branch_attn = (RESID_MULT * d_residual).astype(BF16)
-    grad_out = scatter(over_rows(attended, d_branch_attn).astype(BF16), EVERY).astype(F32)
+    grad_out = over_rows(attended, d_branch_attn).astype(BF16).reshape(grps, devs, w_rows, D)
+    grad_out = plane_reduce(grad_out, chips, 6, dtype=BF16, inner=True)
+    grad_out, grad_down = lax.optimization_barrier((grad_out, grad_down))
+    grad_out = scatter(grad_out, "grp").reshape(w_rows, D).astype(F32)
     d_attended = over_cols(d_branch_attn, out_full).astype(BF16)
-    d_attended = lax.all_to_all(d_attended, PLANE, split_axis=1, concat_axis=0, tiled=True)
+    d_attended = plane_exchange(
+        d_attended, (devs * rows, q_cols), by_cols(q_cols), by_rows(rows), chips, 7
+    )
     d_b = d_attended.reshape(row_blocks, BLOCK, q_cols)[order]
     d_b = d_b.reshape(row_groups, GROUP_BLOCKS, BLOCK, kv_heads, per_kv, HEAD_DIM)
 
@@ -207,15 +516,18 @@
     d_qkv = d_qkv.reshape(row_blocks, BLOCK, q_cols + 2 * kv_cols)[rank]
     d_qkv = d_qkv.reshape(row_blocks * BLOCK, q_cols + 2 * kv_cols)
 
-    d_normed_one = scatter(over_cols(d_qkv, w_qkv).astype(BF16), PLANE).astype(F32)
+    d_normed_one = over_cols(d_qkv, w_qkv).astype(BF16).reshape(devs, rows, D)
+    d_normed_one = plane_reduce(d_normed_one, chips, 5)
     d_input_norm, d_gain_one = norm_back(layer_in, norm_parts(layer_in), gain_one, d_normed_one)
     tokens_grad = (d_residual + d_input_norm).astype(BF16)
 
     grad_qkv = over_rows(normed_one, d_qkv)
     d_gains = jnp.pad(jnp.stack([d_gain_one, d_gain_two], axis=1), ((0, 0), (0, 126)))
-    sent = scatter(jnp.concatenate([grad_qkv, d_gains], axis=1).astype(BF16), "grp")
+    sent = jnp.concatenate([grad_qkv, d_gains], axis=1).astype(BF16)
+    sent, grad_gate, grad_up = lax.optimization_barrier((sent, grad_gate, grad_up))
+    sent = scatter(sent, "grp")
     sent = sent.reshape(devs, w_rows, q_cols + 2 * kv_cols + 128)
-    sent = lax.all_to_all(sent, PLANE, split_axis=0, concat_axis=0, tiled=True).astype(F32)
+    sent = plane_exchange(sent, sent.shape, by_slot, by_slot, chips, 1).astype(F32)
 
     def kv_join(g):
         g = g.reshape(devs // kv_copies, kv_copies, w_rows, kv_cols)
@@ -227,6 +539,10 @@
     grad_value = kv_join(sent[:, :, q_cols + kv_cols : q_cols + 2 * kv_cols])
     gains_sum = jnp.sum(sent[:, :, q_cols + 2 * kv_cols :], axis=0)
 
+    branch_mlp = matmul(hidden, down_w).astype(BF16).reshape(devs, rows, D)
+    branch_mlp, d_qkv = lax.optimization_barrier((branch_mlp, d_qkv))
+    branch_mlp = plane_reduce(branch_mlp, chips, 5)
+    layer_out = residual + RESID_MULT * branch_mlp
     scaled_attn = RESID_MULT * branch_attn
     scaled_mlp = RESID_MULT * branch_mlp
     squares = jnp.stack(
@@ -247,14 +563,11 @@
         grad_value,
         grad_out,
         gains_sum[:, 1],
-        grad_gate,
-        grad_up,
-        grad_down,
+        grad_gate.astype(F32),
+        grad_up.astype(F32),
+        grad_down.astype(F32),
         rms_stats,
     )
-
-
-TOK_AXES, WEIGHT_AXES = PLANE, ("grp",)
 
 
 def solution(mesh):

time: 1430 us -> 882 us (0.62)
  waiting for transfers between devices: 899 us -> 11.3 us
  Pallas kernels: 0 us -> 379 us
  blocking collectives: 95.7 us -> 37.4 us
    reduce_scatter x8 -> x5, waiting for transfers between devices: 490 us -> 0.03 us  [scatter(): return lax.psum_scatter(values, axes, scatter_dimension=axis, tiled=True)]
    all_gather x8 -> x5, waiting for transfers between devices: 405 us -> 9.47 us  [gather(): return lax.all_gather(values, axes, axis=axis, tiled=True)]
    pallas_call x0 -> x12, Pallas kernels: none -> 379 us  [the longest x4 166 us: plane_reduce(): pl.pallas_call(functools.partial(reduce_kernel, chips, inner), out_shape=...]
    all_to_all x3 -> x0, blocking collectives: 51.3 us -> none  [the longest x1 18.6 us: on_device(): lax.all_to_all(attended.reshape(row_blocks * BLOCK, q_cols), PLANE, split...]
  transfers between devices with their start and end apart: 17 -> 10, of which waited for: 14 -> 1; matrix products, arithmetic and copies ran while one was open for 15% -> 40% of each run, Pallas kernels for 0% -> 41%
where the time goes in v2:
time: 882 us; the launch traced here: 873 us
  Pallas kernels  379 us (43%)
  matrix products  293 us (33%)
  other arithmetic  101 us (11%)
  blocking collectives  37.4 us (4%)
  local copies, waits for them, and re-layouts  34.8 us (4%)
  between operations  15.6 us (2%)
  waiting for transfers between devices  11.3 us (1%)
    pallas_call x4, Pallas kernels, plane_reduce(): pl.pallas_call(functools.partial(reduce_kernel, chips, inner), out_shape=...  166 us
    pallas_call x4, Pallas kernels, plane_gather(): pl.pallas_call(functools.partial(gather_kernel, chips, inner), out_shape=...  160 us
    dot_general x5, matrix products, matmul(): return jnp.dot(left, right, preferred_element_type=F32)  70.3 us
    dot_general x5, matrix products, over_cols(): lax.dot_general(left, right, (((1,), (1,)), ((), ())), preferred_element_...  69 us
    dot_general x5, matrix products, over_rows(): lax.dot_general(left, right, (((0,), (0,)), ((), ())), preferred_element_...  54.9 us
    pallas_call x4, Pallas kernels, plane_exchange(): pl.pallas_call(functools.partial(exchange_kernel, chips, cut, paste), out...  52.6 us
    psum x1, blocking collectives, on_device(): totals = lax.psum(squares, EVERY)  37.4 us
    another operation x3, other arithmetic  31.5 us
  transfers between devices with their start and end apart: 10, of which 1 were waited for; matrix products, arithmetic and copies ran while one was open for 40% of the time, Pallas kernels for 41%

profile of v2, /device:TPU:0, one launch (start us, length us, event | category | flops | bytes accessed | tf_op | source)
XLA Modules:
  0.0 873.0 jit_solution(715456125310787688)
XLA Ops:
  12.1 11.5 %shard_map.221 = bf16[8,64,512]{2,1,0:T(8,128)(2,1)} custom-call(bf16[8,64,512]{2,1,0:T(8,128)(2,1)} %maximum_bitcast_fusion.x_ref), custom_call_target="tpu_custom_call" | custom-call | tf_op jit(solution)/shard_map/pallas_call | solution.py:297
  29.5 39.8 %shard_map.225 = bf16[8,256,2048]{2,1,0:T(8,128)(2,1)} custom-call(bf16[256,2048]{1,0:T(8,128)(2,1)} %fusion.21.x_ref), custom_call_target="tpu_custom_call" | custom-call | tf_op jit(solution)/shard_map/pallas_call | solution.py:159
  69.3 40.0 %shard_map.220 = bf16[8,256,2048]{2,1,0:T(8,128)(2,1)} custom-call(bf16[256,2048]{1,0:T(8,128)(2,1)} %x_ref.1), custom_call_target="tpu_custom_call" | custom-call | tf_op jit(solution)/shard_map/pallas_call | solution.py:159
  115.2 40.0 %shard_map.223 = bf16[4,8,64,2048]{3,2,1,0:T(8,128)(2,1)} custom-call(bf16[4,64,2048]{2,1,0:T(8,128)(2,1)} %bitcast.336), custom_call_target="tpu_custom_call" | custom-call | tf_op jit(solution)/shard_map/pallas_call | solution.py:159
  156.1 8.6 fusion.12
  197.9 9.2 %fusion.4 = f32[16,4,128]{2,1,0:T(4,128)S(1)} fusion(f32[1024,16,128,4]{2,0,3,1:T(8,128)S(1)} %get-tuple-element.65, f32[16,4,128]{2,1,0:T(4,128)S(1)} %max.8, pred[16,1024]{1,0:T(8,128)(4,1)S(1)} %iota_compare_fusion.2), kind=kLoop, calls=%fused_computation.12 | loop fusion | flops 33546240 | bytes 33636352 | tf_op jit(solution)/shard_map/reduce_sum | solution.py:440
  208.4 15.5 %fusion.32 = bf16[1,16,128,1,4,64]{2,5,4,1,3,0:T(8,128)(2,1)S(1)} fusion(f32[16,64,4,128]{3,1,2,0:T(8,128)S(1)} %fusion.35, bf16[1,2048,1,64]{1,3,2,0:T(8,128)(2,1)S(1)} %bitcast.338, f32[16,4,128]{2,1,0:T(4,128)S(1)} %add.134, f32[16,4,128]{2,1,0:T(4,128)S(1)} %max.8, f32[1024,16,128,4]{2,0,3,1:T(8,128)} %copy-done, ...), kind=kOutput, calls=%fused_computation.72 | convolution fusion | flops 1116733440 | bytes 36913152 | tf_op jit(solution)/shard_map/gbkpij,gjkd->gbikpd/dot_general | solution.py:442
  226.1 15.3 %shard_map.222 = bf16[256,2048]{1,0:T(8,128)(2,1)} custom-call(bf16[2048,256]{1,0:T(8,128)(2,1)} %bitcast.319), custom_call_target="tpu_custom_call" | custom-call | tf_op jit(solution)/shard_map/pallas_call | solution.py:297
  251.1 40.0 %shard_map.224 = bf16[8,256,2048]{2,1,0:T(8,128)(2,1)} custom-call(bf16[256,2048]{1,0:T(8,128)(2,1)} %multiply_convert_fusion.5.x_ref), custom_call_target="tpu_custom_call" | custom-call | tf_op jit(solution)/shard_map/pallas_call | solution.py:159
  291.1 26.2 %fusion.84 = f32[2048,1024]{1,0:T(8,128)} fusion(bf16[2048,2048]{1,0:T(8,128)(2,1)} %bitcast.314, bf16[2048,1024]{1,0:T(8,128)(2,1)} %all-gather.11.cloned.1.call-done), kind=kOutput, calls=%fused_computation.159 | convolution fusion | flops 8589934592 | bytes 20971520 | tf_op jit(solution)/shard_map/dot_general | solution.py:324
  317.2 14.4 %fusion.83 = f32[2048,1024]{1,0:T(8,128)} fusion(bf16[2048,2048]{1,0:T(8,128)(2,1)} %bitcast.315, bf16[2048,1024]{1,0:T(8,128)(2,1)} %all-gather.9.cloned.1.call-done), kind=kOutput, calls=%fused_computation.158 | convolution fusion | flops 8589934592 | bytes 20971520 | tf_op jit(solution)/shard_map/dot_general | solution.py:324
  331.7 9.4 %all-gather.13.cloned.1.call-done = bf16[1024,2048]{1,0:T(8,128)(2,1)} async-done(((bf16[256,2048]{1,0:T(8,128)(2,1)}), bf16[1024,2048]{1,0:T(8,128)(2,1)}) %all-gather.13.cloned.1.call-update) | async-done | bytes 4194320 | tf_op jit(solution)/shard_map/all_gather | solution.py:336
  341.1 23.3 %multiply_convert_fusion.1 = (bf16[2048,1024]{1,0:T(8,128)(2,1)}, bf16[2048,1024]{1,0:T(8,128)(2,1)}, bf16[2048,1024]{1,0:T(8,128)(2,1)}) fusion(f32[2048,1024]{1,0:T(8,128)} %fusion.83, f32[2048,1024]{1,0:T(8,128)} %fusion.84, bf16[2048,2048]{1,0:T(8,128)(2,1)} %bitcast.312, bf16[1024,2048]{1,0:T(8,128)(2,1)} %all-gather.13.cloned.1.call-done), kind=kOutput, calls=%fused_computation.26 | convolution fusion | flops 8621391872 | bytes 41943040 | tf_op jit(solution)/shard_map/dot_general | solution.py:332
  364.4 14.0 %convolution_convert_fusion.3 = bf16[1024,2048]{1,0:T(8,128)(2,1)} fusion(bf16[2048,1024]{1,0:T(8,128)(2,1)} %get-tuple-element.50, bf16[2048,2048]{1,0:T(8,128)(2,1)} %bitcast.313), kind=kOutput, calls=%fused_computation.46 | convolution fusion | flops 8592031744 | bytes 16777216 | tf_op jit(solution)/shard_map/dot_general | solution.py:328
  378.4 14.4 %convolution_convert_fusion.4 = bf16[2048,1024]{1,0:T(8,128)(2,1)} fusion(bf16[2048,2048]{1,0:T(8,128)(2,1)} %bitcast.316, bf16[2048,1024]{1,0:T(8,128)(2,1)} %get-tuple-element.28), kind=kOutput, calls=%fused_computation.47 | convolution fusion | flops 8592031744 | bytes 16777216 | tf_op jit(solution)/shard_map/dot_general | solution.py:328
  392.8 14.0 %convolution_convert_fusion.5 = bf16[2048,1024]{1,0:T(8,128)(2,1)} fusion(bf16[2048,2048]{1,0:T(8,128)(2,1)} %bitcast.317, bf16[2048,1024]{1,0:T(8,128)(2,1)} %get-tuple-element.27), kind=kOutput, calls=%fused_computation.48 | convolution fusion | flops 8592031744 | bytes 16777216 | tf_op jit(solution)/shard_map/dot_general | solution.py:328
  416.1 15.5 %fusion.85 = f32[2048,2048]{1,0:T(8,128)} fusion(bf16[2048,1024]{1,0:T(8,128)(2,1)} %get-tuple-element.27, bf16[2048,1024]{1,0:T(8,128)(2,1)} %all-gather.9.cloned.1.call-done), kind=kOutput, calls=%fused_computation.160 | convolution fusion | flops 8589934592 | bytes 25165824 | tf_op jit(solution)/shard_map/dot_general | solution.py:332
  431.6 14.1 %add_convert_fusion = bf16[2048,2048]{1,0:T(8,128)(2,1)} fusion(f32[2048,2048]{1,0:T(8,128)} %fusion.85, bf16[2048,1024]{1,0:T(8,128)(2,1)S(1)} %copy-done.60, bf16[2048,1024]{1,0:T(8,128)(2,1)S(1)} %copy-done.59), kind=kOutput, calls=%fused_computation.23 | convolution fusion | flops 8598323200 | bytes 33554432 | tf_op jit(solution)/shard_map/dot_general | solution.py:332
  445.7 41.9 %shard_map.226 = f32[256,2048]{1,0:T(8,128)} custom-call(bf16[8,256,2048]{2,1,0:T(8,128)(2,1)} %bitcast.307), custom_call_target="tpu_custom_call" | custom-call | tf_op jit(solution)/shard_map/pallas_call | solution.py:244
  498.2 15.0 %shard_map.227 = bf16[2048,256]{1,0:T(8,128)(2,1)} custom-call(bf16[256,2048]{1,0:T(8,128)(2,1)} %convolution_convert_fusion.8.x_ref), custom_call_target="tpu_custom_call" | custom-call | tf_op jit(solution)/shard_map/pallas_call | solution.py:297
  521.5 17.1 %fusion.53 = bf16[1,1024,64]{1,2,0:T(8,128)(2,1)S(1)} fusion(bf16[16,128,4,64]{1,3,2,0:T(8,128)(2,1)} %bitcast.342, f32[1,1024,64]{1,0,2:T(1,128)S(1)} %slice.91, f32[16,4,128]{2,1,0:T(4,128)S(1)} %copy-done.37, f32[16,4,128]{2,1,0:T(4,128)S(1)} %copy-done.33, f32[1024,16,128,4]{2,0,3,1:T(8,128)} %copy-done, pred[16,1024]{1,0:T(8,128)(4,1)S(1)} %copy-done.35), kind=kOutput, calls=%fused_computation.97 | convolution fusion | flops 1115815936 | bytes 35078144 | tf_op jit(solution)/shard_map/gbkpij,gbikpd->gjkd/dot_general | solution.py:512
  545.5 41.6 %shard_map.231 = bf16[4,64,2048]{2,1,0:T(8,128)(2,1)} custom-call(bf16[4,8,64,2048]{3,2,1,0:T(8,128)(2,1)} %bitcast.303), custom_call_target="tpu_custom_call" | custom-call | tf_op jit(solution)/shard_map/pallas_call | solution.py:244
  590.8 26.3 %fusion = (f32[16,4,128]{2,1,0:T(4,128)S(1)}, f32[1024,16,128,4]{2,0,3,1:T(8,128)}) fusion(f32[16,4,128]{2,1,0:T(4,128)S(1)} %copy-done.37, f32[16,4,128]{2,1,0:T(4,128)S(1)} %copy-done.33, f32[1024,16,128,4]{2,0,3,1:T(8,128)} %copy-done, pred[16,1024]{1,0:T(8,128)(4,1)S(1)} %copy-done.35, bf16[16,128,4,64]{1,3,2,0:T(8,128)(2,1)S(1)} %bitcast.344, ...), kind=kOutput, calls=%fused_computation.7 | convolution fusion | flops 1124065280 | bytes 68403200 | tf_op jit(solution)/shard_map/gbikpd,gjkd->gbkpij/dot_general | solution.py:499
  621.0 29.7 %fusion.6 = bf16[16,4,128,1024]{2,3,1,0:T(8,128)(2,1)} fusion(f32[1024,16,128,4]{2,0,3,1:T(8,128)} %get-tuple-element.69, f32[16,4,128]{2,1,0:T(4,128)S(1)} %add.143, f32[16,4,128]{2,1,0:T(4,128)S(1)} %copy-done.37, f32[16,4,128]{2,1,0:T(4,128)S(1)} %copy-done.33, f32[1024,16,128,4]{2,0,3,1:T(8,128)} %copy-done, pred[16,1024]{1,0:T(8,128)(4,1)S(1)} %copy-done.35), kind=kLoop, calls=%fused_computation.14 | loop fusion | flops 58720256 | bytes 84000768 | tf_op jit(solution)/shard_map/reshape.26
  650.6 8.9 %fusion.68 = f32[64,16,4,128]{3,0,2,1:T(8,128)S(1)} fusion(bf16[16,4,128,1024]{2,3,1,0:T(8,128)(2,1)} %fusion.6, bf16[1,2048,1,64]{1,3,2,0:T(8,128)(2,1)S(1)} %bitcast.323), kind=kOutput, calls=%fused_computation.124 | convolution fusion | flops 1073741824 | bytes 19005440 | tf_op jit(solution)/shard_map/gbkpij,gjkd->gbikpd/dot_general | solution.py:506
  663.7 11.0 %fusion.49 = f32[1024,64]{0,1:T(8,128)S(1)} fusion(bf16[16,128,4,64]{1,3,2,0:T(8,128)(2,1)S(1)} %copy-done.7, bf16[16,4,128,1024]{2,3,1,0:T(8,128)(2,1)} %fusion.6, f32[1,1024,64]{1,0,2:T(1,128)S(1)} %get-tuple-element.60), kind=kOutput, calls=%fused_computation.95 | convolution fusion | flops 1073807360 | bytes 18350080 | tf_op jit(solution)/shard_map/gbkpij,gbikpd->gjkd/dot_general | solution.py:511
  678.3 8.6 convolution_convert_fusion.1
  687.0 41.5 %shard_map.229 = f32[256,2048]{1,0:T(8,128)} custom-call(bf16[8,256,2048]{2,1,0:T(8,128)(2,1)} %bitcast.309), custom_call_target="tpu_custom_call" | custom-call | tf_op jit(solution)/shard_map/pallas_call | solution.py:244
  739.3 14.2 %convolution_convert_fusion.2 = bf16[2048,2048]{1,0:T(8,128)(2,1)} fusion(bf16[2048,1024]{1,0:T(8,128)(2,1)} %get-tuple-element.50, bf16[1024,2048]{1,0:T(8,128)(2,1)} %all-gather.13.cloned.1.call-done), kind=kOutput, calls=%fused_computation.33 | convolution fusion | flops 8594128896 | bytes 16777216 | tf_op jit(solution)/shard_map/dot_general | solution.py:324
  753.5 41.5 %shard_map.228 = f32[256,2048]{1,0:T(8,128)} custom-call(bf16[8,256,2048]{2,1,0:T(8,128)(2,1)} %bitcast.308), custom_call_target="tpu_custom_call" | custom-call | tf_op jit(solution)/shard_map/pallas_call | solution.py:244
  800.9 37.4 %psum.7 = f32[3]{0:T(128)S(1)} all-reduce(f32[3]{0:T(128)S(1)} %pad_maximum_fusion.4), channel_id=1, replica_groups=mesh['grp'=4,'chip'=4,'core'=2] {'grp','chip','core'}, use_global_device_ids=true, to_apply=%region_24.25 | all-reduce | flops 3 | bytes 24 | tf_op jit(solution)/shard_map/psum | solution.py:555
  850.4 10.8 %shard_map.230 = bf16[8,64,512]{2,1,0:T(8,128)(2,1)} custom-call(bf16[8,64,512]{2,1,0:T(8,128)(2,1)} %bitcast.332), custom_call_target="tpu_custom_call" | custom-call | tf_op jit(solution)/shard_map/pallas_call | solution.py:297
  (253 shorter events, 146.7 us)
Async XLA Ops:
  7.2 108.0 %all-gather.15.cloned.1.call-start = ((), (), s32[]{:S(2)}) async-start(), calls=%async_computation.14 | async-start | bytes 1310720 | tf_op jit(solution)/shard_map/all_gather | solution.py:336
  23.6 131.6 %all-gather.7.cloned.1.call-start = ((), (), s32[]{:S(2)}) async-start(), calls=%async_computation.5 | async-start | bytes 2621440 | tf_op jit(solution)/shard_map/all_gather | solution.py:336
  25.8 265.3 %all-gather.11.cloned.1.call-start = ((), (), s32[]{:S(2)}) async-start(), calls=%async_computation.7 | async-start | bytes 5242880 | tf_op jit(solution)/shard_map/all_gather | solution.py:336
  26.5 290.7 %all-gather.9.cloned.1.call-start = ((), (), s32[]{:S(2)}) async-start(), calls=%async_computation.6 | async-start | bytes 5242880 | tf_op jit(solution)/shard_map/all_gather | solution.py:336
  27.1 314.0 %all-gather.13.cloned.1.call-start = ((), (), s32[]{:S(2)}) async-start(), calls=%async_computation.8 | async-start | bytes 5242880 | tf_op jit(solution)/shard_map/all_gather | solution.py:336
  27.7 650.6 %reduce-scatter.12.cloned.1.call-start = ((), (), s32[]{:S(2)}) async-start(), calls=%async_computation.12 | async-start | bytes 5242880 | tf_op jit(solution)/shard_map/reduce_scatter | solution.py:340
  28.2 179.0 %copy-start.40 = (pred[128,128]{0,1:T(8,128)(4,1)}, pred[128,128]{0,1:T(8,128)(4,1)S(1)}, u32[]{:S(2)}) copy-start(pred[128,128]{0,1:T(8,128)(4,1)S(1)} %iota_compare_fusion.1) | copy-start | bytes 49156
  28.2 144.9 %copy-start.52 = (s32[1024]{0:T(1024)}, s32[1024]{0:T(1024)S(1)}, u32[]{:S(2)}) copy-start(s32[1024]{0:T(1024)S(1)} %pad_clamp_fusion.1) | copy-start | bytes 12292
  28.2 196.3 %copy-start.51 = (s32[1024]{0:T(1024)}, s32[1024]{0:T(1024)S(1)}, u32[]{:S(2)}) copy-start(s32[1024]{0:T(1024)S(1)} %pad_clamp_fusion) | copy-start | bytes 12292
  28.3 180.1 %copy-start.34 = (pred[16,1024]{1,0:T(8,128)(4,1)}, pred[16,1024]{1,0:T(8,128)(4,1)S(1)}, u32[]{:S(2)}) copy-start(pred[16,1024]{1,0:T(8,128)(4,1)S(1)} %iota_compare_fusion.2) | copy-start | bytes 49156
  156.1 92.5 %copy-start.45 = (f32[2048,1]{0,1:T(1,128)}, f32[2048,1]{0,1:T(1,128)S(1)}, u32[]{:S(2)}) copy-start(f32[2048,1]{0,1:T(1,128)S(1)} %get-tuple-element.53) | copy-start | bytes 24580
  248.5 42.5 %copy-start.55 = (f32[256]{0:T(256)}, f32[256]{0:T(256)S(1)}, u32[]{:S(2)}) copy-start(f32[256]{0:T(256)S(1)} %get-tuple-element.46) | copy-start | bytes 3076
  248.5 158.4 %copy-start.53 = (f32[256]{0:T(256)}, f32[256]{0:T(256)S(1)}, u32[]{:S(2)}) copy-start(f32[256]{0:T(256)S(1)} %get-tuple-element.57) | copy-start | bytes 3076
  406.9 332.4 %reduce-scatter.6.cloned.1.call-start = ((), (), s32[]{:S(2)}) async-start(), calls=%async_computation.9 | async-start | bytes 5242880 | tf_op jit(solution)/shard_map/reduce_scatter | solution.py:340
  445.7 41.9 %copy-start.4 = (f32[256,2048]{1,0:T(8,128)S(1)}, f32[256,2048]{1,0:T(8,128)}, u32[]{:S(2)}) copy-start(f32[256,2048]{1,0:T(8,128)} %copy-done.3) | copy-start | bytes 6291460
  445.7 41.9 %copy-start.46 = (f32[2048,1]{0,1:T(1,128)S(1)}, f32[2048,1]{0,1:T(1,128)}, u32[]{:S(2)}) copy-start(f32[2048,1]{0,1:T(1,128)} %copy-done.45) | copy-start | bytes 24580
  445.7 41.9 %copy-start.49 = (f32[256]{0:T(256)S(1)}, f32[256]{0:T(256)}, u32[]{:S(2)}) copy-start(f32[256]{0:T(256)} %copy-done.48) | copy-start | bytes 3076
  490.7 49.2 %copy-start.8 = (f32[256,2048]{1,0:T(8,128)}, f32[256,2048]{1,0:T(8,128)S(1)}, u32[]{:S(2)}) copy-start(f32[256,2048]{1,0:T(8,128)S(1)} %convert_add_fusion.1) | copy-start | bytes 6291460
  521.5 217.8 %reduce-scatter.8.cloned.1.call-start = ((), (), s32[]{:S(2)}) async-start(), calls=%async_computation.10 | async-start | bytes 5242880 | tf_op jit(solution)/shard_map/reduce_scatter | solution.py:340
  545.5 41.6 %copy-start.31 = (bf16[16,128,256]{1,2,0:T(8,128)(2,1)S(1)}, bf16[16,128,256]{1,2,0:T(8,128)(2,1)}, u32[]{:S(2)}) copy-start(bf16[16,128,256]{1,2,0:T(8,128)(2,1)} %copy.203) | copy-start | bytes 3145732
  545.5 41.6 %copy-start.39 = (bf16[8,8,16,128]{3,2,1,0:T(8,128)(2,1)S(1)}, bf16[8,8,16,128]{3,2,1,0:T(8,128)(2,1)}, u32[]{:S(2)}) copy-start(bf16[8,8,16,128]{3,2,1,0:T(8,128)(2,1)} %copy.270) | copy-start | bytes 786436
  590.8 26.3 %copy-start.2 = (f32[16,128,128,4]{2,1,3,0:T(8,128)S(1)}, f32[16,128,128,4]{2,1,3,0:T(8,128)}, u32[]{:S(2)}) copy-start(f32[16,128,128,4]{2,1,3,0:T(8,128)} %get-tuple-element.67) | copy-start | bytes 12582916
  620.9 225.7 %reduce-scatter.14.cloned.1.call-start = ((), (), s32[]{:S(2)}) async-start(), calls=%async_computation.13 | async-start | bytes 1310720 | tf_op jit(solution)/shard_map/reduce_scatter | solution.py:340
  620.9 29.7 %copy-start.18 = (bf16[1,2048,64]{1,2,0:T(8,128)(2,1)S(1)}, bf16[1,2048,64]{1,2,0:T(8,128)(2,1)}, u32[]{:S(2)}) copy-start(bf16[1,2048,64]{1,2,0:T(8,128)(2,1)} %copy-done.16) | copy-start | bytes 786436
  678.3 170.0 %reduce-scatter.10.cloned.1.call-start = ((), (), s32[]{:S(2)}) async-start(), calls=%async_computation.11 | async-start | bytes 2621440 | tf_op jit(solution)/shard_map/reduce_scatter | solution.py:340
  687.0 41.5 %copy-start.12 = (bf16[256,2048]{1,0:T(8,128)(2,1)S(1)}, bf16[256,2048]{1,0:T(8,128)(2,1)}, u32[]{:S(2)}) copy-start(bf16[256,2048]{1,0:T(8,128)(2,1)} %x_ref.1) | copy-start | bytes 3145732
  687.0 41.5 %copy-start.44 = (f32[2048,1]{0,1:T(1,128)S(1)}, f32[2048,1]{0,1:T(1,128)}, u32[]{:S(2)}) copy-start(f32[2048,1]{0,1:T(1,128)} %copy-done.42) | copy-start | bytes 24580
  687.0 41.5 %copy-start.50 = (f32[256]{0:T(256)S(1)}, f32[256]{0:T(256)}, u32[]{:S(2)}) copy-start(f32[256]{0:T(256)} %add_rsqrt_fusion.1) | copy-start | bytes 3076
  687.0 43.8 %copy-start.24 = (bf16[16,128,384]{2,1,0:T(8,128)(2,1)S(1)}, bf16[16,128,384]{2,1,0:T(8,128)(2,1)}, u32[]{:S(2)}) copy-start(bf16[16,128,384]{2,1,0:T(8,128)(2,1)} %copy-done.23) | copy-start | bytes 4718596
  753.5 41.5 %copy-start.5 = (f32[256,2048]{1,0:T(8,128)S(1)}, f32[256,2048]{1,0:T(8,128)}, u32[]{:S(2)}) copy-start(f32[256,2048]{1,0:T(8,128)} %copy-done.3) | copy-start | bytes 6291460
  795.0 43.8 %copy-start.54 = (f32[256]{0:T(256)S(1)}, f32[256]{0:T(256)}, u32[]{:S(2)}) copy-start(f32[256]{0:T(256)} %copy-done.53) | copy-start | bytes 3076
  795.0 43.8 %copy-start.9 = (f32[256,2048]{1,0:T(8,128)S(1)}, f32[256,2048]{1,0:T(8,128)}, u32[]{:S(2)}) copy-start(f32[256,2048]{1,0:T(8,128)} %copy-done.8) | copy-start | bytes 6291460
  (39 other events, 334.8 us)
Sparse Core Ops, SparseCore 0:
  23.8 28.2 all-gather.14
  54.2 45.4 all-gather.6
  101.2 79.2 all-gather.10
  181.9 78.7 all-gather.8
  262.1 78.9 all-gather.12
  407.0 75.2 reduce-scatter.11
  521.6 74.7 reduce-scatter.5
  621.0 74.7 reduce-scatter.7
  698.3 27.6 reduce-scatter.13
  739.4 41.3 reduce-scatter.9

commit v3 on v2

--- a/solution.py
+++ b/solution.py
@@ -29,6 +29,7 @@
 
 
 MESH = pl.DeviceIdType.MESH
+BRIEF = pl.CostEstimate(flops=1000, bytes_accessed=1000, transcendentals=0)
 ANY = pl.BlockSpec(memory_space=pl.ANY)
 VMEM = pl.BlockSpec(memory_space=pltpu.VMEM)
 
@@ -162,6 +163,7 @@
         in_specs=[ANY],
         out_specs=ANY,
         scratch_shapes=gather_sems(chips),
+        cost_estimate=BRIEF,
         compiler_params=pltpu.CompilerParams(collective_id=call_id, has_side_effects=True),
     )(x)
 
@@ -261,6 +263,7 @@
             pltpu.SemaphoreType.DMA((2,)),
             pltpu.SemaphoreType.DMA((2,)),
         ],
+        cost_estimate=BRIEF,
         compiler_params=pltpu.CompilerParams(
             collective_id=call_id, has_side_effects=True, vmem_limit_bytes=56 << 20
         ),
@@ -304,6 +307,7 @@
             pltpu.SemaphoreType.DMA((2 * chips,)),
             pltpu.SemaphoreType.DMA,
         ],
+        cost_estimate=BRIEF,
         compiler_params=pltpu.CompilerParams(collective_id=call_id, has_side_effects=True),
     )(x)
 
@@ -338,6 +342,258 @@
 
 def scatter(values, axes, axis=0):
     return lax.psum_scatter(values, axes, scatter_dimension=axis, tiled=True)
+
+
+def dot_nt(left, right):
+    return lax.dot_general(left, right, (((1,), (1,)), ((), ())), preferred_element_type=F32)
+
+
+def head_stack(values, heads):
+    col_head = lax.broadcasted_iota(jnp.int32, values.shape, 1) // HEAD_DIM
+    return jnp.concatenate(
+        [jnp.where(col_head == h, values, jnp.zeros_like(values)) for h in range(heads)], axis=0
+    )
+
+
+def head_pick(stacked, heads):
+    rows = stacked.shape[0] // heads
+    col_head = lax.broadcasted_iota(jnp.int32, (rows, stacked.shape[1]), 1) // HEAD_DIM
+    total = jnp.zeros((rows, stacked.shape[1]), F32)
+    for h in range(heads):
+        total = jnp.where(col_head == h, stacked[h * rows : (h + 1) * rows], total)
+    return total
+
+
+def head_fold(values, heads):
+    total = values[:, :HEAD_DIM]
+    for h in range(1, heads):
+        total = total + values[:, h * HEAD_DIM : (h + 1) * HEAD_DIM]
+    return total
+
+
+def repeat_heads(values, heads):
+    return jnp.concatenate([values] * heads, axis=1)
+
+
+def own_rows(order_ref, slot):
+    return pl.ds(pl.multiple_of(order_ref[slot] * BLOCK, BLOCK), BLOCK)
+
+
+def load_prompt(heads, order_ref, qkv_ref, k_ref, v_ref, first):
+    q_cols = heads * HEAD_DIM
+    for s in range(PROMPT_BLOCKS):
+        pair = qkv_ref[own_rows(order_ref, first + s), q_cols:]
+        at = pl.ds(s * BLOCK, BLOCK)
+        k_ref[at] = repeat_heads(pair[:, :HEAD_DIM], heads)
+        v_ref[at] = repeat_heads(pair[:, HEAD_DIM:], heads)
+
+
+def soft_parts(heads, slot, q_stack, k_far, k_own):
+    far = dot_nt(k_far, q_stack)
+    own = dot_nt(k_own, q_stack)
+    limit = jnp.minimum(slot, PROMPT_BLOCKS) * BLOCK
+    far = jnp.where(lax.broadcasted_iota(jnp.int32, far.shape, 0) < limit, far, MASKED)
+    key = lax.broadcasted_iota(jnp.int32, own.shape, 0)
+    row = lax.broadcasted_iota(jnp.int32, own.shape, 1) % BLOCK
+    own = jnp.where(key <= row, own, MASKED)
+    peak = jnp.maximum(jnp.max(far, axis=0, keepdims=True), jnp.max(own, axis=0, keepdims=True))
+    far, own = jnp.exp(far - peak), jnp.exp(own - peak)
+    scale = 1.0 / (jnp.sum(far, axis=0, keepdims=True) + jnp.sum(own, axis=0, keepdims=True))
+    return far * scale, own * scale
+
+
+def scaled_stack(q, heads):
+    return head_stack((q.astype(F32) * ATTN_MULT).astype(BF16), heads)
+
+
+def attend_kernel(heads, order_ref, qkv_ref, o_ref, k_ref, v_ref, vt_ref):
+    first, slot = pl.program_id(0) * GROUP_BLOCKS, pl.program_id(1)
+    q_cols = heads * HEAD_DIM
+
+    @pl.when(slot == 0)
+    def _():
+        load_prompt(heads, order_ref, qkv_ref, k_ref, v_ref, first)
+        vt_ref[...] = v_ref[...].astype(F32).T.astype(BF16)
+
+    rows = own_rows(order_ref, first + slot)
+    mine = qkv_ref[rows, :]
+    k_own = repeat_heads(mine[:, q_cols : q_cols + HEAD_DIM], heads)
+    v_own = repeat_heads(mine[:, q_cols + HEAD_DIM :], heads)
+    far, own = soft_parts(heads, slot, scaled_stack(mine[:, :q_cols], heads), k_ref[...], k_own)
+    mixed = matmul(vt_ref[...], far.astype(BF16))
+    mixed += matmul(v_own.astype(F32).T.astype(BF16), own.astype(BF16))
+    o_ref[rows, :] = head_pick(mixed.T, heads).astype(BF16)
+
+
+def attend_back_kernel(
+    heads, order_ref, qkv_ref, d_ref, o_ref, k_ref, v_ref, kt_ref, dk_ref, dv_ref
+):
+    first, slot = pl.program_id(0) * GROUP_BLOCKS, pl.program_id(1)
+    q_cols = heads * HEAD_DIM
+
+    @pl.when(slot == 0)
+    def _():
+        load_prompt(heads, order_ref, qkv_ref, k_ref, v_ref, first)
+        kt_ref[...] = k_ref[...].astype(F32).T.astype(BF16)
+        dk_ref[...] = jnp.zeros_like(dk_ref)
+        dv_ref[...] = jnp.zeros_like(dv_ref)
+
+    rows = own_rows(order_ref, first + slot)
+    mine = qkv_ref[rows, :]
+    k_own = repeat_heads(mine[:, q_cols : q_cols + HEAD_DIM], heads)
+    v_own = repeat_heads(mine[:, q_cols + HEAD_DIM :], heads)
+    q_stack = scaled_stack(mine[:, :q_cols], heads)
+    d_stack = head_stack(d_ref[rows, :], heads)
+    far, own = soft_parts(heads, slot, q_stack, k_ref[...], k_own)
+    d_far, d_own = dot_nt(v_ref[...], d_stack), dot_nt(v_own, d_stack)
+    mean = jnp.sum(far * d_far, axis=0, keepdims=True) + jnp.sum(own * d_own, axis=0, keepdims=True)
+    d_far = (far * (d_far - mean)).astype(BF16)
+    d_own = (own * (d_own - mean)).astype(BF16)
+    dv_ref[...] += matmul(far.astype(BF16), d_stack)
+    dk_ref[...] += matmul(d_far, q_stack)
+    dv_own = matmul(own.astype(BF16), d_stack)
+    dk_own = matmul(d_own, q_stack)
+    d_q = matmul(kt_ref[...], d_far) + matmul(k_own.astype(F32).T.astype(BF16), d_own)
+    o_ref[rows, :q_cols] = (head_pick(d_q.T, heads) * ATTN_MULT).astype(BF16)
+
+    def fold(d_k, d_v):
+        return jnp.concatenate([head_fold(d_k, heads), head_fold(d_v, heads)], axis=1).astype(BF16)
+
+    @pl.when(slot < PROMPT_BLOCKS)
+    def _():
+        at = pl.ds(pl.multiple_of(slot * BLOCK, BLOCK), BLOCK)
+        dk_ref[at] += dk_own
+        dv_ref[at] += dv_own
+
+    @pl.when(slot >= PROMPT_BLOCKS)
+    def _():
+        o_ref[rows, q_cols:] = fold(dk_own, dv_own)
+
+    @pl.when(slot == GROUP_BLOCKS - 1)
+    def _():
+        for s in range(PROMPT_BLOCKS):
+            at = pl.ds(s * BLOCK, BLOCK)
+            o_ref[own_rows(order_ref, first + s), q_cols:] = fold(dk_ref[at], dv_ref[at])
+
+
+def whole(shape):
+    return pl.BlockSpec(shape, lambda g, s, order: (0,) * len(shape))
+
+
+def attend(qkv, order, heads):
+    tokens, cols = qkv.shape
+    prompt, q_cols = PROMPT_BLOCKS * BLOCK, heads * HEAD_DIM
+    return pl.pallas_call(
+        functools.partial(attend_kernel, heads),
+        out_shape=jax.ShapeDtypeStruct((tokens, q_cols), BF16),
+        grid_spec=pltpu.PrefetchScalarGridSpec(
+            num_scalar_prefetch=1,
+            grid=(tokens // (GROUP_BLOCKS * BLOCK), GROUP_BLOCKS),
+            in_specs=[whole((tokens, cols))],
+            out_specs=whole((tokens, q_cols)),
+            scratch_shapes=[
+                pltpu.VMEM((prompt, q_cols), BF16),
+                pltpu.VMEM((prompt, q_cols), BF16),
+                pltpu.VMEM((q_cols, prompt), BF16),
+            ],
+        ),
+        cost_estimate=BRIEF,
+        compiler_params=pltpu.CompilerParams(vmem_limit_bytes=40 << 20),
+    )(order, qkv)
+
+
+def attend_back(qkv, d_attended, order, heads):
+    tokens, cols = qkv.shape
+    prompt, q_cols = PROMPT_BLOCKS * BLOCK, heads * HEAD_DIM
+    return pl.pallas_call(
+        functools.partial(attend_back_kernel, heads),
+        out_shape=jax.ShapeDtypeStruct((tokens, cols), BF16),
+        grid_spec=pltpu.PrefetchScalarGridSpec(
+            num_scalar_prefetch=1,
+            grid=(tokens // (GROUP_BLOCKS * BLOCK), GROUP_BLOCKS),
+            in_specs=[whole((tokens, cols)), whole((tokens, q_cols))],
+            out_specs=whole((tokens, cols)),
+            scratch_shapes=[
+                pltpu.VMEM((prompt, q_cols), BF16),
+                pltpu.VMEM((prompt, q_cols), BF16),
+                pltpu.VMEM((q_cols, prompt), BF16),
+                pltpu.VMEM((prompt, q_cols), F32),
+                pltpu.VMEM((prompt, q_cols), F32),
+            ],
+        ),
+        cost_estimate=BRIEF,
+        compiler_params=pltpu.CompilerParams(vmem_limit_bytes=40 << 20),
+    )(order, qkv, d_attended)
+
+
+def total_kernel(grps, chips, x_ref, o_ref, over_z, over_plane, send, recv, psend, precv):
+    grp = lax.axis_index("grp")
+    chip, core = place()
+    me = chip * 2 + core
+    far = [lax.rem(grp + s, grps) for s in range(1, grps)]
+    near = [(flip(chip, s, chips), c) for s in range(1, chips) for c in (core, 1 - core)]
+    near = near + [(chip, 1 - core)]
+    barrier = pltpu.get_barrier_semaphore()
+    for g in far:
+        pl.semaphore_signal(barrier, inc=1, device_id={"grp": g}, device_id_type=MESH)
+    for to, c in near:
+        pl.semaphore_signal(
+            barrier, inc=1, device_id={"chip": to, "core": c}, device_id_type=MESH
+        )
+    pl.semaphore_wait(barrier, len(far) + len(near))
+    copies = []
+    for i, g in enumerate(far):
+        copy = pltpu.make_async_remote_copy(
+            src_ref=x_ref,
+            dst_ref=over_z.at[grp],
+            send_sem=send.at[i],
+            recv_sem=recv.at[grp],
+            device_id={"grp": g},
+            device_id_type=MESH,
+        )
+        copy.start()
+        copies.append(copy)
+    over_z[grp] = x_ref[...]
+    for g in far:
+        pltpu.make_async_remote_copy(
+            src_ref=x_ref,
+            dst_ref=over_z.at[g],
+            send_sem=send.at[0],
+            recv_sem=recv.at[g],
+            device_id={"grp": g},
+            device_id_type=MESH,
+        ).wait_recv()
+    over_plane[me] = jnp.sum(over_z[...], axis=0)
+    for i, (to, c) in enumerate(near):
+        copy = remote(over_plane.at[me], over_plane.at[me], psend.at[i], precv.at[me], to, c)
+        copy.start()
+        copies.append(copy)
+    for to, c in near:
+        slot = to * 2 + c
+        remote(over_plane.at[me], over_plane.at[slot], psend.at[0], precv.at[slot], to, c).wait_recv()
+    for copy in copies:
+        copy.wait_send()
+    o_ref[...] = jnp.sum(over_plane[...], axis=0)
+
+
+def total(x, grps, chips, call_id):
+    devs = 2 * chips
+    return pl.pallas_call(
+        functools.partial(total_kernel, grps, chips),
+        out_shape=jax.ShapeDtypeStruct(x.shape, F32),
+        in_specs=[VMEM],
+        out_specs=VMEM,
+        scratch_shapes=[
+            pltpu.VMEM((grps,) + x.shape, F32),
+            pltpu.VMEM((devs,) + x.shape, F32),
+            pltpu.SemaphoreType.DMA((grps,)),
+            pltpu.SemaphoreType.DMA((grps,)),
+            pltpu.SemaphoreType.DMA((devs,)),
+            pltpu.SemaphoreType.DMA((devs,)),
+        ],
+        cost_estimate=BRIEF,
+        compiler_params=pltpu.CompilerParams(collective_id=call_id, has_side_effects=True),
+    )(x)
 
 
 def norm_parts(values):
@@ -374,7 +630,8 @@
     rows = tokens.shape[0]
     w_rows = w_query.shape[0]
     q_heads = HEADS // devs
-    kv_heads = max(1, KV_HEADS // devs)
+    kv_heads = 1
+    assert devs % KV_HEADS == 0
     kv_copies = max(1, devs // KV_HEADS)
     q_cols, kv_cols = q_heads * HEAD_DIM, kv_heads * HEAD_DIM
     row_blocks = rows // BLOCK * devs
@@ -392,16 +649,19 @@
         return jnp.repeat(w, kv_copies, axis=1) if kv_copies > 1 else w
 
     gains = jnp.stack([attn_gain, mlp_gain], axis=1)
-    gains = jnp.broadcast_to(
-        jnp.pad(gains, ((0, 0), (0, 126)))[:, None, :], (w_rows, devs, 128)
-    )
+    cols = D // 4
+    room = cols - q_cols - 2 * kv_cols
+    gains = jnp.pad(gains, ((0, 0), (0, room - 2)))
+    gains = jnp.broadcast_to(gains[:, None, :], (w_rows, devs, room))
     packed = jnp.concatenate(
         [w_query.reshape(w_rows, devs, q_cols), kv_split(w_key), kv_split(w_value), gains], axis=2
     )
     packed = jnp.swapaxes(packed, 0, 1)
     packed = plane_exchange(packed, packed.shape, by_slot, by_slot, chips, 1)
-    packed, w_out = lax.optimization_barrier((packed, w_out))
-    packed = gather(packed.reshape(devs * w_rows, q_cols + 2 * kv_cols + 128), "grp")
+    packed = jnp.concatenate([packed.reshape(devs * w_rows, cols), w_out.reshape(-1, cols)])
+    packed = gather(packed[None], "grp")
+    out_full = packed[:, devs * w_rows :].reshape(grps, w_rows, D)
+    packed = packed[:, : devs * w_rows].reshape(D, cols)
     w_qkv = packed[:, : q_cols + 2 * kv_cols]
     gain_one = packed[:, q_cols + 2 * kv_cols].astype(F32)
     gain_two = packed[:, q_cols + 2 * kv_cols + 1].astype(F32)
@@ -410,44 +670,11 @@
     layer_all = all_tokens.astype(F32)
     normed_one = (layer_all * norm_parts(layer_all) * gain_one).astype(BF16)
     qkv = matmul(normed_one, w_qkv).astype(BF16)
-    qkv = qkv.reshape(row_blocks, BLOCK, q_cols + 2 * kv_cols)[order]
-    qkv = qkv.reshape(row_groups, GROUP_BLOCKS * BLOCK, q_cols + 2 * kv_cols)
-    seq = GROUP_BLOCKS * BLOCK
-    per_kv = q_heads // kv_heads
-    q = qkv[:, :, :q_cols].reshape(row_groups, seq, kv_heads, per_kv, HEAD_DIM)
-    k = qkv[:, :, q_cols : q_cols + kv_cols].reshape(row_groups, seq, kv_heads, HEAD_DIM)
-    v = qkv[:, :, q_cols + kv_cols :].reshape(row_groups, seq, kv_heads, HEAD_DIM)
-    prompt = PROMPT_BLOCKS * BLOCK
-    row_id = jnp.arange(seq)
-    q_b = q.reshape(row_groups, GROUP_BLOCKS, BLOCK, kv_heads, per_kv, HEAD_DIM)
-    k_b = k.reshape(row_groups, GROUP_BLOCKS, BLOCK, kv_heads, HEAD_DIM)
-    v_b = v.reshape(row_groups, GROUP_BLOCKS, BLOCK, kv_heads, HEAD_DIM)
-    k_p, v_p = k[:, :prompt], v[:, :prompt]
-    starts = jnp.minimum(jnp.arange(GROUP_BLOCKS), PROMPT_BLOCKS) * BLOCK
-    see_p = jnp.arange(prompt)[None, :] < starts[:, None]
-    see_o = jnp.arange(BLOCK)[None, :] <= jnp.arange(BLOCK)[:, None]
-
-    def all_scores():
-        far = jnp.einsum("gbikpd,gjkd->gbkpij", q_b, k_p, preferred_element_type=F32)
-        far = jnp.where(see_p[None, :, None, None, None, :], far * ATTN_MULT, MASKED)
-        own = jnp.einsum("gbikpd,gbjkd->gbkpij", q_b, k_b, preferred_element_type=F32)
-        own = jnp.where(see_o[None, None, None, None, :, :], own * ATTN_MULT, MASKED)
-        return far, own
-
-    far, own = all_scores()
-    peak = jnp.maximum(far.max(-1, keepdims=True), own.max(-1, keepdims=True))
-    far, own = jnp.exp(far - peak), jnp.exp(own - peak)
-    total = far.sum(-1, keepdims=True) + own.sum(-1, keepdims=True)
-    far_p, own_p = far / total, own / total
-    attended = jnp.einsum(
-        "gbkpij,gjkd->gbikpd", far_p.astype(BF16), v_p, preferred_element_type=F32
-    ) + jnp.einsum("gbkpij,gbjkd->gbikpd", own_p.astype(BF16), v_b, preferred_element_type=F32)
-    attended = attended.astype(BF16).reshape(row_blocks, BLOCK, q_cols)[rank]
+    attended = attend(qkv, order, q_heads)
     attended = plane_exchange(
-        attended.reshape(row_blocks * BLOCK, q_cols), (rows, D), by_rows(rows), by_cols(q_cols), chips, 3
-    )
-
-    out_full = gather(w_out[None], "grp")
+        attended, (rows, D), by_rows(rows), by_cols(q_cols), chips, 3
+    )
+
     out_full = plane_gather(out_full, chips, 4, inner=True).reshape(D, D)
     layer_in = tokens.astype(F32)
     branch_attn = matmul(attended, out_full)
@@ -456,7 +683,9 @@
     normed_two = (residual * factor_two * gain_two).astype(BF16)
     normed_two = plane_gather(normed_two, chips, 2).reshape(devs * rows, D)
     upstream = cotangent.astype(F32)
-    d_branch_mlp = plane_gather((RESID_MULT * upstream).astype(BF16), chips, 2)
+    d_branch_mlp = (RESID_MULT * upstream).astype(BF16)
+    d_branch_mlp, normed_two = lax.optimization_barrier((d_branch_mlp, normed_two))
+    d_branch_mlp = plane_gather(d_branch_mlp, chips, 2)
     d_branch_mlp = d_branch_mlp.reshape(devs * rows, D)
 
     gate_w = gather(w_gate, "grp", axis=1)
@@ -493,41 +722,19 @@
     d_attended = plane_exchange(
         d_attended, (devs * rows, q_cols), by_cols(q_cols), by_rows(rows), chips, 7
     )
-    d_b = d_attended.reshape(row_blocks, BLOCK, q_cols)[order]
-    d_b = d_b.reshape(row_groups, GROUP_BLOCKS, BLOCK, kv_heads, per_kv, HEAD_DIM)
-
-    far_s = jnp.einsum("gbikpd,gjkd->gbkpij", d_b, v_p, preferred_element_type=F32)
-    own_s = jnp.einsum("gbikpd,gbjkd->gbkpij", d_b, v_b, preferred_element_type=F32)
-    mean_s = (far_p * far_s).sum(-1, keepdims=True) + (own_p * own_s).sum(-1, keepdims=True)
-    far_d = (far_p * (far_s - mean_s)).astype(BF16)
-    own_d = (own_p * (own_s - mean_s)).astype(BF16)
-    far_p, own_p = far_p.astype(BF16), own_p.astype(BF16)
-    d_q = ATTN_MULT * (
-        jnp.einsum("gbkpij,gjkd->gbikpd", far_d, k_p, preferred_element_type=F32)
-        + jnp.einsum("gbkpij,gbjkd->gbikpd", own_d, k_b, preferred_element_type=F32)
-    )
-    d_k = jnp.einsum("gbkpij,gbikpd->gbjkd", own_d, q_b, preferred_element_type=F32)
-    d_v = jnp.einsum("gbkpij,gbikpd->gbjkd", own_p, d_b, preferred_element_type=F32)
-    d_kp = jnp.einsum("gbkpij,gbikpd->gjkd", far_d, q_b, preferred_element_type=F32)
-    d_vp = jnp.einsum("gbkpij,gbikpd->gjkd", far_p, d_b, preferred_element_type=F32)
-    d_k = ATTN_MULT * jnp.concatenate([d_k.reshape(row_groups, seq, kv_cols)[:, :prompt] + d_kp.reshape(row_groups, prompt, kv_cols), d_k.reshape(row_groups, seq, kv_cols)[:, prompt:]], axis=1)
-    d_v = jnp.concatenate([d_v.reshape(row_groups, seq, kv_cols)[:, :prompt] + d_vp.reshape(row_groups, prompt, kv_cols), d_v.reshape(row_groups, seq, kv_cols)[:, prompt:]], axis=1)
-    d_qkv = jnp.concatenate([d_q.reshape(row_groups, seq, q_cols), d_k, d_v], axis=2).astype(BF16)
-    d_qkv = d_qkv.reshape(row_blocks, BLOCK, q_cols + 2 * kv_cols)[rank]
-    d_qkv = d_qkv.reshape(row_blocks * BLOCK, q_cols + 2 * kv_cols)
+    d_qkv = attend_back(qkv, d_attended, order, q_heads)
+    sent = over_rows(normed_one, d_qkv).astype(BF16)
+    sent, d_qkv = lax.optimization_barrier((sent, d_qkv))
+    sent, grad_gate, grad_up = lax.optimization_barrier((sent, grad_gate, grad_up))
+    sent = scatter(sent, "grp")
 
     d_normed_one = over_cols(d_qkv, w_qkv).astype(BF16).reshape(devs, rows, D)
     d_normed_one = plane_reduce(d_normed_one, chips, 5)
     d_input_norm, d_gain_one = norm_back(layer_in, norm_parts(layer_in), gain_one, d_normed_one)
     tokens_grad = (d_residual + d_input_norm).astype(BF16)
 
-    grad_qkv = over_rows(normed_one, d_qkv)
-    d_gains = jnp.pad(jnp.stack([d_gain_one, d_gain_two], axis=1), ((0, 0), (0, 126)))
-    sent = jnp.concatenate([grad_qkv, d_gains], axis=1).astype(BF16)
-    sent, grad_gate, grad_up = lax.optimization_barrier((sent, grad_gate, grad_up))
-    sent = scatter(sent, "grp")
-    sent = sent.reshape(devs, w_rows, q_cols + 2 * kv_cols + 128)
-    sent = plane_exchange(sent, sent.shape, by_slot, by_slot, chips, 1).astype(F32)
+    sent = sent.reshape(devs, w_rows, q_cols + 2 * kv_cols)
+    sent = plane_exchange(sent, sent.shape, by_slot, by_slot, chips, 9).astype(F32)
 
     def kv_join(g):
         g = g.reshape(devs // kv_copies, kv_copies, w_rows, kv_cols)
@@ -537,10 +744,9 @@
     grad_query = jnp.swapaxes(sent[:, :, :q_cols], 0, 1).reshape(w_rows, D)
     grad_key = kv_join(sent[:, :, q_cols : q_cols + kv_cols])
     grad_value = kv_join(sent[:, :, q_cols + kv_cols : q_cols + 2 * kv_cols])
-    gains_sum = jnp.sum(sent[:, :, q_cols + 2 * kv_cols :], axis=0)
 
     branch_mlp = matmul(hidden, down_w).astype(BF16).reshape(devs, rows, D)
-    branch_mlp, d_qkv = lax.optimization_barrier((branch_mlp, d_qkv))
+    branch_mlp, d_normed_one = lax.optimization_barrier((branch_mlp, d_normed_one))
     branch_mlp = plane_reduce(branch_mlp, chips, 5)
     layer_out = residual + RESID_MULT * branch_mlp
     scaled_attn = RESID_MULT * branch_attn
@@ -552,17 +758,20 @@
             jnp.sum(scaled_mlp * scaled_mlp),
         ]
     )
-    totals = lax.psum(squares, EVERY)
-    rms_stats = jnp.sqrt(totals / (rows * grps * devs * D))
+    totals = jnp.stack([d_gain_one, d_gain_two, jnp.pad(squares, (0, D - 3))])
+    totals = total(jnp.pad(totals, ((0, 5), (0, 0))), grps, chips, 8)
+    rms_stats = jnp.sqrt(totals[2, :3] / (rows * grps * devs * D))
+    gain_first = (lax.axis_index("grp") * devs + lax.axis_index(PLANE)) * w_rows
+    gain_grads = lax.dynamic_slice(totals, (0, gain_first), (2, w_rows))
     return (
         layer_out.astype(BF16),
         tokens_grad,
-        gains_sum[:, 0],
+        gain_grads[0],
         grad_query,
         grad_key,
         grad_value,
         grad_out,
-        gains_sum[:, 1],
+        gain_grads[1],
         grad_gate.astype(F32),
         grad_up.astype(F32),
         grad_down.astype(F32),

time: 882 us -> 803 us (0.910)
  matrix products: 293 us -> 184 us
  Pallas kernels: 379 us -> 468 us
  other arithmetic: 101 us -> 42.7 us
  waiting for transfers between devices: 11.3 us -> 62.2 us
  blocking collectives: 37.4 us -> 0 us
  local copies, waits for them, and re-layouts: 34.8 us -> 21.2 us
    dot_general x12 -> x0, matrix products: 99.1 us -> none  [the longest x1 26.3 us: on_device(): jnp.einsum('gbikpd,gjkd->gbkpij', d_b, v_p, preferred_element_type=F32)]
    pallas_call x0 -> x3, Pallas kernels: none -> 92.5 us  [the longest x1 48.3 us: attend_back(): pl.pallas_call(functools.partial(attend_back_kernel, heads), out_shape=ja...]
    psum x1 -> x0, blocking collectives: 37.4 us -> none  [on_device(): totals = lax.psum(squares, EVERY)]
    another operation x4 -> x1, other arithmetic: 31.5 us -> 0.66 us  [on_device(): totals = jnp.stack([d_gain_one, d_gain_two, jnp.pad(squares, (0, D - 3))])]
    reduce_scatter x5, waiting for transfers between devices: 0.03 us -> 28.8 us  [scatter(): return lax.psum_scatter(values, axes, scatter_dimension=axis, tiled=True)]
    all_gather x5 -> x4, waiting for transfers between devices: 9.47 us -> 30.8 us  [gather(): return lax.all_gather(values, axes, axis=axis, tiled=True)]
    reduce_sum x3 -> x0, other arithmetic: 15.8 us -> none  [the longest x2 15.8 us: on_device(): total = far.sum(-1, keepdims=True) + own.sum(-1, keepdims=True)]
    dot_general x5, matrix products: 70.3 us -> 58.1 us  [matmul(): return jnp.dot(left, right, preferred_element_type=F32)]
  transfers between devices with their start and end apart: 10 -> 9, of which waited for: 1 -> 3; matrix products, arithmetic and copies ran while one was open for 40% -> 21% of each run, Pallas kernels for 41% -> 57%
where the time goes in v3:
time: 803 us; the launch traced here: 794 us
  Pallas kernels  468 us (58%)
  matrix products  184 us (23%)
  waiting for transfers between devices  62.2 us (8%)
  other arithmetic  42.7 us (5%)
  local copies, waits for them, and re-layouts  21.2 us (3%)
  between operations  15 us (2%)
    pallas_call x4, Pallas kernels, plane_reduce(): pl.pallas_call(functools.partial(reduce_kernel, chips, inner), out_shape=...  166 us
    pallas_call x4, Pallas kernels, plane_gather(): pl.pallas_call(functools.partial(gather_kernel, chips, inner), out_shape=...  160 us
    dot_general x5, matrix products, over_cols(): lax.dot_general(left, right, (((1,), (1,)), ((), ())), preferred_element_...  68.6 us
    dot_general x5, matrix products, matmul(): return jnp.dot(left, right, preferred_element_type=F32)  58.1 us
    dot_general x5, matrix products, over_rows(): lax.dot_general(left, right, (((0,), (0,)), ((), ())), preferred_element_...  57.1 us
    pallas_call x4, Pallas kernels, plane_exchange(): pl.pallas_call(functools.partial(exchange_kernel, chips, cut, paste), out...  49.7 us
    pallas_call x1, Pallas kernels, attend_back(): pl.pallas_call(functools.partial(attend_back_kernel, heads), out_shape=ja...  48.3 us
    all_gather x4, waiting for transfers between devices, gather(): return lax.all_gather(values, axes, axis=axis, tiled=True)  30.8 us
  transfers between devices with their start and end apart: 9, of which 3 were waited for; matrix products, arithmetic and copies ran while one was open for 21% of the time, Pallas kernels for 57%

profile of v3, /device:TPU:0, one launch (start us, length us, event | category | flops | bytes accessed | tf_op | source)
XLA Modules:
  0.0 793.9 jit_solution(17393977901045769224)
XLA Ops:
  12.0 11.5 %shard_map.221 = bf16[8,64,512]{2,1,0:T(8,128)(2,1)} custom-call(bf16[8,64,512]{2,1,0:T(8,128)(2,1)} %maximum_bitcast_fusion.x_ref), custom_call_target="tpu_custom_call" | custom-call | flops 1000 | bytes 1000 | tf_op jit(solution)/shard_map/pallas_call | solution.py:300
  28.1 39.9 %shard_map.220 = bf16[8,256,2048]{2,1,0:T(8,128)(2,1)} custom-call(bf16[256,2048]{1,0:T(8,128)(2,1)} %x_ref.1), custom_call_target="tpu_custom_call" | custom-call | flops 1000 | bytes 1000 | tf_op jit(solution)/shard_map/pallas_call | solution.py:160
  73.6 17.0 %all-gather.12.cloned.1.call-done = bf16[3072,512]{1,0:T(8,128)(2,1)} async-done(((bf16[768,512]{1,0:T(8,128)(2,1)}), bf16[3072,512]{1,0:T(8,128)(2,1)}) %all-gather.12.cloned.1.call-update) | async-done | bytes 3145744 | tf_op jit(solution)/shard_map/all_gather | solution.py:340
  95.2 9.1 %fusion.1 = bf16[2048,2048]{1,0:T(8,128)(2,1)} fusion(f32[2048]{0:T(1024)S(1)} %bitcast.101, f32[2048]{0:T(1024)S(1)} %bitcast.107, bf16[8,256,2048]{2,1,0:T(8,128)(2,1)} %shard_map.220), kind=kLoop, calls=%fused_computation.2 | loop fusion | flops 16777216 | bytes 16793600 | tf_op jit(solution)/shard_map/convert_element_type | solution.py:671
  104.3 8.0 %convolution_convert_fusion.7.qkv_ref = bf16[2048,384]{1,0:T(8,128)(2,1)S(1)} fusion(bf16[2048,2048]{1,0:T(8,128)(2,1)} %fusion.1, bf16[2048,512]{1,0:T(8,128)(2,1)S(1)} %bitcast.92), kind=kOutput, calls=%fused_computation.22 | convolution fusion | flops 3222011904 | bytes 11534336 | tf_op jit(solution)/shard_map/dot_general | solution.py:328
  112.3 25.6 %shard_map.222.x_ref = bf16[2048,256]{1,0:T(8,128)(2,1)S(1)} custom-call(s32[16]{0:T(128)S(1)} %select_reduce_fusion.order_ref, bf16[2048,384]{1,0:T(8,128)(2,1)S(1)} %convolution_convert_fusion.7.qkv_ref), custom_call_target="tpu_custom_call" | custom-call | flops 1000 | bytes 1000 | tf_op jit(solution)/shard_map/pallas_call | solution.py:486
  143.1 15.4 %shard_map.223 = bf16[256,2048]{1,0:T(8,128)(2,1)} custom-call(bf16[2048,256]{1,0:T(8,128)(2,1)} %copy-done.3), custom_call_target="tpu_custom_call" | custom-call | flops 1000 | bytes 1000 | tf_op jit(solution)/shard_map/pallas_call | solution.py:300
  158.5 40.0 %shard_map.224 = bf16[4,8,64,2048]{3,2,1,0:T(8,128)(2,1)} custom-call(bf16[4,64,2048]{2,1,0:T(8,128)(2,1)} %reshape.168.x_ref), custom_call_target="tpu_custom_call" | custom-call | flops 1000 | bytes 1000 | tf_op jit(solution)/shard_map/pallas_call | solution.py:160
  209.4 40.0 %shard_map.225 = bf16[8,256,2048]{2,1,0:T(8,128)(2,1)} custom-call(bf16[256,2048]{1,0:T(8,128)(2,1)} %multiply_convert_fusion.4.x_ref), custom_call_target="tpu_custom_call" | custom-call | flops 1000 | bytes 1000 | tf_op jit(solution)/shard_map/pallas_call | solution.py:160
  249.4 40.0 %shard_map.226 = bf16[8,256,2048]{2,1,0:T(8,128)(2,1)} custom-call(bf16[256,2048]{1,0:T(8,128)(2,1)} %fusion.3.x_ref), custom_call_target="tpu_custom_call" | custom-call | flops 1000 | bytes 1000 | tf_op jit(solution)/shard_map/pallas_call | solution.py:160
  289.4 14.5 %fusion.18 = f32[2048,1024]{1,0:T(8,128)} fusion(bf16[2048,2048]{1,0:T(8,128)(2,1)} %bitcast.87, bf16[2048,1024]{1,0:T(8,128)(2,1)} %all-gather.6.cloned.1.call-done), kind=kOutput, calls=%fused_computation.80 | convolution fusion | flops 8589934592 | bytes 20971520 | tf_op jit(solution)/shard_map/dot_general | solution.py:328
  303.9 14.5 %fusion.19 = f32[2048,1024]{1,0:T(8,128)} fusion(bf16[2048,2048]{1,0:T(8,128)(2,1)} %bitcast.88, bf16[2048,1024]{1,0:T(8,128)(2,1)} %all-gather.8.cloned.1.call-done), kind=kOutput, calls=%fused_computation.81 | convolution fusion | flops 8589934592 | bytes 20971520 | tf_op jit(solution)/shard_map/dot_general | solution.py:328
  318.3 13.8 %all-gather.10.cloned.1.call-done = bf16[1024,2048]{1,0:T(8,128)(2,1)} async-done(((bf16[256,2048]{1,0:T(8,128)(2,1)}), bf16[1024,2048]{1,0:T(8,128)(2,1)}) %all-gather.10.cloned.1.call-update) | async-done | bytes 4194320 | tf_op jit(solution)/shard_map/all_gather | solution.py:340
  332.1 23.4 %multiply_convert_fusion = (bf16[2048,1024]{1,0:T(8,128)(2,1)}, bf16[2048,1024]{1,0:T(8,128)(2,1)}, bf16[2048,1024]{1,0:T(8,128)(2,1)}) fusion(f32[2048,1024]{1,0:T(8,128)} %fusion.18, f32[2048,1024]{1,0:T(8,128)} %fusion.19, bf16[2048,2048]{1,0:T(8,128)(2,1)} %bitcast.85, bf16[1024,2048]{1,0:T(8,128)(2,1)} %all-gather.10.cloned.1.call-done), kind=kOutput, calls=%fused_computation.5 | convolution fusion | flops 8621391872 | bytes 41943040 | tf_op jit(solution)/shard_map/dot_general | solution.py:336
  355.5 14.0 %convolution_convert_fusion.4 = bf16[2048,1024]{1,0:T(8,128)(2,1)} fusion(bf16[2048,2048]{1,0:T(8,128)(2,1)} %bitcast.89, bf16[2048,1024]{1,0:T(8,128)(2,1)} %get-tuple-element.30), kind=kOutput, calls=%fused_computation.19 | convolution fusion | flops 8592031744 | bytes 16777216 | tf_op jit(solution)/shard_map/dot_general | solution.py:332
  369.5 14.2 %convolution_convert_fusion.5 = bf16[2048,1024]{1,0:T(8,128)(2,1)} fusion(bf16[2048,2048]{1,0:T(8,128)(2,1)} %bitcast.90, bf16[2048,1024]{1,0:T(8,128)(2,1)} %get-tuple-element.29), kind=kOutput, calls=%fused_computation.20 | convolution fusion | flops 8592031744 | bytes 16777216 | tf_op jit(solution)/shard_map/dot_general | solution.py:332
  383.7 14.1 %convolution_convert_fusion.3 = bf16[1024,2048]{1,0:T(8,128)(2,1)} fusion(bf16[2048,1024]{1,0:T(8,128)(2,1)} %get-tuple-element.52, bf16[2048,2048]{1,0:T(8,128)(2,1)} %bitcast.86), kind=kOutput, calls=%fused_computation.18 | convolution fusion | flops 8592031744 | bytes 16777216 | tf_op jit(solution)/shard_map/dot_general | solution.py:332
  399.2 16.3 %fusion.20 = f32[2048,2048]{1,0:T(8,128)} fusion(bf16[2048,1024]{1,0:T(8,128)(2,1)} %get-tuple-element.29, bf16[2048,1024]{1,0:T(8,128)(2,1)} %all-gather.6.cloned.1.call-done), kind=kOutput, calls=%fused_computation.82 | convolution fusion | flops 8589934592 | bytes 25165824 | tf_op jit(solution)/shard_map/dot_general | solution.py:336
  415.5 14.3 %add_convert_fusion = bf16[2048,2048]{1,0:T(8,128)(2,1)} fusion(f32[2048,2048]{1,0:T(8,128)} %fusion.20, bf16[2048,1024]{1,0:T(8,128)(2,1)S(1)} %copy-done.35, bf16[2048,1024]{1,0:T(8,128)(2,1)S(1)} %copy-done.34), kind=kOutput, calls=%fused_computation.3 | convolution fusion | flops 8598323200 | bytes 33554432 | tf_op jit(solution)/shard_map/dot_general | solution.py:336
  429.9 41.6 %shard_map.227 = f32[256,2048]{1,0:T(8,128)} custom-call(bf16[8,256,2048]{2,1,0:T(8,128)(2,1)} %bitcast.81), custom_call_target="tpu_custom_call" | custom-call | flops 1000 | bytes 1000 | tf_op jit(solution)/shard_map/pallas_call | solution.py:246
  480.8 41.2 %shard_map.234 = bf16[4,64,2048]{2,1,0:T(8,128)(2,1)} custom-call(bf16[4,8,64,2048]{3,2,1,0:T(8,128)(2,1)} %bitcast.79), custom_call_target="tpu_custom_call" | custom-call | flops 1000 | bytes 1000 | tf_op jit(solution)/shard_map/pallas_call | solution.py:246
  522.2 7.5 convolution_convert_fusion.8.x_ref
  529.7 15.1 %shard_map.228.d_ref = bf16[2048,256]{1,0:T(8,128)(2,1)} custom-call(bf16[256,2048]{1,0:T(8,128)(2,1)} %convolution_convert_fusion.8.x_ref), custom_call_target="tpu_custom_call" | custom-call | flops 1000 | bytes 1000 | tf_op jit(solution)/shard_map/pallas_call | solution.py:300
  546.0 48.3 %shard_map.229 = bf16[2048,384]{1,0:T(8,128)(2,1)S(1)} custom-call(s32[16]{0:T(128)S(1)} %copy-done.5, bf16[2048,384]{1,0:T(8,128)(2,1)S(1)} %copy-done.1, bf16[2048,256]{1,0:T(8,128)(2,1)S(1)} %copy-done.2), custom_call_target="tpu_custom_call" | custom-call | flops 1000 | bytes 1000 | tf_op jit(solution)/shard_map/pallas_call | solution.py:508
  594.3 9.3 %convolution_convert_fusion.6 = bf16[2048,384]{1,0:T(8,128)(2,1)} fusion(bf16[2048,2048]{1,0:T(8,128)(2,1)} %fusion.1, bf16[2048,384]{1,0:T(8,128)(2,1)S(1)} %shard_map.229), kind=kOutput, calls=%fused_computation.21 | convolution fusion | flops 3222011904 | bytes 11534336 | tf_op jit(solution)/shard_map/dot_general | solution.py:332
  603.6 28.8 %reduce-scatter.8.cloned.1.call-done = bf16[2048,256]{1,0:T(8,128)(2,1)} async-done(((bf16[2048,1024]{1,0:T(8,128)(2,1)}), bf16[2048,256]{1,0:T(8,128)(2,1)}) %reduce-scatter.8.cloned.1.call-update) | async-done | bytes 1048592 | tf_op jit(solution)/shard_map/reduce_scatter | solution.py:344
  632.4 14.3 %convolution_convert_fusion.2 = bf16[2048,2048]{1,0:T(8,128)(2,1)} fusion(bf16[2048,1024]{1,0:T(8,128)(2,1)} %get-tuple-element.52, bf16[1024,2048]{1,0:T(8,128)(2,1)} %all-gather.10.cloned.1.call-done), kind=kOutput, calls=%fused_computation.12 | convolution fusion | flops 8594128896 | bytes 16777216 | tf_op jit(solution)/shard_map/dot_general | solution.py:328
  646.8 7.1 convolution_convert_fusion.1
  653.8 42.0 %shard_map.230 = f32[256,2048]{1,0:T(8,128)} custom-call(bf16[8,256,2048]{2,1,0:T(8,128)(2,1)} %bitcast.82), custom_call_target="tpu_custom_call" | custom-call | flops 1000 | bytes 1000 | tf_op jit(solution)/shard_map/pallas_call | solution.py:246
  695.9 41.6 %shard_map.231 = f32[256,2048]{1,0:T(8,128)} custom-call(bf16[8,256,2048]{2,1,0:T(8,128)(2,1)} %bitcast.80), custom_call_target="tpu_custom_call" | custom-call | flops 1000 | bytes 1000 | tf_op jit(solution)/shard_map/pallas_call | solution.py:246
  746.6 18.6 %shard_map.232 = f32[8,2048]{1,0:T(8,128)} custom-call(f32[8,2048]{1,0:T(8,128)} %select_maximum_fusion.x_ref), custom_call_target="tpu_custom_call" | custom-call | flops 1000 | bytes 1000 | tf_op jit(solution)/shard_map/pallas_call | solution.py:581
  775.2 7.7 shard_map.233
  (149 shorter events, 70.5 us)
Async XLA Ops:
  7.2 83.4 %all-gather.12.cloned.1.call-start = ((), (), s32[]{:S(2)}) async-start(), calls=%async_computation.13 | async-start | bytes 3932160 | tf_op jit(solution)/shard_map/all_gather | solution.py:340
  26.6 262.8 %all-gather.6.cloned.1.call-start = ((), (), s32[]{:S(2)}) async-start(), calls=%async_computation.5 | async-start | bytes 5242880 | tf_op jit(solution)/shard_map/all_gather | solution.py:340
  27.4 276.5 %all-gather.8.cloned.1.call-start = ((), (), s32[]{:S(2)}) async-start(), calls=%async_computation.6 | async-start | bytes 5242880 | tf_op jit(solution)/shard_map/all_gather | solution.py:340
  28.1 304.0 %all-gather.10.cloned.1.call-start = ((), (), s32[]{:S(2)}) async-start(), calls=%async_computation.7 | async-start | bytes 5242880 | tf_op jit(solution)/shard_map/all_gather | solution.py:340
  73.6 38.7 %copy-start.4 = (s32[16]{0:T(128)}, s32[16]{0:T(128)S(1)}, u32[]{:S(2)}) copy-start(s32[16]{0:T(128)S(1)} %select_reduce_fusion.order_ref) | copy-start | bytes 196
  92.3 12.0 %copy-start.17 = (bf16[4,512,512]{2,1,0:T(8,128)(2,1)}, bf16[4,512,512]{2,1,0:T(8,128)(2,1)S(1)}, u32[]{:S(2)}) copy-start(bf16[4,512,512]{2,1,0:T(8,128)(2,1)S(1)} %slice.44) | copy-start | bytes 6291460
  95.2 9.1 %copy-start.23 = (f32[2048,1]{0,1:T(1,128)}, f32[2048,1]{0,1:T(1,128)S(1)}, u32[]{:S(2)}) copy-start(f32[2048,1]{0,1:T(1,128)S(1)} %copy.50) | copy-start | bytes 24580
  142.8 379.2 %reduce-scatter.12.cloned.1.call-start = ((), (), s32[]{:S(2)}) async-start(), calls=%async_computation.11 | async-start | bytes 5242880 | tf_op jit(solution)/shard_map/reduce_scatter | solution.py:344
  158.5 40.3 %copy-start.13 = (bf16[256,2048]{1,0:T(8,128)(2,1)S(1)}, bf16[256,2048]{1,0:T(8,128)(2,1)}, u32[]{:S(2)}) copy-start(bf16[256,2048]{1,0:T(8,128)(2,1)} %x_ref.1) | copy-start | bytes 3145732
  158.5 40.3 %copy-start.15 = (bf16[256,2048]{1,0:T(8,128)(2,1)S(1)}, bf16[256,2048]{1,0:T(8,128)(2,1)}, u32[]{:S(2)}) copy-start(bf16[256,2048]{1,0:T(8,128)(2,1)} %shard_map.223) | copy-start | bytes 3145732
  198.8 6.9 copy-start.25
  198.8 9.4 %copy-start.19 = (bf16[256,2048]{1,0:T(8,128)(2,1)S(1)}, bf16[256,2048]{1,0:T(8,128)(2,1)}, u32[]{:S(2)}) copy-start(bf16[256,2048]{1,0:T(8,128)(2,1)} %param.25) | copy-start | bytes 3145732
  205.7 43.7 %copy-start.30 = (f32[256]{0:T(256)}, f32[256]{0:T(256)S(1)}, u32[]{:S(2)}) copy-start(f32[256]{0:T(256)S(1)} %get-tuple-element.48) | copy-start | bytes 3076
  397.8 205.8 %reduce-scatter.6.cloned.1.call-start = ((), (), s32[]{:S(2)}) async-start(), calls=%async_computation.8 | async-start | bytes 5242880 | tf_op jit(solution)/shard_map/reduce_scatter | solution.py:344
  398.4 234.0 %reduce-scatter.8.cloned.1.call-start = ((), (), s32[]{:S(2)}) async-start(), calls=%async_computation.9 | async-start | bytes 5242880 | tf_op jit(solution)/shard_map/reduce_scatter | solution.py:344
  399.1 374.3 %reduce-scatter.14.cloned.1.call-start = ((), (), s32[]{:S(2)}) async-start(), calls=%async_computation.12 | async-start | bytes 1310720 | tf_op jit(solution)/shard_map/reduce_scatter | solution.py:344
  399.2 16.3 %copy-start.34 = (bf16[2048,1024]{1,0:T(8,128)(2,1)S(1)}, bf16[2048,1024]{1,0:T(8,128)(2,1)}, u32[]{:S(2)}) copy-start(bf16[2048,1024]{1,0:T(8,128)(2,1)} %all-gather.8.cloned.1.call-done) | copy-start | bytes 12582916
  399.2 16.3 %copy-start.35 = (bf16[2048,1024]{1,0:T(8,128)(2,1)S(1)}, bf16[2048,1024]{1,0:T(8,128)(2,1)}, u32[]{:S(2)}) copy-start(bf16[2048,1024]{1,0:T(8,128)(2,1)} %get-tuple-element.30) | copy-start | bytes 12582916
  429.8 41.7 %copy-start.7 = (f32[256,2048]{1,0:T(8,128)S(1)}, f32[256,2048]{1,0:T(8,128)}, u32[]{:S(2)}) copy-start(f32[256,2048]{1,0:T(8,128)} %copy-done.6) | copy-start | bytes 6291460
  429.8 41.7 %copy-start.26 = (f32[2048,1]{0,1:T(1,128)S(1)}, f32[2048,1]{0,1:T(1,128)}, u32[]{:S(2)}) copy-start(f32[2048,1]{0,1:T(1,128)} %copy-done.25) | copy-start | bytes 24580
  429.9 41.7 %copy-start.28 = (f32[256]{0:T(256)S(1)}, f32[256]{0:T(256)}, u32[]{:S(2)}) copy-start(f32[256]{0:T(256)} %copy-done.27) | copy-start | bytes 3076
  522.1 253.2 %reduce-scatter.10.cloned.1.call-start = ((), (), s32[]{:S(2)}) async-start(), calls=%async_computation.10 | async-start | bytes 1966080 | tf_op jit(solution)/shard_map/reduce_scatter | solution.py:344
  522.1 22.6 %copy-start.29 = (f32[256]{0:T(256)S(1)}, f32[256]{0:T(256)}, u32[]{:S(2)}) copy-start(f32[256]{0:T(256)} %get-tuple-element.57) | copy-start | bytes 3076
  522.1 22.6 %copy-start.1 = (bf16[2048,384]{1,0:T(8,128)(2,1)S(1)}, bf16[2048,384]{1,0:T(8,128)(2,1)}, u32[]{:S(2)}) copy-start(bf16[2048,384]{1,0:T(8,128)(2,1)} %copy-done) | copy-start | bytes 4718596
  522.2 22.6 %copy-start.5 = (s32[16]{0:T(128)S(1)}, s32[16]{0:T(128)}, u32[]{:S(2)}) copy-start(s32[16]{0:T(128)} %copy-done.4) | copy-start | bytes 196
  632.4 14.4 %copy-start.18 = (bf16[4,512,512]{2,1,0:T(8,128)(2,1)S(1)}, bf16[4,512,512]{2,1,0:T(8,128)(2,1)}, u32[]{:S(2)}) copy-start(bf16[4,512,512]{2,1,0:T(8,128)(2,1)} %copy-done.17) | copy-start | bytes 6291460
  695.9 41.6 %copy-start.12 = (f32[256,2048]{1,0:T(8,128)S(1)}, f32[256,2048]{1,0:T(8,128)}, u32[]{:S(2)}) copy-start(f32[256,2048]{1,0:T(8,128)} %shard_map.230) | copy-start | bytes 6291460
  695.9 41.6 %copy-start.14 = (bf16[256,2048]{1,0:T(8,128)(2,1)S(1)}, bf16[256,2048]{1,0:T(8,128)(2,1)}, u32[]{:S(2)}) copy-start(bf16[256,2048]{1,0:T(8,128)(2,1)} %x_ref.1) | copy-start | bytes 3145732
  695.9 41.6 %copy-start.24 = (f32[2048,1]{0,1:T(1,128)S(1)}, f32[2048,1]{0,1:T(1,128)}, u32[]{:S(2)}) copy-start(f32[2048,1]{0,1:T(1,128)} %copy-done.23) | copy-start | bytes 24580
  695.9 42.3 %copy-start.10 = (f32[256,2048]{1,0:T(8,128)S(1)}, f32[256,2048]{1,0:T(8,128)}, u32[]{:S(2)}) copy-start(f32[256,2048]{1,0:T(8,128)} %copy-done.9) | copy-start | bytes 6291460
  739.1 28.6 %copy-start.21 = (bf16[256,2048]{1,0:T(8,128)(2,1)S(1)}, bf16[256,2048]{1,0:T(8,128)(2,1)}, u32[]{:S(2)}) copy-start(bf16[256,2048]{1,0:T(8,128)(2,1)} %reduce-scatter.12.cloned.1.call-done) | copy-start | bytes 3145732
  739.1 30.1 %copy-start.22 = (bf16[2048,256]{1,0:T(8,128)(2,1)S(1)}, bf16[2048,256]{1,0:T(8,128)(2,1)}, u32[]{:S(2)}) copy-start(bf16[2048,256]{1,0:T(8,128)(2,1)} %reduce-scatter.6.cloned.1.call-done) | copy-start | bytes 3145732
  (13 other events, 33.4 us)
Sparse Core Ops, SparseCore 0:
  26.7 63.7 all-gather.11
  92.1 79.2 all-gather.5
  172.9 78.7 all-gather.7
  253.1 78.9 all-gather.9
  397.9 75.2 reduce-scatter.11
  475.5 77.2 reduce-scatter.5
  555.1 77.2 reduce-scatter.7
  634.8 27.6 reduce-scatter.13
  664.8 33.9 reduce-scatter.9

commit v4 on v3

--- a/solution.py
+++ b/solution.py
@@ -268,6 +268,37 @@
             collective_id=call_id, has_side_effects=True, vmem_limit_bytes=56 << 20
         ),
     )(p)
+
+
+class Drift:
+    def __init__(self, pairs, axis):
+        self.axis = axis
+        self.chip, self.core = place()
+        away = lax.dynamic_index_in_dim(pairs, 1 - self.core, axis + 1, keepdims=False)
+        self.mine = lax.dynamic_index_in_dim(pairs, self.core, axis + 1, keepdims=False)
+        self.twin = lax.ppermute(away, "core", [(0, 1), (1, 0)])
+
+    def part(self, step):
+        at = jnp.bitwise_xor(self.chip, step)
+        mine = lax.dynamic_index_in_dim(self.mine, at, self.axis, keepdims=False)
+        twin = lax.dynamic_index_in_dim(self.twin, at, self.axis, keepdims=False)
+        return mine.astype(F32) + twin.astype(F32)
+
+    def parts(self):
+        return tuple(self.part(step).astype(BF16) for step in (1, 2, 3))
+
+    @staticmethod
+    def send(parts):
+        return tuple(
+            lax.ppermute(part, "chip", [(c, c ^ step) for c in range(4)])
+            for step, part in zip((3, 1, 2), (parts[2], parts[0], parts[1]))
+        )
+
+    def finish(self, came):
+        total = self.part(0)
+        for part in came:
+            total = total + part.astype(F32)
+        return total
 
 
 def exchange_kernel(chips, cut, paste, x_ref, o_ref, send, recv, local):
@@ -596,6 +627,193 @@
     )(x)
 
 
+def params(axes, mib=56):
+    return pltpu.CompilerParams(
+        dimension_semantics=("arbitrary",) * axes, vmem_limit_bytes=mib << 20
+    )
+
+
+def tile_rows(count, limit):
+    while count % limit:
+        limit //= 2
+    return limit
+
+
+def widen_kernel(n_ref, w_ref, h_ref, ht_ref, s_ref, t_ref, nt_ref):
+    values = n_ref[...]
+    gate, up = matmul(values, w_ref[0, 0]), matmul(values, w_ref[0, 1])
+    sig = 1.0 / (1.0 + jnp.exp(-gate))
+    silu = gate * sig
+    hidden = (silu * up).astype(BF16)
+    h_ref[0] = hidden
+    ht_ref[0] = hidden.T
+    s_ref[0] = silu.astype(BF16)
+    t_ref[0] = (up * (sig * (1.0 + gate * (1.0 - sig)))).astype(BF16)
+
+    @pl.when(pl.program_id(1) == 0)
+    def _():
+        nt_ref[...] = values.T
+
+
+def widen(normed, weights):
+    tokens, depth = normed.shape
+    shards, _, _, width = weights.shape
+    rows = tile_rows(tokens, 1024)
+    tall = jax.ShapeDtypeStruct((shards, tokens, width), BF16)
+    tall_spec = pl.BlockSpec((1, rows, width), lambda r, s: (s, r, 0))
+    return pl.pallas_call(
+        widen_kernel,
+        out_shape=(
+            tall,
+            jax.ShapeDtypeStruct((shards, width, tokens), BF16),
+            tall,
+            tall,
+            jax.ShapeDtypeStruct((depth, tokens), BF16),
+        ),
+        grid=(tokens // rows, shards),
+        in_specs=[
+            pl.BlockSpec((rows, depth), lambda r, s: (r, 0)),
+            pl.BlockSpec((1, 2, depth, width), lambda r, s: (s, 0, 0, 0)),
+        ],
+        out_specs=(
+            tall_spec,
+            pl.BlockSpec((1, width, rows), lambda r, s: (s, 0, r)),
+            tall_spec,
+            tall_spec,
+            pl.BlockSpec((depth, rows), lambda r, s: (0, r)),
+        ),
+        cost_estimate=BRIEF,
+        compiler_params=params(2),
+    )(normed, weights)
+
+
+def down_part_kernel(ht_ref, d_ref, o_ref):
+    o_ref[0] = matmul(ht_ref[0], d_ref[...]).astype(BF16)
+
+
+def down_part(hidden_t, upstream):
+    shards, width, tokens = hidden_t.shape
+    depth = upstream.shape[1]
+    cols = tile_rows(depth, 1024)
+    return pl.pallas_call(
+        down_part_kernel,
+        out_shape=jax.ShapeDtypeStruct((shards, width, depth), BF16),
+        grid=(depth // cols, shards),
+        in_specs=[
+            pl.BlockSpec((1, width, tokens), lambda c, s: (s, 0, 0)),
+            pl.BlockSpec((tokens, cols), lambda c, s: (0, c)),
+        ],
+        out_specs=pl.BlockSpec((1, width, cols), lambda c, s: (s, 0, c)),
+        cost_estimate=BRIEF,
+        compiler_params=params(2),
+    )(hidden_t, upstream)
+
+
+def mix_kernel(h_ref, w_ref, m_ref):
+    mixed = None
+    for i in range(w_ref.shape[0]):
+        part = matmul(h_ref[i], w_ref[i])
+        mixed = part if mixed is None else mixed + part
+    m_ref[...] = mixed.astype(BF16)
+
+
+def narrow_specs(hidden, weights):
+    shards, tokens, width = hidden.shape
+    depth = weights.shape[2]
+    rows = tile_rows(tokens, 512)
+    return (
+        tokens // rows,
+        pl.BlockSpec((shards, rows, width), lambda r: (0, r, 0)),
+        pl.BlockSpec((rows, depth), lambda r: (r, 0)),
+        pl.BlockSpec(weights.shape, lambda r: (0, 0, 0), pipeline_mode=pl.Buffered(1)),
+    )
+
+
+def mix(hidden, weights):
+    steps, tall_spec, flat_spec, weight_spec = narrow_specs(hidden, weights)
+    return pl.pallas_call(
+        mix_kernel,
+        out_shape=jax.ShapeDtypeStruct((hidden.shape[1], weights.shape[2]), BF16),
+        grid=(steps,),
+        in_specs=[tall_spec, weight_spec],
+        out_specs=flat_spec,
+        cost_estimate=BRIEF,
+        compiler_params=params(1),
+    )(hidden, weights)
+
+
+def narrow_back_kernel(s_ref, t_ref, d_ref, w_ref, dg_ref, du_ref):
+    upstream = d_ref[...]
+    for i in range(w_ref.shape[0]):
+        d_hidden = dot_nt(upstream, w_ref[i])
+        dg_ref[i] = (d_hidden * t_ref[i].astype(F32)).astype(BF16)
+        du_ref[i] = (d_hidden * s_ref[i].astype(F32)).astype(BF16)
+
+
+def narrow_back(silu, slope, upstream, weights):
+    steps, tall_spec, flat_spec, weight_spec = narrow_specs(silu, weights)
+    tall = jax.ShapeDtypeStruct(silu.shape, BF16)
+    return pl.pallas_call(
+        narrow_back_kernel,
+        out_shape=(tall, tall),
+        grid=(steps,),
+        in_specs=[tall_spec, tall_spec, flat_spec, weight_spec],
+        out_specs=(tall_spec, tall_spec),
+        cost_estimate=BRIEF,
+        compiler_params=params(1),
+    )(silu, slope, upstream, weights)
+
+
+def widen_part_kernel(nt_ref, dg_ref, du_ref, o_ref):
+    values = nt_ref[...]
+    o_ref[0, 0] = matmul(values, dg_ref[0]).astype(BF16)
+    o_ref[0, 1] = matmul(values, du_ref[0]).astype(BF16)
+
+
+def widen_part(normed_t, d_gate, d_up):
+    depth, tokens = normed_t.shape
+    shards, _, width = d_gate.shape
+    rows = tile_rows(depth, 1024)
+    tall_spec = pl.BlockSpec((1, tokens, width), lambda r, s: (s, 0, 0))
+    return pl.pallas_call(
+        widen_part_kernel,
+        out_shape=jax.ShapeDtypeStruct((shards, 2, depth, width), BF16),
+        grid=(depth // rows, shards),
+        in_specs=[pl.BlockSpec((rows, tokens), lambda r, s: (r, 0)), tall_spec, tall_spec],
+        out_specs=pl.BlockSpec((1, 2, rows, width), lambda r, s: (s, 0, r, 0)),
+        cost_estimate=BRIEF,
+        compiler_params=params(2),
+    )(normed_t, d_gate, d_up)
+
+
+def widen_back_kernel(dg_ref, du_ref, w_ref, o_ref):
+    total = None
+    for i in range(w_ref.shape[0]):
+        part = dot_nt(dg_ref[i], w_ref[i, 0]) + dot_nt(du_ref[i], w_ref[i, 1])
+        total = part if total is None else total + part
+    o_ref[...] = total.astype(BF16)
+
+
+def widen_back(d_gate, d_up, weights):
+    shards, tokens, width = d_gate.shape
+    depth = weights.shape[2]
+    rows = tile_rows(tokens, 512)
+    tall_spec = pl.BlockSpec((shards, rows, width), lambda r: (0, r, 0))
+    return pl.pallas_call(
+        widen_back_kernel,
+        out_shape=jax.ShapeDtypeStruct((tokens, depth), BF16),
+        grid=(tokens // rows,),
+        in_specs=[
+            tall_spec,
+            tall_spec,
+            pl.BlockSpec(weights.shape, lambda r: (0, 0, 0, 0), pipeline_mode=pl.Buffered(1)),
+        ],
+        out_specs=pl.BlockSpec((rows, depth), lambda r: (r, 0)),
+        cost_estimate=BRIEF,
+        compiler_params=params(1),
+    )(d_gate, d_up, weights)
+
+
 def norm_parts(values):
     factor = lax.rsqrt(jnp.mean(values * values, axis=-1, keepdims=True) + EPSILON)
     return factor
@@ -688,44 +906,61 @@
     d_branch_mlp = plane_gather(d_branch_mlp, chips, 2)
     d_branch_mlp = d_branch_mlp.reshape(devs * rows, D)
 
-    gate_w = gather(w_gate, "grp", axis=1)
-    up_w = gather(w_up, "grp", axis=1)
-    down_w = gather(w_down, "grp")
-    gate_act = matmul(normed_two, gate_w)
-    up_act = matmul(normed_two, up_w)
-    sig = jax.nn.sigmoid(gate_act)
-    silu = gate_act * sig
-    hidden = (silu * up_act).astype(BF16)
-    part_down = over_rows(hidden, d_branch_mlp).astype(BF16)
-    d_hidden = over_cols(d_branch_mlp, down_w)
-    d_gate = (d_hidden * up_act * (sig * (1.0 + gate_act * (1.0 - sig)))).astype(BF16)
-    d_up = (d_hidden * silu).astype(BF16)
-    part_gate = over_rows(normed_two, d_gate).astype(BF16)
-    part_up = over_rows(normed_two, d_up).astype(BF16)
-    d_gate, d_up, part_down, part_gate, part_up = lax.optimization_barrier(
-        (d_gate, d_up, part_down, part_gate, part_up)
-    )
+    wide_w = gather(jnp.stack([w_gate, w_up])[None], "grp")
+    down_w = gather(w_down[None], "grp")
+    normed_two, d_branch_mlp = lax.optimization_barrier((normed_two, d_branch_mlp))
+    hidden, hidden_t, silu, slope, normed_t = widen(normed_two, wide_w)
+    part_down = down_part(hidden_t, d_branch_mlp)
+    part_down, hidden, silu = lax.optimization_barrier((part_down, hidden, silu))
     grad_down = scatter(part_down, "grp")
-    grad_gate = scatter(part_gate, "grp", axis=1)
-    grad_up = scatter(part_up, "grp", axis=1)
-    d_normed_two = over_cols(d_gate, gate_w) + over_cols(d_up, up_w)
-    d_normed_two = plane_reduce(d_normed_two.astype(BF16).reshape(devs, rows, D), chips, 5)
+    branch_mlp = mix(hidden, down_w)
+    drift_mlp = None
+    if chips == 4:
+        drift_mlp = Drift(branch_mlp.reshape(4, 2, rows, D), 0)
+    branch_mlp, silu = lax.optimization_barrier((branch_mlp, silu))
+    d_gate, d_up = narrow_back(silu, slope, d_branch_mlp, down_w)
+    if chips == 4:
+        sent_mlp, d_gate, d_up = lax.optimization_barrier((drift_mlp.parts(), d_gate, d_up))
+        sent_mlp = Drift.send(sent_mlp)
+    part_wide = widen_part(normed_t, d_gate, d_up)
+    part_wide, d_gate, d_up = lax.optimization_barrier((part_wide, d_gate, d_up))
+    grad_wide = scatter(part_wide, "grp")
+    d_normed_two = widen_back(d_gate, d_up, wide_w)
+    if chips == 4:
+        sent_mlp, d_normed_two = lax.optimization_barrier((sent_mlp, d_normed_two))
+        branch_mlp = drift_mlp.finish(sent_mlp)
+    d_normed_two = plane_reduce(d_normed_two.reshape(devs, rows, D), chips, 5)
+    if chips != 4:
+        branch_mlp = plane_reduce(branch_mlp.reshape(devs, rows, D), chips, 5)
+    layer_out = residual + RESID_MULT * branch_mlp
 
     d_residual_norm, d_gain_two = norm_back(residual, factor_two, gain_two, d_normed_two)
     d_residual = upstream + d_residual_norm
     d_branch_attn = (RESID_MULT * d_residual).astype(BF16)
-    grad_out = over_rows(attended, d_branch_attn).astype(BF16).reshape(grps, devs, w_rows, D)
-    grad_out = plane_reduce(grad_out, chips, 6, dtype=BF16, inner=True)
-    grad_out, grad_down = lax.optimization_barrier((grad_out, grad_down))
-    grad_out = scatter(grad_out, "grp").reshape(w_rows, D).astype(F32)
+    grad_out = over_rows(attended, d_branch_attn).astype(BF16)
+    grad_out, d_branch_attn = lax.optimization_barrier((grad_out, d_branch_attn))
+    if chips == 4:
+        drift_out = Drift(grad_out.reshape(grps, 4, 2, w_rows, D), 1)
     d_attended = over_cols(d_branch_attn, out_full).astype(BF16)
     d_attended = plane_exchange(
         d_attended, (devs * rows, q_cols), by_cols(q_cols), by_rows(rows), chips, 7
     )
+    if chips == 4:
+        sent_out, d_attended = lax.optimization_barrier((drift_out.parts(), d_attended))
+        sent_out = Drift.send(sent_out)
+    d_attended, grad_down = lax.optimization_barrier((d_attended, grad_down))
     d_qkv = attend_back(qkv, d_attended, order, q_heads)
+    if chips == 4:
+        sent_out, d_qkv = lax.optimization_barrier((sent_out, d_qkv))
+        grad_out = drift_out.finish(sent_out).astype(BF16)
+    else:
+        grad_out = plane_reduce(
+            grad_out.reshape(grps, devs, w_rows, D), chips, 6, dtype=BF16, inner=True
+        )
+    grad_out = scatter(grad_out, "grp").reshape(w_rows, D).astype(F32)
     sent = over_rows(normed_one, d_qkv).astype(BF16)
     sent, d_qkv = lax.optimization_barrier((sent, d_qkv))
-    sent, grad_gate, grad_up = lax.optimization_barrier((sent, grad_gate, grad_up))
+    sent, grad_wide = lax.optimization_barrier((sent, grad_wide))
     sent = scatter(sent, "grp")
 
     d_normed_one = over_cols(d_qkv, w_qkv).astype(BF16).reshape(devs, rows, D)
@@ -745,10 +980,6 @@
     grad_key = kv_join(sent[:, :, q_cols : q_cols + kv_cols])
     grad_value = kv_join(sent[:, :, q_cols + kv_cols : q_cols + 2 * kv_cols])
 
-    branch_mlp = matmul(hidden, down_w).astype(BF16).reshape(devs, rows, D)
-    branch_mlp, d_normed_one = lax.optimization_barrier((branch_mlp, d_normed_one))
-    branch_mlp = plane_reduce(branch_mlp, chips, 5)
-    layer_out = residual + RESID_MULT * branch_mlp
     scaled_attn = RESID_MULT * branch_attn
     scaled_mlp = RESID_MULT * branch_mlp
     squares = jnp.stack(
@@ -772,9 +1003,9 @@
         grad_value,
         grad_out,
         gain_grads[1],
-        grad_gate.astype(F32),
-        grad_up.astype(F32),
-        grad_down.astype(F32),
+        grad_wide[0, 0].astype(F32),
+        grad_wide[0, 1].astype(F32),
+        grad_down[0].astype(F32),
         rms_stats,
     )
 

time: 803 us -> 716 us (0.89)
  matrix products: 184 us -> 38.6 us
  Pallas kernels: 468 us -> 510 us
  other arithmetic: 42.7 us -> 68 us
  waiting for transfers between devices: 62.2 us -> 38.8 us
    pallas_call x0 -> x6, Pallas kernels: none -> 123 us  [the longest x1 30.6 us: widen(): pl.pallas_call(widen_kernel, out_shape=(tall, jax.ShapeDtypeStruct((shard...]
    pallas_call x4 -> x2, Pallas kernels: 166 us -> 83.1 us  [plane_reduce(): pl.pallas_call(functools.partial(reduce_kernel, chips, inner), out_shape=...]
    dot_general x5 -> x2, matrix products: 68.6 us -> 11.7 us  [over_cols(): lax.dot_general(left, right, (((1,), (1,)), ((), ())), preferred_element_...]
    dot_general x5 -> x2, matrix products: 57.1 us -> 11.5 us  [over_rows(): lax.dot_general(left, right, (((0,), (0,)), ((), ())), preferred_element_...]
    dot_general x5 -> x2, matrix products: 58.1 us -> 15.3 us  [matmul(): return jnp.dot(left, right, preferred_element_type=F32)]
    reduce_scatter x5 -> x4, waiting for transfers between devices: 28.8 us -> 0.41 us  [scatter(): return lax.psum_scatter(values, axes, scatter_dimension=axis, tiled=True)]
    convert_element_type x3 -> x7, other arithmetic: 5.75 us -> 28.4 us  [the longest x2 11 us: parts(): return tuple((self.part(step).astype(BF16) for step in (1, 2, 3)))]
    ppermute x0 -> x8, waiting for transfers between devices: none -> 21.5 us  [the longest x6 21.5 us: send(): lax.ppermute(part, 'chip', [(c, c ^ step) for c in range(4)])]
  transfers between devices with their start and end apart: 9 -> 15, of which waited for: 3 -> 4; matrix products, arithmetic and copies ran while one was open for 21% -> 17% of each run, Pallas kernels for 57% -> 69%
where the time goes in v4:
time: 716 us; the launch traced here: 707 us
  Pallas kernels  510 us (71%)
  other arithmetic  68 us (9%)
  waiting for transfers between devices  38.8 us (5%)
  matrix products  38.6 us (5%)
  local copies, waits for them, and re-layouts  28.7 us (4%)
  between operations  15.1 us (2%)
  starting transfers between devices  7.84 us (1%)
    pallas_call x4, Pallas kernels, plane_gather(): pl.pallas_call(functools.partial(gather_kernel, chips, inner), out_shape=...  160 us
    pallas_call x2, Pallas kernels, plane_reduce(): pl.pallas_call(functools.partial(reduce_kernel, chips, inner), out_shape=...  83.1 us
    pallas_call x4, Pallas kernels, plane_exchange(): pl.pallas_call(functools.partial(exchange_kernel, chips, cut, paste), out...  50.2 us
    pallas_call x1, Pallas kernels, attend_back(): pl.pallas_call(functools.partial(attend_back_kernel, heads), out_shape=ja...  48.4 us
    pallas_call x1, Pallas kernels, widen(): pl.pallas_call(widen_kernel, out_shape=(tall, jax.ShapeDtypeStruct((shard...  30.6 us
    pallas_call x1, Pallas kernels, attend(): pl.pallas_call(functools.partial(attend_kernel, heads), out_shape=jax.Sha...  25.6 us
    pallas_call x1, Pallas kernels, widen_back(): pl.pallas_call(widen_back_kernel, out_shape=jax.ShapeDtypeStruct((tokens,...  23.9 us
    pallas_call x1, Pallas kernels, widen_part(): pl.pallas_call(widen_part_kernel, out_shape=jax.ShapeDtypeStruct((shards,...  23.5 us
  transfers between devices with their start and end apart: 15, of which 4 were waited for; matrix products, arithmetic and copies ran while one was open for 17% of the time, Pallas kernels for 69%

profile of v4, /device:TPU:0, one launch (start us, length us, event | category | flops | bytes accessed | tf_op | source)
XLA Modules:
  0.0 706.8 jit_solution(253566418396521262)
XLA Ops:
  12.1 11.5 %shard_map.221 = bf16[8,64,512]{2,1,0:T(8,128)(2,1)} custom-call(bf16[8,64,512]{2,1,0:T(8,128)(2,1)} %maximum_bitcast_fusion.x_ref), custom_call_target="tpu_custom_call" | custom-call | flops 1000 | bytes 1000 | tf_op jit(solution)/shard_map/pallas_call | solution.py:331
  28.1 39.9 %shard_map.220 = bf16[8,256,2048]{2,1,0:T(8,128)(2,1)} custom-call(bf16[256,2048]{1,0:T(8,128)(2,1)} %x_ref.1), custom_call_target="tpu_custom_call" | custom-call | flops 1000 | bytes 1000 | tf_op jit(solution)/shard_map/pallas_call | solution.py:160
  68.0 5.1 multiply_reduce_fusion
  73.6 16.1 %all-gather.7.cloned.1.call-done = bf16[3072,512]{1,0:T(8,128)(2,1)} async-done(((bf16[768,512]{1,0:T(8,128)(2,1)}), bf16[3072,512]{1,0:T(8,128)(2,1)}) %all-gather.7.cloned.1.call-update) | async-done | bytes 3145744 | tf_op jit(solution)/shard_map/all_gather | solution.py:371
  95.6 9.5 %fusion.1 = bf16[2048,2048]{1,0:T(8,128)(2,1)} fusion(f32[2048]{0:T(1024)S(1)} %bitcast.173, f32[2048]{0:T(1024)S(1)} %bitcast.176, bf16[8,256,2048]{2,1,0:T(8,128)(2,1)} %shard_map.220), kind=kLoop, calls=%fused_computation.2 | loop fusion | flops 16777216 | bytes 16793600 | tf_op jit(solution)/shard_map/convert_element_type | solution.py:889
  105.1 8.3 %convolution_convert_fusion.3.qkv_ref = bf16[2048,384]{1,0:T(8,128)(2,1)S(1)} fusion(bf16[2048,2048]{1,0:T(8,128)(2,1)} %fusion.1, bf16[2048,512]{1,0:T(8,128)(2,1)} %bitcast.158), kind=kOutput, calls=%fused_computation.14 | convolution fusion | flops 3222011904 | bytes 11534336 | tf_op jit(solution)/shard_map/dot_general | solution.py:359
  115.1 25.6 %shard_map.222.x_ref = bf16[2048,256]{1,0:T(8,128)(2,1)S(1)} custom-call(s32[16]{0:T(128)S(1)} %select_reduce_fusion.order_ref, bf16[2048,384]{1,0:T(8,128)(2,1)S(1)} %convolution_convert_fusion.3.qkv_ref), custom_call_target="tpu_custom_call" | custom-call | flops 1000 | bytes 1000 | tf_op jit(solution)/shard_map/pallas_call | solution.py:517
  141.6 40.0 %shard_map.224 = bf16[4,8,64,2048]{3,2,1,0:T(8,128)(2,1)} custom-call(bf16[4,64,2048]{2,1,0:T(8,128)(2,1)} %reshape.222.x_ref), custom_call_target="tpu_custom_call" | custom-call | flops 1000 | bytes 1000 | tf_op jit(solution)/shard_map/pallas_call | solution.py:160
  181.6 15.3 %shard_map.223 = bf16[256,2048]{1,0:T(8,128)(2,1)} custom-call(bf16[2048,256]{1,0:T(8,128)(2,1)} %copy-done.1), custom_call_target="tpu_custom_call" | custom-call | flops 1000 | bytes 1000 | tf_op jit(solution)/shard_map/pallas_call | solution.py:331
  198.5 7.0 multiply_reduce_fusion.6
  209.2 40.0 %shard_map.225 = bf16[8,256,2048]{2,1,0:T(8,128)(2,1)} custom-call(bf16[256,2048]{1,0:T(8,128)(2,1)} %multiply_convert_fusion.1.x_ref), custom_call_target="tpu_custom_call" | custom-call | flops 1000 | bytes 1000 | tf_op jit(solution)/shard_map/pallas_call | solution.py:160
  249.2 40.0 %shard_map.226 = bf16[8,256,2048]{2,1,0:T(8,128)(2,1)} custom-call(bf16[256,2048]{1,0:T(8,128)(2,1)} %fusion.2.x_ref), custom_call_target="tpu_custom_call" | custom-call | flops 1000 | bytes 1000 | tf_op jit(solution)/shard_map/pallas_call | solution.py:160
  289.3 30.6 %shard_map.227 = (bf16[4,2048,256]{2,1,0:T(8,128)(2,1)}, bf16[4,256,2048]{2,1,0:T(8,128)(2,1)}, bf16[4,2048,256]{2,1,0:T(8,128)(2,1)}, bf16[4,2048,256]{2,1,0:T(8,128)(2,1)}, bf16[2048,2048]{1,0:T(8,128)(2,1)}) custom-call(bf16[2048,2048]{1,0:T(8,128)(2,1)} %bitcast.149, bf16[4,2,2048,256]{3,2,1,0:T(8,128)(2,1)} %bitcast.144), custom_call_target="tpu_custom_call" | custom-call | flops 1000 | bytes 1000 | tf_op jit(solution)/shard_map/pallas_call | solution.py:664
  319.8 15.4 %shard_map.228 = bf16[4,256,2048]{2,1,0:T(8,128)(2,1)} custom-call(bf16[4,256,2048]{2,1,0:T(8,128)(2,1)} %get-tuple-element.58.ht_ref, bf16[2048,2048]{1,0:T(8,128)(2,1)} %bitcast.138), custom_call_target="tpu_custom_call" | custom-call | flops 1000 | bytes 1000 | tf_op jit(solution)/shard_map/pallas_call | solution.py:698
  335.4 13.8 %shard_map.229 = bf16[2048,2048]{1,0:T(8,128)(2,1)} custom-call(bf16[4,2048,256]{2,1,0:T(8,128)(2,1)} %get-tuple-element.62.h_ref, bf16[4,256,2048]{2,1,0:T(8,128)(2,1)} %bitcast.150), custom_call_target="tpu_custom_call" | custom-call | flops 1000 | bytes 1000 | tf_op jit(solution)/shard_map/pallas_call | solution.py:734
  349.1 4.8 dynamic-slice_bitcast_fusion
  354.3 15.3 %shard_map.230 = (bf16[4,2048,256]{2,1,0:T(8,128)(2,1)}, bf16[4,2048,256]{2,1,0:T(8,128)(2,1)}) custom-call(bf16[4,2048,256]{2,1,0:T(8,128)(2,1)} %get-tuple-element.64.s_ref, bf16[4,2048,256]{2,1,0:T(8,128)(2,1)} %get-tuple-element.65.t_ref, bf16[2048,2048]{1,0:T(8,128)(2,1)} %bitcast.139, bf16[4,256,2048]{2,1,0:T(8,128)(2,1)} %bitcast.151), custom_call_target="tpu_custom_call" | custom-call | flops 1000 | bytes 1000 | tf_op jit(solution)/shard_map/pallas_call | solution.py:756
  369.6 5.4 fusion.17
  375.0 23.5 %shard_map.231 = bf16[4,2,2048,256]{3,2,1,0:T(8,128)(2,1)} custom-call(bf16[2048,2048]{1,0:T(8,128)(2,1)} %get-tuple-element.71.nt_ref, bf16[4,2048,256]{2,1,0:T(8,128)(2,1)} %get-tuple-element.74.dg_ref, bf16[4,2048,256]{2,1,0:T(8,128)(2,1)} %get-tuple-element.75.du_ref), custom_call_target="tpu_custom_call" | custom-call | flops 1000 | bytes 1000 | tf_op jit(solution)/shard_map/pallas_call | solution.py:778
  402.2 23.9 %shard_map.232 = bf16[2048,2048]{1,0:T(8,128)(2,1)} custom-call(bf16[4,2048,256]{2,1,0:T(8,128)(2,1)} %get-tuple-element.74.dg_ref, bf16[4,2048,256]{2,1,0:T(8,128)(2,1)} %get-tuple-element.75.du_ref, bf16[4,2,2048,256]{3,2,1,0:T(8,128)(2,1)} %bitcast.145), custom_call_target="tpu_custom_call" | custom-call | flops 1000 | bytes 1000 | tf_op jit(solution)/shard_map/pallas_call | solution.py:802
  426.1 20.9 %collective-permute-done.2 = bf16[256,2048]{1,0:T(8,128)(2,1)} collective-permute-done((bf16[256,2048]{1,0:T(8,128)(2,1)}, bf16[256,2048]{1,0:T(8,128)(2,1)}, u32[]{:S(2)}, u32[]{:S(2)}) %collective-permute-start.2) | collective-permute-done | bytes 1048608 | tf_op jit(solution)/shard_map/ppermute | solution.py:293
  447.6 41.5 %shard_map.233 = f32[256,2048]{1,0:T(8,128)} custom-call(bf16[8,256,2048]{2,1,0:T(8,128)(2,1)} %bitcast.143), custom_call_target="tpu_custom_call" | custom-call | flops 1000 | bytes 1000 | tf_op jit(solution)/shard_map/pallas_call | solution.py:246
  489.1 7.0 multiply_reduce_fusion.4
  507.8 14.7 %shard_map.234.d_ref = bf16[2048,256]{1,0:T(8,128)(2,1)} custom-call(bf16[256,2048]{1,0:T(8,128)(2,1)} %convolution_convert_fusion.4.x_ref), custom_call_target="tpu_custom_call" | custom-call | flops 1000 | bytes 1000 | tf_op jit(solution)/shard_map/pallas_call | solution.py:331
  522.5 5.5 fusion.14
  531.5 48.4 %shard_map.235 = bf16[2048,384]{1,0:T(8,128)(2,1)S(1)} custom-call(s32[16]{0:T(128)S(1)} %select_reduce_fusion.order_ref, bf16[2048,384]{1,0:T(8,128)(2,1)S(1)} %convolution_convert_fusion.3.qkv_ref, bf16[2048,256]{1,0:T(8,128)(2,1)S(1)} %copy-done), custom_call_target="tpu_custom_call" | custom-call | flops 1000 | bytes 1000 | tf_op jit(solution)/shard_map/pallas_call | solution.py:539
  587.9 9.1 %convolution_convert_fusion.2 = bf16[2048,384]{1,0:T(8,128)(2,1)} fusion(bf16[2048,2048]{1,0:T(8,128)(2,1)} %fusion.1, bf16[2048,384]{1,0:T(8,128)(2,1)S(1)} %copy-done.3), kind=kOutput, calls=%fused_computation.13 | convolution fusion | flops 3222011904 | bytes 11534336 | tf_op jit(solution)/shard_map/dot_general | solution.py:363
  597.0 8.4 %convolution_convert_fusion = bf16[2048,2048]{1,0:T(8,128)(2,1)} fusion(bf16[2048,384]{1,0:T(8,128)(2,1)S(1)} %copy-done.3, bf16[2048,512]{1,0:T(8,128)(2,1)} %bitcast.159), kind=kOutput, calls=%fused_computation.4 | convolution fusion | flops 3225419776 | bytes 11534336 | tf_op jit(solution)/shard_map/dot_general | solution.py:367
  605.4 41.6 %shard_map.236 = f32[256,2048]{1,0:T(8,128)} custom-call(bf16[8,256,2048]{2,1,0:T(8,128)(2,1)} %bitcast.152), custom_call_target="tpu_custom_call" | custom-call | flops 1000 | bytes 1000 | tf_op jit(solution)/shard_map/pallas_call | solution.py:246
  652.6 20.2 %shard_map.237 = f32[8,2048]{1,0:T(8,128)} custom-call(f32[8,2048]{1,0:T(8,128)} %select_maximum_fusion.x_ref), custom_call_target="tpu_custom_call" | custom-call | flops 1000 | bytes 1000 | tf_op jit(solution)/shard_map/pallas_call | solution.py:612
  675.3 5.5 fusion.7
  686.8 8.8 %shard_map.238 = bf16[8,64,384]{2,1,0:T(8,128)(2,1)} custom-call(bf16[8,64,384]{2,1,0:T(8,128)(2,1)} %bitcast.167), custom_call_target="tpu_custom_call" | custom-call | flops 1000 | bytes 1000 | tf_op jit(solution)/shard_map/pallas_call | solution.py:331
  (130 shorter events, 69.3 us)
Async XLA Ops:
  7.2 16.4 %copy-start.16 = (bf16[64,2048]{1,0:T(8,128)(2,1)S(1)}, bf16[64,2048]{1,0:T(8,128)(2,1)}, u32[]{:S(2)}) copy-start(bf16[64,2048]{1,0:T(8,128)(2,1)} %param.20) | copy-start | bytes 786436
  7.2 82.5 %all-gather.7.cloned.1.call-start = ((), (), s32[]{:S(2)}) async-start(), calls=%async_computation.8 | async-start | bytes 3932160 | tf_op jit(solution)/shard_map/all_gather | solution.py:371
  12.1 13.7 %copy-start.14 = (bf16[2048,256]{1,0:T(8,128)(2,1)S(1)}, bf16[2048,256]{1,0:T(8,128)(2,1)}, u32[]{:S(2)}) copy-start(bf16[2048,256]{1,0:T(8,128)(2,1)} %param.23) | copy-start | bytes 3145732
  12.1 13.7 %copy-start.15 = (bf16[2048,256]{1,0:T(8,128)(2,1)S(1)}, bf16[2048,256]{1,0:T(8,128)(2,1)}, u32[]{:S(2)}) copy-start(bf16[2048,256]{1,0:T(8,128)(2,1)} %param.22) | copy-start | bytes 3145732
  25.7 263.5 %all-gather.9.cloned.1.call-start = ((), (), s32[]{:S(2)}) async-start(), calls=%async_computation.9 | async-start | bytes 10485760 | tf_op jit(solution)/shard_map/all_gather | solution.py:371
  27.3 308.0 %all-gather.11.cloned.1.call-start = ((), (), s32[]{:S(2)}) async-start(), calls=%async_computation.10 | async-start | bytes 5242880 | tf_op jit(solution)/shard_map/all_gather | solution.py:371
  28.1 503.4 %reduce-scatter.5.cloned.1.call-start = ((), (), s32[]{:S(2)}) async-start(), calls=%async_computation.4 | async-start | bytes 5242880 | tf_op jit(solution)/shard_map/reduce_scatter | solution.py:375
  68.0 5.2 copy-start.17
  68.0 5.2 copy-start.18
  92.7 1.3 copy-start.13
  181.6 16.9 %copy-start.9 = (bf16[256,2048]{1,0:T(8,128)(2,1)S(1)}, bf16[256,2048]{1,0:T(8,128)(2,1)}, u32[]{:S(2)}) copy-start(bf16[256,2048]{1,0:T(8,128)(2,1)} %x_ref.1) | copy-start | bytes 3145732
  205.5 2.5 copy-start.11
  335.3 313.8 %reduce-scatter.7.cloned.1.call-start = ((), (), s32[]{:S(2)}) async-start(), calls=%async_computation.5 | async-start | bytes 10485760 | tf_op jit(solution)/shard_map/reduce_scatter | solution.py:375
  353.9 15.7 %collective-permute-start = (bf16[4,256,2048]{2,1,0:T(8,128)(2,1)}, bf16[4,256,2048]{2,1,0:T(8,128)(2,1)}, u32[]{:S(2)}, u32[]{:S(2)}) collective-permute-start(bf16[4,256,2048]{2,1,0:T(8,128)(2,1)} %dynamic-slice_bitcast_fusion), channel_id=1, source_target_pairs={{0,1},{1,0},{2,3},{3,2},{4,5},{5,4},{6,7},{7,6},{8,9},{9,8},{10,11... | collective-permute-start | bytes 12582920 | tf_op jit(solution)/shard_map/ppermute | solution.py:279
  398.6 282.2 %reduce-scatter.11.cloned.1.call-start = ((), (), s32[]{:S(2)}) async-start(), calls=%async_computation.7 | async-start | bytes 1310720 | tf_op jit(solution)/shard_map/reduce_scatter | solution.py:375
  398.6 27.5 %collective-permute-start.1 = (bf16[256,2048]{1,0:T(8,128)(2,1)}, bf16[256,2048]{1,0:T(8,128)(2,1)}, u32[]{:S(2)}, u32[]{:S(2)}) collective-permute-start(bf16[256,2048]{1,0:T(8,128)(2,1)} %get-tuple-element.68), channel_id=1, source_target_pairs={{0,6},{2,4},{4,2},{6,0},{1,7},{3,5},{5,3},{7,1},{8,14},{10,12},{12... | collective-permute-start | bytes 3145736 | tf_op jit(solution)/shard_map/ppermute | solution.py:293
  400.4 46.7 %collective-permute-start.2 = (bf16[256,2048]{1,0:T(8,128)(2,1)}, bf16[256,2048]{1,0:T(8,128)(2,1)}, u32[]{:S(2)}, u32[]{:S(2)}) collective-permute-start(bf16[256,2048]{1,0:T(8,128)(2,1)} %get-tuple-element.69), channel_id=1, source_target_pairs={{0,2},{2,0},{4,6},{6,4},{1,3},{3,1},{5,7},{7,5},{8,10},{10,8},{12,... | collective-permute-start | bytes 3145736 | tf_op jit(solution)/shard_map/ppermute | solution.py:293
  401.1 46.5 %collective-permute-start.3 = (bf16[256,2048]{1,0:T(8,128)(2,1)}, bf16[256,2048]{1,0:T(8,128)(2,1)}, u32[]{:S(2)}, u32[]{:S(2)}) collective-permute-start(bf16[256,2048]{1,0:T(8,128)(2,1)} %get-tuple-element.70), channel_id=1, source_target_pairs={{0,4},{2,6},{4,0},{6,2},{1,5},{3,7},{5,1},{7,3},{8,12},{10,14},{12... | collective-permute-start | bytes 3145736 | tf_op jit(solution)/shard_map/ppermute | solution.py:293
  447.6 41.5 %copy-start.6 = (f32[256,2048]{1,0:T(8,128)S(1)}, f32[256,2048]{1,0:T(8,128)}, u32[]{:S(2)}) copy-start(f32[256,2048]{1,0:T(8,128)} %copy-done.5) | copy-start | bytes 6291460
  489.1 7.0 copy-start.8
  496.1 8.3 %slice-start = ((s8[8388608]{0:T(1024)(128)(4,1)}), s8[4194304]{0:T(1024)(128)(4,1)S(1)}, s32[]{:S(2)}) async-start(s8[8388608]{0:T(1024)(128)(4,1)} %bitcast.154), calls=%async_computation.11 | async-start | bytes 8388608
  497.3 7.1 slice-start.1
  499.7 4.5 copy-start.4
  504.3 18.2 %collective-permute-start.4 = (bf16[4,4,64,2048]{3,2,0,1:T(8,128)(2,1)}, bf16[4,4,64,2048]{3,2,0,1:T(8,128)(2,1)}, u32[]{:S(2)}, u32[]{:S(2)}) collective-permute-start(bf16[4,4,64,2048]{3,2,0,1:T(8,128)(2,1)} %copy_bitcast_fusion), channel_id=1, source_target_pairs={{0,1},{1,0},{2,3},{3,2},{4,5},{5,4},{6,7},{7,6},{8,9},{9,8},{10,11... | collective-permute-start | bytes 12582920 | tf_op jit(solution)/shard_map/ppermute | solution.py:279
  522.4 9.0 %copy-start = (bf16[2048,256]{1,0:T(8,128)(2,1)S(1)}, bf16[2048,256]{1,0:T(8,128)(2,1)}, u32[]{:S(2)}) copy-start(bf16[2048,256]{1,0:T(8,128)(2,1)} %shard_map.234.d_ref) | copy-start | bytes 3145732
  528.0 53.1 %collective-permute-start.5 = (bf16[4,64,2048]{2,1,0:T(8,128)(2,1)}, bf16[4,64,2048]{2,1,0:T(8,128)(2,1)}, u32[]{:S(2)}, u32[]{:S(2)}) collective-permute-start(bf16[4,64,2048]{2,1,0:T(8,128)(2,1)} %get-tuple-element.82), channel_id=1, source_target_pairs={{0,6},{2,4},{4,2},{6,0},{1,7},{3,5},{5,3},{7,1},{8,14},{10,12},{12... | collective-permute-start | bytes 3145736 | tf_op jit(solution)/shard_map/ppermute | solution.py:293
  529.5 51.6 %collective-permute-start.6 = (bf16[4,64,2048]{2,1,0:T(8,128)(2,1)}, bf16[4,64,2048]{2,1,0:T(8,128)(2,1)}, u32[]{:S(2)}, u32[]{:S(2)}) collective-permute-start(bf16[4,64,2048]{2,1,0:T(8,128)(2,1)} %get-tuple-element.83), channel_id=1, source_target_pairs={{0,2},{2,0},{4,6},{6,4},{1,3},{3,1},{5,7},{7,5},{8,10},{10,8},{12,... | collective-permute-start | bytes 3145736 | tf_op jit(solution)/shard_map/ppermute | solution.py:293
  531.1 50.1 %collective-permute-start.7 = (bf16[4,64,2048]{2,1,0:T(8,128)(2,1)}, bf16[4,64,2048]{2,1,0:T(8,128)(2,1)}, u32[]{:S(2)}, u32[]{:S(2)}) collective-permute-start(bf16[4,64,2048]{2,1,0:T(8,128)(2,1)} %get-tuple-element.84), channel_id=1, source_target_pairs={{0,4},{2,6},{4,0},{6,2},{1,5},{3,7},{5,1},{7,3},{8,12},{10,14},{12... | collective-permute-start | bytes 3145736 | tf_op jit(solution)/shard_map/ppermute | solution.py:293
  581.1 6.8 copy-start.3
  585.8 101.0 %reduce-scatter.9.cloned.1.call-start = ((), (), s32[]{:S(2)}) async-start(), calls=%async_computation.6 | async-start | bytes 1966080 | tf_op jit(solution)/shard_map/reduce_scatter | solution.py:375
  605.4 41.6 %copy-start.10 = (bf16[256,2048]{1,0:T(8,128)(2,1)S(1)}, bf16[256,2048]{1,0:T(8,128)(2,1)}, u32[]{:S(2)}) copy-start(bf16[256,2048]{1,0:T(8,128)(2,1)} %x_ref.1) | copy-start | bytes 3145732
  649.1 26.2 %copy-start.7 = (f32[256,2048]{1,0:T(8,128)S(1)}, f32[256,2048]{1,0:T(8,128)}, u32[]{:S(2)}) copy-start(f32[256,2048]{1,0:T(8,128)} %copy-done.5) | copy-start | bytes 6291460
  (4 other events, 4.7 us)
Sparse Core Ops, SparseCore 0:
  25.8 63.7 all-gather.6
  91.8 148.2 all-gather.8
  241.7 78.9 all-gather.10
  335.4 74.5 reduce-scatter.4
  412.3 145.0 reduce-scatter.6
  585.9 26.3 reduce-scatter.10
  649.3 37.4 reduce-scatter.8

commit v5 on v4

--- a/solution.py
+++ b/solution.py
@@ -270,6 +270,10 @@
     )(p)
 
 
+def swap_chips(values, step):
+    return lax.ppermute(values, "chip", [(c, c ^ step) for c in range(4)])
+
+
 class Drift:
     def __init__(self, pairs, axis):
         self.axis = axis
@@ -290,7 +294,7 @@
     @staticmethod
     def send(parts):
         return tuple(
-            lax.ppermute(part, "chip", [(c, c ^ step) for c in range(4)])
+            swap_chips(part, step)
             for step, part in zip((3, 1, 2), (parts[2], parts[0], parts[1]))
         )
 
@@ -814,6 +818,234 @@
     )(d_gate, d_up, weights)
 
 
+def stage_step(stage):
+    return jnp.where(stage == 0, 3, jnp.where(stage == 3, 0, stage))
+
+
+class Square:
+    def __init__(self, acc, mine, away, twin, moved, corner, landed, tsend, trecv, msend, mrecv, csend, crecv):
+        self.acc, self.mine, self.away, self.twin = acc, mine, away, twin
+        self.moved, self.corner, self.landed = moved, corner, landed
+        self.tsend, self.trecv, self.msend, self.mrecv = tsend, trecv, msend, mrecv
+        self.csend, self.crecv = csend, crecv
+        self.chip, self.core = place()
+        self.rows = mine.shape[1]
+        self.half = self.rows // 2
+
+    def greet(self):
+        peers = [(flip(self.chip, s, 4), self.core) for s in (1, 2)]
+        greet(peers + [(self.chip, 1 - self.core)])
+
+    def twin_copy(self, stage):
+        return remote(
+            self.away.at[stage], self.twin.at[stage], self.tsend.at[stage], self.trecv.at[stage],
+            self.chip, 1 - self.core,
+        )
+
+    def offer(self, stage):
+        own, other = self.core * self.rows, (1 - self.core) * self.rows
+        self.mine[stage] = self.acc[pl.ds(pl.multiple_of(own, self.rows), self.rows)].astype(BF16)
+        self.away[stage] = self.acc[pl.ds(pl.multiple_of(other, self.rows), self.rows)].astype(BF16)
+        self.twin_copy(stage).start()
+
+    def at(self, h):
+        return pl.ds(h * self.half, self.half)
+
+    def both(self, stage, h):
+        return self.mine[stage, self.at(h)].astype(F32) + self.twin[stage, self.at(h)].astype(F32)
+
+    def corner_copy(self, h):
+        return remote(
+            self.moved.at[0, self.at(h)], self.corner.at[h], self.csend.at[h], self.crecv.at[h],
+            flip(self.chip, h + 1, 4), self.core,
+        )
+
+    def copy(self, stage, h):
+        return remote(
+            self.moved.at[stage, self.at(h)], self.landed.at[stage - 1, self.at(h)],
+            self.msend.at[stage - 1, h], self.mrecv.at[stage - 1, h],
+            flip(self.chip, stage, 4), self.core,
+        )
+
+    def corners(self):
+        self.twin_copy(0).wait_recv()
+        for h in range(2):
+            self.moved[0, self.at(h)] = self.both(0, h).astype(BF16)
+            self.corner_copy(h).start()
+
+    def plain(self, stage):
+        self.twin_copy(stage).wait_recv()
+        h = stage - 1
+        self.moved[stage, self.at(h)] = self.both(stage, h).astype(BF16)
+        self.copy(stage, h).start()
+
+    def joined(self, stage):
+        h = 2 - stage
+        self.corner_copy(h).wait_recv()
+        total = self.both(stage, h) + self.corner[h].astype(F32)
+        self.moved[stage, self.at(h)] = total.astype(BF16)
+        self.copy(stage, h).start()
+
+    def finish(self, o_ref):
+        self.twin_copy(3).wait_recv()
+        for h in range(2):
+            o_ref[self.at(h)] = self.both(3, h)
+        for stage, h in ((1, 0), (2, 1), (2, 0), (1, 1)):
+            self.copy(stage, h).wait_recv()
+            o_ref[self.at(h)] += self.landed[stage - 1, self.at(h)].astype(F32)
+        for stage in (1, 2):
+            for h in range(2):
+                self.copy(stage, h).wait_send()
+        for h in range(2):
+            self.corner_copy(h).wait_send()
+        for stage in range(4):
+            self.twin_copy(stage).wait_send()
+
+
+def square_kernel(compute, count, *refs):
+    operands, o_ref, scratch = refs[:count], refs[count], refs[count + 1 :]
+    run = Square(*scratch)
+    stage = pl.program_id(0)
+
+    @pl.when(stage == 0)
+    def _():
+        run.greet()
+
+    target = jnp.bitwise_xor(run.chip, stage_step(stage))
+    width = 2 * run.rows
+    run.acc[...] = compute(operands, pl.ds(pl.multiple_of(target * width, width), width))
+    run.offer(stage)
+
+    @pl.when(stage == 1)
+    def _():
+        run.corners()
+
+    @pl.when(stage == 2)
+    def _():
+        run.plain(1)
+
+    @pl.when(stage == 3)
+    def _():
+        run.plain(2)
+        run.joined(2)
+        run.joined(1)
+        run.finish(o_ref)
+
+
+def square_reduce(compute, operands, rows, call_id):
+    block = (rows, D)
+
+    def held(shape):
+        return pl.BlockSpec(shape, lambda s: (0,) * len(shape), pipeline_mode=pl.Buffered(1))
+
+    return pl.pallas_call(
+        functools.partial(square_kernel, compute, len(operands)),
+        out_shape=jax.ShapeDtypeStruct(block, F32),
+        grid=(4,),
+        in_specs=[held(x.shape) for x in operands],
+        out_specs=held(block),
+        scratch_shapes=[
+            pltpu.VMEM((2 * rows, D), F32),
+            pltpu.VMEM((4,) + block, BF16),
+            pltpu.VMEM((4,) + block, BF16),
+            pltpu.VMEM((4,) + block, BF16),
+            pltpu.VMEM((3,) + block, BF16),
+            pltpu.VMEM((2, rows // 2, D), BF16),
+            pltpu.VMEM((2,) + block, BF16),
+            pltpu.SemaphoreType.DMA((4,)),
+            pltpu.SemaphoreType.DMA((4,)),
+            pltpu.SemaphoreType.DMA((2, 2)),
+            pltpu.SemaphoreType.DMA((2, 2)),
+            pltpu.SemaphoreType.DMA((2,)),
+            pltpu.SemaphoreType.DMA((2,)),
+        ],
+        cost_estimate=BRIEF,
+        compiler_params=pltpu.CompilerParams(
+            collective_id=call_id, has_side_effects=True, vmem_limit_bytes=60 << 20
+        ),
+    )(*operands)
+
+
+def widen_back_rows(refs, rows):
+    dg_ref, du_ref, w_ref = refs
+    total = None
+    for i in range(w_ref.shape[0]):
+        part = dot_nt(dg_ref[i, rows], w_ref[i, 0]) + dot_nt(du_ref[i, rows], w_ref[i, 1])
+        total = part if total is None else total + part
+    return total
+
+
+def project_back_rows(refs, rows):
+    d_ref, w_ref = refs
+    return dot_nt(d_ref[rows], w_ref[...])
+
+
+def twin_kernel(h_ref, w_ref, o_ref, corner_ref, x_ref, y_ref, acc, mine, away, twin, tsend, trecv):
+    chip, core = place()
+    stage = pl.program_id(0)
+    rows = o_ref.shape[0]
+
+    def copy(s):
+        return remote(away.at[s], twin.at[s], tsend.at[s], trecv.at[s], chip, 1 - core)
+
+    def both(s):
+        copy(s).wait_recv()
+        return mine[s].astype(F32) + twin[s].astype(F32)
+
+    @pl.when(stage == 0)
+    def _():
+        greet([(chip, 1 - core)])
+
+    target = jnp.bitwise_xor(chip, stage_step(stage)) * 2 * rows
+    total = None
+    for i in range(w_ref.shape[0]):
+        part = matmul(h_ref[i, pl.ds(pl.multiple_of(target, 2 * rows), 2 * rows)], w_ref[i])
+        total = part if total is None else total + part
+    acc[...] = total
+    mine[stage] = acc[pl.ds(pl.multiple_of(core * rows, rows), rows)].astype(BF16)
+    away[stage] = acc[pl.ds(pl.multiple_of((1 - core) * rows, rows), rows)].astype(BF16)
+    copy(stage).start()
+
+    for s, part_ref in enumerate((corner_ref, x_ref, y_ref)):
+
+        @pl.when(stage == s + 1)
+        def _(s=s, part_ref=part_ref):
+            part_ref[...] = both(s).astype(BF16)
+
+    @pl.when(stage == 3)
+    def _():
+        o_ref[...] = both(3)
+        for s in range(4):
+            copy(s).wait_send()
+
+
+def mix_twin(hidden, weights, rows, call_id):
+    block = (rows, D)
+
+    def held(shape):
+        return pl.BlockSpec(shape, lambda s: (0,) * len(shape), pipeline_mode=pl.Buffered(1))
+
+    return pl.pallas_call(
+        twin_kernel,
+        out_shape=(jax.ShapeDtypeStruct(block, F32),) + (jax.ShapeDtypeStruct(block, BF16),) * 3,
+        grid=(4,),
+        in_specs=[held(hidden.shape), held(weights.shape)],
+        out_specs=(held(block),) * 4,
+        scratch_shapes=[
+            pltpu.VMEM((2 * rows, D), F32),
+            pltpu.VMEM((4,) + block, BF16),
+            pltpu.VMEM((4,) + block, BF16),
+            pltpu.VMEM((4,) + block, BF16),
+            pltpu.SemaphoreType.DMA((4,)),
+            pltpu.SemaphoreType.DMA((4,)),
+        ],
+        cost_estimate=BRIEF,
+        compiler_params=pltpu.CompilerParams(
+            collective_id=call_id, has_side_effects=True, vmem_limit_bytes=60 << 20
+        ),
+    )(hidden, weights)
+
+
 def norm_parts(values):
     factor = lax.rsqrt(jnp.mean(values * values, axis=-1, keepdims=True) + EPSILON)
     return factor
@@ -913,25 +1145,29 @@
     part_down = down_part(hidden_t, d_branch_mlp)
     part_down, hidden, silu = lax.optimization_barrier((part_down, hidden, silu))
     grad_down = scatter(part_down, "grp")
-    branch_mlp = mix(hidden, down_w)
-    drift_mlp = None
     if chips == 4:
-        drift_mlp = Drift(branch_mlp.reshape(4, 2, rows, D), 0)
-    branch_mlp, silu = lax.optimization_barrier((branch_mlp, silu))
+        branch_mlp, *others = mix_twin(hidden, down_w, rows, 11)
+        others, silu = lax.optimization_barrier((others, silu))
+        others = [swap_chips(part, step) for step, part in zip((3, 1, 2), others)]
+    else:
+        branch_mlp = mix(hidden, down_w)
     d_gate, d_up = narrow_back(silu, slope, d_branch_mlp, down_w)
+    part_wide = widen_part(normed_t, d_gate, d_up)
     if chips == 4:
-        sent_mlp, d_gate, d_up = lax.optimization_barrier((drift_mlp.parts(), d_gate, d_up))
-        sent_mlp = Drift.send(sent_mlp)
-    part_wide = widen_part(normed_t, d_gate, d_up)
-    part_wide, d_gate, d_up = lax.optimization_barrier((part_wide, d_gate, d_up))
+        part_wide, others, d_gate, d_up = lax.optimization_barrier(
+            (part_wide, others, d_gate, d_up)
+        )
+    else:
+        part_wide, d_gate, d_up = lax.optimization_barrier((part_wide, d_gate, d_up))
     grad_wide = scatter(part_wide, "grp")
-    d_normed_two = widen_back(d_gate, d_up, wide_w)
     if chips == 4:
-        sent_mlp, d_normed_two = lax.optimization_barrier((sent_mlp, d_normed_two))
-        branch_mlp = drift_mlp.finish(sent_mlp)
-    d_normed_two = plane_reduce(d_normed_two.reshape(devs, rows, D), chips, 5)
-    if chips != 4:
+        for part in others:
+            branch_mlp = branch_mlp + part.astype(F32)
+        d_normed_two = square_reduce(widen_back_rows, (d_gate, d_up, wide_w), rows, 10)
+    else:
         branch_mlp = plane_reduce(branch_mlp.reshape(devs, rows, D), chips, 5)
+        d_normed_two = widen_back(d_gate, d_up, wide_w)
+        d_normed_two = plane_reduce(d_normed_two.reshape(devs, rows, D), chips, 5)
     layer_out = residual + RESID_MULT * branch_mlp
 
     d_residual_norm, d_gain_two = norm_back(residual, factor_two, gain_two, d_normed_two)
@@ -951,7 +1187,7 @@
     d_attended, grad_down = lax.optimization_barrier((d_attended, grad_down))
     d_qkv = attend_back(qkv, d_attended, order, q_heads)
     if chips == 4:
-        sent_out, d_qkv = lax.optimization_barrier((sent_out, d_qkv))
+        sent_out, d_qkv, grad_wide = lax.optimization_barrier((sent_out, d_qkv, grad_wide))
         grad_out = drift_out.finish(sent_out).astype(BF16)
     else:
         grad_out = plane_reduce(
@@ -960,11 +1196,11 @@
     grad_out = scatter(grad_out, "grp").reshape(w_rows, D).astype(F32)
     sent = over_rows(normed_one, d_qkv).astype(BF16)
     sent, d_qkv = lax.optimization_barrier((sent, d_qkv))
-    sent, grad_wide = lax.optimization_barrier((sent, grad_wide))
     sent = scatter(sent, "grp")
 
     d_normed_one = over_cols(d_qkv, w_qkv).astype(BF16).reshape(devs, rows, D)
     d_normed_one = plane_reduce(d_normed_one, chips, 5)
+    d_normed_one, sent = lax.optimization_barrier((d_normed_one, sent))
     d_input_norm, d_gain_one = norm_back(layer_in, norm_parts(layer_in), gain_one, d_normed_one)
     tokens_grad = (d_residual + d_input_norm).astype(BF16)
 
@@ -989,20 +1225,21 @@
             jnp.sum(scaled_mlp * scaled_mlp),
         ]
     )
-    totals = jnp.stack([d_gain_one, d_gain_two, jnp.pad(squares, (0, D - 3))])
-    totals = total(jnp.pad(totals, ((0, 5), (0, 0))), grps, chips, 8)
-    rms_stats = jnp.sqrt(totals[2, :3] / (rows * grps * devs * D))
+    totals = jnp.concatenate([d_gain_one, d_gain_two, squares, jnp.zeros((1021,), F32)])
+    totals = total(totals.reshape(8, 5 * D // 16), grps, chips, 8).reshape(-1)
+    rms_stats = jnp.sqrt(totals[2 * D : 2 * D + 3] / (rows * grps * devs * D))
     gain_first = (lax.axis_index("grp") * devs + lax.axis_index(PLANE)) * w_rows
-    gain_grads = lax.dynamic_slice(totals, (0, gain_first), (2, w_rows))
+    gain_one_grad = lax.dynamic_slice(totals, (gain_first,), (w_rows,))
+    gain_two_grad = lax.dynamic_slice(totals, (gain_first + D,), (w_rows,))
     return (
         layer_out.astype(BF16),
         tokens_grad,
-        gain_grads[0],
+        gain_one_grad,
         grad_query,
         grad_key,
         grad_value,
         grad_out,
-        gain_grads[1],
+        gain_two_grad,
         grad_wide[0, 0].astype(F32),
         grad_wide[0, 1].astype(F32),
         grad_down[0].astype(F32),

time: 716 us -> 684 us (0.955)
  waiting for transfers between devices: 38.8 us -> 24.3 us
  Pallas kernels: 510 us -> 498 us
  other arithmetic: 68 us -> 56.6 us
    pallas_call x2 -> x1, Pallas kernels: 83.1 us -> 41.7 us  [plane_reduce(): pl.pallas_call(functools.partial(reduce_kernel, chips, inner), out_shape=...]
    pallas_call x2, Pallas kernels: 37.7 us -> 76 us  [the longest x1 54.9 us: square_reduce(): pl.pallas_call(functools.partial(square_kernel, compute, len(operands)),...]
    ppermute x6, waiting for transfers between devices: 21.5 us -> 6.76 us  [swap_chips(): return lax.ppermute(values, 'chip', [(c, c ^ step) for c in range(4)])]
    pallas_call x1, Pallas kernels: 20.2 us -> 12.1 us  [total(): pl.pallas_call(functools.partial(total_kernel, grps, chips), out_shape=ja...]
    reduce_sum x2 -> x1, other arithmetic: 9.11 us -> 1.82 us  [norm_back(): jnp.sum(grad * values * factor, axis=0)]
    reduce_sum x0 -> x1, other arithmetic: none -> 7.26 us  [on_device(): jnp.sum(scaled_mlp * scaled_mlp)]
  transfers between devices with their start and end apart: 15 -> 14, of which waited for: 4 -> 4; matrix products, arithmetic and copies ran while one was open for 17% -> 13% of each run, Pallas kernels for 69% -> 69%
where the time goes in v5:
time: 684 us; the launch traced here: 676 us
  Pallas kernels  498 us (73%)
  other arithmetic  56.6 us (8%)
  matrix products  41 us (6%)
  local copies, waits for them, and re-layouts  33.2 us (5%)
  waiting for transfers between devices  24.3 us (4%)
  between operations  14.9 us (2%)
  starting transfers between devices  7.36 us (1%)
    pallas_call x4, Pallas kernels, plane_gather(): pl.pallas_call(functools.partial(gather_kernel, chips, inner), out_shape=...  160 us
    pallas_call x1, Pallas kernels, square_reduce(): pl.pallas_call(functools.partial(square_kernel, compute, len(operands)),...  54.9 us
    pallas_call x4, Pallas kernels, plane_exchange(): pl.pallas_call(functools.partial(exchange_kernel, chips, cut, paste), out...  49.4 us
    pallas_call x1, Pallas kernels, attend_back(): pl.pallas_call(functools.partial(attend_back_kernel, heads), out_shape=ja...  48.4 us
    pallas_call x1, Pallas kernels, plane_reduce(): pl.pallas_call(functools.partial(reduce_kernel, chips, inner), out_shape=...  41.7 us
    pallas_call x1, Pallas kernels, widen(): pl.pallas_call(widen_kernel, out_shape=(tall, jax.ShapeDtypeStruct((shard...  30.7 us
    pallas_call x1, Pallas kernels, attend(): pl.pallas_call(functools.partial(attend_kernel, heads), out_shape=jax.Sha...  25.4 us
    pallas_call x1, Pallas kernels, widen_part(): pl.pallas_call(widen_part_kernel, out_shape=jax.ShapeDtypeStruct((shards,...  23.5 us
  transfers between devices with their start and end apart: 14, of which 4 were waited for; matrix products, arithmetic and copies ran while one was open for 13% of the time, Pallas kernels for 69%

profile of v5, /device:TPU:0, one launch (start us, length us, event | category | flops | bytes accessed | tf_op | source)
XLA Modules:
  0.0 675.5 jit_solution(13338806778375730569)
XLA Ops:
  12.1 11.5 %shard_map.221 = bf16[8,64,512]{2,1,0:T(8,128)(2,1)} custom-call(bf16[8,64,512]{2,1,0:T(8,128)(2,1)} %maximum_bitcast_fusion.x_ref), custom_call_target="tpu_custom_call" | custom-call | flops 1000 | bytes 1000 | tf_op jit(solution)/shard_map/pallas_call | solution.py:335
  28.1 39.9 %shard_map.220 = bf16[8,256,2048]{2,1,0:T(8,128)(2,1)} custom-call(bf16[256,2048]{1,0:T(8,128)(2,1)} %x_ref.1), custom_call_target="tpu_custom_call" | custom-call | flops 1000 | bytes 1000 | tf_op jit(solution)/shard_map/pallas_call | solution.py:160
  68.0 5.1 multiply_reduce_fusion
  73.6 16.1 %all-gather.7.cloned.1.call-done = bf16[3072,512]{1,0:T(8,128)(2,1)} async-done(((bf16[768,512]{1,0:T(8,128)(2,1)}), bf16[3072,512]{1,0:T(8,128)(2,1)}) %all-gather.7.cloned.1.call-update) | async-done | bytes 3145744 | tf_op jit(solution)/shard_map/all_gather | solution.py:375
  95.6 9.6 %fusion.1 = bf16[2048,2048]{1,0:T(8,128)(2,1)} fusion(f32[2048]{0:T(1024)S(1)} %bitcast.128, f32[2048]{0:T(1024)S(1)} %bitcast.131, bf16[8,256,2048]{2,1,0:T(8,128)(2,1)} %shard_map.220), kind=kLoop, calls=%fused_computation.2 | loop fusion | flops 16777216 | bytes 16793600 | tf_op jit(solution)/shard_map/convert_element_type | solution.py:1121
  105.1 8.3 %convolution_convert_fusion.3.qkv_ref = bf16[2048,384]{1,0:T(8,128)(2,1)S(1)} fusion(bf16[2048,2048]{1,0:T(8,128)(2,1)} %fusion.1, bf16[2048,512]{1,0:T(8,128)(2,1)} %bitcast.113), kind=kOutput, calls=%fused_computation.13 | convolution fusion | flops 3222011904 | bytes 11534336 | tf_op jit(solution)/shard_map/dot_general | solution.py:363
  115.1 25.4 %shard_map.222.x_ref = bf16[2048,256]{1,0:T(8,128)(2,1)S(1)} custom-call(s32[16]{0:T(128)S(1)} %select_reduce_fusion.order_ref, bf16[2048,384]{1,0:T(8,128)(2,1)S(1)} %convolution_convert_fusion.3.qkv_ref), custom_call_target="tpu_custom_call" | custom-call | flops 1000 | bytes 1000 | tf_op jit(solution)/shard_map/pallas_call | solution.py:521
  141.4 40.3 %shard_map.224 = bf16[4,8,64,2048]{3,2,1,0:T(8,128)(2,1)} custom-call(bf16[4,64,2048]{2,1,0:T(8,128)(2,1)} %reshape.195.x_ref), custom_call_target="tpu_custom_call" | custom-call | flops 1000 | bytes 1000 | tf_op jit(solution)/shard_map/pallas_call | solution.py:160
  181.8 14.9 %shard_map.223 = bf16[256,2048]{1,0:T(8,128)(2,1)} custom-call(bf16[2048,256]{1,0:T(8,128)(2,1)} %copy-done.1), custom_call_target="tpu_custom_call" | custom-call | flops 1000 | bytes 1000 | tf_op jit(solution)/shard_map/pallas_call | solution.py:335
  198.3 7.0 %multiply_reduce_fusion.6 = (f32[256]{0:T(256)S(1)}, f32[256,2048]{1,0:T(8,128)S(1)}, f32[]{:T(128)}, f32[256]{0:T(256)S(1)}) fusion(bf16[256,2048]{1,0:T(8,128)(2,1)S(1)} %copy-done.10, bf16[256,2048]{1,0:T(8,128)(2,1)} %shard_map.223, bf16[2048,2048]{1,0:T(8,128)(2,1)} %bitcast.110), kind=kOutput, calls=%fused_computation.46 | convolution fusion | flops 2152201728 | bytes 12584964 | tf_op jit(solution)/shard_map/dot_general | solution.py:363
  209.1 40.1 %shard_map.225 = bf16[8,256,2048]{2,1,0:T(8,128)(2,1)} custom-call(bf16[256,2048]{1,0:T(8,128)(2,1)} %multiply_convert_fusion.1.x_ref), custom_call_target="tpu_custom_call" | custom-call | flops 1000 | bytes 1000 | tf_op jit(solution)/shard_map/pallas_call | solution.py:160
  249.2 40.0 %shard_map.226 = bf16[8,256,2048]{2,1,0:T(8,128)(2,1)} custom-call(bf16[256,2048]{1,0:T(8,128)(2,1)} %fusion.2.x_ref), custom_call_target="tpu_custom_call" | custom-call | flops 1000 | bytes 1000 | tf_op jit(solution)/shard_map/pallas_call | solution.py:160
  289.2 30.7 %shard_map.227 = (bf16[4,2048,256]{2,1,0:T(8,128)(2,1)}, bf16[4,256,2048]{2,1,0:T(8,128)(2,1)}, bf16[4,2048,256]{2,1,0:T(8,128)(2,1)}, bf16[4,2048,256]{2,1,0:T(8,128)(2,1)}, bf16[2048,2048]{1,0:T(8,128)(2,1)}) custom-call(bf16[2048,2048]{1,0:T(8,128)(2,1)} %bitcast.106, bf16[4,2,2048,256]{3,2,1,0:T(8,128)(2,1)} %bitcast.104), custom_call_target="tpu_custom_call" | custom-call | flops 1000 | bytes 1000 | tf_op jit(solution)/shard_map/pallas_call | solution.py:668
  319.9 15.4 %shard_map.228 = bf16[4,256,2048]{2,1,0:T(8,128)(2,1)} custom-call(bf16[4,256,2048]{2,1,0:T(8,128)(2,1)} %get-tuple-element.60.ht_ref, bf16[2048,2048]{1,0:T(8,128)(2,1)} %bitcast.99), custom_call_target="tpu_custom_call" | custom-call | flops 1000 | bytes 1000 | tf_op jit(solution)/shard_map/pallas_call | solution.py:702
  335.5 21.1 %shard_map.229 = (f32[256,2048]{1,0:T(8,128)}, bf16[256,2048]{1,0:T(8,128)(2,1)}, bf16[256,2048]{1,0:T(8,128)(2,1)}, bf16[256,2048]{1,0:T(8,128)(2,1)}) custom-call(bf16[4,2048,256]{2,1,0:T(8,128)(2,1)} %get-tuple-element.64.h_ref, bf16[4,256,2048]{2,1,0:T(8,128)(2,1)} %bitcast.107), custom_call_target="tpu_custom_call" | custom-call | flops 1000 | bytes 1000 | tf_op jit(solution)/shard_map/pallas_call | solution.py:1028
  360.2 15.4 %shard_map.230 = (bf16[4,2048,256]{2,1,0:T(8,128)(2,1)}, bf16[4,2048,256]{2,1,0:T(8,128)(2,1)}) custom-call(bf16[4,2048,256]{2,1,0:T(8,128)(2,1)} %get-tuple-element.71.s_ref, bf16[4,2048,256]{2,1,0:T(8,128)(2,1)} %get-tuple-element.72.t_ref, bf16[2048,2048]{1,0:T(8,128)(2,1)} %bitcast.100, bf16[4,256,2048]{2,1,0:T(8,128)(2,1)} %bitcast.108), custom_call_target="tpu_custom_call" | custom-call | flops 1000 | bytes 1000 | tf_op jit(solution)/shard_map/pallas_call | solution.py:760
  375.6 23.5 %shard_map.231 = bf16[4,2,2048,256]{3,2,1,0:T(8,128)(2,1)} custom-call(bf16[2048,2048]{1,0:T(8,128)(2,1)} %get-tuple-element.66.nt_ref, bf16[4,2048,256]{2,1,0:T(8,128)(2,1)} %get-tuple-element.81.dg_ref.refs_0_, bf16[4,2048,256]{2,1,0:T(8,128)(2,1)} %get-tuple-element.82.du_ref.refs_1_), custom_call_target="tpu_custom_call" | custom-call | flops 1000 | bytes 1000 | tf_op jit(solution)/shard_map/pallas_call | solution.py:782
  399.0 6.2 collective-permute-done.1
  405.9 54.9 %shard_map.232 = f32[256,2048]{1,0:T(8,128)} custom-call(bf16[4,2048,256]{2,1,0:T(8,128)(2,1)} %get-tuple-element.81.dg_ref.refs_0_, bf16[4,2048,256]{2,1,0:T(8,128)(2,1)} %get-tuple-element.82.du_ref.refs_1_, bf16[4,2,2048,256]{3,2,1,0:T(8,128)(2,1)} %bitcast.105), custom_call_target="tpu_custom_call" | custom-call | flops 1000 | bytes 1000 | tf_op jit(solution)/shard_map/pallas_call | solution.py:941
  460.8 7.3 %multiply_reduce_fusion.1 = (f32[]{:T(128)}, f32[]{:T(128)}, f32[256]{0:T(256)S(1)}, f32[2048]{0:T(1024)}, f32[256,2048]{1,0:T(8,128)}) fusion(f32[256,2048]{1,0:T(8,128)} %copy-done.7, f32[256,2048]{1,0:T(8,128)} %shard_map.232, f32[2048]{0:T(1024)S(1)} %bitcast.125, f32[256]{0:T(256)S(1)} %get-tuple-element.129, ...), kind=kLoop, calls=%fused_computation.38 | loop fusion | flops 9434878 | bytes 11552776 | tf_op jit(solution)/shard_map/reduce_sum | solution.py:1225
  476.3 7.1 %convolution_convert_fusion.4.x_ref = bf16[256,2048]{1,0:T(8,128)(2,1)} fusion(bf16[256,2048]{1,0:T(8,128)(2,1)S(1)} %copy-done.17, bf16[2048,2048]{1,0:T(8,128)(2,1)} %bitcast.111), kind=kOutput, calls=%fused_computation.17 | convolution fusion | flops 2148007936 | bytes 10485760 | tf_op jit(solution)/shard_map/dot_general | solution.py:371
  483.4 14.8 %shard_map.233.d_ref = bf16[2048,256]{1,0:T(8,128)(2,1)} custom-call(bf16[256,2048]{1,0:T(8,128)(2,1)} %convolution_convert_fusion.4.x_ref), custom_call_target="tpu_custom_call" | custom-call | flops 1000 | bytes 1000 | tf_op jit(solution)/shard_map/pallas_call | solution.py:335
  498.2 5.5 fusion.14
  507.2 48.4 %shard_map.234 = bf16[2048,384]{1,0:T(8,128)(2,1)S(1)} custom-call(s32[16]{0:T(128)S(1)} %select_reduce_fusion.order_ref, bf16[2048,384]{1,0:T(8,128)(2,1)S(1)} %convolution_convert_fusion.3.qkv_ref, bf16[2048,256]{1,0:T(8,128)(2,1)S(1)} %copy-done), custom_call_target="tpu_custom_call" | custom-call | flops 1000 | bytes 1000 | tf_op jit(solution)/shard_map/pallas_call | solution.py:543
  557.3 4.4 fusion.13
  561.9 9.1 %convolution_convert_fusion.2 = bf16[2048,384]{1,0:T(8,128)(2,1)} fusion(bf16[2048,2048]{1,0:T(8,128)(2,1)} %fusion.1, bf16[2048,384]{1,0:T(8,128)(2,1)S(1)} %copy-done.3), kind=kOutput, calls=%fused_computation.12 | convolution fusion | flops 3222011904 | bytes 11534336 | tf_op jit(solution)/shard_map/dot_general | solution.py:367
  574.5 7.1 %convolution_convert_fusion = bf16[2048,2048]{1,0:T(8,128)(2,1)} fusion(bf16[2048,384]{1,0:T(8,128)(2,1)S(1)} %copy-done.3, bf16[2048,512]{1,0:T(8,128)(2,1)S(1)} %bitcast.114), kind=kOutput, calls=%fused_computation.4 | convolution fusion | flops 3225419776 | bytes 11534336 | tf_op jit(solution)/shard_map/dot_general | solution.py:371
  581.6 41.7 %shard_map.235 = f32[256,2048]{1,0:T(8,128)} custom-call(bf16[8,256,2048]{2,1,0:T(8,128)(2,1)} %bitcast.109), custom_call_target="tpu_custom_call" | custom-call | flops 1000 | bytes 1000 | tf_op jit(solution)/shard_map/pallas_call | solution.py:246
  627.5 8.2 %shard_map.237 = bf16[8,64,384]{2,1,0:T(8,128)(2,1)} custom-call(bf16[8,64,384]{2,1,0:T(8,128)(2,1)} %bitcast.122), custom_call_target="tpu_custom_call" | custom-call | flops 1000 | bytes 1000 | tf_op jit(solution)/shard_map/pallas_call | solution.py:335
  637.6 2.7 concatenate.11
  642.7 12.1 %shard_map.236 = f32[8,640]{1,0:T(8,128)} custom-call(f32[8,640]{1,0:T(8,128)} %reshape.201.x_ref), custom_call_target="tpu_custom_call" | custom-call | flops 1000 | bytes 1000 | tf_op jit(solution)/shard_map/pallas_call | solution.py:616
  662.4 5.5 fusion.7
  (148 shorter events, 61.3 us)
Async XLA Ops:
  7.2 16.4 %copy-start.23 = (bf16[64,2048]{1,0:T(8,128)(2,1)S(1)}, bf16[64,2048]{1,0:T(8,128)(2,1)}, u32[]{:S(2)}) copy-start(bf16[64,2048]{1,0:T(8,128)(2,1)} %param.20) | copy-start | bytes 786436
  7.2 82.5 %all-gather.7.cloned.1.call-start = ((), (), s32[]{:S(2)}) async-start(), calls=%async_computation.8 | async-start | bytes 3932160 | tf_op jit(solution)/shard_map/all_gather | solution.py:375
  12.1 13.7 %copy-start.21 = (bf16[2048,256]{1,0:T(8,128)(2,1)S(1)}, bf16[2048,256]{1,0:T(8,128)(2,1)}, u32[]{:S(2)}) copy-start(bf16[2048,256]{1,0:T(8,128)(2,1)} %param.23) | copy-start | bytes 3145732
  12.1 13.7 %copy-start.22 = (bf16[2048,256]{1,0:T(8,128)(2,1)S(1)}, bf16[2048,256]{1,0:T(8,128)(2,1)}, u32[]{:S(2)}) copy-start(bf16[2048,256]{1,0:T(8,128)(2,1)} %param.22) | copy-start | bytes 3145732
  25.7 263.5 %all-gather.9.cloned.1.call-start = ((), (), s32[]{:S(2)}) async-start(), calls=%async_computation.9 | async-start | bytes 10485760 | tf_op jit(solution)/shard_map/all_gather | solution.py:375
  27.3 308.1 %all-gather.11.cloned.1.call-start = ((), (), s32[]{:S(2)}) async-start(), calls=%async_computation.10 | async-start | bytes 5242880 | tf_op jit(solution)/shard_map/all_gather | solution.py:375
  28.1 479.1 %reduce-scatter.5.cloned.1.call-start = ((), (), s32[]{:S(2)}) async-start(), calls=%async_computation.4 | async-start | bytes 5242880 | tf_op jit(solution)/shard_map/reduce_scatter | solution.py:379
  68.0 5.2 copy-start.31
  181.8 16.5 %copy-start.10 = (bf16[256,2048]{1,0:T(8,128)(2,1)S(1)}, bf16[256,2048]{1,0:T(8,128)(2,1)}, u32[]{:S(2)}) copy-start(bf16[256,2048]{1,0:T(8,128)(2,1)} %x_ref.1) | copy-start | bytes 3145732
  205.9 262.2 %copy-start.24 = (f32[256]{0:T(256)}, f32[256]{0:T(256)S(1)}, u32[]{:S(2)}) copy-start(f32[256]{0:T(256)S(1)} %get-tuple-element.129) | copy-start | bytes 3076
  335.4 221.9 %reduce-scatter.7.cloned.1.call-start = ((), (), s32[]{:S(2)}) async-start(), calls=%async_computation.5 | async-start | bytes 10485760 | tf_op jit(solution)/shard_map/reduce_scatter | solution.py:379
  356.6 42.5 %collective-permute-start = (bf16[256,2048]{1,0:T(8,128)(2,1)}, bf16[256,2048]{1,0:T(8,128)(2,1)}, u32[]{:S(2)}, u32[]{:S(2)}) collective-permute-start(bf16[256,2048]{1,0:T(8,128)(2,1)} %get-tuple-element.75), channel_id=1, source_target_pairs={{0,6},{2,4},{4,2},{6,0},{1,7},{3,5},{5,3},{7,1},{8,14},{10,12},{12... | collective-permute-start | bytes 3145736 | tf_op jit(solution)/shard_map/ppermute | solution.py:274
  358.1 47.1 %collective-permute-start.1 = (bf16[256,2048]{1,0:T(8,128)(2,1)}, bf16[256,2048]{1,0:T(8,128)(2,1)}, u32[]{:S(2)}, u32[]{:S(2)}) collective-permute-start(bf16[256,2048]{1,0:T(8,128)(2,1)} %get-tuple-element.76), channel_id=1, source_target_pairs={{0,2},{2,0},{4,6},{6,4},{1,3},{3,1},{5,7},{7,5},{8,10},{10,8},{12,... | collective-permute-start | bytes 3145736 | tf_op jit(solution)/shard_map/ppermute | solution.py:274
  359.0 46.7 %collective-permute-start.2 = (bf16[256,2048]{1,0:T(8,128)(2,1)}, bf16[256,2048]{1,0:T(8,128)(2,1)}, u32[]{:S(2)}, u32[]{:S(2)}) collective-permute-start(bf16[256,2048]{1,0:T(8,128)(2,1)} %get-tuple-element.77), channel_id=1, source_target_pairs={{0,4},{2,6},{4,0},{6,2},{1,5},{3,7},{5,1},{7,3},{8,12},{10,14},{12... | collective-permute-start | bytes 3145736 | tf_op jit(solution)/shard_map/ppermute | solution.py:274
  405.8 219.8 %reduce-scatter.11.cloned.1.call-start = ((), (), s32[]{:S(2)}) async-start(), calls=%async_computation.7 | async-start | bytes 1310720 | tf_op jit(solution)/shard_map/reduce_scatter | solution.py:379
  460.8 7.3 %copy-start.5 = (f32[256,2048]{1,0:T(8,128)S(1)}, f32[256,2048]{1,0:T(8,128)}, u32[]{:S(2)}) copy-start(f32[256,2048]{1,0:T(8,128)} %shard_map.232) | copy-start | bytes 6291460
  460.8 7.3 %copy-start.8 = (f32[256,2048]{1,0:T(8,128)S(1)}, f32[256,2048]{1,0:T(8,128)}, u32[]{:S(2)}) copy-start(f32[256,2048]{1,0:T(8,128)} %copy-done.7) | copy-start | bytes 6291460
  476.3 21.9 %collective-permute-start.3 = (bf16[4,4,64,2048]{3,2,0,1:T(8,128)(2,1)}, bf16[4,4,64,2048]{3,2,0,1:T(8,128)(2,1)}, u32[]{:S(2)}, u32[]{:S(2)}) collective-permute-start(bf16[4,4,64,2048]{3,2,0,1:T(8,128)(2,1)} %copy_bitcast_fusion), channel_id=1, source_target_pairs={{0,1},{1,0},{2,3},{3,2},{4,5},{5,4},{6,7},{7,6},{8,9},{9,8},{10,11... | collective-permute-start | bytes 12582920 | tf_op jit(solution)/shard_map/ppermute | solution.py:283
  498.2 9.0 %copy-start = (bf16[2048,256]{1,0:T(8,128)(2,1)S(1)}, bf16[2048,256]{1,0:T(8,128)(2,1)}, u32[]{:S(2)}) copy-start(bf16[2048,256]{1,0:T(8,128)(2,1)} %shard_map.233.d_ref) | copy-start | bytes 3145732
  503.7 53.0 %collective-permute-start.4 = (bf16[4,64,2048]{2,1,0:T(8,128)(2,1)}, bf16[4,64,2048]{2,1,0:T(8,128)(2,1)}, u32[]{:S(2)}, u32[]{:S(2)}) collective-permute-start(bf16[4,64,2048]{2,1,0:T(8,128)(2,1)} %get-tuple-element.85), channel_id=1, source_target_pairs={{0,6},{2,4},{4,2},{6,0},{1,7},{3,5},{5,3},{7,1},{8,14},{10,12},{12... | collective-permute-start | bytes 3145736 | tf_op jit(solution)/shard_map/ppermute | solution.py:274
  505.2 51.6 %collective-permute-start.5 = (bf16[4,64,2048]{2,1,0:T(8,128)(2,1)}, bf16[4,64,2048]{2,1,0:T(8,128)(2,1)}, u32[]{:S(2)}, u32[]{:S(2)}) collective-permute-start(bf16[4,64,2048]{2,1,0:T(8,128)(2,1)} %get-tuple-element.86), channel_id=1, source_target_pairs={{0,2},{2,0},{4,6},{6,4},{1,3},{3,1},{5,7},{7,5},{8,10},{10,8},{12,... | collective-permute-start | bytes 3145736 | tf_op jit(solution)/shard_map/ppermute | solution.py:274
  506.4 50.4 %collective-permute-start.6 = (bf16[4,64,2048]{2,1,0:T(8,128)(2,1)}, bf16[4,64,2048]{2,1,0:T(8,128)(2,1)}, u32[]{:S(2)}, u32[]{:S(2)}) collective-permute-start(bf16[4,64,2048]{2,1,0:T(8,128)(2,1)} %get-tuple-element.87), channel_id=1, source_target_pairs={{0,4},{2,6},{4,0},{6,2},{1,5},{3,7},{5,1},{7,3},{8,12},{10,14},{12... | collective-permute-start | bytes 3145736 | tf_op jit(solution)/shard_map/ppermute | solution.py:274
  561.8 65.7 %reduce-scatter.9.cloned.1.call-start = ((), (), s32[]{:S(2)}) async-start(), calls=%async_computation.6 | async-start | bytes 1966080 | tf_op jit(solution)/shard_map/reduce_scatter | solution.py:379
  581.6 41.7 %copy-start.18 = (bf16[1,2,2048,256]{3,2,1,0:T(8,128)(2,1)S(1)}, bf16[1,2,2048,256]{3,2,1,0:T(8,128)(2,1)}, u32[]{:S(2)}) copy-start(bf16[1,2,2048,256]{3,2,1,0:T(8,128)(2,1)} %reduce-scatter.7.cloned.1.call-done) | copy-start | bytes 6291460
  623.3 12.4 %copy-start.9 = (f32[256,2048]{1,0:T(8,128)S(1)}, f32[256,2048]{1,0:T(8,128)}, u32[]{:S(2)}) copy-start(f32[256,2048]{1,0:T(8,128)} %shard_map.235) | copy-start | bytes 6291460
  625.6 10.1 %copy-start.11 = (bf16[256,2048]{1,0:T(8,128)(2,1)S(1)}, bf16[256,2048]{1,0:T(8,128)(2,1)}, u32[]{:S(2)}) copy-start(bf16[256,2048]{1,0:T(8,128)(2,1)} %x_ref.1) | copy-start | bytes 3145732
  635.7 5.2 copy-start.19
  641.0 14.6 %copy-start.29 = (f32[256]{0:T(256)S(1)}, f32[256]{0:T(256)}, u32[]{:S(2)}) copy-start(f32[256]{0:T(256)} %get-tuple-element.105) | copy-start | bytes 3076
  641.8 20.6 %copy-start.6 = (f32[256,2048]{1,0:T(8,128)S(1)}, f32[256,2048]{1,0:T(8,128)}, u32[]{:S(2)}) copy-start(f32[256,2048]{1,0:T(8,128)} %shard_map.232) | copy-start | bytes 6291460
  641.8 20.6 %copy-start.25 = (f32[256]{0:T(256)S(1)}, f32[256]{0:T(256)}, u32[]{:S(2)}) copy-start(f32[256]{0:T(256)} %copy-done.24) | copy-start | bytes 3076
  641.8 20.6 %copy-start.27 = (f32[256]{0:T(256)S(1)}, f32[256]{0:T(256)}, u32[]{:S(2)}) copy-start(f32[256]{0:T(256)} %copy-done.26) | copy-start | bytes 3076
  641.8 20.6 %copy-start.28 = (f32[256]{0:T(256)S(1)}, f32[256]{0:T(256)}, u32[]{:S(2)}) copy-start(f32[256]{0:T(256)} %get-tuple-element.128) | copy-start | bytes 3076
  (15 other events, 38.4 us)
Sparse Core Ops, SparseCore 0:
  25.8 63.7 all-gather.6
  91.8 148.2 all-gather.8
  241.7 78.9 all-gather.10
  335.5 74.4 reduce-scatter.4
  412.3 144.9 reduce-scatter.6
  561.9 27.8 reduce-scatter.10
  592.1 33.9 reduce-scatter.8

commit v6 on v5

--- a/solution.py
+++ b/solution.py
@@ -116,12 +116,12 @@
         self.mine = pltpu.make_async_copy(self.x, whole, self.local)
         self.mine.start()
 
-    def relay(self):
+    def relay(self, first=0, last=None):
         if self.chips == 4:
             plan = ((1, 0, 2), (2, 1, 1), (1, 1, 0), (2, 0, 0), (3, 0, 0), (3, 1, 0))
         else:
             plan = tuple((s, h, 0) for s in range(1, self.chips) for h in range(2))
-        for s, h, onward in plan:
+        for s, h, onward in plan[first:last]:
             slot = self.slot(unflip(self.chip, s, self.chips), self.core)
             self.wait_for(slot, h)
             if onward:
@@ -1046,6 +1046,164 @@
     )(hidden, weights)
 
 
+def entry_kernel(
+    grps, chips, tok_ref, cot_ref, pack_ref, all_tok, all_cot, all_pack,
+    tsend, trecv, tlocal, csend, crecv, clocal, psend, precv, plocal, zsend, zrecv, usend, dsend,
+):
+    grp = lax.axis_index("grp")
+    chip, core = place()
+    me = chip * 2 + core
+    above, below = lax.rem(grp + 1, grps), lax.rem(grp + grps - 1, grps)
+    near = [(flip(chip, s, chips), c) for s in range(1, chips) for c in (core, 1 - core)]
+    near = near + [(chip, 1 - core)]
+    barrier = pltpu.get_barrier_semaphore()
+    for g in (above, below):
+        pl.semaphore_signal(barrier, inc=1, device_id={"grp": g}, device_id_type=MESH)
+    for to, c in near:
+        pl.semaphore_signal(
+            barrier, inc=1, device_id={"chip": to, "core": c}, device_id_type=MESH
+        )
+    pl.semaphore_wait(barrier, len(near) + 2)
+
+    tok = Gather(chips, False, tok_ref, all_tok, tsend, trecv, tlocal)
+    cot = Gather(chips, False, cot_ref, all_cot, csend, crecv, clocal)
+    packs = []
+    for i, (to, c) in enumerate(near):
+        copy = remote(
+            pack_ref.at[to * 2 + c], all_pack.at[grp, me], psend.at[i], precv.at[me], to, c
+        )
+        copy.start()
+        packs.append(copy)
+    mine = pltpu.make_async_copy(pack_ref.at[me], all_pack.at[grp, me], plocal)
+    mine.start()
+    tok.start()
+    for to, c in near:
+        slot = to * 2 + c
+        remote(
+            pack_ref.at[me], all_pack.at[grp, slot], psend.at[0], precv.at[slot], to, c
+        ).wait_recv()
+    mine.wait()
+
+    def z_copy(block, sem, to):
+        return pltpu.make_async_remote_copy(
+            src_ref=all_pack.at[block],
+            dst_ref=all_pack.at[block],
+            send_sem=sem,
+            recv_sem=zrecv.at[block],
+            device_id={"grp": to},
+            device_id_type=MESH,
+        )
+
+    has_above, has_below = grp + 1 < grps, grp > 0
+
+    def send(step, block, up):
+        @pl.when(has_above if up else has_below)
+        def _():
+            z_copy(block, (usend if up else dsend).at[step], above if up else below).start()
+
+    def relay(step):
+        low, high = grp - step, grp + step
+
+        @pl.when(low >= 0)
+        def _():
+            z_copy(low, zsend, below).wait_recv()
+            send(step, low, True)
+
+        @pl.when(high < grps)
+        def _():
+            z_copy(high, zsend, above).wait_recv()
+            send(step, high, False)
+
+    send(0, grp, True)
+    send(0, grp, False)
+    tok.relay(0, 4)
+    relay(1)
+    cot.start()
+    tok.relay(4, None)
+    for step in range(2, grps - 1):
+        relay(step)
+    cot.relay(0, 4)
+    if grps > 2:
+        relay(grps - 1)
+    cot.relay(4, None)
+    tok.finish()
+    cot.finish()
+    for copy in packs:
+        copy.wait_send()
+    for step in range(grps):
+        for up in (True, False):
+            held = grp - step >= 0 if up else grp + step < grps
+
+            @pl.when(held & (has_above if up else has_below))
+            def _(step=step, up=up):
+                block = grp - step if up else grp + step
+                z_copy(block, (usend if up else dsend).at[step], above if up else below).wait_send()
+
+
+def entry(tokens, cotangent, packed, grps, chips, call_id):
+    devs = 2 * chips
+    return pl.pallas_call(
+        functools.partial(entry_kernel, grps, chips),
+        out_shape=(
+            jax.ShapeDtypeStruct((devs,) + tokens.shape, BF16),
+            jax.ShapeDtypeStruct((devs,) + cotangent.shape, BF16),
+            jax.ShapeDtypeStruct((grps,) + packed.shape, BF16),
+        ),
+        in_specs=[ANY] * 3,
+        out_specs=(ANY,) * 3,
+        scratch_shapes=gather_sems(chips)
+        + gather_sems(chips)
+        + [
+            pltpu.SemaphoreType.DMA((devs,)),
+            pltpu.SemaphoreType.DMA((devs,)),
+            pltpu.SemaphoreType.DMA,
+            pltpu.SemaphoreType.DMA,
+            pltpu.SemaphoreType.DMA((grps,)),
+            pltpu.SemaphoreType.DMA((grps,)),
+            pltpu.SemaphoreType.DMA((grps,)),
+        ],
+        cost_estimate=BRIEF,
+        compiler_params=pltpu.CompilerParams(collective_id=call_id, has_side_effects=True),
+    )(tokens, cotangent, packed)
+
+
+def project_kernel(used, x_ref, w_ref, n_ref, qkv_ref, gain_ref):
+    @pl.when(pl.program_id(0) == 0)
+    def _():
+        gain_ref[...] = w_ref[:, used:].astype(F32).T[:8]
+
+    values = x_ref[...].astype(F32)
+    factor = lax.rsqrt(jnp.mean(values * values, axis=-1, keepdims=True) + EPSILON)
+    normed = (values * factor * gain_ref[0:1]).astype(BF16)
+    n_ref[...] = normed
+    qkv_ref[...] = matmul(normed, w_ref[:, :used]).astype(BF16)
+
+
+def project(tokens, packed, used):
+    count, depth = tokens.shape
+    rows = tile_rows(count, 256)
+    return pl.pallas_call(
+        functools.partial(project_kernel, used),
+        out_shape=(
+            jax.ShapeDtypeStruct((count, depth), BF16),
+            jax.ShapeDtypeStruct((count, used), BF16),
+            jax.ShapeDtypeStruct((8, depth), F32),
+        ),
+        grid=(count // rows,),
+        in_specs=[
+            pl.BlockSpec((rows, depth), lambda r: (r, 0)),
+            pl.BlockSpec(packed.shape, lambda r: (0, 0)),
+        ],
+        out_specs=(
+            pl.BlockSpec((rows, depth), lambda r: (r, 0)),
+            pl.BlockSpec((rows, used), lambda r: (r, 0)),
+            pl.BlockSpec((8, depth), lambda r: (0, 0)),
+        ),
+        cost_estimate=BRIEF,
+        compiler_params=params(1),
+    )(tokens, packed)
+
+
 def norm_parts(values):
     factor = lax.rsqrt(jnp.mean(values * values, axis=-1, keepdims=True) + EPSILON)
     return factor
@@ -1107,19 +1265,15 @@
         [w_query.reshape(w_rows, devs, q_cols), kv_split(w_key), kv_split(w_value), gains], axis=2
     )
     packed = jnp.swapaxes(packed, 0, 1)
-    packed = plane_exchange(packed, packed.shape, by_slot, by_slot, chips, 1)
-    packed = jnp.concatenate([packed.reshape(devs * w_rows, cols), w_out.reshape(-1, cols)])
-    packed = gather(packed[None], "grp")
-    out_full = packed[:, devs * w_rows :].reshape(grps, w_rows, D)
-    packed = packed[:, : devs * w_rows].reshape(D, cols)
-    w_qkv = packed[:, : q_cols + 2 * kv_cols]
-    gain_one = packed[:, q_cols + 2 * kv_cols].astype(F32)
-    gain_two = packed[:, q_cols + 2 * kv_cols + 1].astype(F32)
-
-    all_tokens = plane_gather(tokens, chips, 2).reshape(devs * rows, D)
-    layer_all = all_tokens.astype(F32)
-    normed_one = (layer_all * norm_parts(layer_all) * gain_one).astype(BF16)
-    qkv = matmul(normed_one, w_qkv).astype(BF16)
+    used = q_cols + 2 * kv_cols
+    out_full = gather(w_out[None], "grp")
+    upstream = cotangent.astype(F32)
+    d_branch_mlp = (RESID_MULT * upstream).astype(BF16)
+    all_tokens, d_branch_mlp, packed = entry(tokens, d_branch_mlp, packed, grps, chips, 2)
+    packed = packed.reshape(D, cols)
+    normed_one, qkv, gains = project(all_tokens.reshape(devs * rows, D), packed, used)
+    gain_one, gain_two, w_qkv = gains[0], gains[1], packed[:, :used]
+    d_branch_mlp = d_branch_mlp.reshape(devs * rows, D)
     attended = attend(qkv, order, q_heads)
     attended = plane_exchange(
         attended, (rows, D), by_rows(rows), by_cols(q_cols), chips, 3
@@ -1131,16 +1285,9 @@
     residual = layer_in + RESID_MULT * branch_attn
     factor_two = norm_parts(residual)
     normed_two = (residual * factor_two * gain_two).astype(BF16)
-    normed_two = plane_gather(normed_two, chips, 2).reshape(devs * rows, D)
-    upstream = cotangent.astype(F32)
-    d_branch_mlp = (RESID_MULT * upstream).astype(BF16)
-    d_branch_mlp, normed_two = lax.optimization_barrier((d_branch_mlp, normed_two))
-    d_branch_mlp = plane_gather(d_branch_mlp, chips, 2)
-    d_branch_mlp = d_branch_mlp.reshape(devs * rows, D)
-
+    normed_two = plane_gather(normed_two, chips, 1).reshape(devs * rows, D)
     wide_w = gather(jnp.stack([w_gate, w_up])[None], "grp")
     down_w = gather(w_down[None], "grp")
-    normed_two, d_branch_mlp = lax.optimization_barrier((normed_two, d_branch_mlp))
     hidden, hidden_t, silu, slope, normed_t = widen(normed_two, wide_w)
     part_down = down_part(hidden_t, d_branch_mlp)
     part_down, hidden, silu = lax.optimization_barrier((part_down, hidden, silu))

time: 684 us -> 657 us (0.961)
  Pallas kernels: 498 us -> 521 us
  other arithmetic: 56.6 us -> 39.3 us
  waiting for transfers between devices: 24.3 us -> 8.47 us
  local copies, waits for them, and re-layouts: 33.2 us -> 24.1 us
  matrix products: 41 us -> 32.7 us
    pallas_call x0 -> x2, Pallas kernels: none -> 113 us  [the longest x1 102 us: entry(): pl.pallas_call(functools.partial(entry_kernel, grps, chips), out_shape=(j...]
    pallas_call x4 -> x2, Pallas kernels: 160 us -> 79.8 us  [plane_gather(): pl.pallas_call(functools.partial(gather_kernel, chips, inner), out_shape=...]
    all_gather x3, waiting for transfers between devices: 16.1 us -> 0.06 us  [gather(): return lax.all_gather(values, axes, axis=axis, tiled=True)]
    convert_element_type x2 -> x0, other arithmetic: 10.8 us -> none  [the longest x1 9.57 us: on_device(): normed_one = (layer_all * norm_parts(layer_all) * gain_one).astype(BF16)]
    pallas_call x4 -> x3, Pallas kernels: 49.4 us -> 38.8 us  [plane_exchange(): pl.pallas_call(functools.partial(exchange_kernel, chips, cut, paste), out...]
    dot_general x2 -> x1, matrix products: 15.3 us -> 7.01 us  [matmul(): return jnp.dot(left, right, preferred_element_type=F32)]
  transfers between devices with their start and end apart: 14 -> 14, of which waited for: 4 -> 3; matrix products, arithmetic and copies ran while one was open for 13% -> 10% of each run, Pallas kernels for 69% -> 77%
where the time goes in v6:
time: 657 us; the launch traced here: 648 us
  Pallas kernels  521 us (79%)
  other arithmetic  39.3 us (6%)
  matrix products  32.7 us (5%)
  local copies, waits for them, and re-layouts  24.1 us (4%)
  between operations  15.1 us (2%)
  waiting for transfers between devices  8.47 us (1%)
  starting transfers between devices  7.79 us (1%)
    pallas_call x1, Pallas kernels, entry(): pl.pallas_call(functools.partial(entry_kernel, grps, chips), out_shape=(j...  102 us
    pallas_call x2, Pallas kernels, plane_gather(): pl.pallas_call(functools.partial(gather_kernel, chips, inner), out_shape=...  79.8 us
    pallas_call x1, Pallas kernels, square_reduce(): pl.pallas_call(functools.partial(square_kernel, compute, len(operands)),...  54.3 us
    pallas_call x1, Pallas kernels, attend_back(): pl.pallas_call(functools.partial(attend_back_kernel, heads), out_shape=ja...  48.4 us
    pallas_call x1, Pallas kernels, plane_reduce(): pl.pallas_call(functools.partial(reduce_kernel, chips, inner), out_shape=...  41.6 us
    pallas_call x3, Pallas kernels, plane_exchange(): pl.pallas_call(functools.partial(exchange_kernel, chips, cut, paste), out...  38.8 us
    pallas_call x1, Pallas kernels, widen(): pl.pallas_call(widen_kernel, out_shape=(tall, jax.ShapeDtypeStruct((shard...  30.7 us
    pallas_call x1, Pallas kernels, attend(): pl.pallas_call(functools.partial(attend_kernel, heads), out_shape=jax.Sha...  25.5 us
  transfers between devices with their start and end apart: 14, of which 3 were waited for; matrix products, arithmetic and copies ran while one was open for 10% of the time, Pallas kernels for 77%

profile of v6, /device:TPU:0, one launch (start us, length us, event | category | flops | bytes accessed | tf_op | source)
XLA Modules:
  0.0 648.0 jit_solution(13628177604273576025)
XLA Ops:
  8.0 3.1 pad_maximum_fusion
  14.6 101.7 %shard_map.220 = (bf16[8,256,2048]{2,1,0:T(8,128)(2,1)}, bf16[8,256,2048]{2,1,0:T(8,128)(2,1)}, bf16[4,8,64,512]{3,2,1,0:T(8,128)(2,1)}) custom-call(bf16[256,2048]{1,0:T(8,128)(2,1)} %tok_ref.1, bf16[256,2048]{1,0:T(8,128)(2,1)} %fusion.cot_ref, bf16[8,64,512]{2,1,0:T(8,128)(2,1)} %maximum_bitcast_fusion.pack_ref), custom_call_target="tpu_custom_call" | custom-call | flops 1000 | bytes 1000 | tf_op jit(solution)/shard_map/pallas_call | solution.py:1145
  116.3 11.8 %shard_map.221 = (bf16[2048,2048]{1,0:T(8,128)(2,1)}, bf16[2048,384]{1,0:T(8,128)(2,1)}, f32[8,2048]{1,0:T(8,128)}) custom-call(bf16[2048,2048]{1,0:T(8,128)(2,1)} %bitcast.99, bf16[2048,512]{1,0:T(8,128)(2,1)} %bitcast.103), custom_call_target="tpu_custom_call" | custom-call | flops 1000 | bytes 1000 | tf_op jit(solution)/shard_map/pallas_call | solution.py:1185
  129.9 25.5 %shard_map.222.x_ref = bf16[2048,256]{1,0:T(8,128)(2,1)S(1)} custom-call(s32[16]{0:T(128)S(1)} %select_reduce_fusion.order_ref, bf16[2048,384]{1,0:T(8,128)(2,1)S(1)} %copy-done), custom_call_target="tpu_custom_call" | custom-call | flops 1000 | bytes 1000 | tf_op jit(solution)/shard_map/pallas_call | solution.py:521
  156.4 15.7 %shard_map.223 = bf16[256,2048]{1,0:T(8,128)(2,1)} custom-call(bf16[2048,256]{1,0:T(8,128)(2,1)} %copy-done.3), custom_call_target="tpu_custom_call" | custom-call | flops 1000 | bytes 1000 | tf_op jit(solution)/shard_map/pallas_call | solution.py:335
  173.1 39.8 %shard_map.224 = bf16[4,8,64,2048]{3,2,1,0:T(8,128)(2,1)} custom-call(bf16[4,64,2048]{2,1,0:T(8,128)(2,1)} %bitcast.105), custom_call_target="tpu_custom_call" | custom-call | flops 1000 | bytes 1000 | tf_op jit(solution)/shard_map/pallas_call | solution.py:160
  212.9 7.0 %multiply_reduce_fusion.5 = (f32[256]{0:T(256)S(1)}, f32[256,2048]{1,0:T(8,128)S(1)}, f32[]{:T(128)}, f32[256]{0:T(256)S(1)}) fusion(bf16[256,2048]{1,0:T(8,128)(2,1)S(1)} %copy-done.11, bf16[256,2048]{1,0:T(8,128)(2,1)} %shard_map.223, bf16[2048,2048]{1,0:T(8,128)(2,1)} %bitcast.101), kind=kOutput, calls=%fused_computation.41 | convolution fusion | flops 2152201728 | bytes 12584964 | tf_op jit(solution)/shard_map/dot_general | solution.py:363
  221.8 40.0 %shard_map.225 = bf16[8,256,2048]{2,1,0:T(8,128)(2,1)} custom-call(bf16[256,2048]{1,0:T(8,128)(2,1)} %multiply_convert_fusion.1.x_ref), custom_call_target="tpu_custom_call" | custom-call | flops 1000 | bytes 1000 | tf_op jit(solution)/shard_map/pallas_call | solution.py:160
  261.8 30.7 %shard_map.226 = (bf16[4,2048,256]{2,1,0:T(8,128)(2,1)}, bf16[4,256,2048]{2,1,0:T(8,128)(2,1)}, bf16[4,2048,256]{2,1,0:T(8,128)(2,1)}, bf16[4,2048,256]{2,1,0:T(8,128)(2,1)}, bf16[2048,2048]{1,0:T(8,128)(2,1)}) custom-call(bf16[2048,2048]{1,0:T(8,128)(2,1)} %bitcast.96, bf16[4,2,2048,256]{3,2,1,0:T(8,128)(2,1)} %bitcast.92), custom_call_target="tpu_custom_call" | custom-call | flops 1000 | bytes 1000 | tf_op jit(solution)/shard_map/pallas_call | solution.py:668
  292.5 15.4 %shard_map.227 = bf16[4,256,2048]{2,1,0:T(8,128)(2,1)} custom-call(bf16[4,256,2048]{2,1,0:T(8,128)(2,1)} %get-tuple-element.63.ht_ref, bf16[2048,2048]{1,0:T(8,128)(2,1)} %bitcast.94), custom_call_target="tpu_custom_call" | custom-call | flops 1000 | bytes 1000 | tf_op jit(solution)/shard_map/pallas_call | solution.py:702
  308.5 21.4 %shard_map.228 = (f32[256,2048]{1,0:T(8,128)}, bf16[256,2048]{1,0:T(8,128)(2,1)}, bf16[256,2048]{1,0:T(8,128)(2,1)}, bf16[256,2048]{1,0:T(8,128)(2,1)}) custom-call(bf16[4,2048,256]{2,1,0:T(8,128)(2,1)} %get-tuple-element.67.h_ref, bf16[4,256,2048]{2,1,0:T(8,128)(2,1)} %bitcast.97), custom_call_target="tpu_custom_call" | custom-call | flops 1000 | bytes 1000 | tf_op jit(solution)/shard_map/pallas_call | solution.py:1028
  333.5 15.4 %shard_map.229 = (bf16[4,2048,256]{2,1,0:T(8,128)(2,1)}, bf16[4,2048,256]{2,1,0:T(8,128)(2,1)}) custom-call(bf16[4,2048,256]{2,1,0:T(8,128)(2,1)} %get-tuple-element.74.s_ref, bf16[4,2048,256]{2,1,0:T(8,128)(2,1)} %get-tuple-element.75.t_ref, bf16[2048,2048]{1,0:T(8,128)(2,1)} %bitcast.95, bf16[4,256,2048]{2,1,0:T(8,128)(2,1)} %bitcast.98), custom_call_target="tpu_custom_call" | custom-call | flops 1000 | bytes 1000 | tf_op jit(solution)/shard_map/pallas_call | solution.py:760
  348.9 23.4 %shard_map.230 = bf16[4,2,2048,256]{3,2,1,0:T(8,128)(2,1)} custom-call(bf16[2048,2048]{1,0:T(8,128)(2,1)} %get-tuple-element.69.nt_ref, bf16[4,2048,256]{2,1,0:T(8,128)(2,1)} %get-tuple-element.84.dg_ref.refs_0_, bf16[4,2048,256]{2,1,0:T(8,128)(2,1)} %get-tuple-element.85.du_ref.refs_1_), custom_call_target="tpu_custom_call" | custom-call | flops 1000 | bytes 1000 | tf_op jit(solution)/shard_map/pallas_call | solution.py:782
  372.4 6.5 %collective-permute-done.1 = bf16[256,2048]{1,0:T(8,128)(2,1)} collective-permute-done((bf16[256,2048]{1,0:T(8,128)(2,1)}, bf16[256,2048]{1,0:T(8,128)(2,1)}, u32[]{:S(2)}, u32[]{:S(2)}) %collective-permute-start.1) | collective-permute-done | bytes 1048608 | tf_op jit(solution)/shard_map/ppermute | solution.py:274
  379.3 54.3 %shard_map.231 = f32[256,2048]{1,0:T(8,128)} custom-call(bf16[4,2048,256]{2,1,0:T(8,128)(2,1)} %get-tuple-element.84.dg_ref.refs_0_, bf16[4,2048,256]{2,1,0:T(8,128)(2,1)} %get-tuple-element.85.du_ref.refs_1_, bf16[4,2,2048,256]{3,2,1,0:T(8,128)(2,1)} %bitcast.93), custom_call_target="tpu_custom_call" | custom-call | flops 1000 | bytes 1000 | tf_op jit(solution)/shard_map/pallas_call | solution.py:941
  433.7 6.7 %multiply_reduce_fusion = (f32[]{:T(128)}, f32[]{:T(128)}, f32[256]{0:T(256)S(1)}, f32[2048]{0:T(1024)}, f32[256,2048]{1,0:T(8,128)}) fusion(f32[256,2048]{1,0:T(8,128)S(1)} %get-tuple-element.116, f32[256,2048]{1,0:T(8,128)} %shard_map.231, f32[2048]{0:T(1024)S(1)} %bitcast.113, f32[256]{0:T(256)S(1)} %get-tuple-element.133, ...), kind=kLoop, calls=%fused_computation.33 | loop fusion | flops 9434878 | bytes 11552776 | tf_op jit(solution)/shard_map/reduce_sum | solution.py:1372
  441.6 2.4 convolution_convert_fusion.1
  444.0 2.5 copy_bitcast_fusion
  446.5 2.0 copy-done.6
  448.5 7.1 %convolution_convert_fusion.3.x_ref = bf16[256,2048]{1,0:T(8,128)(2,1)} fusion(bf16[256,2048]{1,0:T(8,128)(2,1)S(1)} %multiply_convert_fusion, bf16[2048,2048]{1,0:T(8,128)(2,1)} %bitcast.102), kind=kOutput, calls=%fused_computation.12 | convolution fusion | flops 2148007936 | bytes 10485760 | tf_op jit(solution)/shard_map/dot_general | solution.py:371
  455.6 15.0 %shard_map.232.d_ref = bf16[2048,256]{1,0:T(8,128)(2,1)} custom-call(bf16[256,2048]{1,0:T(8,128)(2,1)} %convolution_convert_fusion.3.x_ref), custom_call_target="tpu_custom_call" | custom-call | flops 1000 | bytes 1000 | tf_op jit(solution)/shard_map/pallas_call | solution.py:335
  470.7 5.6 fusion.12
  479.8 48.4 %shard_map.233 = bf16[2048,384]{1,0:T(8,128)(2,1)S(1)} custom-call(s32[16]{0:T(128)S(1)} %select_reduce_fusion.order_ref, bf16[2048,384]{1,0:T(8,128)(2,1)S(1)} %copy-done.1, bf16[2048,256]{1,0:T(8,128)(2,1)S(1)} %copy-done.2), custom_call_target="tpu_custom_call" | custom-call | flops 1000 | bytes 1000 | tf_op jit(solution)/shard_map/pallas_call | solution.py:543
  529.5 4.5 fusion.11
  534.1 9.1 %convolution_convert_fusion.2 = bf16[2048,384]{1,0:T(8,128)(2,1)} fusion(bf16[2048,2048]{1,0:T(8,128)(2,1)} %get-tuple-element.86, bf16[2048,384]{1,0:T(8,128)(2,1)S(1)} %copy-done.5), kind=kOutput, calls=%fused_computation.8 | convolution fusion | flops 3222011904 | bytes 11534336 | tf_op jit(solution)/shard_map/dot_general | solution.py:367
  546.8 7.1 %convolution_convert_fusion = bf16[2048,2048]{1,0:T(8,128)(2,1)} fusion(bf16[2048,384]{1,0:T(8,128)(2,1)S(1)} %copy-done.5, bf16[2048,512]{1,0:T(8,128)(2,1)S(1)} %bitcast.104), kind=kOutput, calls=%fused_computation | convolution fusion | flops 3225419776 | bytes 11534336 | tf_op jit(solution)/shard_map/dot_general | solution.py:371
  553.9 41.6 %shard_map.234 = f32[256,2048]{1,0:T(8,128)} custom-call(bf16[8,256,2048]{2,1,0:T(8,128)(2,1)} %bitcast.100), custom_call_target="tpu_custom_call" | custom-call | flops 1000 | bytes 1000 | tf_op jit(solution)/shard_map/pallas_call | solution.py:246
  595.5 2.3 bitcast_convert_fusion.1
  599.7 8.2 %shard_map.236 = bf16[8,64,384]{2,1,0:T(8,128)(2,1)} custom-call(bf16[8,64,384]{2,1,0:T(8,128)(2,1)} %bitcast.110), custom_call_target="tpu_custom_call" | custom-call | flops 1000 | bytes 1000 | tf_op jit(solution)/shard_map/pallas_call | solution.py:335
  609.8 2.7 concatenate.7
  615.0 12.1 %shard_map.235 = f32[8,640]{1,0:T(8,128)} custom-call(f32[8,640]{1,0:T(8,128)} %reshape.159.x_ref), custom_call_target="tpu_custom_call" | custom-call | flops 1000 | bytes 1000 | tf_op jit(solution)/shard_map/pallas_call | solution.py:616
  634.6 5.5 fusion.5
  (137 shorter events, 38.1 us)
Async XLA Ops:
  7.2 165.9 %all-gather.7.cloned.1.call-start = ((), (), s32[]{:S(2)}) async-start(), calls=%async_computation.8 | async-start | bytes 1310720 | tf_op jit(solution)/shard_map/all_gather | solution.py:375
  7.9 253.9 %all-gather.9.cloned.1.call-start = ((), (), s32[]{:S(2)}) async-start(), calls=%async_computation.9 | async-start | bytes 10485760 | tf_op jit(solution)/shard_map/all_gather | solution.py:375
  11.1 297.4 %all-gather.11.cloned.1.call-start = ((), (), s32[]{:S(2)}) async-start(), calls=%async_computation.10 | async-start | bytes 5242880 | tf_op jit(solution)/shard_map/all_gather | solution.py:375
  11.8 468.0 %reduce-scatter.5.cloned.1.call-start = ((), (), s32[]{:S(2)}) async-start(), calls=%async_computation.4 | async-start | bytes 5242880 | tf_op jit(solution)/shard_map/reduce_scatter | solution.py:379
  116.2 11.8 %copy-start.30 = (s32[64]{0:T(128)S(1)}, s32[64]{0:T(128)}, u32[]{:S(2)}) copy-start(s32[64]{0:T(128)} %param.15) | copy-start | bytes 772
  116.2 11.8 %copy-start.31 = (s32[64]{0:T(128)S(1)}, s32[64]{0:T(128)}, u32[]{:S(2)}) copy-start(s32[64]{0:T(128)} %param.14) | copy-start | bytes 772
  173.1 39.8 %copy-start.11 = (bf16[256,2048]{1,0:T(8,128)(2,1)S(1)}, bf16[256,2048]{1,0:T(8,128)(2,1)}, u32[]{:S(2)}) copy-start(bf16[256,2048]{1,0:T(8,128)(2,1)} %tok_ref.1) | copy-start | bytes 3145732
  219.9 41.9 %copy-start.29 = (f32[256]{0:T(256)}, f32[256]{0:T(256)S(1)}, u32[]{:S(2)}) copy-start(f32[256]{0:T(256)S(1)} %get-tuple-element.125) | copy-start | bytes 3076
  219.9 220.4 %copy-start.9 = (f32[256,2048]{1,0:T(8,128)}, f32[256,2048]{1,0:T(8,128)S(1)}, u32[]{:S(2)}) copy-start(f32[256,2048]{1,0:T(8,128)S(1)} %get-tuple-element.116) | copy-start | bytes 6291460
  220.6 219.8 %copy-start.23 = (f32[256]{0:T(256)}, f32[256]{0:T(256)S(1)}, u32[]{:S(2)}) copy-start(f32[256]{0:T(256)S(1)} %get-tuple-element.133) | copy-start | bytes 3076
  308.0 221.5 %reduce-scatter.7.cloned.1.call-start = ((), (), s32[]{:S(2)}) async-start(), calls=%async_computation.5 | async-start | bytes 10485760 | tf_op jit(solution)/shard_map/reduce_scatter | solution.py:379
  330.0 42.4 %collective-permute-start = (bf16[256,2048]{1,0:T(8,128)(2,1)}, bf16[256,2048]{1,0:T(8,128)(2,1)S(1)}, u32[]{:S(2)}, u32[]{:S(2)}) collective-permute-start(bf16[256,2048]{1,0:T(8,128)(2,1)} %get-tuple-element.78), channel_id=1, source_target_pairs={{0,6},{2,4},{4,2},{6,0},{1,7},{3,5},{5,3},{7,1},{8,14},{10,12},{12... | collective-permute-start | bytes 3145736 | tf_op jit(solution)/shard_map/ppermute | solution.py:274
  330.9 48.0 %collective-permute-start.1 = (bf16[256,2048]{1,0:T(8,128)(2,1)}, bf16[256,2048]{1,0:T(8,128)(2,1)}, u32[]{:S(2)}, u32[]{:S(2)}) collective-permute-start(bf16[256,2048]{1,0:T(8,128)(2,1)} %get-tuple-element.79), channel_id=1, source_target_pairs={{0,2},{2,0},{4,6},{6,4},{1,3},{3,1},{5,7},{7,5},{8,10},{10,8},{12,... | collective-permute-start | bytes 3145736 | tf_op jit(solution)/shard_map/ppermute | solution.py:274
  332.5 46.7 %collective-permute-start.2 = (bf16[256,2048]{1,0:T(8,128)(2,1)}, bf16[256,2048]{1,0:T(8,128)(2,1)}, u32[]{:S(2)}, u32[]{:S(2)}) collective-permute-start(bf16[256,2048]{1,0:T(8,128)(2,1)} %get-tuple-element.80), channel_id=1, source_target_pairs={{0,4},{2,6},{4,0},{6,2},{1,5},{3,7},{5,1},{7,3},{8,12},{10,14},{12... | collective-permute-start | bytes 3145736 | tf_op jit(solution)/shard_map/ppermute | solution.py:274
  379.2 218.6 %reduce-scatter.11.cloned.1.call-start = ((), (), s32[]{:S(2)}) async-start(), calls=%async_computation.7 | async-start | bytes 1310720 | tf_op jit(solution)/shard_map/reduce_scatter | solution.py:379
  433.6 6.7 %copy-start.7 = (f32[256,2048]{1,0:T(8,128)S(1)}, f32[256,2048]{1,0:T(8,128)}, u32[]{:S(2)}) copy-start(f32[256,2048]{1,0:T(8,128)} %shard_map.231) | copy-start | bytes 6291460
  433.7 6.7 %copy-start.14 = (bf16[256,2048]{1,0:T(8,128)(2,1)S(1)}, bf16[256,2048]{1,0:T(8,128)(2,1)}, u32[]{:S(2)}) copy-start(bf16[256,2048]{1,0:T(8,128)(2,1)} %param.25) | copy-start | bytes 3145732
  448.5 22.1 %collective-permute-start.3 = (bf16[4,4,64,2048]{3,2,0,1:T(8,128)(2,1)}, bf16[4,4,64,2048]{3,2,0,1:T(8,128)(2,1)}, u32[]{:S(2)}, u32[]{:S(2)}) collective-permute-start(bf16[4,4,64,2048]{3,2,0,1:T(8,128)(2,1)} %copy_bitcast_fusion), channel_id=1, source_target_pairs={{0,1},{1,0},{2,3},{3,2},{4,5},{5,4},{6,7},{7,6},{8,9},{9,8},{10,11... | collective-permute-start | bytes 12582920 | tf_op jit(solution)/shard_map/ppermute | solution.py:283
  470.7 9.1 %copy-start.1 = (bf16[2048,384]{1,0:T(8,128)(2,1)S(1)}, bf16[2048,384]{1,0:T(8,128)(2,1)}, u32[]{:S(2)}) copy-start(bf16[2048,384]{1,0:T(8,128)(2,1)} %get-tuple-element.61.qkv_ref) | copy-start | bytes 4718596
  470.7 9.1 %copy-start.2 = (bf16[2048,256]{1,0:T(8,128)(2,1)S(1)}, bf16[2048,256]{1,0:T(8,128)(2,1)}, u32[]{:S(2)}) copy-start(bf16[2048,256]{1,0:T(8,128)(2,1)} %shard_map.232.d_ref) | copy-start | bytes 3145732
  476.3 53.1 %collective-permute-start.4 = (bf16[4,64,2048]{2,1,0:T(8,128)(2,1)}, bf16[4,64,2048]{2,1,0:T(8,128)(2,1)}, u32[]{:S(2)}, u32[]{:S(2)}) collective-permute-start(bf16[4,64,2048]{2,1,0:T(8,128)(2,1)} %get-tuple-element.89), channel_id=1, source_target_pairs={{0,6},{2,4},{4,2},{6,0},{1,7},{3,5},{5,3},{7,1},{8,14},{10,12},{12... | collective-permute-start | bytes 3145736 | tf_op jit(solution)/shard_map/ppermute | solution.py:274
  477.8 51.6 %collective-permute-start.5 = (bf16[4,64,2048]{2,1,0:T(8,128)(2,1)}, bf16[4,64,2048]{2,1,0:T(8,128)(2,1)}, u32[]{:S(2)}, u32[]{:S(2)}) collective-permute-start(bf16[4,64,2048]{2,1,0:T(8,128)(2,1)} %get-tuple-element.90), channel_id=1, source_target_pairs={{0,2},{2,0},{4,6},{6,4},{1,3},{3,1},{5,7},{7,5},{8,10},{10,8},{12,... | collective-permute-start | bytes 3145736 | tf_op jit(solution)/shard_map/ppermute | solution.py:274
  478.5 50.9 %collective-permute-start.6 = (bf16[4,64,2048]{2,1,0:T(8,128)(2,1)}, bf16[4,64,2048]{2,1,0:T(8,128)(2,1)}, u32[]{:S(2)}, u32[]{:S(2)}) collective-permute-start(bf16[4,64,2048]{2,1,0:T(8,128)(2,1)} %get-tuple-element.91), channel_id=1, source_target_pairs={{0,4},{2,6},{4,0},{6,2},{1,5},{3,7},{5,1},{7,3},{8,12},{10,14},{12... | collective-permute-start | bytes 3145736 | tf_op jit(solution)/shard_map/ppermute | solution.py:274
  534.1 65.7 %reduce-scatter.9.cloned.1.call-start = ((), (), s32[]{:S(2)}) async-start(), calls=%async_computation.6 | async-start | bytes 1966080 | tf_op jit(solution)/shard_map/reduce_scatter | solution.py:379
  553.9 41.6 %copy-start.17 = (bf16[1,2,2048,256]{3,2,1,0:T(8,128)(2,1)S(1)}, bf16[1,2,2048,256]{3,2,1,0:T(8,128)(2,1)}, u32[]{:S(2)}) copy-start(bf16[1,2,2048,256]{3,2,1,0:T(8,128)(2,1)} %reduce-scatter.7.cloned.1.call-done) | copy-start | bytes 6291460
  595.5 12.4 %copy-start.10 = (f32[256,2048]{1,0:T(8,128)S(1)}, f32[256,2048]{1,0:T(8,128)}, u32[]{:S(2)}) copy-start(f32[256,2048]{1,0:T(8,128)} %shard_map.234) | copy-start | bytes 6291460
  597.9 10.1 %copy-start.12 = (bf16[256,2048]{1,0:T(8,128)(2,1)S(1)}, bf16[256,2048]{1,0:T(8,128)(2,1)}, u32[]{:S(2)}) copy-start(bf16[256,2048]{1,0:T(8,128)(2,1)} %tok_ref.1) | copy-start | bytes 3145732
  613.2 14.6 %copy-start.28 = (f32[256]{0:T(256)S(1)}, f32[256]{0:T(256)}, u32[]{:S(2)}) copy-start(f32[256]{0:T(256)} %get-tuple-element.109) | copy-start | bytes 3076
  614.1 20.5 %copy-start.8 = (f32[256,2048]{1,0:T(8,128)S(1)}, f32[256,2048]{1,0:T(8,128)}, u32[]{:S(2)}) copy-start(f32[256,2048]{1,0:T(8,128)} %shard_map.231) | copy-start | bytes 6291460
  614.1 20.5 %copy-start.24 = (f32[256]{0:T(256)S(1)}, f32[256]{0:T(256)}, u32[]{:S(2)}) copy-start(f32[256]{0:T(256)} %copy-done.23) | copy-start | bytes 3076
  614.1 20.5 %copy-start.26 = (f32[256]{0:T(256)S(1)}, f32[256]{0:T(256)}, u32[]{:S(2)}) copy-start(f32[256]{0:T(256)} %copy-done.25) | copy-start | bytes 3076
  614.1 20.5 %copy-start.27 = (f32[256]{0:T(256)S(1)}, f32[256]{0:T(256)}, u32[]{:S(2)}) copy-start(f32[256]{0:T(256)} %get-tuple-element.132) | copy-start | bytes 3076
  (16 other events, 31.1 us)
Sparse Core Ops, SparseCore 0:
  9.6 35.5 all-gather.6
  47.4 163.7 all-gather.8
  212.7 80.5 all-gather.10
  308.1 74.0 reduce-scatter.4
  384.5 144.9 reduce-scatter.6
  534.2 27.7 reduce-scatter.10
  564.3 33.9 reduce-scatter.8

commit v7 on v6

--- a/solution.py
+++ b/solution.py
@@ -822,150 +822,6 @@
     return jnp.where(stage == 0, 3, jnp.where(stage == 3, 0, stage))
 
 
-class Square:
-    def __init__(self, acc, mine, away, twin, moved, corner, landed, tsend, trecv, msend, mrecv, csend, crecv):
-        self.acc, self.mine, self.away, self.twin = acc, mine, away, twin
-        self.moved, self.corner, self.landed = moved, corner, landed
-        self.tsend, self.trecv, self.msend, self.mrecv = tsend, trecv, msend, mrecv
-        self.csend, self.crecv = csend, crecv
-        self.chip, self.core = place()
-        self.rows = mine.shape[1]
-        self.half = self.rows // 2
-
-    def greet(self):
-        peers = [(flip(self.chip, s, 4), self.core) for s in (1, 2)]
-        greet(peers + [(self.chip, 1 - self.core)])
-
-    def twin_copy(self, stage):
-        return remote(
-            self.away.at[stage], self.twin.at[stage], self.tsend.at[stage], self.trecv.at[stage],
-            self.chip, 1 - self.core,
-        )
-
-    def offer(self, stage):
-        own, other = self.core * self.rows, (1 - self.core) * self.rows
-        self.mine[stage] = self.acc[pl.ds(pl.multiple_of(own, self.rows), self.rows)].astype(BF16)
-        self.away[stage] = self.acc[pl.ds(pl.multiple_of(other, self.rows), self.rows)].astype(BF16)
-        self.twin_copy(stage).start()
-
-    def at(self, h):
-        return pl.ds(h * self.half, self.half)
-
-    def both(self, stage, h):
-        return self.mine[stage, self.at(h)].astype(F32) + self.twin[stage, self.at(h)].astype(F32)
-
-    def corner_copy(self, h):
-        return remote(
-            self.moved.at[0, self.at(h)], self.corner.at[h], self.csend.at[h], self.crecv.at[h],
-            flip(self.chip, h + 1, 4), self.core,
-        )
-
-    def copy(self, stage, h):
-        return remote(
-            self.moved.at[stage, self.at(h)], self.landed.at[stage - 1, self.at(h)],
-            self.msend.at[stage - 1, h], self.mrecv.at[stage - 1, h],
-            flip(self.chip, stage, 4), self.core,
-        )
-
-    def corners(self):
-        self.twin_copy(0).wait_recv()
-        for h in range(2):
-            self.moved[0, self.at(h)] = self.both(0, h).astype(BF16)
-            self.corner_copy(h).start()
-
-    def plain(self, stage):
-        self.twin_copy(stage).wait_recv()
-        h = stage - 1
-        self.moved[stage, self.at(h)] = self.both(stage, h).astype(BF16)
-        self.copy(stage, h).start()
-
-    def joined(self, stage):
-        h = 2 - stage
-        self.corner_copy(h).wait_recv()
-        total = self.both(stage, h) + self.corner[h].astype(F32)
-        self.moved[stage, self.at(h)] = total.astype(BF16)
-        self.copy(stage, h).start()
-
-    def finish(self, o_ref):
-        self.twin_copy(3).wait_recv()
-        for h in range(2):
-            o_ref[self.at(h)] = self.both(3, h)
-        for stage, h in ((1, 0), (2, 1), (2, 0), (1, 1)):
-            self.copy(stage, h).wait_recv()
-            o_ref[self.at(h)] += self.landed[stage - 1, self.at(h)].astype(F32)
-        for stage in (1, 2):
-            for h in range(2):
-                self.copy(stage, h).wait_send()
-        for h in range(2):
-            self.corner_copy(h).wait_send()
-        for stage in range(4):
-            self.twin_copy(stage).wait_send()
-
-
-def square_kernel(compute, count, *refs):
-    operands, o_ref, scratch = refs[:count], refs[count], refs[count + 1 :]
-    run = Square(*scratch)
-    stage = pl.program_id(0)
-
-    @pl.when(stage == 0)
-    def _():
-        run.greet()
-
-    target = jnp.bitwise_xor(run.chip, stage_step(stage))
-    width = 2 * run.rows
-    run.acc[...] = compute(operands, pl.ds(pl.multiple_of(target * width, width), width))
-    run.offer(stage)
-
-    @pl.when(stage == 1)
-    def _():
-        run.corners()
-
-    @pl.when(stage == 2)
-    def _():
-        run.plain(1)
-
-    @pl.when(stage == 3)
-    def _():
-        run.plain(2)
-        run.joined(2)
-        run.joined(1)
-        run.finish(o_ref)
-
-
-def square_reduce(compute, operands, rows, call_id):
-    block = (rows, D)
-
-    def held(shape):
-        return pl.BlockSpec(shape, lambda s: (0,) * len(shape), pipeline_mode=pl.Buffered(1))
-
-    return pl.pallas_call(
-        functools.partial(square_kernel, compute, len(operands)),
-        out_shape=jax.ShapeDtypeStruct(block, F32),
-        grid=(4,),
-        in_specs=[held(x.shape) for x in operands],
-        out_specs=held(block),
-        scratch_shapes=[
-            pltpu.VMEM((2 * rows, D), F32),
-            pltpu.VMEM((4,) + block, BF16),
-            pltpu.VMEM((4,) + block, BF16),
-            pltpu.VMEM((4,) + block, BF16),
-            pltpu.VMEM((3,) + block, BF16),
-            pltpu.VMEM((2, rows // 2, D), BF16),
-            pltpu.VMEM((2,) + block, BF16),
-            pltpu.SemaphoreType.DMA((4,)),
-            pltpu.SemaphoreType.DMA((4,)),
-            pltpu.SemaphoreType.DMA((2, 2)),
-            pltpu.SemaphoreType.DMA((2, 2)),
-            pltpu.SemaphoreType.DMA((2,)),
-            pltpu.SemaphoreType.DMA((2,)),
-        ],
-        cost_estimate=BRIEF,
-        compiler_params=pltpu.CompilerParams(
-            collective_id=call_id, has_side_effects=True, vmem_limit_bytes=60 << 20
-        ),
-    )(*operands)
-
-
 def widen_back_rows(refs, rows):
     dg_ref, du_ref, w_ref = refs
     total = None
@@ -980,7 +836,18 @@
     return dot_nt(d_ref[rows], w_ref[...])
 
 
-def twin_kernel(h_ref, w_ref, o_ref, corner_ref, x_ref, y_ref, acc, mine, away, twin, tsend, trecv):
+def mix_rows(refs, rows):
+    h_ref, w_ref = refs
+    total = None
+    for i in range(w_ref.shape[0]):
+        part = matmul(h_ref[i, rows], w_ref[i])
+        total = part if total is None else total + part
+    return total
+
+
+def twin_kernel(compute, count, *refs):
+    operands, (o_ref, corner_ref, x_ref, y_ref) = refs[:count], refs[count : count + 4]
+    acc, mine, away, twin, tsend, trecv = refs[count + 4 :]
     chip, core = place()
     stage = pl.program_id(0)
     rows = o_ref.shape[0]
@@ -997,11 +864,7 @@
         greet([(chip, 1 - core)])
 
     target = jnp.bitwise_xor(chip, stage_step(stage)) * 2 * rows
-    total = None
-    for i in range(w_ref.shape[0]):
-        part = matmul(h_ref[i, pl.ds(pl.multiple_of(target, 2 * rows), 2 * rows)], w_ref[i])
-        total = part if total is None else total + part
-    acc[...] = total
+    acc[...] = compute(operands, pl.ds(pl.multiple_of(target, 2 * rows), 2 * rows))
     mine[stage] = acc[pl.ds(pl.multiple_of(core * rows, rows), rows)].astype(BF16)
     away[stage] = acc[pl.ds(pl.multiple_of((1 - core) * rows, rows), rows)].astype(BF16)
     copy(stage).start()
@@ -1019,17 +882,17 @@
             copy(s).wait_send()
 
 
-def mix_twin(hidden, weights, rows, call_id):
+def twin_reduce(compute, operands, rows, call_id):
     block = (rows, D)
 
     def held(shape):
         return pl.BlockSpec(shape, lambda s: (0,) * len(shape), pipeline_mode=pl.Buffered(1))
 
     return pl.pallas_call(
-        twin_kernel,
+        functools.partial(twin_kernel, compute, len(operands)),
         out_shape=(jax.ShapeDtypeStruct(block, F32),) + (jax.ShapeDtypeStruct(block, BF16),) * 3,
         grid=(4,),
-        in_specs=[held(hidden.shape), held(weights.shape)],
+        in_specs=[held(x.shape) for x in operands],
         out_specs=(held(block),) * 4,
         scratch_shapes=[
             pltpu.VMEM((2 * rows, D), F32),
@@ -1043,7 +906,17 @@
         compiler_params=pltpu.CompilerParams(
             collective_id=call_id, has_side_effects=True, vmem_limit_bytes=60 << 20
         ),
-    )(hidden, weights)
+    )(*operands)
+
+
+def swap_others(parts):
+    return tuple(swap_chips(part, step) for step, part in zip((3, 1, 2), parts))
+
+
+def join(own, came):
+    for part in came:
+        own = own + part.astype(F32)
+    return own
 
 
 def entry_kernel(
@@ -1292,30 +1165,26 @@
     part_down = down_part(hidden_t, d_branch_mlp)
     part_down, hidden, silu = lax.optimization_barrier((part_down, hidden, silu))
     grad_down = scatter(part_down, "grp")
+    d_gate, d_up = narrow_back(silu, slope, d_branch_mlp, down_w)
     if chips == 4:
-        branch_mlp, *others = mix_twin(hidden, down_w, rows, 11)
-        others, silu = lax.optimization_barrier((others, silu))
-        others = [swap_chips(part, step) for step, part in zip((3, 1, 2), others)]
+        d_normed_two, *others = twin_reduce(widen_back_rows, (d_gate, d_up, wide_w), rows, 10)
+        others, d_gate, d_up = lax.optimization_barrier((others, d_gate, d_up))
+        others = swap_others(others)
+        part_wide = widen_part(normed_t, d_gate, d_up)
+        part_wide, hidden = lax.optimization_barrier((part_wide, hidden))
+        branch_mlp, *shares = twin_reduce(mix_rows, (hidden, down_w), rows, 11)
+        others, shares, part_wide = lax.optimization_barrier((others, shares, part_wide))
+        grad_wide = scatter(part_wide, "grp")
+        d_normed_two = join(d_normed_two, others)
+        shares = swap_others(shares)
     else:
-        branch_mlp = mix(hidden, down_w)
-    d_gate, d_up = narrow_back(silu, slope, d_branch_mlp, down_w)
-    part_wide = widen_part(normed_t, d_gate, d_up)
-    if chips == 4:
-        part_wide, others, d_gate, d_up = lax.optimization_barrier(
-            (part_wide, others, d_gate, d_up)
-        )
-    else:
+        part_wide = widen_part(normed_t, d_gate, d_up)
         part_wide, d_gate, d_up = lax.optimization_barrier((part_wide, d_gate, d_up))
-    grad_wide = scatter(part_wide, "grp")
-    if chips == 4:
-        for part in others:
-            branch_mlp = branch_mlp + part.astype(F32)
-        d_normed_two = square_reduce(widen_back_rows, (d_gate, d_up, wide_w), rows, 10)
-    else:
-        branch_mlp = plane_reduce(branch_mlp.reshape(devs, rows, D), chips, 5)
+        grad_wide = scatter(part_wide, "grp")
         d_normed_two = widen_back(d_gate, d_up, wide_w)
         d_normed_two = plane_reduce(d_normed_two.reshape(devs, rows, D), chips, 5)
-    layer_out = residual + RESID_MULT * branch_mlp
+        branch_mlp = mix(hidden, down_w)
+        branch_mlp = plane_reduce(branch_mlp.reshape(devs, rows, D), chips, 5)
 
     d_residual_norm, d_gain_two = norm_back(residual, factor_two, gain_two, d_normed_two)
     d_residual = upstream + d_residual_norm
@@ -1329,40 +1198,23 @@
         d_attended, (devs * rows, q_cols), by_cols(q_cols), by_rows(rows), chips, 7
     )
     if chips == 4:
-        sent_out, d_attended = lax.optimization_barrier((drift_out.parts(), d_attended))
+        sent_out, d_attended, shares = lax.optimization_barrier(
+            (drift_out.parts(), d_attended, shares)
+        )
+        branch_mlp = join(branch_mlp, shares)
         sent_out = Drift.send(sent_out)
     d_attended, grad_down = lax.optimization_barrier((d_attended, grad_down))
     d_qkv = attend_back(qkv, d_attended, order, q_heads)
     if chips == 4:
-        sent_out, d_qkv, grad_wide = lax.optimization_barrier((sent_out, d_qkv, grad_wide))
+        sent_out, d_qkv = lax.optimization_barrier((sent_out, d_qkv))
         grad_out = drift_out.finish(sent_out).astype(BF16)
     else:
         grad_out = plane_reduce(
             grad_out.reshape(grps, devs, w_rows, D), chips, 6, dtype=BF16, inner=True
         )
-    grad_out = scatter(grad_out, "grp").reshape(w_rows, D).astype(F32)
+    layer_out = residual + RESID_MULT * branch_mlp
     sent = over_rows(normed_one, d_qkv).astype(BF16)
-    sent, d_qkv = lax.optimization_barrier((sent, d_qkv))
-    sent = scatter(sent, "grp")
-
-    d_normed_one = over_cols(d_qkv, w_qkv).astype(BF16).reshape(devs, rows, D)
-    d_normed_one = plane_reduce(d_normed_one, chips, 5)
-    d_normed_one, sent = lax.optimization_barrier((d_normed_one, sent))
-    d_input_norm, d_gain_one = norm_back(layer_in, norm_parts(layer_in), gain_one, d_normed_one)
-    tokens_grad = (d_residual + d_input_norm).astype(BF16)
-
-    sent = sent.reshape(devs, w_rows, q_cols + 2 * kv_cols)
-    sent = plane_exchange(sent, sent.shape, by_slot, by_slot, chips, 9).astype(F32)
-
-    def kv_join(g):
-        g = g.reshape(devs // kv_copies, kv_copies, w_rows, kv_cols)
-        g = jnp.sum(g, axis=1) if kv_copies > 1 else g[:, 0]
-        return jnp.swapaxes(g, 0, 1).reshape(w_rows, KV_HEADS * HEAD_DIM)
-
-    grad_query = jnp.swapaxes(sent[:, :, :q_cols], 0, 1).reshape(w_rows, D)
-    grad_key = kv_join(sent[:, :, q_cols : q_cols + kv_cols])
-    grad_value = kv_join(sent[:, :, q_cols + kv_cols : q_cols + 2 * kv_cols])
-
+    d_gain_one = jnp.sum(w_qkv.astype(F32) * sent.astype(F32), axis=1) / gain_one
     scaled_attn = RESID_MULT * branch_attn
     scaled_mlp = RESID_MULT * branch_mlp
     squares = jnp.stack(
@@ -1373,7 +1225,39 @@
         ]
     )
     totals = jnp.concatenate([d_gain_one, d_gain_two, squares, jnp.zeros((1021,), F32)])
-    totals = total(totals.reshape(8, 5 * D // 16), grps, chips, 8).reshape(-1)
+    sent, d_qkv, totals = lax.optimization_barrier((sent, d_qkv, totals))
+    totals = totals.reshape(8, 5 * D // 16)
+    if chips == 4:
+        d_normed_one, *others = twin_reduce(project_back_rows, (d_qkv, w_qkv), rows, 5)
+        sent, grad_out, _ = lax.optimization_barrier((sent, grad_out, others[0]))
+    sent, grad_out, grad_wide = lax.optimization_barrier((sent, grad_out, grad_wide))
+    sent = scatter(sent, "grp")
+    grad_out = scatter(grad_out, "grp").reshape(w_rows, D).astype(F32)
+    if chips == 4:
+        others, totals = lax.optimization_barrier((others, totals))
+        others = swap_others(others)
+        totals = total(totals, grps, chips, 8)
+        others, totals = lax.optimization_barrier((others, totals))
+        d_normed_one = join(d_normed_one, others)
+    else:
+        totals = total(totals, grps, chips, 8)
+        d_normed_one = over_cols(d_qkv, w_qkv).astype(BF16).reshape(devs, rows, D)
+        d_normed_one = plane_reduce(d_normed_one, chips, 5)
+    d_input_norm, _ = norm_back(layer_in, norm_parts(layer_in), gain_one, d_normed_one)
+    tokens_grad = (d_residual + d_input_norm).astype(BF16)
+    sent = sent.reshape(devs, w_rows, q_cols + 2 * kv_cols)
+    sent = plane_exchange(sent, sent.shape, by_slot, by_slot, chips, 9).astype(F32)
+
+    def kv_join(g):
+        g = g.reshape(devs // kv_copies, kv_copies, w_rows, kv_cols)
+        g = jnp.sum(g, axis=1) if kv_copies > 1 else g[:, 0]
+        return jnp.swapaxes(g, 0, 1).reshape(w_rows, KV_HEADS * HEAD_DIM)
+
+    grad_query = jnp.swapaxes(sent[:, :, :q_cols], 0, 1).reshape(w_rows, D)
+    grad_key = kv_join(sent[:, :, q_cols : q_cols + kv_cols])
+    grad_value = kv_join(sent[:, :, q_cols + kv_cols : q_cols + 2 * kv_cols])
+
+    totals = totals.reshape(-1)
     rms_stats = jnp.sqrt(totals[2 * D : 2 * D + 3] / (rows * grps * devs * D))
     gain_first = (lax.axis_index("grp") * devs + lax.axis_index(PLANE)) * w_rows
     gain_one_grad = lax.dynamic_slice(totals, (gain_first,), (w_rows,))

time: 657 us -> 690 us (1.050)
  Pallas kernels: 521 us -> 543 us
  waiting for transfers between devices: 8.47 us -> 19.5 us
  starting transfers between devices: 7.79 us -> 15.3 us
    pallas_call x3, Pallas kernels: 117 us -> 67.3 us  [twin_reduce(): pl.pallas_call(functools.partial(twin_kernel, compute, len(operands)), ou...]
    pallas_call x1, Pallas kernels: 12.1 us -> 48.1 us  [total(): pl.pallas_call(functools.partial(total_kernel, grps, chips), out_shape=ja...]
    pallas_call x3, Pallas kernels: 38.8 us -> 74.3 us  [plane_exchange(): pl.pallas_call(functools.partial(exchange_kernel, chips, cut, paste), out...]
    reduce_scatter x4, waiting for transfers between devices: 0.13 us -> 16.6 us  [scatter(): return lax.psum_scatter(values, axes, scatter_dimension=axis, tiled=True)]
    dot_general x2 -> x1, matrix products: 14.2 us -> 6.93 us  [over_cols(): lax.dot_general(left, right, (((1,), (1,)), ((), ())), preferred_element_...]
    ppermute x6 -> x12, starting transfers between devices: 7.04 us -> 14.1 us  [swap_chips(): return lax.ppermute(values, 'chip', [(c, c ^ step) for c in range(4)])]
  transfers between devices with their start and end apart: 14 -> 20, of which waited for: 3 -> 3; matrix products, arithmetic and copies ran while one was open for 10% -> 11% of each run, Pallas kernels for 77% -> 78%
where the time goes in v7:
time: 690 us; the launch traced here: 682 us
  Pallas kernels  543 us (79%)
  other arithmetic  44.3 us (6%)
  matrix products  25.9 us (4%)
  waiting for transfers between devices  19.5 us (3%)
  local copies, waits for them, and re-layouts  18.9 us (3%)
  starting transfers between devices  15.3 us (2%)
  between operations  15.1 us (2%)
    pallas_call x1, Pallas kernels, entry(): pl.pallas_call(functools.partial(entry_kernel, grps, chips), out_shape=(j...  102 us
    pallas_call x2, Pallas kernels, plane_gather(): pl.pallas_call(functools.partial(gather_kernel, chips, inner), out_shape=...  79.8 us
    pallas_call x3, Pallas kernels, plane_exchange(): pl.pallas_call(functools.partial(exchange_kernel, chips, cut, paste), out...  74.3 us
    pallas_call x3, Pallas kernels, twin_reduce(): pl.pallas_call(functools.partial(twin_kernel, compute, len(operands)), ou...  67.3 us
    pallas_call x1, Pallas kernels, attend_back(): pl.pallas_call(functools.partial(attend_back_kernel, heads), out_shape=ja...  48.3 us
    pallas_call x1, Pallas kernels, total(): pl.pallas_call(functools.partial(total_kernel, grps, chips), out_shape=ja...  48.1 us
    pallas_call x1, Pallas kernels, widen(): pl.pallas_call(widen_kernel, out_shape=(tall, jax.ShapeDtypeStruct((shard...  30.7 us
    pallas_call x1, Pallas kernels, attend(): pl.pallas_call(functools.partial(attend_kernel, heads), out_shape=jax.Sha...  25.6 us
  transfers between devices with their start and end apart: 20, of which 3 were waited for; matrix products, arithmetic and copies ran while one was open for 11% of the time, Pallas kernels for 78%

profile of v7, /device:TPU:0, one launch (start us, length us, event | category | flops | bytes accessed | tf_op | source)
XLA Modules:
  0.0 681.6 jit_solution(14378490655175846405)
XLA Ops:
  8.0 3.1 pad_maximum_fusion
  14.6 101.7 %shard_map.220 = (bf16[8,256,2048]{2,1,0:T(8,128)(2,1)}, bf16[8,256,2048]{2,1,0:T(8,128)(2,1)}, bf16[4,8,64,512]{3,2,1,0:T(8,128)(2,1)}) custom-call(bf16[256,2048]{1,0:T(8,128)(2,1)} %tok_ref.1, bf16[256,2048]{1,0:T(8,128)(2,1)} %fusion.cot_ref, bf16[8,64,512]{2,1,0:T(8,128)(2,1)} %maximum_bitcast_fusion.pack_ref), custom_call_target="tpu_custom_call" | custom-call | flops 1000 | bytes 1000 | tf_op jit(solution)/shard_map/pallas_call | solution.py:1018
  116.3 11.8 %shard_map.221 = (bf16[2048,2048]{1,0:T(8,128)(2,1)}, bf16[2048,384]{1,0:T(8,128)(2,1)}, f32[8,2048]{1,0:T(8,128)}) custom-call(bf16[2048,2048]{1,0:T(8,128)(2,1)} %bitcast.97, bf16[2048,512]{1,0:T(8,128)(2,1)} %bitcast.100), custom_call_target="tpu_custom_call" | custom-call | flops 1000 | bytes 1000 | tf_op jit(solution)/shard_map/pallas_call | solution.py:1058
  129.9 25.6 %shard_map.222.x_ref = bf16[2048,256]{1,0:T(8,128)(2,1)S(1)} custom-call(s32[16]{0:T(128)S(1)} %select_reduce_fusion.order_ref, bf16[2048,384]{1,0:T(8,128)(2,1)S(1)} %copy-done), custom_call_target="tpu_custom_call" | custom-call | flops 1000 | bytes 1000 | tf_op jit(solution)/shard_map/pallas_call | solution.py:521
  156.5 15.6 %shard_map.223 = bf16[256,2048]{1,0:T(8,128)(2,1)} custom-call(bf16[2048,256]{1,0:T(8,128)(2,1)} %copy-done.4), custom_call_target="tpu_custom_call" | custom-call | flops 1000 | bytes 1000 | tf_op jit(solution)/shard_map/pallas_call | solution.py:335
  173.1 39.8 %shard_map.224 = bf16[4,8,64,2048]{3,2,1,0:T(8,128)(2,1)} custom-call(bf16[4,64,2048]{2,1,0:T(8,128)(2,1)} %bitcast.103), custom_call_target="tpu_custom_call" | custom-call | flops 1000 | bytes 1000 | tf_op jit(solution)/shard_map/pallas_call | solution.py:160
  212.9 6.9 %multiply_reduce_fusion.6 = (f32[256]{0:T(256)S(1)}, f32[256,2048]{1,0:T(8,128)S(1)}, f32[]{:T(128)}) fusion(bf16[256,2048]{1,0:T(8,128)(2,1)S(1)} %copy-done.10, bf16[256,2048]{1,0:T(8,128)(2,1)} %shard_map.223, bf16[2048,2048]{1,0:T(8,128)(2,1)} %bitcast.98), kind=kOutput, calls=%fused_computation.40 | convolution fusion | flops 2151153408 | bytes 12583940 | tf_op jit(solution)/shard_map/dot_general | solution.py:363
  221.3 40.0 %shard_map.225 = bf16[8,256,2048]{2,1,0:T(8,128)(2,1)} custom-call(bf16[256,2048]{1,0:T(8,128)(2,1)} %multiply_convert_fusion.1.x_ref), custom_call_target="tpu_custom_call" | custom-call | flops 1000 | bytes 1000 | tf_op jit(solution)/shard_map/pallas_call | solution.py:160
  261.4 30.7 %shard_map.226 = (bf16[4,2048,256]{2,1,0:T(8,128)(2,1)}, bf16[4,256,2048]{2,1,0:T(8,128)(2,1)}, bf16[4,2048,256]{2,1,0:T(8,128)(2,1)}, bf16[4,2048,256]{2,1,0:T(8,128)(2,1)}, bf16[2048,2048]{1,0:T(8,128)(2,1)}) custom-call(bf16[2048,2048]{1,0:T(8,128)(2,1)} %bitcast.94, bf16[4,2,2048,256]{3,2,1,0:T(8,128)(2,1)} %bitcast.90), custom_call_target="tpu_custom_call" | custom-call | flops 1000 | bytes 1000 | tf_op jit(solution)/shard_map/pallas_call | solution.py:668
  292.0 15.4 %shard_map.227 = bf16[4,256,2048]{2,1,0:T(8,128)(2,1)} custom-call(bf16[4,256,2048]{2,1,0:T(8,128)(2,1)} %get-tuple-element.90.ht_ref, bf16[2048,2048]{1,0:T(8,128)(2,1)} %bitcast.92), custom_call_target="tpu_custom_call" | custom-call | flops 1000 | bytes 1000 | tf_op jit(solution)/shard_map/pallas_call | solution.py:702
  308.0 15.9 %shard_map.228 = (bf16[4,2048,256]{2,1,0:T(8,128)(2,1)}, bf16[4,2048,256]{2,1,0:T(8,128)(2,1)}) custom-call(bf16[4,2048,256]{2,1,0:T(8,128)(2,1)} %get-tuple-element.94.s_ref, bf16[4,2048,256]{2,1,0:T(8,128)(2,1)} %get-tuple-element.95.t_ref, bf16[2048,2048]{1,0:T(8,128)(2,1)} %bitcast.93, bf16[4,256,2048]{2,1,0:T(8,128)(2,1)} %bitcast.95), custom_call_target="tpu_custom_call" | custom-call | flops 1000 | bytes 1000 | tf_op jit(solution)/shard_map/pallas_call | solution.py:760
  324.0 31.7 %shard_map.229 = (f32[256,2048]{1,0:T(8,128)}, bf16[256,2048]{1,0:T(8,128)(2,1)}, bf16[256,2048]{1,0:T(8,128)(2,1)}, bf16[256,2048]{1,0:T(8,128)(2,1)}) custom-call(bf16[4,2048,256]{2,1,0:T(8,128)(2,1)} %get-tuple-element.101.refs_0_.dg_ref, bf16[4,2048,256]{2,1,0:T(8,128)(2,1)} %get-tuple-element.102.refs_1_.du_ref, bf16[4,2,2048,256]{3,2,1,0:T(8,128)(2,1)} %bitcast.91), custom_call_target="tpu_custom_call" | custom-call | flops 1000 | bytes 1000 | tf_op jit(solution)/shard_map/pallas_call | solution.py:891
  359.2 23.5 %shard_map.230 = bf16[4,2,2048,256]{3,2,1,0:T(8,128)(2,1)} custom-call(bf16[2048,2048]{1,0:T(8,128)(2,1)} %get-tuple-element.89.nt_ref, bf16[4,2048,256]{2,1,0:T(8,128)(2,1)} %get-tuple-element.101.refs_0_.dg_ref, bf16[4,2048,256]{2,1,0:T(8,128)(2,1)} %get-tuple-element.102.refs_1_.du_ref), custom_call_target="tpu_custom_call" | custom-call | flops 1000 | bytes 1000 | tf_op jit(solution)/shard_map/pallas_call | solution.py:782
  382.7 20.8 %shard_map.231 = (f32[256,2048]{1,0:T(8,128)}, bf16[256,2048]{1,0:T(8,128)(2,1)}, bf16[256,2048]{1,0:T(8,128)(2,1)}, bf16[256,2048]{1,0:T(8,128)(2,1)}) custom-call(bf16[4,2048,256]{2,1,0:T(8,128)(2,1)} %get-tuple-element.104.refs_0_, bf16[4,256,2048]{2,1,0:T(8,128)(2,1)} %bitcast.96), custom_call_target="tpu_custom_call" | custom-call | flops 1000 | bytes 1000 | tf_op jit(solution)/shard_map/pallas_call | solution.py:891
  405.2 3.8 multiply_reduce_fusion.4
  411.5 2.4 convolution_convert_fusion
  413.9 2.3 copy_bitcast_fusion
  421.9 6.9 %convolution_convert_fusion.2.x_ref = bf16[256,2048]{1,0:T(8,128)(2,1)} fusion(bf16[256,2048]{1,0:T(8,128)(2,1)S(1)} %copy-done.19, bf16[2048,2048]{1,0:T(8,128)(2,1)} %bitcast.99), kind=kOutput, calls=%fused_computation.11 | convolution fusion | flops 2148007936 | bytes 10485760 | tf_op jit(solution)/shard_map/dot_general | solution.py:371
  428.9 50.1 %shard_map.232.d_ref = bf16[2048,256]{1,0:T(8,128)(2,1)} custom-call(bf16[256,2048]{1,0:T(8,128)(2,1)} %convolution_convert_fusion.2.x_ref), custom_call_target="tpu_custom_call" | custom-call | flops 1000 | bytes 1000 | tf_op jit(solution)/shard_map/pallas_call | solution.py:335
  479.0 5.7 fusion.10
  489.6 6.1 multiply_reduce_fusion.1
  497.0 48.3 %shard_map.233.refs_0_ = bf16[2048,384]{1,0:T(8,128)(2,1)S(1)} custom-call(s32[16]{0:T(128)S(1)} %select_reduce_fusion.order_ref, bf16[2048,384]{1,0:T(8,128)(2,1)S(1)} %copy-done.1, bf16[2048,256]{1,0:T(8,128)(2,1)S(1)} %copy-done.3), custom_call_target="tpu_custom_call" | custom-call | flops 1000 | bytes 1000 | tf_op jit(solution)/shard_map/pallas_call | solution.py:543
  545.4 9.7 %multiply_reduce_fusion = (f32[2048]{0:T(1024)S(1)}, bf16[2048,384]{1,0:T(8,128)(2,1)}) fusion(bf16[2048,512]{1,0:T(8,128)(2,1)S(1)} %bitcast.102, bf16[2048,2048]{1,0:T(8,128)(2,1)} %get-tuple-element.125, bf16[2048,384]{1,0:T(8,128)(2,1)S(1)} %shard_map.233.refs_0_), kind=kOutput, calls=%fused_computation.6 | convolution fusion | flops 3225155584 | bytes 13115392 | tf_op jit(solution)/shard_map/dot_general | solution.py:367
  557.1 14.8 %shard_map.234 = (f32[256,2048]{1,0:T(8,128)}, bf16[256,2048]{1,0:T(8,128)(2,1)}, bf16[256,2048]{1,0:T(8,128)(2,1)}, bf16[256,2048]{1,0:T(8,128)(2,1)}) custom-call(bf16[2048,384]{1,0:T(8,128)(2,1)} %copy-done.2, bf16[2048,384]{1,0:T(8,128)(2,1)} %slice.36.refs_1_), custom_call_target="tpu_custom_call" | custom-call | flops 1000 | bytes 1000 | tf_op jit(solution)/shard_map/pallas_call | solution.py:891
  572.0 4.4 fusion.9
  580.9 48.1 %shard_map.235 = f32[8,640]{1,0:T(8,128)} custom-call(f32[8,640]{1,0:T(8,128)} %reshape.155.x_ref), custom_call_target="tpu_custom_call" | custom-call | flops 1000 | bytes 1000 | tf_op jit(solution)/shard_map/pallas_call | solution.py:616
  629.0 2.9 bitcast_convert_fusion
  632.6 3.6 fusion.1
  636.7 4.4 fusion.5
  641.1 2.3 bitcast_convert_fusion.1
  645.2 16.6 %reduce-scatter.9.cloned.1.call-done = bf16[512,384]{1,0:T(8,128)(2,1)} async-done(((bf16[2048,384]{1,0:T(8,128)(2,1)}), bf16[512,384]{1,0:T(8,128)(2,1)}) %reduce-scatter.9.cloned.1.call-update) | async-done | bytes 393232 | tf_op jit(solution)/shard_map/reduce_scatter | solution.py:379
  661.8 8.6 %shard_map.236 = bf16[8,64,384]{2,1,0:T(8,128)(2,1)} custom-call(bf16[8,64,384]{2,1,0:T(8,128)(2,1)} %bitcast.108), custom_call_target="tpu_custom_call" | custom-call | flops 1000 | bytes 1000 | tf_op jit(solution)/shard_map/pallas_call | solution.py:335
  (143 shorter events, 42.8 us)
Async XLA Ops:
  7.2 165.9 %all-gather.7.cloned.1.call-start = ((), (), s32[]{:S(2)}) async-start(), calls=%async_computation.8 | async-start | bytes 1310720 | tf_op jit(solution)/shard_map/all_gather | solution.py:375
  7.9 253.4 %all-gather.9.cloned.1.call-start = ((), (), s32[]{:S(2)}) async-start(), calls=%async_computation.9 | async-start | bytes 10485760 | tf_op jit(solution)/shard_map/all_gather | solution.py:375
  11.1 296.9 %all-gather.11.cloned.1.call-start = ((), (), s32[]{:S(2)}) async-start(), calls=%async_computation.10 | async-start | bytes 5242880 | tf_op jit(solution)/shard_map/all_gather | solution.py:375
  11.8 483.9 %reduce-scatter.5.cloned.1.call-start = ((), (), s32[]{:S(2)}) async-start(), calls=%async_computation.4 | async-start | bytes 5242880 | tf_op jit(solution)/shard_map/reduce_scatter | solution.py:379
  116.2 11.9 %copy-start.26 = (s32[64]{0:T(128)S(1)}, s32[64]{0:T(128)}, u32[]{:S(2)}) copy-start(s32[64]{0:T(128)} %param.15) | copy-start | bytes 772
  116.2 11.8 %copy-start.27 = (s32[64]{0:T(128)S(1)}, s32[64]{0:T(128)}, u32[]{:S(2)}) copy-start(s32[64]{0:T(128)} %param.14) | copy-start | bytes 772
  173.1 39.8 %copy-start.10 = (bf16[256,2048]{1,0:T(8,128)(2,1)S(1)}, bf16[256,2048]{1,0:T(8,128)(2,1)}, u32[]{:S(2)}) copy-start(bf16[256,2048]{1,0:T(8,128)(2,1)} %tok_ref.1) | copy-start | bytes 3145732
  219.8 189.2 %copy-start.5 = (f32[256,2048]{1,0:T(8,128)}, f32[256,2048]{1,0:T(8,128)S(1)}, u32[]{:S(2)}) copy-start(f32[256,2048]{1,0:T(8,128)S(1)} %get-tuple-element.167) | copy-start | bytes 6291460
  307.5 269.0 %reduce-scatter.7.cloned.1.call-start = ((), (), s32[]{:S(2)}) async-start(), calls=%async_computation.5 | async-start | bytes 10485760 | tf_op jit(solution)/shard_map/reduce_scatter | solution.py:379
  355.6 47.9 %collective-permute-start = (bf16[256,2048]{1,0:T(8,128)(2,1)}, bf16[256,2048]{1,0:T(8,128)(2,1)}, u32[]{:S(2)}, u32[]{:S(2)}) collective-permute-start(bf16[256,2048]{1,0:T(8,128)(2,1)} %get-tuple-element.107), channel_id=1, source_target_pairs={{0,6},{2,4},{4,2},{6,0},{1,7},{3,5},{5,3},{7,1},{8,14},{10,12},{12... | collective-permute-start | bytes 3145736 | tf_op jit(solution)/shard_map/ppermute | solution.py:274
  356.6 48.0 %collective-permute-start.1 = (bf16[256,2048]{1,0:T(8,128)(2,1)}, bf16[256,2048]{1,0:T(8,128)(2,1)}, u32[]{:S(2)}, u32[]{:S(2)}) collective-permute-start(bf16[256,2048]{1,0:T(8,128)(2,1)} %get-tuple-element.108), channel_id=1, source_target_pairs={{0,2},{2,0},{4,6},{6,4},{1,3},{3,1},{5,7},{7,5},{8,10},{10,8},{12,... | collective-permute-start | bytes 3145736 | tf_op jit(solution)/shard_map/ppermute | solution.py:274
  358.3 46.6 %collective-permute-start.2 = (bf16[256,2048]{1,0:T(8,128)(2,1)}, bf16[256,2048]{1,0:T(8,128)(2,1)}, u32[]{:S(2)}, u32[]{:S(2)}) collective-permute-start(bf16[256,2048]{1,0:T(8,128)(2,1)} %get-tuple-element.109), channel_id=1, source_target_pairs={{0,4},{2,6},{4,0},{6,2},{1,5},{3,7},{5,1},{7,3},{8,12},{10,14},{12... | collective-permute-start | bytes 3145736 | tf_op jit(solution)/shard_map/ppermute | solution.py:274
  405.0 238.5 %reduce-scatter.11.cloned.1.call-start = ((), (), s32[]{:S(2)}) async-start(), calls=%async_computation.7 | async-start | bytes 1310720 | tf_op jit(solution)/shard_map/reduce_scatter | solution.py:379
  405.2 5.1 copy-start.12
  413.9 8.0 %copy-start.19 = (bf16[256,2048]{1,0:T(8,128)(2,1)S(1)}, bf16[256,2048]{1,0:T(8,128)(2,1)}, u32[]{:S(2)}) copy-start(bf16[256,2048]{1,0:T(8,128)(2,1)} %copy-done.18) | copy-start | bytes 3145732
  418.4 60.6 %collective-permute-start.3 = (bf16[4,4,64,2048]{3,2,0,1:T(8,128)(2,1)}, bf16[4,4,64,2048]{3,2,0,1:T(8,128)(2,1)}, u32[]{:S(2)}, u32[]{:S(2)}) collective-permute-start(bf16[4,4,64,2048]{3,2,0,1:T(8,128)(2,1)} %copy_bitcast_fusion), channel_id=1, source_target_pairs={{0,1},{1,0},{2,3},{3,2},{4,5},{5,4},{6,7},{7,6},{8,9},{9,8},{10,11... | collective-permute-start | bytes 12582920 | tf_op jit(solution)/shard_map/ppermute | solution.py:283
  418.4 66.3 %collective-permute-start.4 = (bf16[256,2048]{1,0:T(8,128)(2,1)}, bf16[256,2048]{1,0:T(8,128)(2,1)S(1)}, u32[]{:S(2)}, u32[]{:S(2)}) collective-permute-start(bf16[256,2048]{1,0:T(8,128)(2,1)} %get-tuple-element.119), channel_id=1, source_target_pairs={{0,6},{2,4},{4,2},{6,0},{1,7},{3,5},{5,3},{7,1},{8,14},{10,12},{12... | collective-permute-start | bytes 3145736 | tf_op jit(solution)/shard_map/ppermute | solution.py:274
  419.6 65.1 %collective-permute-start.5 = (bf16[256,2048]{1,0:T(8,128)(2,1)}, bf16[256,2048]{1,0:T(8,128)(2,1)}, u32[]{:S(2)}, u32[]{:S(2)}) collective-permute-start(bf16[256,2048]{1,0:T(8,128)(2,1)} %get-tuple-element.120), channel_id=1, source_target_pairs={{0,2},{2,0},{4,6},{6,4},{1,3},{3,1},{5,7},{7,5},{8,10},{10,8},{12,... | collective-permute-start | bytes 3145736 | tf_op jit(solution)/shard_map/ppermute | solution.py:274
  421.1 63.7 %collective-permute-start.6 = (bf16[256,2048]{1,0:T(8,128)(2,1)}, bf16[256,2048]{1,0:T(8,128)(2,1)}, u32[]{:S(2)}, u32[]{:S(2)}) collective-permute-start(bf16[256,2048]{1,0:T(8,128)(2,1)} %get-tuple-element.121), channel_id=1, source_target_pairs={{0,4},{2,6},{4,0},{6,2},{1,5},{3,7},{5,1},{7,3},{8,12},{10,14},{12... | collective-permute-start | bytes 3145736 | tf_op jit(solution)/shard_map/ppermute | solution.py:274
  479.0 9.3 %copy-start.15 = (bf16[4,8,64,512]{3,2,1,0:T(8,128)(2,1)S(1)}, bf16[4,8,64,512]{3,2,1,0:T(8,128)(2,1)}, u32[]{:S(2)}) copy-start(bf16[4,8,64,512]{3,2,1,0:T(8,128)(2,1)} %get-tuple-element.86) | copy-start | bytes 6291460
  484.7 4.9 copy-start.21
  484.7 60.6 %collective-permute-start.7 = (bf16[4,64,2048]{2,1,0:T(8,128)(2,1)}, bf16[4,64,2048]{2,1,0:T(8,128)(2,1)}, u32[]{:S(2)}, u32[]{:S(2)}) collective-permute-start(bf16[4,64,2048]{2,1,0:T(8,128)(2,1)} %get-tuple-element.126), channel_id=1, source_target_pairs={{0,6},{2,4},{4,2},{6,0},{1,7},{3,5},{5,3},{7,1},{8,14},{10,12},{12... | collective-permute-start | bytes 3145736 | tf_op jit(solution)/shard_map/ppermute | solution.py:274
  486.3 59.1 %collective-permute-start.8 = (bf16[4,64,2048]{2,1,0:T(8,128)(2,1)}, bf16[4,64,2048]{2,1,0:T(8,128)(2,1)}, u32[]{:S(2)}, u32[]{:S(2)}) collective-permute-start(bf16[4,64,2048]{2,1,0:T(8,128)(2,1)} %get-tuple-element.127), channel_id=1, source_target_pairs={{0,2},{2,0},{4,6},{6,4},{1,3},{3,1},{5,7},{7,5},{8,10},{10,8},{12,... | collective-permute-start | bytes 3145736 | tf_op jit(solution)/shard_map/ppermute | solution.py:274
  487.5 57.9 %collective-permute-start.9 = (bf16[4,64,2048]{2,1,0:T(8,128)(2,1)}, bf16[4,64,2048]{2,1,0:T(8,128)(2,1)}, u32[]{:S(2)}, u32[]{:S(2)}) collective-permute-start(bf16[4,64,2048]{2,1,0:T(8,128)(2,1)} %get-tuple-element.128), channel_id=1, source_target_pairs={{0,4},{2,6},{4,0},{6,2},{1,5},{3,7},{5,1},{7,3},{8,12},{10,14},{12... | collective-permute-start | bytes 3145736 | tf_op jit(solution)/shard_map/ppermute | solution.py:274
  489.6 6.1 copy-start.1
  497.0 48.4 %copy-start.16 = (bf16[4,8,64,512]{3,2,1,0:T(8,128)(2,1)S(1)}, bf16[4,8,64,512]{3,2,1,0:T(8,128)(2,1)}, u32[]{:S(2)}) copy-start(bf16[4,8,64,512]{3,2,1,0:T(8,128)(2,1)} %get-tuple-element.86) | copy-start | bytes 6291460
  545.3 9.8 %copy-start.2 = (bf16[2048,384]{1,0:T(8,128)(2,1)}, bf16[2048,384]{1,0:T(8,128)(2,1)S(1)}, u32[]{:S(2)}) copy-start(bf16[2048,384]{1,0:T(8,128)(2,1)S(1)} %shard_map.233.refs_0_) | copy-start | bytes 4718596
  576.5 85.3 %reduce-scatter.9.cloned.1.call-start = ((), (), s32[]{:S(2)}) async-start(), calls=%async_computation.6 | async-start | bytes 1966080 | tf_op jit(solution)/shard_map/reduce_scatter | solution.py:379
  577.4 54.6 %collective-permute-start.10 = (bf16[256,2048]{1,0:T(8,128)(2,1)}, bf16[256,2048]{1,0:T(8,128)(2,1)}, u32[]{:S(2)}, u32[]{:S(2)}) collective-permute-start(bf16[256,2048]{1,0:T(8,128)(2,1)} %get-tuple-element.139), channel_id=1, source_target_pairs={{0,6},{2,4},{4,2},{6,0},{1,7},{3,5},{5,3},{7,1},{8,14},{10,12},{12... | collective-permute-start | bytes 3145736 | tf_op jit(solution)/shard_map/ppermute | solution.py:274
  579.0 53.0 %collective-permute-start.11 = (bf16[256,2048]{1,0:T(8,128)(2,1)}, bf16[256,2048]{1,0:T(8,128)(2,1)}, u32[]{:S(2)}, u32[]{:S(2)}) collective-permute-start(bf16[256,2048]{1,0:T(8,128)(2,1)} %get-tuple-element.140), channel_id=1, source_target_pairs={{0,2},{2,0},{4,6},{6,4},{1,3},{3,1},{5,7},{7,5},{8,10},{10,8},{12,... | collective-permute-start | bytes 3145736 | tf_op jit(solution)/shard_map/ppermute | solution.py:274
  580.1 51.8 %collective-permute-start.12 = (bf16[256,2048]{1,0:T(8,128)(2,1)}, bf16[256,2048]{1,0:T(8,128)(2,1)}, u32[]{:S(2)}, u32[]{:S(2)}) collective-permute-start(bf16[256,2048]{1,0:T(8,128)(2,1)} %get-tuple-element.141), channel_id=1, source_target_pairs={{0,4},{2,6},{4,0},{6,2},{1,5},{3,7},{5,1},{7,3},{8,12},{10,14},{12... | collective-permute-start | bytes 3145736 | tf_op jit(solution)/shard_map/ppermute | solution.py:274
  629.0 7.7 %copy-start.14 = (f32[256,2048]{1,0:T(8,128)S(1)}, f32[256,2048]{1,0:T(8,128)}, u32[]{:S(2)}) copy-start(f32[256,2048]{1,0:T(8,128)} %get-tuple-element.164) | copy-start | bytes 6291460
  (18 other events, 40.4 us)
Sparse Core Ops, SparseCore 0:
  9.6 35.5 all-gather.6
  47.3 163.7 all-gather.8
  212.7 80.5 all-gather.10
  307.6 74.0 reduce-scatter.4
  405.1 141.4 reduce-scatter.6
  576.6 25.9 reduce-scatter.10
  629.1 32.6 reduce-scatter.8

commit v8 on v7

--- a/solution.py
+++ b/solution.py
@@ -290,13 +290,6 @@
 
     def parts(self):
         return tuple(self.part(step).astype(BF16) for step in (1, 2, 3))
-
-    @staticmethod
-    def send(parts):
-        return tuple(
-            swap_chips(part, step)
-            for step, part in zip((3, 1, 2), (parts[2], parts[0], parts[1]))
-        )
 
     def finish(self, came):
         total = self.part(0)
@@ -1176,7 +1169,6 @@
         others, shares, part_wide = lax.optimization_barrier((others, shares, part_wide))
         grad_wide = scatter(part_wide, "grp")
         d_normed_two = join(d_normed_two, others)
-        shares = swap_others(shares)
     else:
         part_wide = widen_part(normed_t, d_gate, d_up)
         part_wide, d_gate, d_up = lax.optimization_barrier((part_wide, d_gate, d_up))
@@ -1201,20 +1193,36 @@
         sent_out, d_attended, shares = lax.optimization_barrier(
             (drift_out.parts(), d_attended, shares)
         )
-        branch_mlp = join(branch_mlp, shares)
-        sent_out = Drift.send(sent_out)
+        sent_out = (sent_out[2], sent_out[0], sent_out[1])
+        shares = [
+            jnp.concatenate([share, part.reshape(rows, D)]) for share, part in zip(shares, sent_out)
+        ]
+        shares = swap_others(shares)
     d_attended, grad_down = lax.optimization_barrier((d_attended, grad_down))
     d_qkv = attend_back(qkv, d_attended, order, q_heads)
     if chips == 4:
-        sent_out, d_qkv = lax.optimization_barrier((sent_out, d_qkv))
+        d_normed_one, *others = twin_reduce(project_back_rows, (d_qkv, w_qkv), rows, 5)
+        shares, others, d_qkv = lax.optimization_barrier((shares, others, d_qkv))
+        others = swap_others(others)
+        branch_mlp = join(branch_mlp, [share[:rows] for share in shares])
+        sent_out = [share[rows:].reshape(grps, w_rows, D) for share in shares]
         grad_out = drift_out.finish(sent_out).astype(BF16)
     else:
         grad_out = plane_reduce(
             grad_out.reshape(grps, devs, w_rows, D), chips, 6, dtype=BF16, inner=True
         )
+    sent = over_rows(normed_one, d_qkv).astype(BF16)
+    sent, grad_wide = lax.optimization_barrier((sent, grad_wide))
+    sent = scatter(sent, "grp")
+    grad_out = scatter(grad_out, "grp").reshape(w_rows, D).astype(F32)
+    if chips == 4:
+        d_normed_one = join(d_normed_one, others)
+    else:
+        d_normed_one = over_cols(d_qkv, w_qkv).astype(BF16).reshape(devs, rows, D)
+        d_normed_one = plane_reduce(d_normed_one, chips, 5)
+    d_input_norm, _ = norm_back(layer_in, norm_parts(layer_in), gain_one, d_normed_one)
+    tokens_grad = (d_residual + d_input_norm).astype(BF16)
     layer_out = residual + RESID_MULT * branch_mlp
-    sent = over_rows(normed_one, d_qkv).astype(BF16)
-    d_gain_one = jnp.sum(w_qkv.astype(F32) * sent.astype(F32), axis=1) / gain_one
     scaled_attn = RESID_MULT * branch_attn
     scaled_mlp = RESID_MULT * branch_mlp
     squares = jnp.stack(
@@ -1224,27 +1232,9 @@
             jnp.sum(scaled_mlp * scaled_mlp),
         ]
     )
-    totals = jnp.concatenate([d_gain_one, d_gain_two, squares, jnp.zeros((1021,), F32)])
-    sent, d_qkv, totals = lax.optimization_barrier((sent, d_qkv, totals))
-    totals = totals.reshape(8, 5 * D // 16)
-    if chips == 4:
-        d_normed_one, *others = twin_reduce(project_back_rows, (d_qkv, w_qkv), rows, 5)
-        sent, grad_out, _ = lax.optimization_barrier((sent, grad_out, others[0]))
-    sent, grad_out, grad_wide = lax.optimization_barrier((sent, grad_out, grad_wide))
-    sent = scatter(sent, "grp")
-    grad_out = scatter(grad_out, "grp").reshape(w_rows, D).astype(F32)
-    if chips == 4:
-        others, totals = lax.optimization_barrier((others, totals))
-        others = swap_others(others)
-        totals = total(totals, grps, chips, 8)
-        others, totals = lax.optimization_barrier((others, totals))
-        d_normed_one = join(d_normed_one, others)
-    else:
-        totals = total(totals, grps, chips, 8)
-        d_normed_one = over_cols(d_qkv, w_qkv).astype(BF16).reshape(devs, rows, D)
-        d_normed_one = plane_reduce(d_normed_one, chips, 5)
-    d_input_norm, _ = norm_back(layer_in, norm_parts(layer_in), gain_one, d_normed_one)
-    tokens_grad = (d_residual + d_input_norm).astype(BF16)
+    totals = jnp.concatenate([d_gain_two, squares, jnp.zeros((1021,), F32)])
+    totals, tokens_grad = lax.optimization_barrier((totals, tokens_grad))
+    totals = total(totals.reshape(8, 3 * D // 16), grps, chips, 8)
     sent = sent.reshape(devs, w_rows, q_cols + 2 * kv_cols)
     sent = plane_exchange(sent, sent.shape, by_slot, by_slot, chips, 9).astype(F32)
 
@@ -1257,11 +1247,14 @@
     grad_key = kv_join(sent[:, :, q_cols : q_cols + kv_cols])
     grad_value = kv_join(sent[:, :, q_cols + kv_cols : q_cols + 2 * kv_cols])
 
+    gain_one_grad = sum(
+        jnp.sum(weight.astype(F32) * grad, axis=1)
+        for weight, grad in ((w_query, grad_query), (w_key, grad_key), (w_value, grad_value))
+    ) / attn_gain.astype(F32)
     totals = totals.reshape(-1)
-    rms_stats = jnp.sqrt(totals[2 * D : 2 * D + 3] / (rows * grps * devs * D))
+    rms_stats = jnp.sqrt(totals[D : D + 3] / (rows * grps * devs * D))
     gain_first = (lax.axis_index("grp") * devs + lax.axis_index(PLANE)) * w_rows
-    gain_one_grad = lax.dynamic_slice(totals, (gain_first,), (w_rows,))
-    gain_two_grad = lax.dynamic_slice(totals, (gain_first + D,), (w_rows,))
+    gain_two_grad = lax.dynamic_slice(totals, (gain_first,), (w_rows,))
     return (
         layer_out.astype(BF16),
         tokens_grad,

time: 690 us -> 654 us (0.948)
  Pallas kernels: 543 us -> 469 us
  waiting for transfers between devices: 19.5 us -> 52.3 us
    ppermute x12 -> x9, waiting for transfers between devices: 1.39 us -> 50.8 us  [swap_chips(): return lax.ppermute(values, 'chip', [(c, c ^ step) for c in range(4)])]
    pallas_call x1, Pallas kernels: 48.1 us -> 10.3 us  [total(): pl.pallas_call(functools.partial(total_kernel, grps, chips), out_shape=ja...]
    pallas_call x3, Pallas kernels: 74.3 us -> 38.9 us  [plane_exchange(): pl.pallas_call(functools.partial(exchange_kernel, chips, cut, paste), out...]
    reduce_scatter x4, waiting for transfers between devices: 16.6 us -> 0.01 us  [scatter(): return lax.psum_scatter(values, axes, scatter_dimension=axis, tiled=True)]
    ppermute x12 -> x9, starting transfers between devices: 14.1 us -> 10.6 us  [swap_chips(): return lax.ppermute(values, 'chip', [(c, c ^ step) for c in range(4)])]
  transfers between devices with their start and end apart: 20 -> 17, of which waited for: 3 -> 6; matrix products, arithmetic and copies ran while one was open for 11% -> 13% of each run, Pallas kernels for 78% -> 71%
where the time goes in v8:
time: 654 us; the launch traced here: 646 us
  Pallas kernels  469 us (72%)
  waiting for transfers between devices  52.3 us (8%)
  other arithmetic  47.3 us (7%)
  matrix products  25.3 us (4%)
  local copies, waits for them, and re-layouts  24.5 us (4%)
  between operations  15.2 us (2%)
  starting transfers between devices  11.8 us (2%)
    pallas_call x1, Pallas kernels, entry(): pl.pallas_call(functools.partial(entry_kernel, grps, chips), out_shape=(j...  102 us
    pallas_call x2, Pallas kernels, plane_gather(): pl.pallas_call(functools.partial(gather_kernel, chips, inner), out_shape=...  79.8 us
    pallas_call x3, Pallas kernels, twin_reduce(): pl.pallas_call(functools.partial(twin_kernel, compute, len(operands)), ou...  67.3 us
    ppermute x9, waiting for transfers between devices, swap_chips(): return lax.ppermute(values, 'chip', [(c, c ^ step) for c in range(4)])  50.8 us
    pallas_call x1, Pallas kernels, attend_back(): pl.pallas_call(functools.partial(attend_back_kernel, heads), out_shape=ja...  48.4 us
    pallas_call x3, Pallas kernels, plane_exchange(): pl.pallas_call(functools.partial(exchange_kernel, chips, cut, paste), out...  38.9 us
    pallas_call x1, Pallas kernels, widen(): pl.pallas_call(widen_kernel, out_shape=(tall, jax.ShapeDtypeStruct((shard...  30.7 us
    pallas_call x1, Pallas kernels, attend(): pl.pallas_call(functools.partial(attend_kernel, heads), out_shape=jax.Sha...  25.6 us
  transfers between devices with their start and end apart: 17, of which 6 were waited for; matrix products, arithmetic and copies ran while one was open for 13% of the time, Pallas kernels for 71%

profile of v8, /device:TPU:0, one launch (start us, length us, event | category | flops | bytes accessed | tf_op | source)
XLA Modules:
  0.0 645.7 jit_solution(3873667147397441087)
XLA Ops:
  8.0 3.1 pad_maximum_fusion
  14.6 101.7 %shard_map.220 = (bf16[8,256,2048]{2,1,0:T(8,128)(2,1)}, bf16[8,256,2048]{2,1,0:T(8,128)(2,1)}, bf16[4,8,64,512]{3,2,1,0:T(8,128)(2,1)}) custom-call(bf16[256,2048]{1,0:T(8,128)(2,1)} %tok_ref.1, bf16[256,2048]{1,0:T(8,128)(2,1)} %fusion.cot_ref, bf16[8,64,512]{2,1,0:T(8,128)(2,1)} %maximum_bitcast_fusion.pack_ref), custom_call_target="tpu_custom_call" | custom-call | flops 1000 | bytes 1000 | tf_op jit(solution)/shard_map/pallas_call | solution.py:1011
  116.3 11.8 %shard_map.221 = (bf16[2048,2048]{1,0:T(8,128)(2,1)}, bf16[2048,384]{1,0:T(8,128)(2,1)}, f32[8,2048]{1,0:T(8,128)}) custom-call(bf16[2048,2048]{1,0:T(8,128)(2,1)} %bitcast.106, bf16[2048,512]{1,0:T(8,128)(2,1)} %bitcast.109), custom_call_target="tpu_custom_call" | custom-call | flops 1000 | bytes 1000 | tf_op jit(solution)/shard_map/pallas_call | solution.py:1051
  129.9 25.6 %shard_map.222.x_ref = bf16[2048,256]{1,0:T(8,128)(2,1)S(1)} custom-call(s32[16]{0:T(128)S(1)} %select_reduce_fusion.order_ref, bf16[2048,384]{1,0:T(8,128)(2,1)S(1)} %copy-done), custom_call_target="tpu_custom_call" | custom-call | flops 1000 | bytes 1000 | tf_op jit(solution)/shard_map/pallas_call | solution.py:514
  156.5 15.6 %shard_map.223 = bf16[256,2048]{1,0:T(8,128)(2,1)} custom-call(bf16[2048,256]{1,0:T(8,128)(2,1)} %copy-done.5), custom_call_target="tpu_custom_call" | custom-call | flops 1000 | bytes 1000 | tf_op jit(solution)/shard_map/pallas_call | solution.py:328
  173.7 39.8 %shard_map.224 = bf16[4,8,64,2048]{3,2,1,0:T(8,128)(2,1)} custom-call(bf16[4,64,2048]{2,1,0:T(8,128)(2,1)} %bitcast.119), custom_call_target="tpu_custom_call" | custom-call | flops 1000 | bytes 1000 | tf_op jit(solution)/shard_map/pallas_call | solution.py:160
  213.5 6.9 %multiply_reduce_fusion.5 = (f32[256]{0:T(256)S(1)}, f32[256,2048]{1,0:T(8,128)S(1)}, f32[]{:T(128)}) fusion(bf16[256,2048]{1,0:T(8,128)(2,1)S(1)} %copy-done.11, bf16[256,2048]{1,0:T(8,128)(2,1)} %shard_map.223, bf16[2048,2048]{1,0:T(8,128)(2,1)} %bitcast.107), kind=kOutput, calls=%fused_computation.42 | convolution fusion | flops 2151153408 | bytes 12583940 | tf_op jit(solution)/shard_map/dot_general | solution.py:356
  222.2 40.0 %shard_map.225 = bf16[8,256,2048]{2,1,0:T(8,128)(2,1)} custom-call(bf16[256,2048]{1,0:T(8,128)(2,1)} %multiply_convert_fusion.1.x_ref), custom_call_target="tpu_custom_call" | custom-call | flops 1000 | bytes 1000 | tf_op jit(solution)/shard_map/pallas_call | solution.py:160
  262.2 30.7 %shard_map.226 = (bf16[4,2048,256]{2,1,0:T(8,128)(2,1)}, bf16[4,256,2048]{2,1,0:T(8,128)(2,1)}, bf16[4,2048,256]{2,1,0:T(8,128)(2,1)}, bf16[4,2048,256]{2,1,0:T(8,128)(2,1)}, bf16[2048,2048]{1,0:T(8,128)(2,1)}) custom-call(bf16[2048,2048]{1,0:T(8,128)(2,1)} %bitcast.103, bf16[4,2,2048,256]{3,2,1,0:T(8,128)(2,1)} %bitcast.99), custom_call_target="tpu_custom_call" | custom-call | flops 1000 | bytes 1000 | tf_op jit(solution)/shard_map/pallas_call | solution.py:661
  292.9 15.4 %shard_map.227 = bf16[4,256,2048]{2,1,0:T(8,128)(2,1)} custom-call(bf16[4,256,2048]{2,1,0:T(8,128)(2,1)} %get-tuple-element.81.ht_ref, bf16[2048,2048]{1,0:T(8,128)(2,1)} %bitcast.101), custom_call_target="tpu_custom_call" | custom-call | flops 1000 | bytes 1000 | tf_op jit(solution)/shard_map/pallas_call | solution.py:695
  308.9 16.0 %shard_map.228 = (bf16[4,2048,256]{2,1,0:T(8,128)(2,1)}, bf16[4,2048,256]{2,1,0:T(8,128)(2,1)}) custom-call(bf16[4,2048,256]{2,1,0:T(8,128)(2,1)} %get-tuple-element.85.s_ref, bf16[4,2048,256]{2,1,0:T(8,128)(2,1)} %get-tuple-element.86.t_ref, bf16[2048,2048]{1,0:T(8,128)(2,1)} %bitcast.102, bf16[4,256,2048]{2,1,0:T(8,128)(2,1)} %bitcast.104), custom_call_target="tpu_custom_call" | custom-call | flops 1000 | bytes 1000 | tf_op jit(solution)/shard_map/pallas_call | solution.py:753
  324.9 31.7 %shard_map.229 = (f32[256,2048]{1,0:T(8,128)}, bf16[256,2048]{1,0:T(8,128)(2,1)}, bf16[256,2048]{1,0:T(8,128)(2,1)}, bf16[256,2048]{1,0:T(8,128)(2,1)}) custom-call(bf16[4,2048,256]{2,1,0:T(8,128)(2,1)} %get-tuple-element.92.refs_0_.dg_ref, bf16[4,2048,256]{2,1,0:T(8,128)(2,1)} %get-tuple-element.93.refs_1_.du_ref, bf16[4,2,2048,256]{3,2,1,0:T(8,128)(2,1)} %bitcast.100), custom_call_target="tpu_custom_call" | custom-call | flops 1000 | bytes 1000 | tf_op jit(solution)/shard_map/pallas_call | solution.py:884
  360.1 23.6 %shard_map.230 = bf16[4,2,2048,256]{3,2,1,0:T(8,128)(2,1)} custom-call(bf16[2048,2048]{1,0:T(8,128)(2,1)} %get-tuple-element.80.nt_ref, bf16[4,2048,256]{2,1,0:T(8,128)(2,1)} %get-tuple-element.92.refs_0_.dg_ref, bf16[4,2048,256]{2,1,0:T(8,128)(2,1)} %get-tuple-element.93.refs_1_.du_ref), custom_call_target="tpu_custom_call" | custom-call | flops 1000 | bytes 1000 | tf_op jit(solution)/shard_map/pallas_call | solution.py:775
  383.7 20.8 %shard_map.231 = (f32[256,2048]{1,0:T(8,128)}, bf16[256,2048]{1,0:T(8,128)(2,1)}, bf16[256,2048]{1,0:T(8,128)(2,1)}, bf16[256,2048]{1,0:T(8,128)(2,1)}) custom-call(bf16[4,2048,256]{2,1,0:T(8,128)(2,1)} %get-tuple-element.95.refs_0_, bf16[4,256,2048]{2,1,0:T(8,128)(2,1)} %bitcast.105), custom_call_target="tpu_custom_call" | custom-call | flops 1000 | bytes 1000 | tf_op jit(solution)/shard_map/pallas_call | solution.py:884
  406.2 4.0 multiply_reduce_fusion.3
  419.7 6.8 %convolution_convert_fusion.2.x_ref = bf16[256,2048]{1,0:T(8,128)(2,1)} fusion(bf16[256,2048]{1,0:T(8,128)(2,1)S(1)} %multiply_convert_fusion, bf16[2048,2048]{1,0:T(8,128)(2,1)} %bitcast.108), kind=kOutput, calls=%fused_computation.10 | convolution fusion | flops 2148007936 | bytes 10485760 | tf_op jit(solution)/shard_map/dot_general | solution.py:364
  426.6 15.1 %shard_map.232.d_ref = bf16[2048,256]{1,0:T(8,128)(2,1)} custom-call(bf16[256,2048]{1,0:T(8,128)(2,1)} %convolution_convert_fusion.2.x_ref), custom_call_target="tpu_custom_call" | custom-call | flops 1000 | bytes 1000 | tf_op jit(solution)/shard_map/pallas_call | solution.py:328
  441.7 4.3 fusion.7
  454.2 2.8 slice.60.refs_1_
  457.0 48.4 %shard_map.233.refs_0_ = bf16[2048,384]{1,0:T(8,128)(2,1)S(1)} custom-call(s32[16]{0:T(128)S(1)} %select_reduce_fusion.order_ref, bf16[2048,384]{1,0:T(8,128)(2,1)S(1)} %copy-done.1, bf16[2048,256]{1,0:T(8,128)(2,1)S(1)} %copy-done.4), custom_call_target="tpu_custom_call" | custom-call | flops 1000 | bytes 1000 | tf_op jit(solution)/shard_map/pallas_call | solution.py:536
  506.6 14.8 %shard_map.234 = (f32[256,2048]{1,0:T(8,128)}, bf16[256,2048]{1,0:T(8,128)(2,1)}, bf16[256,2048]{1,0:T(8,128)(2,1)}, bf16[256,2048]{1,0:T(8,128)(2,1)}) custom-call(bf16[2048,384]{1,0:T(8,128)(2,1)} %copy-done.2, bf16[2048,384]{1,0:T(8,128)(2,1)} %slice.60.refs_1_), custom_call_target="tpu_custom_call" | custom-call | flops 1000 | bytes 1000 | tf_op jit(solution)/shard_map/pallas_call | solution.py:884
  521.4 22.2 %collective-permute-done.4 = bf16[512,2048]{1,0:T(8,128)(2,1)} collective-permute-done((bf16[512,2048]{1,0:T(8,128)(2,1)}, bf16[512,2048]{1,0:T(8,128)(2,1)}, u32[]{:S(2)}, u32[]{:S(2)}) %collective-permute-start.4) | collective-permute-done | bytes 2097184 | tf_op jit(solution)/shard_map/ppermute | solution.py:274
  547.6 3.5 fusion.6
  554.9 6.3 multiply_reduce_fusion
  563.2 9.1 %convolution_convert_fusion.1 = bf16[2048,384]{1,0:T(8,128)(2,1)} fusion(bf16[2048,2048]{1,0:T(8,128)(2,1)} %get-tuple-element.133, bf16[2048,384]{1,0:T(8,128)(2,1)S(1)} %copy-done.3), kind=kOutput, calls=%fused_computation.6 | convolution fusion | flops 3222011904 | bytes 11534336 | tf_op jit(solution)/shard_map/dot_general | solution.py:360
  572.4 6.3 collective-permute-done.7
  578.7 20.6 %collective-permute-done.8 = bf16[256,2048]{1,0:T(8,128)(2,1)} collective-permute-done((bf16[256,2048]{1,0:T(8,128)(2,1)}, bf16[256,2048]{1,0:T(8,128)(2,1)}, u32[]{:S(2)}, u32[]{:S(2)}) %collective-permute-start.8) | collective-permute-done | bytes 1048608 | tf_op jit(solution)/shard_map/ppermute | solution.py:274
  599.6 3.3 fusion.1
  603.4 4.5 fusion.5
  608.5 2.8 bitcast_convert_fusion
  611.3 10.3 %shard_map.236 = f32[8,384]{1,0:T(8,128)} custom-call(f32[8,384]{1,0:T(8,128)} %reshape.180.x_ref), custom_call_target="tpu_custom_call" | custom-call | flops 1000 | bytes 1000 | tf_op jit(solution)/shard_map/pallas_call | solution.py:609
  627.6 8.1 %shard_map.235 = bf16[8,64,384]{2,1,0:T(8,128)(2,1)} custom-call(bf16[8,64,384]{2,1,0:T(8,128)(2,1)} %bitcast.124), custom_call_target="tpu_custom_call" | custom-call | flops 1000 | bytes 1000 | tf_op jit(solution)/shard_map/pallas_call | solution.py:328
  (161 shorter events, 54.6 us)
Async XLA Ops:
  7.2 166.5 %all-gather.7.cloned.1.call-start = ((), (), s32[]{:S(2)}) async-start(), calls=%async_computation.8 | async-start | bytes 1310720 | tf_op jit(solution)/shard_map/all_gather | solution.py:368
  7.9 254.3 %all-gather.9.cloned.1.call-start = ((), (), s32[]{:S(2)}) async-start(), calls=%async_computation.9 | async-start | bytes 10485760 | tf_op jit(solution)/shard_map/all_gather | solution.py:368
  11.1 297.8 %all-gather.11.cloned.1.call-start = ((), (), s32[]{:S(2)}) async-start(), calls=%async_computation.10 | async-start | bytes 5242880 | tf_op jit(solution)/shard_map/all_gather | solution.py:368
  11.8 445.2 %reduce-scatter.5.cloned.1.call-start = ((), (), s32[]{:S(2)}) async-start(), calls=%async_computation.4 | async-start | bytes 5242880 | tf_op jit(solution)/shard_map/reduce_scatter | solution.py:372
  116.2 11.9 %copy-start.35 = (s32[64]{0:T(128)S(1)}, s32[64]{0:T(128)}, u32[]{:S(2)}) copy-start(s32[64]{0:T(128)} %param.15) | copy-start | bytes 772
  116.2 11.9 %copy-start.36 = (s32[64]{0:T(128)S(1)}, s32[64]{0:T(128)}, u32[]{:S(2)}) copy-start(s32[64]{0:T(128)} %param.14) | copy-start | bytes 772
  173.7 39.8 %copy-start.11 = (bf16[256,2048]{1,0:T(8,128)(2,1)S(1)}, bf16[256,2048]{1,0:T(8,128)(2,1)}, u32[]{:S(2)}) copy-start(bf16[256,2048]{1,0:T(8,128)(2,1)} %tok_ref.1) | copy-start | bytes 3145732
  220.4 189.8 %copy-start.6 = (f32[256,2048]{1,0:T(8,128)}, f32[256,2048]{1,0:T(8,128)S(1)}, u32[]{:S(2)}) copy-start(f32[256,2048]{1,0:T(8,128)S(1)} %get-tuple-element.149) | copy-start | bytes 6291460
  308.4 264.0 %reduce-scatter.7.cloned.1.call-start = ((), (), s32[]{:S(2)}) async-start(), calls=%async_computation.5 | async-start | bytes 10485760 | tf_op jit(solution)/shard_map/reduce_scatter | solution.py:372
  356.6 48.0 %collective-permute-start = (bf16[256,2048]{1,0:T(8,128)(2,1)}, bf16[256,2048]{1,0:T(8,128)(2,1)S(1)}, u32[]{:S(2)}, u32[]{:S(2)}) collective-permute-start(bf16[256,2048]{1,0:T(8,128)(2,1)} %get-tuple-element.98), channel_id=1, source_target_pairs={{0,6},{2,4},{4,2},{6,0},{1,7},{3,5},{5,3},{7,1},{8,14},{10,12},{12... | collective-permute-start | bytes 3145736 | tf_op jit(solution)/shard_map/ppermute | solution.py:274
  357.6 48.1 %collective-permute-start.1 = (bf16[256,2048]{1,0:T(8,128)(2,1)}, bf16[256,2048]{1,0:T(8,128)(2,1)}, u32[]{:S(2)}, u32[]{:S(2)}) collective-permute-start(bf16[256,2048]{1,0:T(8,128)(2,1)} %get-tuple-element.99), channel_id=1, source_target_pairs={{0,2},{2,0},{4,6},{6,4},{1,3},{3,1},{5,7},{7,5},{8,10},{10,8},{12,... | collective-permute-start | bytes 3145736 | tf_op jit(solution)/shard_map/ppermute | solution.py:274
  359.3 46.6 %collective-permute-start.2 = (bf16[256,2048]{1,0:T(8,128)(2,1)}, bf16[256,2048]{1,0:T(8,128)(2,1)}, u32[]{:S(2)}, u32[]{:S(2)}) collective-permute-start(bf16[256,2048]{1,0:T(8,128)(2,1)} %get-tuple-element.100), channel_id=1, source_target_pairs={{0,4},{2,6},{4,0},{6,2},{1,5},{3,7},{5,1},{7,3},{8,12},{10,14},{12... | collective-permute-start | bytes 3145736 | tf_op jit(solution)/shard_map/ppermute | solution.py:274
  405.9 217.5 %reduce-scatter.11.cloned.1.call-start = ((), (), s32[]{:S(2)}) async-start(), calls=%async_computation.7 | async-start | bytes 1310720 | tf_op jit(solution)/shard_map/reduce_scatter | solution.py:372
  406.2 4.1 copy-start.32
  406.2 5.4 copy-start.14
  415.2 4.5 copy-start.8
  419.7 22.0 %collective-permute-start.3 = (bf16[4,4,64,2048]{3,2,0,1:T(8,128)(2,1)}, bf16[4,4,64,2048]{3,2,0,1:T(8,128)(2,1)}, u32[]{:S(2)}, u32[]{:S(2)}) collective-permute-start(bf16[4,4,64,2048]{3,2,0,1:T(8,128)(2,1)} %copy_bitcast_fusion), channel_id=1, source_target_pairs={{0,1},{1,0},{2,3},{3,2},{4,5},{5,4},{6,7},{7,6},{8,9},{9,8},{10,11... | collective-permute-start | bytes 12582920 | tf_op jit(solution)/shard_map/ppermute | solution.py:283
  441.7 4.4 copy-start.22
  447.6 73.8 %collective-permute-start.6 = (bf16[512,2048]{1,0:T(8,128)(2,1)}, bf16[512,2048]{1,0:T(8,128)(2,1)}, u32[]{:S(2)}, u32[]{:S(2)}) collective-permute-start(bf16[512,2048]{1,0:T(8,128)(2,1)} %pad_maximum_fusion.3), channel_id=1, source_target_pairs={{0,4},{2,6},{4,0},{6,2},{1,5},{3,7},{5,1},{7,3},{8,12},{10,14},{12... | collective-permute-start | bytes 6291464 | tf_op jit(solution)/shard_map/ppermute | solution.py:274
  449.7 71.7 %collective-permute-start.5 = (bf16[512,2048]{1,0:T(8,128)(2,1)}, bf16[512,2048]{1,0:T(8,128)(2,1)}, u32[]{:S(2)}, u32[]{:S(2)}) collective-permute-start(bf16[512,2048]{1,0:T(8,128)(2,1)} %pad_maximum_fusion.2), channel_id=1, source_target_pairs={{0,2},{2,0},{4,6},{6,4},{1,3},{3,1},{5,7},{7,5},{8,10},{10,8},{12,... | collective-permute-start | bytes 6291464 | tf_op jit(solution)/shard_map/ppermute | solution.py:274
  452.8 4.2 copy-start.1
  452.8 4.2 copy-start.4
  452.8 90.8 %collective-permute-start.4 = (bf16[512,2048]{1,0:T(8,128)(2,1)}, bf16[512,2048]{1,0:T(8,128)(2,1)}, u32[]{:S(2)}, u32[]{:S(2)}) collective-permute-start(bf16[512,2048]{1,0:T(8,128)(2,1)} %pad_maximum_fusion.1), channel_id=1, source_target_pairs={{0,6},{2,4},{4,2},{6,0},{1,7},{3,5},{5,3},{7,1},{8,14},{10,12},{12... | collective-permute-start | bytes 6291464 | tf_op jit(solution)/shard_map/ppermute | solution.py:274
  551.1 76.5 %reduce-scatter.9.cloned.1.call-start = ((), (), s32[]{:S(2)}) async-start(), calls=%async_computation.6 | async-start | bytes 1966080 | tf_op jit(solution)/shard_map/reduce_scatter | solution.py:372
  551.4 27.3 %collective-permute-start.7 = (bf16[256,2048]{1,0:T(8,128)(2,1)}, bf16[256,2048]{1,0:T(8,128)(2,1)S(1)}, u32[]{:S(2)}, u32[]{:S(2)}) collective-permute-start(bf16[256,2048]{1,0:T(8,128)(2,1)} %get-tuple-element.129), channel_id=1, source_target_pairs={{0,6},{2,4},{4,2},{6,0},{1,7},{3,5},{5,3},{7,1},{8,14},{10,12},{12... | collective-permute-start | bytes 3145736 | tf_op jit(solution)/shard_map/ppermute | solution.py:274
  552.9 46.4 %collective-permute-start.8 = (bf16[256,2048]{1,0:T(8,128)(2,1)}, bf16[256,2048]{1,0:T(8,128)(2,1)}, u32[]{:S(2)}, u32[]{:S(2)}) collective-permute-start(bf16[256,2048]{1,0:T(8,128)(2,1)} %get-tuple-element.130), channel_id=1, source_target_pairs={{0,2},{2,0},{4,6},{6,4},{1,3},{3,1},{5,7},{7,5},{8,10},{10,8},{12,... | collective-permute-start | bytes 3145736 | tf_op jit(solution)/shard_map/ppermute | solution.py:274
  553.8 45.8 %collective-permute-start.9 = (bf16[256,2048]{1,0:T(8,128)(2,1)}, bf16[256,2048]{1,0:T(8,128)(2,1)}, u32[]{:S(2)}, u32[]{:S(2)}) collective-permute-start(bf16[256,2048]{1,0:T(8,128)(2,1)} %get-tuple-element.131), channel_id=1, source_target_pairs={{0,4},{2,6},{4,0},{6,2},{1,5},{3,7},{5,1},{7,3},{8,12},{10,14},{12... | collective-permute-start | bytes 3145736 | tf_op jit(solution)/shard_map/ppermute | solution.py:274
  554.9 6.3 copy-start.28
  554.9 8.3 %copy-start.3 = (bf16[2048,384]{1,0:T(8,128)(2,1)S(1)}, bf16[2048,384]{1,0:T(8,128)(2,1)}, u32[]{:S(2)}) copy-start(bf16[2048,384]{1,0:T(8,128)(2,1)} %copy-done.2) | copy-start | bytes 4718596
  563.2 36.4 %copy-start.27 = (f32[1,2048]{1,0:T(1,128)S(1)}, f32[1,2048]{1,0:T(1,128)}, u32[]{:S(2)}) copy-start(f32[1,2048]{1,0:T(1,128)} %get-tuple-element.160) | copy-start | bytes 24580
  572.4 27.2 %copy-start.12 = (bf16[256,2048]{1,0:T(8,128)(2,1)S(1)}, bf16[256,2048]{1,0:T(8,128)(2,1)}, u32[]{:S(2)}) copy-start(bf16[256,2048]{1,0:T(8,128)(2,1)} %tok_ref.1) | copy-start | bytes 3145732
  607.9 17.3 %copy-start.17 = (bf16[1,2,2048,256]{3,2,1,0:T(8,128)(2,1)S(1)}, bf16[1,2,2048,256]{3,2,1,0:T(8,128)(2,1)}, u32[]{:S(2)}) copy-start(bf16[1,2,2048,256]{3,2,1,0:T(8,128)(2,1)} %reduce-scatter.7.cloned.1.call-done) | copy-start | bytes 6291460
  (23 other events, 39.0 us)
Sparse Core Ops, SparseCore 0:
  9.6 35.5 all-gather.6
  47.4 163.7 all-gather.8
  212.7 80.5 all-gather.10
  308.5 74.0 reduce-scatter.4
  406.1 141.4 reduce-scatter.6
  551.2 26.5 reduce-scatter.10
  580.0 33.9 reduce-scatter.8

commit v9 on v6

--- a/solution.py
+++ b/solution.py
@@ -291,13 +291,6 @@
     def parts(self):
         return tuple(self.part(step).astype(BF16) for step in (1, 2, 3))
 
-    @staticmethod
-    def send(parts):
-        return tuple(
-            swap_chips(part, step)
-            for step, part in zip((3, 1, 2), (parts[2], parts[0], parts[1]))
-        )
-
     def finish(self, came):
         total = self.part(0)
         for part in came:
@@ -561,12 +554,16 @@
     )(order, qkv, d_attended)
 
 
-def total_kernel(grps, chips, x_ref, o_ref, over_z, over_plane, send, recv, psend, precv):
+def exchange_total_kernel(
+    grps, chips, cut, paste, x_ref, t_ref, o_ref, sum_ref,
+    over_z, over_plane, send, recv, local, zsend, zrecv, psend, precv,
+):
     grp = lax.axis_index("grp")
     chip, core = place()
     me = chip * 2 + core
     far = [lax.rem(grp + s, grps) for s in range(1, grps)]
-    near = [(flip(chip, s, chips), c) for s in range(1, chips) for c in (core, 1 - core)]
+    steps = (3, 1, 2) if chips == 4 else tuple(range(1, chips))
+    near = [(flip(chip, s, chips), c) for s in steps for c in (core, 1 - core)]
     near = near + [(chip, 1 - core)]
     barrier = pltpu.get_barrier_semaphore()
     for g in far:
@@ -576,28 +573,31 @@
             barrier, inc=1, device_id={"chip": to, "core": c}, device_id_type=MESH
         )
     pl.semaphore_wait(barrier, len(far) + len(near))
+
+    def z_copy(slot, sem, to):
+        return pltpu.make_async_remote_copy(
+            src_ref=t_ref,
+            dst_ref=over_z.at[slot],
+            send_sem=sem,
+            recv_sem=zrecv.at[slot],
+            device_id={"grp": to},
+            device_id_type=MESH,
+        )
+
     copies = []
     for i, g in enumerate(far):
-        copy = pltpu.make_async_remote_copy(
-            src_ref=x_ref,
-            dst_ref=over_z.at[grp],
-            send_sem=send.at[i],
-            recv_sem=recv.at[grp],
-            device_id={"grp": g},
-            device_id_type=MESH,
-        )
+        copy = z_copy(grp, zsend.at[i], g)
         copy.start()
         copies.append(copy)
-    over_z[grp] = x_ref[...]
+    for i, (to, c) in enumerate(near):
+        copy = remote(cut(x_ref, to * 2 + c), paste(o_ref, me), send.at[i], recv.at[me], to, c)
+        copy.start()
+        copies.append(copy)
+    mine = pltpu.make_async_copy(cut(x_ref, me), paste(o_ref, me), local)
+    mine.start()
+    over_z[grp] = t_ref[...]
     for g in far:
-        pltpu.make_async_remote_copy(
-            src_ref=x_ref,
-            dst_ref=over_z.at[g],
-            send_sem=send.at[0],
-            recv_sem=recv.at[g],
-            device_id={"grp": g},
-            device_id_type=MESH,
-        ).wait_recv()
+        z_copy(g, zsend.at[0], g).wait_recv()
     over_plane[me] = jnp.sum(over_z[...], axis=0)
     for i, (to, c) in enumerate(near):
         copy = remote(over_plane.at[me], over_plane.at[me], psend.at[i], precv.at[me], to, c)
@@ -605,22 +605,30 @@
         copies.append(copy)
     for to, c in near:
         slot = to * 2 + c
+        remote(cut(x_ref, me), paste(o_ref, slot), send.at[0], recv.at[slot], to, c).wait_recv()
         remote(over_plane.at[me], over_plane.at[slot], psend.at[0], precv.at[slot], to, c).wait_recv()
     for copy in copies:
         copy.wait_send()
-    o_ref[...] = jnp.sum(over_plane[...], axis=0)
-
-
-def total(x, grps, chips, call_id):
+    mine.wait()
+    sum_ref[...] = jnp.sum(over_plane[...], axis=0)
+
+
+def exchange_total(x, t, shape, rows, cols, grps, chips, call_id):
     devs = 2 * chips
     return pl.pallas_call(
-        functools.partial(total_kernel, grps, chips),
-        out_shape=jax.ShapeDtypeStruct(x.shape, F32),
-        in_specs=[VMEM],
-        out_specs=VMEM,
+        functools.partial(exchange_total_kernel, grps, chips, by_cols(cols), by_rows(rows)),
+        out_shape=(
+            jax.ShapeDtypeStruct(shape, x.dtype),
+            jax.ShapeDtypeStruct(t.shape, F32),
+        ),
+        in_specs=[ANY, VMEM],
+        out_specs=(ANY, VMEM),
         scratch_shapes=[
-            pltpu.VMEM((grps,) + x.shape, F32),
-            pltpu.VMEM((devs,) + x.shape, F32),
+            pltpu.VMEM((grps,) + t.shape, F32),
+            pltpu.VMEM((devs,) + t.shape, F32),
+            pltpu.SemaphoreType.DMA((devs,)),
+            pltpu.SemaphoreType.DMA((devs,)),
+            pltpu.SemaphoreType.DMA,
             pltpu.SemaphoreType.DMA((grps,)),
             pltpu.SemaphoreType.DMA((grps,)),
             pltpu.SemaphoreType.DMA((devs,)),
@@ -628,7 +636,7 @@
         ],
         cost_estimate=BRIEF,
         compiler_params=pltpu.CompilerParams(collective_id=call_id, has_side_effects=True),
-    )(x)
+    )(x, t)
 
 
 def params(axes, mib=56):
@@ -980,7 +988,18 @@
     return dot_nt(d_ref[rows], w_ref[...])
 
 
-def twin_kernel(h_ref, w_ref, o_ref, corner_ref, x_ref, y_ref, acc, mine, away, twin, tsend, trecv):
+def mix_rows(refs, rows):
+    h_ref, w_ref = refs
+    total = None
+    for i in range(w_ref.shape[0]):
+        part = matmul(h_ref[i, rows], w_ref[i])
+        total = part if total is None else total + part
+    return total
+
+
+def twin_kernel(compute, count, *refs):
+    operands, (o_ref, corner_ref, x_ref, y_ref) = refs[:count], refs[count : count + 4]
+    acc, mine, away, twin, tsend, trecv = refs[count + 4 :]
     chip, core = place()
     stage = pl.program_id(0)
     rows = o_ref.shape[0]
@@ -997,11 +1016,7 @@
         greet([(chip, 1 - core)])
 
     target = jnp.bitwise_xor(chip, stage_step(stage)) * 2 * rows
-    total = None
-    for i in range(w_ref.shape[0]):
-        part = matmul(h_ref[i, pl.ds(pl.multiple_of(target, 2 * rows), 2 * rows)], w_ref[i])
-        total = part if total is None else total + part
-    acc[...] = total
+    acc[...] = compute(operands, pl.ds(pl.multiple_of(target, 2 * rows), 2 * rows))
     mine[stage] = acc[pl.ds(pl.multiple_of(core * rows, rows), rows)].astype(BF16)
     away[stage] = acc[pl.ds(pl.multiple_of((1 - core) * rows, rows), rows)].astype(BF16)
     copy(stage).start()
@@ -1019,17 +1034,17 @@
             copy(s).wait_send()
 
 
-def mix_twin(hidden, weights, rows, call_id):
+def twin_reduce(compute, operands, rows, call_id):
     block = (rows, D)
 
     def held(shape):
         return pl.BlockSpec(shape, lambda s: (0,) * len(shape), pipeline_mode=pl.Buffered(1))
 
     return pl.pallas_call(
-        twin_kernel,
+        functools.partial(twin_kernel, compute, len(operands)),
         out_shape=(jax.ShapeDtypeStruct(block, F32),) + (jax.ShapeDtypeStruct(block, BF16),) * 3,
         grid=(4,),
-        in_specs=[held(hidden.shape), held(weights.shape)],
+        in_specs=[held(x.shape) for x in operands],
         out_specs=(held(block),) * 4,
         scratch_shapes=[
             pltpu.VMEM((2 * rows, D), F32),
@@ -1043,7 +1058,17 @@
         compiler_params=pltpu.CompilerParams(
             collective_id=call_id, has_side_effects=True, vmem_limit_bytes=60 << 20
         ),
-    )(hidden, weights)
+    )(*operands)
+
+
+def swap_others(parts):
+    return tuple(swap_chips(part, step) for step, part in zip((3, 1, 2), parts))
+
+
+def join(own, came):
+    for part in came:
+        own = own + part.astype(F32)
+    return own
 
 
 def entry_kernel(
@@ -1293,29 +1318,26 @@
     part_down, hidden, silu = lax.optimization_barrier((part_down, hidden, silu))
     grad_down = scatter(part_down, "grp")
     if chips == 4:
-        branch_mlp, *others = mix_twin(hidden, down_w, rows, 11)
-        others, silu = lax.optimization_barrier((others, silu))
-        others = [swap_chips(part, step) for step, part in zip((3, 1, 2), others)]
-    else:
-        branch_mlp = mix(hidden, down_w)
+        branch_mlp, *shares = twin_reduce(mix_rows, (hidden, down_w), rows, 11)
+        shares, silu = lax.optimization_barrier((shares, silu))
+        shares = swap_others(shares)
     d_gate, d_up = narrow_back(silu, slope, d_branch_mlp, down_w)
-    part_wide = widen_part(normed_t, d_gate, d_up)
     if chips == 4:
-        part_wide, others, d_gate, d_up = lax.optimization_barrier(
-            (part_wide, others, d_gate, d_up)
+        part_wide = widen_part(normed_t, d_gate, d_up)
+        part_wide, shares, d_gate, d_up = lax.optimization_barrier(
+            (part_wide, shares, d_gate, d_up)
         )
-    else:
-        part_wide, d_gate, d_up = lax.optimization_barrier((part_wide, d_gate, d_up))
-    grad_wide = scatter(part_wide, "grp")
-    if chips == 4:
-        for part in others:
-            branch_mlp = branch_mlp + part.astype(F32)
+        grad_wide = scatter(part_wide, "grp")
+        branch_mlp = join(branch_mlp, shares)
         d_normed_two = square_reduce(widen_back_rows, (d_gate, d_up, wide_w), rows, 10)
     else:
-        branch_mlp = plane_reduce(branch_mlp.reshape(devs, rows, D), chips, 5)
+        part_wide = widen_part(normed_t, d_gate, d_up)
+        part_wide, d_gate, d_up = lax.optimization_barrier((part_wide, d_gate, d_up))
+        grad_wide = scatter(part_wide, "grp")
         d_normed_two = widen_back(d_gate, d_up, wide_w)
         d_normed_two = plane_reduce(d_normed_two.reshape(devs, rows, D), chips, 5)
-    layer_out = residual + RESID_MULT * branch_mlp
+        branch_mlp = mix(hidden, down_w)
+        branch_mlp = plane_reduce(branch_mlp.reshape(devs, rows, D), chips, 5)
 
     d_residual_norm, d_gain_two = norm_back(residual, factor_two, gain_two, d_normed_two)
     d_residual = upstream + d_residual_norm
@@ -1325,44 +1347,7 @@
     if chips == 4:
         drift_out = Drift(grad_out.reshape(grps, 4, 2, w_rows, D), 1)
     d_attended = over_cols(d_branch_attn, out_full).astype(BF16)
-    d_attended = plane_exchange(
-        d_attended, (devs * rows, q_cols), by_cols(q_cols), by_rows(rows), chips, 7
-    )
-    if chips == 4:
-        sent_out, d_attended = lax.optimization_barrier((drift_out.parts(), d_attended))
-        sent_out = Drift.send(sent_out)
-    d_attended, grad_down = lax.optimization_barrier((d_attended, grad_down))
-    d_qkv = attend_back(qkv, d_attended, order, q_heads)
-    if chips == 4:
-        sent_out, d_qkv, grad_wide = lax.optimization_barrier((sent_out, d_qkv, grad_wide))
-        grad_out = drift_out.finish(sent_out).astype(BF16)
-    else:
-        grad_out = plane_reduce(
-            grad_out.reshape(grps, devs, w_rows, D), chips, 6, dtype=BF16, inner=True
-        )
-    grad_out = scatter(grad_out, "grp").reshape(w_rows, D).astype(F32)
-    sent = over_rows(normed_one, d_qkv).astype(BF16)
-    sent, d_qkv = lax.optimization_barrier((sent, d_qkv))
-    sent = scatter(sent, "grp")
-
-    d_normed_one = over_cols(d_qkv, w_qkv).astype(BF16).reshape(devs, rows, D)
-    d_normed_one = plane_reduce(d_normed_one, chips, 5)
-    d_normed_one, sent = lax.optimization_barrier((d_normed_one, sent))
-    d_input_norm, d_gain_one = norm_back(layer_in, norm_parts(layer_in), gain_one, d_normed_one)
-    tokens_grad = (d_residual + d_input_norm).astype(BF16)
-
-    sent = sent.reshape(devs, w_rows, q_cols + 2 * kv_cols)
-    sent = plane_exchange(sent, sent.shape, by_slot, by_slot, chips, 9).astype(F32)
-
-    def kv_join(g):
-        g = g.reshape(devs // kv_copies, kv_copies, w_rows, kv_cols)
-        g = jnp.sum(g, axis=1) if kv_copies > 1 else g[:, 0]
-        return jnp.swapaxes(g, 0, 1).reshape(w_rows, KV_HEADS * HEAD_DIM)
-
-    grad_query = jnp.swapaxes(sent[:, :, :q_cols], 0, 1).reshape(w_rows, D)
-    grad_key = kv_join(sent[:, :, q_cols : q_cols + kv_cols])
-    grad_value = kv_join(sent[:, :, q_cols + kv_cols : q_cols + 2 * kv_cols])
-
+    layer_out = residual + RESID_MULT * branch_mlp
     scaled_attn = RESID_MULT * branch_attn
     scaled_mlp = RESID_MULT * branch_mlp
     squares = jnp.stack(
@@ -1372,12 +1357,56 @@
             jnp.sum(scaled_mlp * scaled_mlp),
         ]
     )
-    totals = jnp.concatenate([d_gain_one, d_gain_two, squares, jnp.zeros((1021,), F32)])
-    totals = total(totals.reshape(8, 5 * D // 16), grps, chips, 8).reshape(-1)
-    rms_stats = jnp.sqrt(totals[2 * D : 2 * D + 3] / (rows * grps * devs * D))
+    totals = jnp.concatenate([d_gain_two, squares, jnp.zeros((1021,), F32)])
+    d_attended, totals = exchange_total(
+        d_attended, totals.reshape(8, 3 * D // 16), (devs * rows, q_cols), rows, q_cols, grps, chips, 7
+    )
+    if chips == 4:
+        sent_out, d_attended = lax.optimization_barrier((drift_out.parts(), d_attended))
+        sent_out = swap_others((sent_out[2], sent_out[0], sent_out[1]))
+    d_attended, grad_down = lax.optimization_barrier((d_attended, grad_down))
+    d_qkv = attend_back(qkv, d_attended, order, q_heads)
+    if chips == 4:
+        sent_out, d_qkv = lax.optimization_barrier((sent_out, d_qkv))
+        d_normed_one, *others = twin_reduce(project_back_rows, (d_qkv, w_qkv), rows, 5)
+        others, d_qkv = lax.optimization_barrier((others, d_qkv))
+        others = swap_others(others)
+        grad_out = drift_out.finish(sent_out).astype(BF16)
+    else:
+        grad_out = plane_reduce(
+            grad_out.reshape(grps, devs, w_rows, D), chips, 6, dtype=BF16, inner=True
+        )
+    sent = over_rows(normed_one, d_qkv).astype(BF16)
+    sent, grad_wide = lax.optimization_barrier((sent, grad_wide))
+    sent = scatter(sent, "grp")
+    grad_out = scatter(grad_out, "grp").reshape(w_rows, D).astype(F32)
+    if chips == 4:
+        d_normed_one = join(d_normed_one, others)
+    else:
+        d_normed_one = over_cols(d_qkv, w_qkv).astype(BF16).reshape(devs, rows, D)
+        d_normed_one = plane_reduce(d_normed_one, chips, 5)
+    d_input_norm, _ = norm_back(layer_in, norm_parts(layer_in), gain_one, d_normed_one)
+    tokens_grad = (d_residual + d_input_norm).astype(BF16)
+    sent = sent.reshape(devs, w_rows, q_cols + 2 * kv_cols)
+    sent = plane_exchange(sent, sent.shape, by_slot, by_slot, chips, 9).astype(F32)
+
+    def kv_join(g):
+        g = g.reshape(devs // kv_copies, kv_copies, w_rows, kv_cols)
+        g = jnp.sum(g, axis=1) if kv_copies > 1 else g[:, 0]
+        return jnp.swapaxes(g, 0, 1).reshape(w_rows, KV_HEADS * HEAD_DIM)
+
+    grad_query = jnp.swapaxes(sent[:, :, :q_cols], 0, 1).reshape(w_rows, D)
+    grad_key = kv_join(sent[:, :, q_cols : q_cols + kv_cols])
+    grad_value = kv_join(sent[:, :, q_cols + kv_cols : q_cols + 2 * kv_cols])
+
+    gain_one_grad = sum(
+        jnp.sum(weight.astype(F32) * grad, axis=1)
+        for weight, grad in ((w_query, grad_query), (w_key, grad_key), (w_value, grad_value))
+    ) / attn_gain.astype(F32)
+    totals = totals.reshape(-1)
+    rms_stats = jnp.sqrt(totals[D : D + 3] / (rows * grps * devs * D))
     gain_first = (lax.axis_index("grp") * devs + lax.axis_index(PLANE)) * w_rows
-    gain_one_grad = lax.dynamic_slice(totals, (gain_first,), (w_rows,))
-    gain_two_grad = lax.dynamic_slice(totals, (gain_first + D,), (w_rows,))
+    gain_two_grad = lax.dynamic_slice(totals, (gain_first,), (w_rows,))
     return (
         layer_out.astype(BF16),
         tokens_grad,

time: 657 us -> 646 us (0.983)
  Pallas kernels: 521 us -> 484 us
  waiting for transfers between devices: 8.47 us -> 39.4 us
  matrix products: 32.7 us -> 25.3 us
    ppermute x6 -> x9, waiting for transfers between devices: 6.84 us -> 37.9 us  [swap_chips(): return lax.ppermute(values, 'chip', [(c, c ^ step) for c in range(4)])]
    pallas_call x3, Pallas kernels: 75.1 us -> 53.9 us  [the longest x2 36 us: twin_reduce(): pl.pallas_call(functools.partial(twin_kernel, compute, len(operands)), ou...]
    pallas_call x3 -> x2, Pallas kernels: 38.8 us -> 23.6 us  [plane_exchange(): pl.pallas_call(functools.partial(exchange_kernel, chips, cut, paste), out...]
    dot_general x2 -> x1, matrix products: 14.2 us -> 6.84 us  [over_cols(): lax.dot_general(left, right, (((1,), (1,)), ((), ())), preferred_element_...]
  transfers between devices with their start and end apart: 14 -> 17, of which waited for: 3 -> 5; matrix products, arithmetic and copies ran while one was open for 10% -> 12% of each run, Pallas kernels for 77% -> 75%
where the time goes in v9:
time: 646 us; the launch traced here: 637 us
  Pallas kernels  484 us (75%)
  other arithmetic  43 us (7%)
  waiting for transfers between devices  39.4 us (6%)
  matrix products  25.3 us (4%)
  local copies, waits for them, and re-layouts  18.9 us (3%)
  between operations  14.9 us (2%)
  starting transfers between devices  11.1 us (2%)
    pallas_call x1, Pallas kernels, entry(): pl.pallas_call(functools.partial(entry_kernel, grps, chips), out_shape=(j...  102 us
    pallas_call x2, Pallas kernels, plane_gather(): pl.pallas_call(functools.partial(gather_kernel, chips, inner), out_shape=...  79.9 us
    pallas_call x1, Pallas kernels, square_reduce(): pl.pallas_call(functools.partial(square_kernel, compute, len(operands)),...  54.6 us
    pallas_call x1, Pallas kernels, attend_back(): pl.pallas_call(functools.partial(attend_back_kernel, heads), out_shape=ja...  48.4 us
    ppermute x9, waiting for transfers between devices, swap_chips(): return lax.ppermute(values, 'chip', [(c, c ^ step) for c in range(4)])  37.9 us
    pallas_call x2, Pallas kernels, twin_reduce(): pl.pallas_call(functools.partial(twin_kernel, compute, len(operands)), ou...  36 us
    pallas_call x1, Pallas kernels, widen(): pl.pallas_call(widen_kernel, out_shape=(tall, jax.ShapeDtypeStruct((shard...  30.6 us
    pallas_call x1, Pallas kernels, attend(): pl.pallas_call(functools.partial(attend_kernel, heads), out_shape=jax.Sha...  25.6 us
  transfers between devices with their start and end apart: 17, of which 5 were waited for; matrix products, arithmetic and copies ran while one was open for 12% of the time, Pallas kernels for 75%

profile of v9, /device:TPU:0, one launch (start us, length us, event | category | flops | bytes accessed | tf_op | source)
XLA Modules:
  0.0 636.8 jit_solution(2547879740898674672)
XLA Ops:
  8.0 3.1 pad_maximum_fusion
  14.6 101.7 %shard_map.220 = (bf16[8,256,2048]{2,1,0:T(8,128)(2,1)}, bf16[8,256,2048]{2,1,0:T(8,128)(2,1)}, bf16[4,8,64,512]{3,2,1,0:T(8,128)(2,1)}) custom-call(bf16[256,2048]{1,0:T(8,128)(2,1)} %tok_ref.1, bf16[256,2048]{1,0:T(8,128)(2,1)} %fusion.cot_ref, bf16[8,64,512]{2,1,0:T(8,128)(2,1)} %maximum_bitcast_fusion.pack_ref), custom_call_target="tpu_custom_call" | custom-call | flops 1000 | bytes 1000 | tf_op jit(solution)/shard_map/pallas_call | solution.py:1170
  116.3 11.8 %shard_map.221 = (bf16[2048,2048]{1,0:T(8,128)(2,1)}, bf16[2048,384]{1,0:T(8,128)(2,1)}, f32[8,2048]{1,0:T(8,128)}) custom-call(bf16[2048,2048]{1,0:T(8,128)(2,1)} %bitcast.97, bf16[2048,512]{1,0:T(8,128)(2,1)} %bitcast.100), custom_call_target="tpu_custom_call" | custom-call | flops 1000 | bytes 1000 | tf_op jit(solution)/shard_map/pallas_call | solution.py:1210
  129.9 25.6 %shard_map.222.x_ref = bf16[2048,256]{1,0:T(8,128)(2,1)S(1)} custom-call(s32[16]{0:T(128)S(1)} %select_reduce_fusion.order_ref, bf16[2048,384]{1,0:T(8,128)(2,1)S(1)} %copy-done), custom_call_target="tpu_custom_call" | custom-call | flops 1000 | bytes 1000 | tf_op jit(solution)/shard_map/pallas_call | solution.py:514
  156.4 15.6 %shard_map.223 = bf16[256,2048]{1,0:T(8,128)(2,1)} custom-call(bf16[2048,256]{1,0:T(8,128)(2,1)} %copy-done.4), custom_call_target="tpu_custom_call" | custom-call | flops 1000 | bytes 1000 | tf_op jit(solution)/shard_map/pallas_call | solution.py:328
  173.5 39.9 %shard_map.224 = bf16[4,8,64,2048]{3,2,1,0:T(8,128)(2,1)} custom-call(bf16[4,64,2048]{2,1,0:T(8,128)(2,1)} %bitcast.104), custom_call_target="tpu_custom_call" | custom-call | flops 1000 | bytes 1000 | tf_op jit(solution)/shard_map/pallas_call | solution.py:160
  213.4 6.9 %multiply_reduce_fusion.5 = (f32[256]{0:T(256)S(1)}, f32[256,2048]{1,0:T(8,128)S(1)}, f32[]{:T(128)}) fusion(bf16[256,2048]{1,0:T(8,128)(2,1)S(1)} %copy-done.11, bf16[256,2048]{1,0:T(8,128)(2,1)} %shard_map.223, bf16[2048,2048]{1,0:T(8,128)(2,1)} %bitcast.98), kind=kOutput, calls=%fused_computation.38 | convolution fusion | flops 2151153408 | bytes 12583940 | tf_op jit(solution)/shard_map/dot_general | solution.py:356
  222.2 40.0 %shard_map.225 = bf16[8,256,2048]{2,1,0:T(8,128)(2,1)} custom-call(bf16[256,2048]{1,0:T(8,128)(2,1)} %multiply_convert_fusion.1.x_ref), custom_call_target="tpu_custom_call" | custom-call | flops 1000 | bytes 1000 | tf_op jit(solution)/shard_map/pallas_call | solution.py:160
  262.2 30.6 %shard_map.226 = (bf16[4,2048,256]{2,1,0:T(8,128)(2,1)}, bf16[4,256,2048]{2,1,0:T(8,128)(2,1)}, bf16[4,2048,256]{2,1,0:T(8,128)(2,1)}, bf16[4,2048,256]{2,1,0:T(8,128)(2,1)}, bf16[2048,2048]{1,0:T(8,128)(2,1)}) custom-call(bf16[2048,2048]{1,0:T(8,128)(2,1)} %bitcast.94, bf16[4,2,2048,256]{3,2,1,0:T(8,128)(2,1)} %bitcast.90), custom_call_target="tpu_custom_call" | custom-call | flops 1000 | bytes 1000 | tf_op jit(solution)/shard_map/pallas_call | solution.py:676
  292.8 15.5 %shard_map.227 = bf16[4,256,2048]{2,1,0:T(8,128)(2,1)} custom-call(bf16[4,256,2048]{2,1,0:T(8,128)(2,1)} %get-tuple-element.70.ht_ref, bf16[2048,2048]{1,0:T(8,128)(2,1)} %bitcast.92), custom_call_target="tpu_custom_call" | custom-call | flops 1000 | bytes 1000 | tf_op jit(solution)/shard_map/pallas_call | solution.py:710
  308.5 21.2 %shard_map.228 = (f32[256,2048]{1,0:T(8,128)}, bf16[256,2048]{1,0:T(8,128)(2,1)}, bf16[256,2048]{1,0:T(8,128)(2,1)}, bf16[256,2048]{1,0:T(8,128)(2,1)}) custom-call(bf16[4,2048,256]{2,1,0:T(8,128)(2,1)} %get-tuple-element.74.refs_0_, bf16[4,256,2048]{2,1,0:T(8,128)(2,1)} %bitcast.95), custom_call_target="tpu_custom_call" | custom-call | flops 1000 | bytes 1000 | tf_op jit(solution)/shard_map/pallas_call | solution.py:1043
  333.3 15.4 %shard_map.229 = (bf16[4,2048,256]{2,1,0:T(8,128)(2,1)}, bf16[4,2048,256]{2,1,0:T(8,128)(2,1)}) custom-call(bf16[4,2048,256]{2,1,0:T(8,128)(2,1)} %get-tuple-element.81.s_ref, bf16[4,2048,256]{2,1,0:T(8,128)(2,1)} %get-tuple-element.82.t_ref, bf16[2048,2048]{1,0:T(8,128)(2,1)} %bitcast.93, bf16[4,256,2048]{2,1,0:T(8,128)(2,1)} %bitcast.96), custom_call_target="tpu_custom_call" | custom-call | flops 1000 | bytes 1000 | tf_op jit(solution)/shard_map/pallas_call | solution.py:768
  348.7 23.4 %shard_map.230 = bf16[4,2,2048,256]{3,2,1,0:T(8,128)(2,1)} custom-call(bf16[2048,2048]{1,0:T(8,128)(2,1)} %get-tuple-element.76.nt_ref, bf16[4,2048,256]{2,1,0:T(8,128)(2,1)} %get-tuple-element.91.dg_ref.refs_0_, bf16[4,2048,256]{2,1,0:T(8,128)(2,1)} %get-tuple-element.92.du_ref.refs_1_), custom_call_target="tpu_custom_call" | custom-call | flops 1000 | bytes 1000 | tf_op jit(solution)/shard_map/pallas_call | solution.py:790
  372.1 6.6 %collective-permute-done.1 = bf16[256,2048]{1,0:T(8,128)(2,1)} collective-permute-done((bf16[256,2048]{1,0:T(8,128)(2,1)}, bf16[256,2048]{1,0:T(8,128)(2,1)}, u32[]{:S(2)}, u32[]{:S(2)}) %collective-permute-start.1) | collective-permute-done | bytes 1048608 | tf_op jit(solution)/shard_map/ppermute | solution.py:274
  379.0 54.6 %shard_map.231 = f32[256,2048]{1,0:T(8,128)} custom-call(bf16[4,2048,256]{2,1,0:T(8,128)(2,1)} %get-tuple-element.91.dg_ref.refs_0_, bf16[4,2048,256]{2,1,0:T(8,128)(2,1)} %get-tuple-element.92.du_ref.refs_1_, bf16[4,2,2048,256]{3,2,1,0:T(8,128)(2,1)} %bitcast.91), custom_call_target="tpu_custom_call" | custom-call | flops 1000 | bytes 1000 | tf_op jit(solution)/shard_map/pallas_call | solution.py:949
  433.7 6.7 %multiply_reduce_fusion = (f32[]{:T(128)}, f32[]{:T(128)}, f32[256]{0:T(256)S(1)}, f32[2048]{0:T(1024)}, f32[256,2048]{1,0:T(8,128)}) fusion(f32[256,2048]{1,0:T(8,128)S(1)} %get-tuple-element.130, f32[256,2048]{1,0:T(8,128)} %shard_map.231, f32[2048]{0:T(1024)S(1)} %bitcast.111, f32[256]{0:T(256)S(1)} %add_rsqrt_fusion.1, ...), kind=kLoop, calls=%fused_computation.30 | loop fusion | flops 9434878 | bytes 11552776 | tf_op jit(solution)/shard_map/reduce_sum | solution.py:1357
  442.1 2.4 convolution_convert_fusion
  444.5 2.5 copy_bitcast_fusion
  451.7 6.8 %convolution_convert_fusion.2.x_ref = bf16[256,2048]{1,0:T(8,128)(2,1)} fusion(bf16[256,2048]{1,0:T(8,128)(2,1)S(1)} %multiply_convert_fusion, bf16[2048,2048]{1,0:T(8,128)(2,1)} %bitcast.99), kind=kOutput, calls=%fused_computation.10 | convolution fusion | flops 2148007936 | bytes 10485760 | tf_op jit(solution)/shard_map/dot_general | solution.py:364
  458.6 17.9 %shard_map.232 = (bf16[2048,256]{1,0:T(8,128)(2,1)}, f32[8,384]{1,0:T(8,128)}) custom-call(bf16[256,2048]{1,0:T(8,128)(2,1)} %convolution_convert_fusion.2.x_ref, f32[8,384]{1,0:T(8,128)} %reshape.155.t_ref), custom_call_target="tpu_custom_call" | custom-call | flops 1000 | bytes 1000 | tf_op jit(solution)/shard_map/pallas_call | solution.py:618
  476.5 5.6 fusion.10
  485.6 48.4 %shard_map.233.refs_0_ = bf16[2048,384]{1,0:T(8,128)(2,1)S(1)} custom-call(s32[16]{0:T(128)S(1)} %select_reduce_fusion.order_ref, bf16[2048,384]{1,0:T(8,128)(2,1)S(1)} %copy-done.1, bf16[2048,256]{1,0:T(8,128)(2,1)S(1)} %copy-done.5), custom_call_target="tpu_custom_call" | custom-call | flops 1000 | bytes 1000 | tf_op jit(solution)/shard_map/pallas_call | solution.py:536
  535.1 4.6 fusion.9
  541.7 14.9 %shard_map.234 = (f32[256,2048]{1,0:T(8,128)}, bf16[256,2048]{1,0:T(8,128)(2,1)}, bf16[256,2048]{1,0:T(8,128)(2,1)}, bf16[256,2048]{1,0:T(8,128)(2,1)}) custom-call(bf16[2048,384]{1,0:T(8,128)(2,1)} %copy-done.2, bf16[2048,384]{1,0:T(8,128)(2,1)} %slice.36.refs_1_), custom_call_target="tpu_custom_call" | custom-call | flops 1000 | bytes 1000 | tf_op jit(solution)/shard_map/pallas_call | solution.py:1043
  560.1 9.1 %convolution_convert_fusion.1 = bf16[2048,384]{1,0:T(8,128)(2,1)} fusion(bf16[2048,2048]{1,0:T(8,128)(2,1)} %get-tuple-element.110, bf16[2048,384]{1,0:T(8,128)(2,1)S(1)} %copy-done.3), kind=kOutput, calls=%fused_computation.6 | convolution fusion | flops 3222011904 | bytes 11534336 | tf_op jit(solution)/shard_map/dot_general | solution.py:360
  571.9 2.9 bitcast_convert_fusion
  574.9 9.0 %collective-permute-done.7 = bf16[256,2048]{1,0:T(8,128)(2,1)} collective-permute-done((bf16[256,2048]{1,0:T(8,128)(2,1)}, bf16[256,2048]{1,0:T(8,128)(2,1)}, u32[]{:S(2)}, u32[]{:S(2)}) %collective-permute-start.7) | collective-permute-done | bytes 1048608 | tf_op jit(solution)/shard_map/ppermute | solution.py:274
  583.9 21.8 %collective-permute-done.8 = bf16[256,2048]{1,0:T(8,128)(2,1)} collective-permute-done((bf16[256,2048]{1,0:T(8,128)(2,1)}, bf16[256,2048]{1,0:T(8,128)(2,1)}, u32[]{:S(2)}, u32[]{:S(2)}) %collective-permute-start.8) | collective-permute-done | bytes 1048608 | tf_op jit(solution)/shard_map/ppermute | solution.py:274
  606.0 2.9 fusion.1
  609.4 4.0 fusion.5
  615.1 3.9 bitcast_convert_fusion.1
  619.0 8.0 %shard_map.235 = bf16[8,64,384]{2,1,0:T(8,128)(2,1)} custom-call(bf16[8,64,384]{2,1,0:T(8,128)(2,1)} %bitcast.109), custom_call_target="tpu_custom_call" | custom-call | flops 1000 | bytes 1000 | tf_op jit(solution)/shard_map/pallas_call | solution.py:328
  (153 shorter events, 38.9 us)
Async XLA Ops:
  7.2 166.4 %all-gather.7.cloned.1.call-start = ((), (), s32[]{:S(2)}) async-start(), calls=%async_computation.8 | async-start | bytes 1310720 | tf_op jit(solution)/shard_map/all_gather | solution.py:368
  7.9 254.3 %all-gather.9.cloned.1.call-start = ((), (), s32[]{:S(2)}) async-start(), calls=%async_computation.9 | async-start | bytes 10485760 | tf_op jit(solution)/shard_map/all_gather | solution.py:368
  11.1 297.4 %all-gather.11.cloned.1.call-start = ((), (), s32[]{:S(2)}) async-start(), calls=%async_computation.10 | async-start | bytes 5242880 | tf_op jit(solution)/shard_map/all_gather | solution.py:368
  11.8 473.7 %reduce-scatter.5.cloned.1.call-start = ((), (), s32[]{:S(2)}) async-start(), calls=%async_computation.4 | async-start | bytes 5242880 | tf_op jit(solution)/shard_map/reduce_scatter | solution.py:372
  116.2 11.8 %copy-start.35 = (s32[64]{0:T(128)S(1)}, s32[64]{0:T(128)}, u32[]{:S(2)}) copy-start(s32[64]{0:T(128)} %param.15) | copy-start | bytes 772
  116.2 11.8 %copy-start.36 = (s32[64]{0:T(128)S(1)}, s32[64]{0:T(128)}, u32[]{:S(2)}) copy-start(s32[64]{0:T(128)} %param.14) | copy-start | bytes 772
  173.5 39.9 %copy-start.11 = (bf16[256,2048]{1,0:T(8,128)(2,1)S(1)}, bf16[256,2048]{1,0:T(8,128)(2,1)}, u32[]{:S(2)}) copy-start(bf16[256,2048]{1,0:T(8,128)(2,1)} %tok_ref.1) | copy-start | bytes 3145732
  220.4 219.9 %copy-start.7 = (f32[256,2048]{1,0:T(8,128)}, f32[256,2048]{1,0:T(8,128)S(1)}, u32[]{:S(2)}) copy-start(f32[256,2048]{1,0:T(8,128)S(1)} %get-tuple-element.130) | copy-start | bytes 6291460
  308.3 261.0 %reduce-scatter.7.cloned.1.call-start = ((), (), s32[]{:S(2)}) async-start(), calls=%async_computation.5 | async-start | bytes 10485760 | tf_op jit(solution)/shard_map/reduce_scatter | solution.py:372
  329.7 42.4 %collective-permute-start = (bf16[256,2048]{1,0:T(8,128)(2,1)}, bf16[256,2048]{1,0:T(8,128)(2,1)S(1)}, u32[]{:S(2)}, u32[]{:S(2)}) collective-permute-start(bf16[256,2048]{1,0:T(8,128)(2,1)} %get-tuple-element.85), channel_id=1, source_target_pairs={{0,6},{2,4},{4,2},{6,0},{1,7},{3,5},{5,3},{7,1},{8,14},{10,12},{12... | collective-permute-start | bytes 3145736 | tf_op jit(solution)/shard_map/ppermute | solution.py:274
  330.9 47.8 %collective-permute-start.1 = (bf16[256,2048]{1,0:T(8,128)(2,1)}, bf16[256,2048]{1,0:T(8,128)(2,1)}, u32[]{:S(2)}, u32[]{:S(2)}) collective-permute-start(bf16[256,2048]{1,0:T(8,128)(2,1)} %get-tuple-element.86), channel_id=1, source_target_pairs={{0,2},{2,0},{4,6},{6,4},{1,3},{3,1},{5,7},{7,5},{8,10},{10,8},{12,... | collective-permute-start | bytes 3145736 | tf_op jit(solution)/shard_map/ppermute | solution.py:274
  332.4 46.6 %collective-permute-start.2 = (bf16[256,2048]{1,0:T(8,128)(2,1)}, bf16[256,2048]{1,0:T(8,128)(2,1)}, u32[]{:S(2)}, u32[]{:S(2)}) collective-permute-start(bf16[256,2048]{1,0:T(8,128)(2,1)} %get-tuple-element.87), channel_id=1, source_target_pairs={{0,4},{2,6},{4,0},{6,2},{1,5},{3,7},{5,1},{7,3},{8,12},{10,14},{12... | collective-permute-start | bytes 3145736 | tf_op jit(solution)/shard_map/ppermute | solution.py:274
  379.0 234.3 %reduce-scatter.11.cloned.1.call-start = ((), (), s32[]{:S(2)}) async-start(), calls=%async_computation.7 | async-start | bytes 1310720 | tf_op jit(solution)/shard_map/reduce_scatter | solution.py:372
  433.6 6.7 %copy-start.32 = (f32[256]{0:T(256)S(1)}, f32[256]{0:T(256)}, u32[]{:S(2)}) copy-start(f32[256]{0:T(256)} %copy-done.31) | copy-start | bytes 3076
  433.6 7.3 %copy-start.9 = (f32[256,2048]{1,0:T(8,128)S(1)}, f32[256,2048]{1,0:T(8,128)}, u32[]{:S(2)}) copy-start(f32[256,2048]{1,0:T(8,128)} %shard_map.231) | copy-start | bytes 6291460
  433.6 7.3 %copy-start.14 = (bf16[256,2048]{1,0:T(8,128)(2,1)S(1)}, bf16[256,2048]{1,0:T(8,128)(2,1)}, u32[]{:S(2)}) copy-start(bf16[256,2048]{1,0:T(8,128)(2,1)} %param.25) | copy-start | bytes 3145732
  444.5 4.6 copy-start.6
  449.1 27.4 %collective-permute-start.3 = (bf16[4,4,64,2048]{3,2,0,1:T(8,128)(2,1)}, bf16[4,4,64,2048]{3,2,0,1:T(8,128)(2,1)}, u32[]{:S(2)}, u32[]{:S(2)}) collective-permute-start(bf16[4,4,64,2048]{3,2,0,1:T(8,128)(2,1)} %copy_bitcast_fusion), channel_id=1, source_target_pairs={{0,1},{1,0},{2,3},{3,2},{4,5},{5,4},{6,7},{7,6},{8,9},{9,8},{10,11... | collective-permute-start | bytes 12582920 | tf_op jit(solution)/shard_map/ppermute | solution.py:283
  476.4 9.1 %copy-start.1 = (bf16[2048,384]{1,0:T(8,128)(2,1)S(1)}, bf16[2048,384]{1,0:T(8,128)(2,1)}, u32[]{:S(2)}) copy-start(bf16[2048,384]{1,0:T(8,128)(2,1)} %get-tuple-element.68.qkv_ref) | copy-start | bytes 4718596
  476.5 9.1 %copy-start.5 = (bf16[2048,256]{1,0:T(8,128)(2,1)S(1)}, bf16[2048,256]{1,0:T(8,128)(2,1)}, u32[]{:S(2)}) copy-start(bf16[2048,256]{1,0:T(8,128)(2,1)} %get-tuple-element.101.d_ref) | copy-start | bytes 3145732
  482.1 53.0 %collective-permute-start.4 = (bf16[4,64,2048]{2,1,0:T(8,128)(2,1)}, bf16[4,64,2048]{2,1,0:T(8,128)(2,1)}, u32[]{:S(2)}, u32[]{:S(2)}) collective-permute-start(bf16[4,64,2048]{2,1,0:T(8,128)(2,1)} %get-tuple-element.96), channel_id=1, source_target_pairs={{0,6},{2,4},{4,2},{6,0},{1,7},{3,5},{5,3},{7,1},{8,14},{10,12},{12... | collective-permute-start | bytes 3145736 | tf_op jit(solution)/shard_map/ppermute | solution.py:274
  483.6 51.5 %collective-permute-start.5 = (bf16[4,64,2048]{2,1,0:T(8,128)(2,1)}, bf16[4,64,2048]{2,1,0:T(8,128)(2,1)}, u32[]{:S(2)}, u32[]{:S(2)}) collective-permute-start(bf16[4,64,2048]{2,1,0:T(8,128)(2,1)} %get-tuple-element.97), channel_id=1, source_target_pairs={{0,2},{2,0},{4,6},{6,4},{1,3},{3,1},{5,7},{7,5},{8,10},{10,8},{12,... | collective-permute-start | bytes 3145736 | tf_op jit(solution)/shard_map/ppermute | solution.py:274
  484.7 50.4 %collective-permute-start.6 = (bf16[4,64,2048]{2,1,0:T(8,128)(2,1)}, bf16[4,64,2048]{2,1,0:T(8,128)(2,1)}, u32[]{:S(2)}, u32[]{:S(2)}) collective-permute-start(bf16[4,64,2048]{2,1,0:T(8,128)(2,1)} %get-tuple-element.98), channel_id=1, source_target_pairs={{0,4},{2,6},{4,0},{6,2},{1,5},{3,7},{5,1},{7,3},{8,12},{10,14},{12... | collective-permute-start | bytes 3145736 | tf_op jit(solution)/shard_map/ppermute | solution.py:274
  535.1 4.7 copy-start.18
  539.7 79.2 %reduce-scatter.9.cloned.1.call-start = ((), (), s32[]{:S(2)}) async-start(), calls=%async_computation.6 | async-start | bytes 1966080 | tf_op jit(solution)/shard_map/reduce_scatter | solution.py:372
  541.1 19.0 %copy-start.3 = (bf16[2048,384]{1,0:T(8,128)(2,1)S(1)}, bf16[2048,384]{1,0:T(8,128)(2,1)}, u32[]{:S(2)}) copy-start(bf16[2048,384]{1,0:T(8,128)(2,1)} %copy-done.2) | copy-start | bytes 4718596
  556.6 27.3 %collective-permute-start.7 = (bf16[256,2048]{1,0:T(8,128)(2,1)}, bf16[256,2048]{1,0:T(8,128)(2,1)}, u32[]{:S(2)}, u32[]{:S(2)}) collective-permute-start(bf16[256,2048]{1,0:T(8,128)(2,1)} %get-tuple-element.107), channel_id=1, source_target_pairs={{0,6},{2,4},{4,2},{6,0},{1,7},{3,5},{5,3},{7,1},{8,14},{10,12},{12... | collective-permute-start | bytes 3145736 | tf_op jit(solution)/shard_map/ppermute | solution.py:274
  558.1 47.5 %collective-permute-start.8 = (bf16[256,2048]{1,0:T(8,128)(2,1)}, bf16[256,2048]{1,0:T(8,128)(2,1)}, u32[]{:S(2)}, u32[]{:S(2)}) collective-permute-start(bf16[256,2048]{1,0:T(8,128)(2,1)} %get-tuple-element.108), channel_id=1, source_target_pairs={{0,2},{2,0},{4,6},{6,4},{1,3},{3,1},{5,7},{7,5},{8,10},{10,8},{12,... | collective-permute-start | bytes 3145736 | tf_op jit(solution)/shard_map/ppermute | solution.py:274
  559.3 46.6 %collective-permute-start.9 = (bf16[256,2048]{1,0:T(8,128)(2,1)}, bf16[256,2048]{1,0:T(8,128)(2,1)}, u32[]{:S(2)}, u32[]{:S(2)}) collective-permute-start(bf16[256,2048]{1,0:T(8,128)(2,1)} %get-tuple-element.109), channel_id=1, source_target_pairs={{0,4},{2,6},{4,0},{6,2},{1,5},{3,7},{5,1},{7,3},{8,12},{10,14},{12... | collective-permute-start | bytes 3145736 | tf_op jit(solution)/shard_map/ppermute | solution.py:274
  569.3 36.6 %copy-start.12 = (bf16[256,2048]{1,0:T(8,128)(2,1)S(1)}, bf16[256,2048]{1,0:T(8,128)(2,1)}, u32[]{:S(2)}) copy-start(bf16[256,2048]{1,0:T(8,128)(2,1)} %tok_ref.1) | copy-start | bytes 3145732
  569.3 36.6 %copy-start.17 = (f32[256,2048]{1,0:T(8,128)S(1)}, f32[256,2048]{1,0:T(8,128)}, u32[]{:S(2)}) copy-start(f32[256,2048]{1,0:T(8,128)} %get-tuple-element.103) | copy-start | bytes 6291460
  571.9 37.0 %copy-start.16 = (f32[256,2048]{1,0:T(8,128)S(1)}, f32[256,2048]{1,0:T(8,128)}, u32[]{:S(2)}) copy-start(f32[256,2048]{1,0:T(8,128)} %get-tuple-element.128) | copy-start | bytes 6291460
  (23 other events, 39.7 us)
Sparse Core Ops, SparseCore 0:
  9.6 35.5 all-gather.6
  47.4 163.7 all-gather.8
  212.7 80.5 all-gather.10
  308.4 74.0 reduce-scatter.4
  384.8 145.7 reduce-scatter.6
  539.9 26.1 reduce-scatter.10
  569.4 34.2 reduce-scatter.8

commit v10 on v9

--- a/solution.py
+++ b/solution.py
@@ -416,6 +416,18 @@
         v_ref[at] = repeat_heads(pair[:, HEAD_DIM:], heads)
 
 
+def by_keys(slot, body):
+    prompt = PROMPT_BLOCKS * BLOCK
+    quarter = prompt // 4
+    seen = jnp.minimum(slot, PROMPT_BLOCKS) * BLOCK
+    for n in range(1, 5):
+        low = (n - 1) * quarter if n > 1 else -1
+
+        @pl.when((seen > low) & (seen <= n * quarter))
+        def _(n=n):
+            body(n * quarter)
+
+
 def soft_parts(heads, slot, q_stack, k_far, k_own):
     far = dot_nt(k_far, q_stack)
     own = dot_nt(k_own, q_stack)
@@ -447,10 +459,15 @@
     mine = qkv_ref[rows, :]
     k_own = repeat_heads(mine[:, q_cols : q_cols + HEAD_DIM], heads)
     v_own = repeat_heads(mine[:, q_cols + HEAD_DIM :], heads)
-    far, own = soft_parts(heads, slot, scaled_stack(mine[:, :q_cols], heads), k_ref[...], k_own)
-    mixed = matmul(vt_ref[...], far.astype(BF16))
-    mixed += matmul(v_own.astype(F32).T.astype(BF16), own.astype(BF16))
-    o_ref[rows, :] = head_pick(mixed.T, heads).astype(BF16)
+    q_stack = scaled_stack(mine[:, :q_cols], heads)
+
+    def body(count):
+        far, own = soft_parts(heads, slot, q_stack, k_ref[:count], k_own)
+        mixed = matmul(vt_ref[:, :count], far.astype(BF16))
+        mixed += matmul(v_own.astype(F32).T.astype(BF16), own.astype(BF16))
+        o_ref[rows, :] = head_pick(mixed.T, heads).astype(BF16)
+
+    by_keys(slot, body)
 
 
 def attend_back_kernel(
@@ -472,30 +489,35 @@
     v_own = repeat_heads(mine[:, q_cols + HEAD_DIM :], heads)
     q_stack = scaled_stack(mine[:, :q_cols], heads)
     d_stack = head_stack(d_ref[rows, :], heads)
-    far, own = soft_parts(heads, slot, q_stack, k_ref[...], k_own)
-    d_far, d_own = dot_nt(v_ref[...], d_stack), dot_nt(v_own, d_stack)
-    mean = jnp.sum(far * d_far, axis=0, keepdims=True) + jnp.sum(own * d_own, axis=0, keepdims=True)
-    d_far = (far * (d_far - mean)).astype(BF16)
-    d_own = (own * (d_own - mean)).astype(BF16)
-    dv_ref[...] += matmul(far.astype(BF16), d_stack)
-    dk_ref[...] += matmul(d_far, q_stack)
-    dv_own = matmul(own.astype(BF16), d_stack)
-    dk_own = matmul(d_own, q_stack)
-    d_q = matmul(kt_ref[...], d_far) + matmul(k_own.astype(F32).T.astype(BF16), d_own)
-    o_ref[rows, :q_cols] = (head_pick(d_q.T, heads) * ATTN_MULT).astype(BF16)
 
     def fold(d_k, d_v):
         return jnp.concatenate([head_fold(d_k, heads), head_fold(d_v, heads)], axis=1).astype(BF16)
 
-    @pl.when(slot < PROMPT_BLOCKS)
-    def _():
-        at = pl.ds(pl.multiple_of(slot * BLOCK, BLOCK), BLOCK)
-        dk_ref[at] += dk_own
-        dv_ref[at] += dv_own
-
-    @pl.when(slot >= PROMPT_BLOCKS)
-    def _():
-        o_ref[rows, q_cols:] = fold(dk_own, dv_own)
+    def body(count):
+        far, own = soft_parts(heads, slot, q_stack, k_ref[:count], k_own)
+        d_far, d_own = dot_nt(v_ref[:count], d_stack), dot_nt(v_own, d_stack)
+        mean = jnp.sum(far * d_far, axis=0, keepdims=True)
+        mean += jnp.sum(own * d_own, axis=0, keepdims=True)
+        d_far = (far * (d_far - mean)).astype(BF16)
+        d_own = (own * (d_own - mean)).astype(BF16)
+        dv_ref[:count] += matmul(far.astype(BF16), d_stack)
+        dk_ref[:count] += matmul(d_far, q_stack)
+        dv_own = matmul(own.astype(BF16), d_stack)
+        dk_own = matmul(d_own, q_stack)
+        d_q = matmul(kt_ref[:, :count], d_far) + matmul(k_own.astype(F32).T.astype(BF16), d_own)
+        o_ref[rows, :q_cols] = (head_pick(d_q.T, heads) * ATTN_MULT).astype(BF16)
+
+        @pl.when(slot < PROMPT_BLOCKS)
+        def _():
+            at = pl.ds(pl.multiple_of(slot * BLOCK, BLOCK), BLOCK)
+            dk_ref[at] += dk_own
+            dv_ref[at] += dv_own
+
+        @pl.when(slot >= PROMPT_BLOCKS)
+        def _():
+            o_ref[rows, q_cols:] = fold(dk_own, dv_own)
+
+    by_keys(slot, body)
 
     @pl.when(slot == GROUP_BLOCKS - 1)
     def _():
@@ -919,24 +941,27 @@
     def _():
         run.greet()
 
-    target = jnp.bitwise_xor(run.chip, stage_step(stage))
-    width = 2 * run.rows
-    run.acc[...] = compute(operands, pl.ds(pl.multiple_of(target * width, width), width))
-    run.offer(stage)
-
-    @pl.when(stage == 1)
-    def _():
-        run.corners()
-
-    @pl.when(stage == 2)
-    def _():
-        run.plain(1)
-
     @pl.when(stage == 3)
     def _():
         run.plain(2)
         run.joined(2)
         run.joined(1)
+
+    target = jnp.bitwise_xor(run.chip, stage_step(stage))
+    width = 2 * run.rows
+    run.acc[...] = compute(operands, pl.ds(pl.multiple_of(target * width, width), width))
+    run.offer(stage)
+
+    @pl.when(stage == 1)
+    def _():
+        run.corners()
+
+    @pl.when(stage == 2)
+    def _():
+        run.plain(1)
+
+    @pl.when(stage == 3)
+    def _():
         run.finish(o_ref)
 
 
@@ -1368,27 +1393,27 @@
     d_qkv = attend_back(qkv, d_attended, order, q_heads)
     if chips == 4:
         sent_out, d_qkv = lax.optimization_barrier((sent_out, d_qkv))
-        d_normed_one, *others = twin_reduce(project_back_rows, (d_qkv, w_qkv), rows, 5)
-        others, d_qkv = lax.optimization_barrier((others, d_qkv))
-        others = swap_others(others)
+    sent = over_rows(normed_one, d_qkv).astype(BF16)
+    sent, d_qkv, grad_wide = lax.optimization_barrier((sent, d_qkv, grad_wide))
+    sent = scatter(sent, "grp")
+    d_normed_one = over_cols(d_qkv, w_qkv).astype(BF16).reshape(devs, rows, D)
+    if chips == 4:
+        sent_out, d_normed_one = lax.optimization_barrier((sent_out, d_normed_one))
         grad_out = drift_out.finish(sent_out).astype(BF16)
     else:
         grad_out = plane_reduce(
             grad_out.reshape(grps, devs, w_rows, D), chips, 6, dtype=BF16, inner=True
         )
-    sent = over_rows(normed_one, d_qkv).astype(BF16)
-    sent, grad_wide = lax.optimization_barrier((sent, grad_wide))
-    sent = scatter(sent, "grp")
-    grad_out = scatter(grad_out, "grp").reshape(w_rows, D).astype(F32)
-    if chips == 4:
-        d_normed_one = join(d_normed_one, others)
-    else:
-        d_normed_one = over_cols(d_qkv, w_qkv).astype(BF16).reshape(devs, rows, D)
-        d_normed_one = plane_reduce(d_normed_one, chips, 5)
+    grad_out, d_normed_one = lax.optimization_barrier((grad_out, d_normed_one))
+    grad_out = scatter(grad_out, "grp")
+    d_normed_one = plane_reduce(d_normed_one, chips, 5)
+    d_normed_one, sent = lax.optimization_barrier((d_normed_one, sent))
     d_input_norm, _ = norm_back(layer_in, norm_parts(layer_in), gain_one, d_normed_one)
     tokens_grad = (d_residual + d_input_norm).astype(BF16)
     sent = sent.reshape(devs, w_rows, q_cols + 2 * kv_cols)
-    sent = plane_exchange(sent, sent.shape, by_slot, by_slot, chips, 9).astype(F32)
+    sent = plane_exchange(sent, sent.shape, by_slot, by_slot, chips, 9)
+    sent, grad_out = lax.optimization_barrier((sent, grad_out))
+    sent, grad_out = sent.astype(F32), grad_out.reshape(w_rows, D).astype(F32)
 
     def kv_join(g):
         g = g.reshape(devs // kv_copies, kv_copies, w_rows, kv_cols)

time: 646 us -> 642 us (level)
  waiting for transfers between devices: 39.4 us -> 9.86 us
  Pallas kernels: 484 us -> 513 us
  matrix products: 25.3 us -> 33.8 us
    pallas_call x0 -> x1, Pallas kernels: none -> 41.4 us  [plane_reduce(): pl.pallas_call(functools.partial(reduce_kernel, chips, inner), out_shape=...]
    ppermute x9 -> x6, waiting for transfers between devices: 37.9 us -> 8.32 us  [swap_chips(): return lax.ppermute(values, 'chip', [(c, c ^ step) for c in range(4)])]
    pallas_call x2 -> x1, Pallas kernels: 36 us -> 20.9 us  [twin_reduce(): pl.pallas_call(functools.partial(twin_kernel, compute, len(operands)), ou...]
    pallas_call x1, Pallas kernels: 15.5 us -> 25.4 us  [down_part(): pl.pallas_call(down_part_kernel, out_shape=jax.ShapeDtypeStruct((shards,...]
    dot_general x1 -> x2, matrix products: 6.84 us -> 15.3 us  [over_cols(): lax.dot_general(left, right, (((1,), (1,)), ((), ())), preferred_element_...]
  transfers between devices with their start and end apart: 17 -> 14, of which waited for: 5 -> 3; matrix products, arithmetic and copies ran while one was open for 12% -> 11% of each run, Pallas kernels for 75% -> 80%
where the time goes in v10:
time: 642 us; the launch traced here: 637 us
  Pallas kernels  513 us (80%)
  other arithmetic  39.6 us (6%)
  matrix products  33.8 us (5%)
  local copies, waits for them, and re-layouts  19.3 us (3%)
  between operations  14.9 us (2%)
  waiting for transfers between devices  9.86 us (2%)
  starting transfers between devices  7.32 us (1%)
    pallas_call x1, Pallas kernels, entry(): pl.pallas_call(functools.partial(entry_kernel, grps, chips), out_shape=(j...  102 us
    pallas_call x2, Pallas kernels, plane_gather(): pl.pallas_call(functools.partial(gather_kernel, chips, inner), out_shape=...  79.8 us
    pallas_call x1, Pallas kernels, square_reduce(): pl.pallas_call(functools.partial(square_kernel, compute, len(operands)),...  54.5 us
    pallas_call x1, Pallas kernels, attend_back(): pl.pallas_call(functools.partial(attend_back_kernel, heads), out_shape=ja...  42.9 us
    pallas_call x1, Pallas kernels, plane_reduce(): pl.pallas_call(functools.partial(reduce_kernel, chips, inner), out_shape=...  41.4 us
    pallas_call x1, Pallas kernels, widen(): pl.pallas_call(widen_kernel, out_shape=(tall, jax.ShapeDtypeStruct((shard...  30.7 us
    pallas_call x1, Pallas kernels, down_part(): pl.pallas_call(down_part_kernel, out_shape=jax.ShapeDtypeStruct((shards,...  25.4 us
    pallas_call x1, Pallas kernels, widen_part(): pl.pallas_call(widen_part_kernel, out_shape=jax.ShapeDtypeStruct((shards,...  23.5 us
  transfers between devices with their start and end apart: 14, of which 3 were waited for; matrix products, arithmetic and copies ran while one was open for 11% of the time, Pallas kernels for 80%

profile of v10, /device:TPU:0, one launch (start us, length us, event | category | flops | bytes accessed | tf_op | source)
XLA Modules:
  0.0 637.3 jit_solution(9045308455511959292)
XLA Ops:
  8.0 3.1 pad_maximum_fusion
  14.6 101.7 %shard_map.220 = (bf16[8,256,2048]{2,1,0:T(8,128)(2,1)}, bf16[8,256,2048]{2,1,0:T(8,128)(2,1)}, bf16[4,8,64,512]{3,2,1,0:T(8,128)(2,1)}) custom-call(bf16[256,2048]{1,0:T(8,128)(2,1)} %tok_ref.1, bf16[256,2048]{1,0:T(8,128)(2,1)} %fusion.cot_ref, bf16[8,64,512]{2,1,0:T(8,128)(2,1)} %maximum_bitcast_fusion.pack_ref), custom_call_target="tpu_custom_call" | custom-call | flops 1000 | bytes 1000 | tf_op jit(solution)/shard_map/pallas_call | solution.py:1195
  116.3 11.8 %shard_map.221 = (bf16[2048,2048]{1,0:T(8,128)(2,1)}, bf16[2048,384]{1,0:T(8,128)(2,1)}, f32[8,2048]{1,0:T(8,128)}) custom-call(bf16[2048,2048]{1,0:T(8,128)(2,1)} %bitcast.100, bf16[2048,512]{1,0:T(8,128)(2,1)} %bitcast.103), custom_call_target="tpu_custom_call" | custom-call | flops 1000 | bytes 1000 | tf_op jit(solution)/shard_map/pallas_call | solution.py:1235
  129.9 23.4 %shard_map.222.x_ref = bf16[2048,256]{1,0:T(8,128)(2,1)S(1)} custom-call(s32[16]{0:T(128)S(1)} %select_reduce_fusion.order_ref, bf16[2048,384]{1,0:T(8,128)(2,1)S(1)} %copy-done), custom_call_target="tpu_custom_call" | custom-call | flops 1000 | bytes 1000 | tf_op jit(solution)/shard_map/pallas_call | solution.py:536
  154.3 15.6 %shard_map.223 = bf16[256,2048]{1,0:T(8,128)(2,1)} custom-call(bf16[2048,256]{1,0:T(8,128)(2,1)} %copy-done.2), custom_call_target="tpu_custom_call" | custom-call | flops 1000 | bytes 1000 | tf_op jit(solution)/shard_map/pallas_call | solution.py:328
  170.9 39.9 %shard_map.224 = bf16[4,8,64,2048]{3,2,1,0:T(8,128)(2,1)} custom-call(bf16[4,64,2048]{2,1,0:T(8,128)(2,1)} %bitcast.107), custom_call_target="tpu_custom_call" | custom-call | flops 1000 | bytes 1000 | tf_op jit(solution)/shard_map/pallas_call | solution.py:160
  210.8 6.9 %multiply_reduce_fusion.5 = (f32[256]{0:T(256)S(1)}, f32[256,2048]{1,0:T(8,128)S(1)}, f32[]{:T(128)}) fusion(bf16[256,2048]{1,0:T(8,128)(2,1)S(1)} %copy-done.10, bf16[256,2048]{1,0:T(8,128)(2,1)} %shard_map.223, bf16[2048,2048]{1,0:T(8,128)(2,1)} %bitcast.101), kind=kOutput, calls=%fused_computation.38 | convolution fusion | flops 2151153408 | bytes 12583940 | tf_op jit(solution)/shard_map/dot_general | solution.py:356
  219.1 40.0 %shard_map.225 = bf16[8,256,2048]{2,1,0:T(8,128)(2,1)} custom-call(bf16[256,2048]{1,0:T(8,128)(2,1)} %multiply_convert_fusion.1.x_ref), custom_call_target="tpu_custom_call" | custom-call | flops 1000 | bytes 1000 | tf_op jit(solution)/shard_map/pallas_call | solution.py:160
  259.1 30.7 %shard_map.226 = (bf16[4,2048,256]{2,1,0:T(8,128)(2,1)}, bf16[4,256,2048]{2,1,0:T(8,128)(2,1)}, bf16[4,2048,256]{2,1,0:T(8,128)(2,1)}, bf16[4,2048,256]{2,1,0:T(8,128)(2,1)}, bf16[2048,2048]{1,0:T(8,128)(2,1)}) custom-call(bf16[2048,2048]{1,0:T(8,128)(2,1)} %bitcast.96, bf16[4,2,2048,256]{3,2,1,0:T(8,128)(2,1)} %bitcast.92), custom_call_target="tpu_custom_call" | custom-call | flops 1000 | bytes 1000 | tf_op jit(solution)/shard_map/pallas_call | solution.py:698
  289.9 25.4 %shard_map.227 = bf16[4,256,2048]{2,1,0:T(8,128)(2,1)} custom-call(bf16[4,256,2048]{2,1,0:T(8,128)(2,1)} %get-tuple-element.73.ht_ref, bf16[2048,2048]{1,0:T(8,128)(2,1)} %bitcast.94), custom_call_target="tpu_custom_call" | custom-call | flops 1000 | bytes 1000 | tf_op jit(solution)/shard_map/pallas_call | solution.py:732
  315.4 20.9 %shard_map.228 = (f32[256,2048]{1,0:T(8,128)}, bf16[256,2048]{1,0:T(8,128)(2,1)}, bf16[256,2048]{1,0:T(8,128)(2,1)}, bf16[256,2048]{1,0:T(8,128)(2,1)}) custom-call(bf16[4,2048,256]{2,1,0:T(8,128)(2,1)} %get-tuple-element.77.refs_0_, bf16[4,256,2048]{2,1,0:T(8,128)(2,1)} %bitcast.97), custom_call_target="tpu_custom_call" | custom-call | flops 1000 | bytes 1000 | tf_op jit(solution)/shard_map/pallas_call | solution.py:1068
  339.9 15.4 %shard_map.229 = (bf16[4,2048,256]{2,1,0:T(8,128)(2,1)}, bf16[4,2048,256]{2,1,0:T(8,128)(2,1)}) custom-call(bf16[4,2048,256]{2,1,0:T(8,128)(2,1)} %get-tuple-element.84.s_ref, bf16[4,2048,256]{2,1,0:T(8,128)(2,1)} %get-tuple-element.85.t_ref, bf16[2048,2048]{1,0:T(8,128)(2,1)} %bitcast.95, bf16[4,256,2048]{2,1,0:T(8,128)(2,1)} %bitcast.98), custom_call_target="tpu_custom_call" | custom-call | flops 1000 | bytes 1000 | tf_op jit(solution)/shard_map/pallas_call | solution.py:790
  355.3 23.5 %shard_map.230 = bf16[4,2,2048,256]{3,2,1,0:T(8,128)(2,1)} custom-call(bf16[2048,2048]{1,0:T(8,128)(2,1)} %get-tuple-element.79.nt_ref, bf16[4,2048,256]{2,1,0:T(8,128)(2,1)} %get-tuple-element.94.dg_ref.refs_0_, bf16[4,2048,256]{2,1,0:T(8,128)(2,1)} %get-tuple-element.95.du_ref.refs_1_), custom_call_target="tpu_custom_call" | custom-call | flops 1000 | bytes 1000 | tf_op jit(solution)/shard_map/pallas_call | solution.py:812
  378.7 6.8 %collective-permute-done.1 = bf16[256,2048]{1,0:T(8,128)(2,1)} collective-permute-done((bf16[256,2048]{1,0:T(8,128)(2,1)}, bf16[256,2048]{1,0:T(8,128)(2,1)}, u32[]{:S(2)}, u32[]{:S(2)}) %collective-permute-start.1) | collective-permute-done | bytes 1048608 | tf_op jit(solution)/shard_map/ppermute | solution.py:274
  385.6 54.5 %shard_map.231 = f32[256,2048]{1,0:T(8,128)} custom-call(bf16[4,2048,256]{2,1,0:T(8,128)(2,1)} %get-tuple-element.94.dg_ref.refs_0_, bf16[4,2048,256]{2,1,0:T(8,128)(2,1)} %get-tuple-element.95.du_ref.refs_1_, bf16[4,2,2048,256]{3,2,1,0:T(8,128)(2,1)} %bitcast.93), custom_call_target="tpu_custom_call" | custom-call | flops 1000 | bytes 1000 | tf_op jit(solution)/shard_map/pallas_call | solution.py:974
  440.2 6.3 multiply_reduce_fusion
  447.7 2.4 convolution_convert_fusion.1
  450.1 2.5 copy_bitcast_fusion
  452.7 2.0 copy-done.4
  454.7 2.0 concatenate.7
  457.3 7.1 %convolution_convert_fusion.3.x_ref = bf16[256,2048]{1,0:T(8,128)(2,1)} fusion(bf16[256,2048]{1,0:T(8,128)(2,1)S(1)} %multiply_convert_fusion, bf16[2048,2048]{1,0:T(8,128)(2,1)} %bitcast.102), kind=kOutput, calls=%fused_computation.11 | convolution fusion | flops 2148007936 | bytes 10485760 | tf_op jit(solution)/shard_map/dot_general | solution.py:364
  464.4 17.9 %shard_map.232 = (bf16[2048,256]{1,0:T(8,128)(2,1)}, f32[8,384]{1,0:T(8,128)}) custom-call(bf16[256,2048]{1,0:T(8,128)(2,1)} %convolution_convert_fusion.3.x_ref, f32[8,384]{1,0:T(8,128)} %reshape.158.t_ref), custom_call_target="tpu_custom_call" | custom-call | flops 1000 | bytes 1000 | tf_op jit(solution)/shard_map/pallas_call | solution.py:640
  482.3 5.5 fusion.6
  492.6 42.9 %shard_map.233 = bf16[2048,384]{1,0:T(8,128)(2,1)S(1)} custom-call(s32[16]{0:T(128)S(1)} %select_reduce_fusion.order_ref, bf16[2048,384]{1,0:T(8,128)(2,1)S(1)} %copy-done.1, bf16[2048,256]{1,0:T(8,128)(2,1)S(1)} %copy-done.3), custom_call_target="tpu_custom_call" | custom-call | flops 1000 | bytes 1000 | tf_op jit(solution)/shard_map/pallas_call | solution.py:558
  536.9 9.2 %convolution_convert_fusion.2 = bf16[2048,384]{1,0:T(8,128)(2,1)} fusion(bf16[2048,2048]{1,0:T(8,128)(2,1)} %get-tuple-element.108, bf16[2048,384]{1,0:T(8,128)(2,1)S(1)} %shard_map.233), kind=kOutput, calls=%fused_computation.7 | convolution fusion | flops 3222011904 | bytes 11534336 | tf_op jit(solution)/shard_map/dot_general | solution.py:360
  546.2 8.2 %convolution_convert_fusion = bf16[2048,2048]{1,0:T(8,128)(2,1)} fusion(bf16[2048,384]{1,0:T(8,128)(2,1)S(1)} %shard_map.233, bf16[2048,512]{1,0:T(8,128)(2,1)} %bitcast.104), kind=kOutput, calls=%fused_computation | convolution fusion | flops 3225419776 | bytes 11534336 | tf_op jit(solution)/shard_map/dot_general | solution.py:364
  554.5 4.5 fusion.12
  561.7 41.4 %shard_map.234 = f32[256,2048]{1,0:T(8,128)} custom-call(bf16[8,256,2048]{2,1,0:T(8,128)(2,1)} %bitcast.99), custom_call_target="tpu_custom_call" | custom-call | flops 1000 | bytes 1000 | tf_op jit(solution)/shard_map/pallas_call | solution.py:246
  603.2 2.3 bitcast_convert_fusion.1
  605.5 7.7 %shard_map.235 = bf16[8,64,384]{2,1,0:T(8,128)(2,1)} custom-call(bf16[8,64,384]{2,1,0:T(8,128)(2,1)} %bitcast.112), custom_call_target="tpu_custom_call" | custom-call | flops 1000 | bytes 1000 | tf_op jit(solution)/shard_map/pallas_call | solution.py:328
  621.8 1.9 bitcast_convert_fusion.3
  625.4 4.3 fusion.5
  (137 shorter events, 34.6 us)
Async XLA Ops:
  7.2 163.7 %all-gather.7.cloned.1.call-start = ((), (), s32[]{:S(2)}) async-start(), calls=%async_computation.8 | async-start | bytes 1310720 | tf_op jit(solution)/shard_map/all_gather | solution.py:368
  7.9 251.2 %all-gather.9.cloned.1.call-start = ((), (), s32[]{:S(2)}) async-start(), calls=%async_computation.9 | async-start | bytes 10485760 | tf_op jit(solution)/shard_map/all_gather | solution.py:368
  11.1 304.3 %all-gather.11.cloned.1.call-start = ((), (), s32[]{:S(2)}) async-start(), calls=%async_computation.10 | async-start | bytes 5242880 | tf_op jit(solution)/shard_map/all_gather | solution.py:368
  11.8 479.5 %reduce-scatter.5.cloned.1.call-start = ((), (), s32[]{:S(2)}) async-start(), calls=%async_computation.4 | async-start | bytes 5242880 | tf_op jit(solution)/shard_map/reduce_scatter | solution.py:372
  116.2 11.8 %copy-start.30 = (s32[64]{0:T(128)S(1)}, s32[64]{0:T(128)}, u32[]{:S(2)}) copy-start(s32[64]{0:T(128)} %param.15) | copy-start | bytes 772
  116.2 11.8 %copy-start.31 = (s32[64]{0:T(128)S(1)}, s32[64]{0:T(128)}, u32[]{:S(2)}) copy-start(s32[64]{0:T(128)} %param.14) | copy-start | bytes 772
  170.9 39.9 %copy-start.10 = (bf16[256,2048]{1,0:T(8,128)(2,1)S(1)}, bf16[256,2048]{1,0:T(8,128)(2,1)}, u32[]{:S(2)}) copy-start(bf16[256,2048]{1,0:T(8,128)(2,1)} %tok_ref.1) | copy-start | bytes 3145732
  217.7 228.8 %copy-start.7 = (f32[256,2048]{1,0:T(8,128)}, f32[256,2048]{1,0:T(8,128)S(1)}, u32[]{:S(2)}) copy-start(f32[256,2048]{1,0:T(8,128)S(1)} %get-tuple-element.136) | copy-start | bytes 6291460
  217.7 228.8 %copy-start.22 = (f32[256]{0:T(256)}, f32[256]{0:T(256)S(1)}, u32[]{:S(2)}) copy-start(f32[256]{0:T(256)S(1)} %add_rsqrt_fusion.1) | copy-start | bytes 3076
  315.3 230.9 %reduce-scatter.7.cloned.1.call-start = ((), (), s32[]{:S(2)}) async-start(), calls=%async_computation.5 | async-start | bytes 10485760 | tf_op jit(solution)/shard_map/reduce_scatter | solution.py:372
  336.3 42.4 %collective-permute-start = (bf16[256,2048]{1,0:T(8,128)(2,1)}, bf16[256,2048]{1,0:T(8,128)(2,1)S(1)}, u32[]{:S(2)}, u32[]{:S(2)}) collective-permute-start(bf16[256,2048]{1,0:T(8,128)(2,1)} %get-tuple-element.88), channel_id=1, source_target_pairs={{0,6},{2,4},{4,2},{6,0},{1,7},{3,5},{5,3},{7,1},{8,14},{10,12},{12... | collective-permute-start | bytes 3145736 | tf_op jit(solution)/shard_map/ppermute | solution.py:274
  337.8 47.8 %collective-permute-start.1 = (bf16[256,2048]{1,0:T(8,128)(2,1)}, bf16[256,2048]{1,0:T(8,128)(2,1)}, u32[]{:S(2)}, u32[]{:S(2)}) collective-permute-start(bf16[256,2048]{1,0:T(8,128)(2,1)} %get-tuple-element.89), channel_id=1, source_target_pairs={{0,2},{2,0},{4,6},{6,4},{1,3},{3,1},{5,7},{7,5},{8,10},{10,8},{12,... | collective-permute-start | bytes 3145736 | tf_op jit(solution)/shard_map/ppermute | solution.py:274
  339.2 46.4 %collective-permute-start.2 = (bf16[256,2048]{1,0:T(8,128)(2,1)}, bf16[256,2048]{1,0:T(8,128)(2,1)}, u32[]{:S(2)}, u32[]{:S(2)}) collective-permute-start(bf16[256,2048]{1,0:T(8,128)(2,1)} %get-tuple-element.90), channel_id=1, source_target_pairs={{0,4},{2,6},{4,0},{6,2},{1,5},{3,7},{5,1},{7,3},{8,12},{10,14},{12... | collective-permute-start | bytes 3145736 | tf_op jit(solution)/shard_map/ppermute | solution.py:274
  385.6 219.9 %reduce-scatter.9.cloned.1.call-start = ((), (), s32[]{:S(2)}) async-start(), calls=%async_computation.6 | async-start | bytes 1966080 | tf_op jit(solution)/shard_map/reduce_scatter | solution.py:372
  440.2 6.3 copy-start.5
  440.2 6.3 copy-start.13
  450.1 4.5 copy-start.4
  454.7 27.6 %collective-permute-start.3 = (bf16[4,4,64,2048]{3,2,0,1:T(8,128)(2,1)}, bf16[4,4,64,2048]{3,2,0,1:T(8,128)(2,1)}, u32[]{:S(2)}, u32[]{:S(2)}) collective-permute-start(bf16[4,4,64,2048]{3,2,0,1:T(8,128)(2,1)} %copy_bitcast_fusion), channel_id=1, source_target_pairs={{0,1},{1,0},{2,3},{3,2},{4,5},{5,4},{6,7},{7,6},{8,9},{9,8},{10,11... | collective-permute-start | bytes 12582920 | tf_op jit(solution)/shard_map/ppermute | solution.py:283
  482.3 9.1 %copy-start.1 = (bf16[2048,384]{1,0:T(8,128)(2,1)S(1)}, bf16[2048,384]{1,0:T(8,128)(2,1)}, u32[]{:S(2)}) copy-start(bf16[2048,384]{1,0:T(8,128)(2,1)} %get-tuple-element.71.qkv_ref) | copy-start | bytes 4718596
  487.8 47.6 %collective-permute-start.4 = (bf16[4,64,2048]{2,1,0:T(8,128)(2,1)}, bf16[4,64,2048]{2,1,0:T(8,128)(2,1)}, u32[]{:S(2)}, u32[]{:S(2)}) collective-permute-start(bf16[4,64,2048]{2,1,0:T(8,128)(2,1)} %get-tuple-element.99), channel_id=1, source_target_pairs={{0,6},{2,4},{4,2},{6,0},{1,7},{3,5},{5,3},{7,1},{8,14},{10,12},{12... | collective-permute-start | bytes 3145736 | tf_op jit(solution)/shard_map/ppermute | solution.py:274
  489.3 47.2 %collective-permute-start.5 = (bf16[4,64,2048]{2,1,0:T(8,128)(2,1)}, bf16[4,64,2048]{2,1,0:T(8,128)(2,1)}, u32[]{:S(2)}, u32[]{:S(2)}) collective-permute-start(bf16[4,64,2048]{2,1,0:T(8,128)(2,1)} %get-tuple-element.100), channel_id=1, source_target_pairs={{0,2},{2,0},{4,6},{6,4},{1,3},{3,1},{5,7},{7,5},{8,10},{10,8},{12,... | collective-permute-start | bytes 3145736 | tf_op jit(solution)/shard_map/ppermute | solution.py:274
  490.5 46.4 %collective-permute-start.6 = (bf16[4,64,2048]{2,1,0:T(8,128)(2,1)}, bf16[4,64,2048]{2,1,0:T(8,128)(2,1)}, u32[]{:S(2)}, u32[]{:S(2)}) collective-permute-start(bf16[4,64,2048]{2,1,0:T(8,128)(2,1)} %get-tuple-element.101), channel_id=1, source_target_pairs={{0,4},{2,6},{4,0},{6,2},{1,5},{3,7},{5,1},{7,3},{8,12},{10,14},{12... | collective-permute-start | bytes 3145736 | tf_op jit(solution)/shard_map/ppermute | solution.py:274
  546.2 67.0 %reduce-scatter.11.cloned.1.call-start = ((), (), s32[]{:S(2)}) async-start(), calls=%async_computation.7 | async-start | bytes 1310720 | tf_op jit(solution)/shard_map/reduce_scatter | solution.py:372
  554.5 4.6 copy-start.24
  554.5 5.7 copy-start.17
  561.7 41.4 %copy-start.15 = (bf16[1,2,2048,256]{3,2,1,0:T(8,128)(2,1)S(1)}, bf16[1,2,2048,256]{3,2,1,0:T(8,128)(2,1)}, u32[]{:S(2)}) copy-start(bf16[1,2,2048,256]{3,2,1,0:T(8,128)(2,1)} %reduce-scatter.7.cloned.1.call-done) | copy-start | bytes 6291460
  616.1 7.6 %copy-start.9 = (f32[256,2048]{1,0:T(8,128)S(1)}, f32[256,2048]{1,0:T(8,128)}, u32[]{:S(2)}) copy-start(f32[256,2048]{1,0:T(8,128)} %shard_map.234) | copy-start | bytes 6291460
  616.1 7.6 %copy-start.11 = (bf16[256,2048]{1,0:T(8,128)(2,1)S(1)}, bf16[256,2048]{1,0:T(8,128)(2,1)}, u32[]{:S(2)}) copy-start(bf16[256,2048]{1,0:T(8,128)(2,1)} %tok_ref.1) | copy-start | bytes 3145732
  616.3 8.0 %copy-start.19 = (f32[64,512]{1,0:T(8,128)}, f32[64,512]{1,0:T(8,128)S(1)}, u32[]{:S(2)}) copy-start(f32[64,512]{1,0:T(8,128)S(1)} %reshape.162) | copy-start | bytes 393220
  621.8 3.6 copy-start.26
  625.4 4.3 copy-start.27
  625.4 4.3 copy-start.29
  (15 other events, 24.6 us)
Sparse Core Ops, SparseCore 0:
  9.6 35.5 all-gather.6
  47.4 163.7 all-gather.8
  212.7 80.5 all-gather.10
  315.4 74.0 reduce-scatter.4
  391.9 145.7 reduce-scatter.6
  546.3 34.2 reduce-scatter.8
  583.6 26.1 reduce-scatter.10

commit v11 on v10

--- a/solution.py
+++ b/solution.py
@@ -1127,6 +1127,7 @@
     mine = pltpu.make_async_copy(pack_ref.at[me], all_pack.at[grp, me], plocal)
     mine.start()
     tok.start()
+    cot.start()
     for to, c in near:
         slot = to * 2 + c
         remote(
@@ -1168,7 +1169,6 @@
     send(0, grp, False)
     tok.relay(0, 4)
     relay(1)
-    cot.start()
     tok.relay(4, None)
     for step in range(2, grps - 1):
         relay(step)
@@ -1252,6 +1252,84 @@
         cost_estimate=BRIEF,
         compiler_params=params(1),
     )(tokens, packed)
+
+
+def turn_kernel(
+    count, res_ref, dn_ref, cot_ref, gain_ref, branch_ref, own_ref, *refs
+):
+    came, (att_ref, w_ref, lay_ref, dres_ref, tot_ref, datt_ref, grad_ref, dba) = refs[:count], refs[count:]
+
+    @pl.when(pl.program_id(0) == 0)
+    def _():
+        residual = res_ref[...]
+        mlp = own_ref[...]
+        for part_ref in came:
+            mlp = mlp + part_ref[...].astype(F32)
+        mlp = RESID_MULT * mlp
+        layer_out = residual + mlp
+        lay_ref[...] = layer_out.astype(BF16)
+        attn = RESID_MULT * branch_ref[...]
+        grad = dn_ref[...]
+        scaled = gain_ref[1:2] * grad
+        factor = lax.rsqrt(jnp.mean(residual * residual, axis=-1, keepdims=True) + EPSILON)
+        inner = jnp.mean(residual * scaled, axis=-1, keepdims=True)
+        d_residual = cot_ref[...].astype(F32) + factor * scaled
+        d_residual = d_residual - residual * (factor * factor * factor * inner)
+        dres_ref[...] = d_residual
+        dba[...] = (RESID_MULT * d_residual).astype(BF16)
+        d_gain = jnp.sum(grad * residual * factor, axis=0, keepdims=True)
+        width = tot_ref.shape[1]
+        tot_ref[...] = jnp.zeros_like(tot_ref)
+        for r in range(pl.cdiv(D, width)):
+            last = min(width, D - r * width)
+            tot_ref[r : r + 1, :last] = d_gain[:, r * width : r * width + last]
+        lane = lax.broadcasted_iota(jnp.int32, (1, 128), 1)
+        row = jnp.zeros((1, 128), F32)
+        for i, part in enumerate((layer_out, attn, mlp)):
+            square = jnp.sum(jnp.sum(part * part, axis=0, keepdims=True), axis=1, keepdims=True)
+            row = jnp.where(lane == i, square, row)
+        tot_ref[7:8, :128] = row
+
+    datt_ref[...] = dot_nt(dba[...], w_ref[...]).astype(BF16)
+    grad_ref[...] = matmul(att_ref[...].T, dba[...]).astype(BF16)
+
+
+def turn(residual, d_normed, cotangent, gains, branch, own, came, attended, weights):
+    rows = residual.shape[0]
+    cols = 256
+    flat = jax.ShapeDtypeStruct((rows, D), F32)
+
+    def held(shape):
+        return pl.BlockSpec(shape, lambda j: (0,) * len(shape), pipeline_mode=pl.Buffered(1))
+
+    return pl.pallas_call(
+        functools.partial(turn_kernel, len(came)),
+        out_shape=(
+            jax.ShapeDtypeStruct((rows, D), BF16),
+            flat,
+            jax.ShapeDtypeStruct((8, 3 * D // 16), F32),
+            jax.ShapeDtypeStruct((rows, D), BF16),
+            jax.ShapeDtypeStruct((D, D), BF16),
+        ),
+        grid=(D // cols,),
+        in_specs=[held((rows, D))] * 3
+        + [held((8, D))]
+        + [held((rows, D))] * (2 + len(came))
+        + [
+            pl.BlockSpec((rows, cols), lambda j: (0, j)),
+            pl.BlockSpec((cols, D), lambda j: (j, 0)),
+        ],
+        out_specs=(
+            held((rows, D)),
+            held((rows, D)),
+            held((8, 3 * D // 16)),
+            pl.BlockSpec((rows, cols), lambda j: (0, j)),
+            pl.BlockSpec((cols, D), lambda j: (j, 0)),
+        ),
+        scratch_shapes=[pltpu.VMEM((rows, D), BF16)],
+        cost_estimate=BRIEF,
+        compiler_params=params(1),
+    )(residual, d_normed, cotangent, gains, branch, own, *came, attended, weights)
 
 
 def norm_parts(values):
@@ -1353,7 +1431,6 @@
             (part_wide, shares, d_gate, d_up)
         )
         grad_wide = scatter(part_wide, "grp")
-        branch_mlp = join(branch_mlp, shares)
         d_normed_two = square_reduce(widen_back_rows, (d_gate, d_up, wide_w), rows, 10)
     else:
         part_wide = widen_part(normed_t, d_gate, d_up)
@@ -1364,27 +1441,21 @@
         branch_mlp = mix(hidden, down_w)
         branch_mlp = plane_reduce(branch_mlp.reshape(devs, rows, D), chips, 5)
 
-    d_residual_norm, d_gain_two = norm_back(residual, factor_two, gain_two, d_normed_two)
-    d_residual = upstream + d_residual_norm
-    d_branch_attn = (RESID_MULT * d_residual).astype(BF16)
-    grad_out = over_rows(attended, d_branch_attn).astype(BF16)
-    grad_out, d_branch_attn = lax.optimization_barrier((grad_out, d_branch_attn))
+    layer_out, d_residual, totals, d_attended, grad_out = turn(
+        residual,
+        d_normed_two,
+        cotangent,
+        gains,
+        branch_attn,
+        branch_mlp,
+        shares if chips == 4 else (),
+        attended,
+        out_full,
+    )
     if chips == 4:
         drift_out = Drift(grad_out.reshape(grps, 4, 2, w_rows, D), 1)
-    d_attended = over_cols(d_branch_attn, out_full).astype(BF16)
-    layer_out = residual + RESID_MULT * branch_mlp
-    scaled_attn = RESID_MULT * branch_attn
-    scaled_mlp = RESID_MULT * branch_mlp
-    squares = jnp.stack(
-        [
-            jnp.sum(layer_out * layer_out),
-            jnp.sum(scaled_attn * scaled_attn),
-            jnp.sum(scaled_mlp * scaled_mlp),
-        ]
-    )
-    totals = jnp.concatenate([d_gain_two, squares, jnp.zeros((1021,), F32)])
     d_attended, totals = exchange_total(
-        d_attended, totals.reshape(8, 3 * D // 16), (devs * rows, q_cols), rows, q_cols, grps, chips, 7
+        d_attended, totals, (devs * rows, q_cols), rows, q_cols, grps, chips, 7
     )
     if chips == 4:
         sent_out, d_attended = lax.optimization_barrier((drift_out.parts(), d_attended))
@@ -1428,12 +1499,11 @@
         jnp.sum(weight.astype(F32) * grad, axis=1)
         for weight, grad in ((w_query, grad_query), (w_key, grad_key), (w_value, grad_value))
     ) / attn_gain.astype(F32)
-    totals = totals.reshape(-1)
-    rms_stats = jnp.sqrt(totals[D : D + 3] / (rows * grps * devs * D))
+    rms_stats = jnp.sqrt(totals[7, :3] / (rows * grps * devs * D))
     gain_first = (lax.axis_index("grp") * devs + lax.axis_index(PLANE)) * w_rows
-    gain_two_grad = lax.dynamic_slice(totals, (gain_first,), (w_rows,))
+    gain_two_grad = lax.dynamic_slice(totals.reshape(-1), (gain_first,), (w_rows,))
     return (
-        layer_out.astype(BF16),
+        layer_out,
         tokens_grad,
         gain_one_grad,
         grad_query,

time: 642 us -> 651 us (1.014)
  Pallas kernels: 513 us -> 538 us
  other arithmetic: 39.6 us -> 28.3 us
  matrix products: 33.8 us -> 24.9 us
    pallas_call x0 -> x1, Pallas kernels: none -> 19.8 us  [turn(): pl.pallas_call(functools.partial(turn_kernel, len(came)), out_shape=(jax....]
    pallas_call x1, Pallas kernels: 102 us -> 118 us  [entry(): pl.pallas_call(functools.partial(entry_kernel, grps, chips), out_shape=(j...]
    pallas_call x1, Pallas kernels: 25.4 us -> 15.9 us  [down_part(): pl.pallas_call(down_part_kernel, out_shape=jax.ShapeDtypeStruct((shards,...]
    dot_general x2 -> x1, matrix products: 15.3 us -> 8.2 us  [over_cols(): lax.dot_general(left, right, (((1,), (1,)), ((), ())), preferred_element_...]
  transfers between devices with their start and end apart: 14 -> 14, of which waited for: 3 -> 4; matrix products, arithmetic and copies ran while one was open for 11% -> 8% of each run, Pallas kernels for 80% -> 84%
where the time goes in v11:
time: 651 us; the launch traced here: 641 us
  Pallas kernels  538 us (83%)
  other arithmetic  28.3 us (4%)
  matrix products  24.9 us (4%)
  local copies, waits for them, and re-layouts  17.4 us (3%)
  between operations  15.1 us (2%)
  waiting for transfers between devices  10 us (2%)
  starting transfers between devices  7.28 us (1%)
    pallas_call x1, Pallas kernels, entry(): pl.pallas_call(functools.partial(entry_kernel, grps, chips), out_shape=(j...  118 us
    pallas_call x2, Pallas kernels, plane_gather(): pl.pallas_call(functools.partial(gather_kernel, chips, inner), out_shape=...  79.9 us
    pallas_call x1, Pallas kernels, square_reduce(): pl.pallas_call(functools.partial(square_kernel, compute, len(operands)),...  54.3 us
    pallas_call x1, Pallas kernels, attend_back(): pl.pallas_call(functools.partial(attend_back_kernel, heads), out_shape=ja...  42.6 us
    pallas_call x1, Pallas kernels, plane_reduce(): pl.pallas_call(functools.partial(reduce_kernel, chips, inner), out_shape=...  41.4 us
    pallas_call x1, Pallas kernels, widen(): pl.pallas_call(widen_kernel, out_shape=(tall, jax.ShapeDtypeStruct((shard...  30.6 us
    pallas_call x1, Pallas kernels, widen_part(): pl.pallas_call(widen_part_kernel, out_shape=jax.ShapeDtypeStruct((shards,...  23.4 us
    pallas_call x1, Pallas kernels, attend(): pl.pallas_call(functools.partial(attend_kernel, heads), out_shape=jax.Sha...  23.4 us
  transfers between devices with their start and end apart: 14, of which 4 were waited for; matrix products, arithmetic and copies ran while one was open for 8% of the time, Pallas kernels for 84%

profile of v11, /device:TPU:0, one launch (start us, length us, event | category | flops | bytes accessed | tf_op | source)
XLA Modules:
  0.0 640.8 jit_solution(330396756492033828)
XLA Ops:
  8.0 3.1 pad_maximum_fusion
  14.6 117.5 %shard_map.220 = (bf16[8,256,2048]{2,1,0:T(8,128)(2,1)}, bf16[8,256,2048]{2,1,0:T(8,128)(2,1)}, bf16[4,8,64,512]{3,2,1,0:T(8,128)(2,1)}) custom-call(bf16[256,2048]{1,0:T(8,128)(2,1)} %tok_ref.1, bf16[256,2048]{1,0:T(8,128)(2,1)} %multiply_convert_fusion.1.cot_ref, bf16[8,64,512]{2,1,0:T(8,128)(2,1)} %maximum_bitcast_fusion.pack_ref), custom_call_target="tpu_custom_call" | custom-call | flops 1000 | bytes 1000 | tf_op jit(solution)/shard_map/pallas_call | solution.py:1195
  132.1 11.8 %shard_map.221 = (bf16[2048,2048]{1,0:T(8,128)(2,1)}, bf16[2048,384]{1,0:T(8,128)(2,1)}, f32[8,2048]{1,0:T(8,128)}) custom-call(bf16[2048,2048]{1,0:T(8,128)(2,1)} %bitcast.94, bf16[2048,512]{1,0:T(8,128)(2,1)} %bitcast.98), custom_call_target="tpu_custom_call" | custom-call | flops 1000 | bytes 1000 | tf_op jit(solution)/shard_map/pallas_call | solution.py:1235
  145.7 23.4 %shard_map.222.x_ref = bf16[2048,256]{1,0:T(8,128)(2,1)S(1)} custom-call(s32[16]{0:T(128)S(1)} %select_reduce_fusion.order_ref, bf16[2048,384]{1,0:T(8,128)(2,1)S(1)} %copy-done), custom_call_target="tpu_custom_call" | custom-call | flops 1000 | bytes 1000 | tf_op jit(solution)/shard_map/pallas_call | solution.py:536
  170.1 15.4 %shard_map.223.refs_3_ = bf16[256,2048]{1,0:T(8,128)(2,1)} custom-call(bf16[2048,256]{1,0:T(8,128)(2,1)} %copy-done.2), custom_call_target="tpu_custom_call" | custom-call | flops 1000 | bytes 1000 | tf_op jit(solution)/shard_map/pallas_call | solution.py:328
  186.5 39.9 %shard_map.224 = bf16[4,8,64,2048]{3,2,1,0:T(8,128)(2,1)} custom-call(bf16[4,64,2048]{2,1,0:T(8,128)(2,1)} %bitcast.102), custom_call_target="tpu_custom_call" | custom-call | flops 1000 | bytes 1000 | tf_op jit(solution)/shard_map/pallas_call | solution.py:160
  226.4 7.5 %multiply_reduce_fusion = (f32[256]{0:T(256)S(1)}, f32[256,2048]{1,0:T(8,128)S(1)}, f32[256,2048]{1,0:T(8,128)}) fusion(bf16[256,2048]{1,0:T(8,128)(2,1)S(1)} %copy-done.5, bf16[256,2048]{1,0:T(8,128)(2,1)} %shard_map.223.refs_3_, bf16[2048,2048]{1,0:T(8,128)(2,1)} %bitcast.86), kind=kOutput, calls=%fused_computation.25 | convolution fusion | flops 2150104832 | bytes 14681088 | tf_op jit(solution)/shard_map/dot_general | solution.py:356
  234.0 1.4 multiply_convert_fusion.x_ref
  235.4 40.0 %shard_map.225 = bf16[8,256,2048]{2,1,0:T(8,128)(2,1)} custom-call(bf16[256,2048]{1,0:T(8,128)(2,1)} %multiply_convert_fusion.x_ref), custom_call_target="tpu_custom_call" | custom-call | flops 1000 | bytes 1000 | tf_op jit(solution)/shard_map/pallas_call | solution.py:160
  275.4 30.6 %shard_map.226 = (bf16[4,2048,256]{2,1,0:T(8,128)(2,1)}, bf16[4,256,2048]{2,1,0:T(8,128)(2,1)}, bf16[4,2048,256]{2,1,0:T(8,128)(2,1)}, bf16[4,2048,256]{2,1,0:T(8,128)(2,1)}, bf16[2048,2048]{1,0:T(8,128)(2,1)}) custom-call(bf16[2048,2048]{1,0:T(8,128)(2,1)} %bitcast.90, bf16[4,2,2048,256]{3,2,1,0:T(8,128)(2,1)} %bitcast.84), custom_call_target="tpu_custom_call" | custom-call | flops 1000 | bytes 1000 | tf_op jit(solution)/shard_map/pallas_call | solution.py:698
  306.0 15.9 %shard_map.227 = bf16[4,256,2048]{2,1,0:T(8,128)(2,1)} custom-call(bf16[4,256,2048]{2,1,0:T(8,128)(2,1)} %get-tuple-element.77.ht_ref, bf16[2048,2048]{1,0:T(8,128)(2,1)} %bitcast.88), custom_call_target="tpu_custom_call" | custom-call | flops 1000 | bytes 1000 | tf_op jit(solution)/shard_map/pallas_call | solution.py:732
  322.0 21.0 %shard_map.228 = (f32[256,2048]{1,0:T(8,128)}, bf16[256,2048]{1,0:T(8,128)(2,1)}, bf16[256,2048]{1,0:T(8,128)(2,1)}, bf16[256,2048]{1,0:T(8,128)(2,1)}) custom-call(bf16[4,2048,256]{2,1,0:T(8,128)(2,1)} %get-tuple-element.81.refs_0_, bf16[4,256,2048]{2,1,0:T(8,128)(2,1)} %bitcast.91), custom_call_target="tpu_custom_call" | custom-call | flops 1000 | bytes 1000 | tf_op jit(solution)/shard_map/pallas_call | solution.py:1068
  343.0 1.4 collective-permute-start
  346.6 15.4 %shard_map.229 = (bf16[4,2048,256]{2,1,0:T(8,128)(2,1)}, bf16[4,2048,256]{2,1,0:T(8,128)(2,1)}) custom-call(bf16[4,2048,256]{2,1,0:T(8,128)(2,1)} %get-tuple-element.86.s_ref, bf16[4,2048,256]{2,1,0:T(8,128)(2,1)} %get-tuple-element.87.t_ref, bf16[2048,2048]{1,0:T(8,128)(2,1)} %bitcast.89, bf16[4,256,2048]{2,1,0:T(8,128)(2,1)} %bitcast.92), custom_call_target="tpu_custom_call" | custom-call | flops 1000 | bytes 1000 | tf_op jit(solution)/shard_map/pallas_call | solution.py:790
  362.0 23.4 %shard_map.230 = bf16[4,2,2048,256]{3,2,1,0:T(8,128)(2,1)} custom-call(bf16[2048,2048]{1,0:T(8,128)(2,1)} %get-tuple-element.76.nt_ref, bf16[4,2048,256]{2,1,0:T(8,128)(2,1)} %get-tuple-element.93.dg_ref.refs_0_, bf16[4,2048,256]{2,1,0:T(8,128)(2,1)} %get-tuple-element.94.du_ref.refs_1_), custom_call_target="tpu_custom_call" | custom-call | flops 1000 | bytes 1000 | tf_op jit(solution)/shard_map/pallas_call | solution.py:812
  385.5 6.5 %collective-permute-done.1.refs_1_ = bf16[256,2048]{1,0:T(8,128)(2,1)S(1)} collective-permute-done((bf16[256,2048]{1,0:T(8,128)(2,1)}, bf16[256,2048]{1,0:T(8,128)(2,1)S(1)}, u32[]{:S(2)}, u32[]{:S(2)}) %collective-permute-start.1) | collective-permute-done | bytes 1048608 | tf_op jit(solution)/shard_map/ppermute | solution.py:274
  393.2 54.3 %shard_map.231.dn_ref = f32[256,2048]{1,0:T(8,128)} custom-call(bf16[4,2048,256]{2,1,0:T(8,128)(2,1)} %get-tuple-element.93.dg_ref.refs_0_, bf16[4,2048,256]{2,1,0:T(8,128)(2,1)} %get-tuple-element.94.du_ref.refs_1_, bf16[4,2,2048,256]{3,2,1,0:T(8,128)(2,1)} %bitcast.85), custom_call_target="tpu_custom_call" | custom-call | flops 1000 | bytes 1000 | tf_op jit(solution)/shard_map/pallas_call | solution.py:974
  447.5 19.8 %shard_map.232 = (bf16[256,2048]{1,0:T(8,128)(2,1)}, f32[256,2048]{1,0:T(8,128)}, f32[8,384]{1,0:T(8,128)}, bf16[256,2048]{1,0:T(8,128)(2,1)}, bf16[2048,2048]{1,0:T(8,128)(2,1)}) custom-call(f32[256,2048]{1,0:T(8,128)} %copy-done.7, f32[256,2048]{1,0:T(8,128)} %shard_map.231.dn_ref, bf16[256,2048]{1,0:T(8,128)(2,1)} %cot_ref.1, ...), custom_call_target="tpu_custom_call" | custom-call | flops 1000 | bytes 1000 | tf_op jit(solution)/shard_map/pallas_call | solution.py:1305
  467.3 4.8 copy_bitcast_fusion
  472.1 17.9 %shard_map.233 = (bf16[2048,256]{1,0:T(8,128)(2,1)}, f32[8,384]{1,0:T(8,128)}) custom-call(bf16[256,2048]{1,0:T(8,128)(2,1)} %get-tuple-element.102.x_ref, f32[8,384]{1,0:T(8,128)} %get-tuple-element.103.t_ref), custom_call_target="tpu_custom_call" | custom-call | flops 1000 | bytes 1000 | tf_op jit(solution)/shard_map/pallas_call | solution.py:640
  490.0 5.5 fusion.5
  495.6 1.4 collective-permute-start.4
  500.3 42.6 %shard_map.234 = bf16[2048,384]{1,0:T(8,128)(2,1)S(1)} custom-call(s32[16]{0:T(128)S(1)} %select_reduce_fusion.order_ref, bf16[2048,384]{1,0:T(8,128)(2,1)S(1)} %copy-done.1, bf16[2048,256]{1,0:T(8,128)(2,1)S(1)} %copy-done.3), custom_call_target="tpu_custom_call" | custom-call | flops 1000 | bytes 1000 | tf_op jit(solution)/shard_map/pallas_call | solution.py:558
  544.7 9.1 %convolution_convert_fusion.1 = bf16[2048,384]{1,0:T(8,128)(2,1)} fusion(bf16[2048,2048]{1,0:T(8,128)(2,1)} %get-tuple-element.114, bf16[2048,384]{1,0:T(8,128)(2,1)S(1)} %shard_map.234), kind=kOutput, calls=%fused_computation.6 | convolution fusion | flops 3222011904 | bytes 11534336 | tf_op jit(solution)/shard_map/dot_general | solution.py:360
  553.9 8.2 %convolution_convert_fusion = bf16[2048,2048]{1,0:T(8,128)(2,1)} fusion(bf16[2048,384]{1,0:T(8,128)(2,1)S(1)} %shard_map.234, bf16[2048,512]{1,0:T(8,128)(2,1)} %bitcast.99), kind=kOutput, calls=%fused_computation | convolution fusion | flops 3225419776 | bytes 11534336 | tf_op jit(solution)/shard_map/dot_general | solution.py:364
  562.1 4.5 fusion.11
  567.8 1.6 bitcast_convert_fusion
  569.3 41.4 %shard_map.235 = f32[256,2048]{1,0:T(8,128)} custom-call(bf16[8,256,2048]{2,1,0:T(8,128)(2,1)} %bitcast.93), custom_call_target="tpu_custom_call" | custom-call | flops 1000 | bytes 1000 | tf_op jit(solution)/shard_map/pallas_call | solution.py:246
  610.7 2.3 bitcast_convert_fusion.1
  613.1 7.7 %shard_map.236 = bf16[8,64,384]{2,1,0:T(8,128)(2,1)} custom-call(bf16[8,64,384]{2,1,0:T(8,128)(2,1)} %bitcast.107), custom_call_target="tpu_custom_call" | custom-call | flops 1000 | bytes 1000 | tf_op jit(solution)/shard_map/pallas_call | solution.py:328
  628.9 1.9 bitcast_convert_fusion.3
  631.5 1.5 fusion.4
  (120 shorter events, 26.9 us)
Async XLA Ops:
  7.2 179.3 %all-gather.7.cloned.1.call-start = ((), (), s32[]{:S(2)}) async-start(), calls=%async_computation.8 | async-start | bytes 1310720 | tf_op jit(solution)/shard_map/all_gather | solution.py:368
  7.9 267.5 %all-gather.9.cloned.1.call-start = ((), (), s32[]{:S(2)}) async-start(), calls=%async_computation.9 | async-start | bytes 10485760 | tf_op jit(solution)/shard_map/all_gather | solution.py:368
  11.1 2.3 copy-start.8
  11.1 310.9 %all-gather.11.cloned.1.call-start = ((), (), s32[]{:S(2)}) async-start(), calls=%async_computation.10 | async-start | bytes 5242880 | tf_op jit(solution)/shard_map/all_gather | solution.py:368
  11.8 487.3 %reduce-scatter.5.cloned.1.call-start = ((), (), s32[]{:S(2)}) async-start(), calls=%async_computation.4 | async-start | bytes 5242880 | tf_op jit(solution)/shard_map/reduce_scatter | solution.py:372
  132.1 11.8 %copy-start.25 = (s32[64]{0:T(128)S(1)}, s32[64]{0:T(128)}, u32[]{:S(2)}) copy-start(s32[64]{0:T(128)} %param.15) | copy-start | bytes 772
  132.1 11.8 %copy-start.26 = (s32[64]{0:T(128)S(1)}, s32[64]{0:T(128)}, u32[]{:S(2)}) copy-start(s32[64]{0:T(128)} %param.14) | copy-start | bytes 772
  144.3 1.4 copy-start
  186.5 39.9 %copy-start.5 = (bf16[256,2048]{1,0:T(8,128)(2,1)S(1)}, bf16[256,2048]{1,0:T(8,128)(2,1)}, u32[]{:S(2)}) copy-start(bf16[256,2048]{1,0:T(8,128)(2,1)} %tok_ref.1) | copy-start | bytes 3145732
  234.0 41.4 %copy-start.7 = (f32[256,2048]{1,0:T(8,128)}, f32[256,2048]{1,0:T(8,128)S(1)}, u32[]{:S(2)}) copy-start(f32[256,2048]{1,0:T(8,128)S(1)} %get-tuple-element.135.res_ref) | copy-start | bytes 6291460
  322.0 231.8 %reduce-scatter.7.cloned.1.call-start = ((), (), s32[]{:S(2)}) async-start(), calls=%async_computation.5 | async-start | bytes 10485760 | tf_op jit(solution)/shard_map/reduce_scatter | solution.py:372
  343.0 42.4 %collective-permute-start = (bf16[256,2048]{1,0:T(8,128)(2,1)}, bf16[256,2048]{1,0:T(8,128)(2,1)S(1)}, u32[]{:S(2)}, u32[]{:S(2)}) collective-permute-start(bf16[256,2048]{1,0:T(8,128)(2,1)} %get-tuple-element.90), channel_id=1, source_target_pairs={{0,6},{2,4},{4,2},{6,0},{1,7},{3,5},{5,3},{7,1},{8,14},{10,12},{12... | collective-permute-start | bytes 3145736 | tf_op jit(solution)/shard_map/ppermute | solution.py:274
  344.5 47.5 %collective-permute-start.1 = (bf16[256,2048]{1,0:T(8,128)(2,1)}, bf16[256,2048]{1,0:T(8,128)(2,1)S(1)}, u32[]{:S(2)}, u32[]{:S(2)}) collective-permute-start(bf16[256,2048]{1,0:T(8,128)(2,1)} %get-tuple-element.91), channel_id=1, source_target_pairs={{0,2},{2,0},{4,6},{6,4},{1,3},{3,1},{5,7},{7,5},{8,10},{10,8},{12,... | collective-permute-start | bytes 3145736 | tf_op jit(solution)/shard_map/ppermute | solution.py:274
  345.8 46.4 %collective-permute-start.2 = (bf16[256,2048]{1,0:T(8,128)(2,1)}, bf16[256,2048]{1,0:T(8,128)(2,1)S(1)}, u32[]{:S(2)}, u32[]{:S(2)}) collective-permute-start(bf16[256,2048]{1,0:T(8,128)(2,1)} %get-tuple-element.92), channel_id=1, source_target_pairs={{0,4},{2,6},{4,0},{6,2},{1,5},{3,7},{5,1},{7,3},{8,12},{10,14},{12... | collective-permute-start | bytes 3145736 | tf_op jit(solution)/shard_map/ppermute | solution.py:274
  385.5 6.7 %copy-start.14 = (bf16[256,2048]{1,0:T(8,128)(2,1)}, bf16[256,2048]{1,0:T(8,128)(2,1)S(1)}, u32[]{:S(2)}) copy-start(bf16[256,2048]{1,0:T(8,128)(2,1)S(1)} %collective-permute-done.refs_0_) | copy-start | bytes 3145732
  393.2 219.8 %reduce-scatter.9.cloned.1.call-start = ((), (), s32[]{:S(2)}) async-start(), calls=%async_computation.6 | async-start | bytes 1966080 | tf_op jit(solution)/shard_map/reduce_scatter | solution.py:372
  472.1 17.9 %collective-permute-start.3 = (bf16[4,4,64,2048]{3,2,0,1:T(8,128)(2,1)}, bf16[4,4,64,2048]{3,2,0,1:T(8,128)(2,1)}, u32[]{:S(2)}, u32[]{:S(2)}) collective-permute-start(bf16[4,4,64,2048]{3,2,0,1:T(8,128)(2,1)} %copy_bitcast_fusion), channel_id=1, source_target_pairs={{0,1},{1,0},{2,3},{3,2},{4,5},{5,4},{6,7},{7,6},{8,9},{9,8},{10,11... | collective-permute-start | bytes 12582920 | tf_op jit(solution)/shard_map/ppermute | solution.py:283
  490.0 9.1 %copy-start.1 = (bf16[2048,384]{1,0:T(8,128)(2,1)S(1)}, bf16[2048,384]{1,0:T(8,128)(2,1)}, u32[]{:S(2)}) copy-start(bf16[2048,384]{1,0:T(8,128)(2,1)} %get-tuple-element.74.qkv_ref) | copy-start | bytes 4718596
  495.6 47.3 %collective-permute-start.4 = (bf16[4,64,2048]{2,1,0:T(8,128)(2,1)}, bf16[4,64,2048]{2,1,0:T(8,128)(2,1)}, u32[]{:S(2)}, u32[]{:S(2)}) collective-permute-start(bf16[4,64,2048]{2,1,0:T(8,128)(2,1)} %get-tuple-element.105), channel_id=1, source_target_pairs={{0,6},{2,4},{4,2},{6,0},{1,7},{3,5},{5,3},{7,1},{8,14},{10,12},{12... | collective-permute-start | bytes 3145736 | tf_op jit(solution)/shard_map/ppermute | solution.py:274
  497.0 47.2 %collective-permute-start.5 = (bf16[4,64,2048]{2,1,0:T(8,128)(2,1)}, bf16[4,64,2048]{2,1,0:T(8,128)(2,1)}, u32[]{:S(2)}, u32[]{:S(2)}) collective-permute-start(bf16[4,64,2048]{2,1,0:T(8,128)(2,1)} %get-tuple-element.106), channel_id=1, source_target_pairs={{0,2},{2,0},{4,6},{6,4},{1,3},{3,1},{5,7},{7,5},{8,10},{10,8},{12,... | collective-permute-start | bytes 3145736 | tf_op jit(solution)/shard_map/ppermute | solution.py:274
  498.2 46.5 %collective-permute-start.6 = (bf16[4,64,2048]{2,1,0:T(8,128)(2,1)}, bf16[4,64,2048]{2,1,0:T(8,128)(2,1)}, u32[]{:S(2)}, u32[]{:S(2)}) collective-permute-start(bf16[4,64,2048]{2,1,0:T(8,128)(2,1)} %get-tuple-element.107), channel_id=1, source_target_pairs={{0,4},{2,6},{4,0},{6,2},{1,5},{3,7},{5,1},{7,3},{8,12},{10,14},{12... | collective-permute-start | bytes 3145736 | tf_op jit(solution)/shard_map/ppermute | solution.py:274
  553.8 67.0 %reduce-scatter.11.cloned.1.call-start = ((), (), s32[]{:S(2)}) async-start(), calls=%async_computation.7 | async-start | bytes 1310720 | tf_op jit(solution)/shard_map/reduce_scatter | solution.py:372
  562.1 4.6 copy-start.23
  562.1 5.7 copy-start.12
  569.3 41.4 %copy-start.10 = (bf16[1,2,2048,256]{3,2,1,0:T(8,128)(2,1)S(1)}, bf16[1,2,2048,256]{3,2,1,0:T(8,128)(2,1)}, u32[]{:S(2)}) copy-start(bf16[1,2,2048,256]{3,2,1,0:T(8,128)(2,1)} %reduce-scatter.7.cloned.1.call-done) | copy-start | bytes 6291460
  623.7 7.1 %copy-start.4 = (f32[256,2048]{1,0:T(8,128)S(1)}, f32[256,2048]{1,0:T(8,128)}, u32[]{:S(2)}) copy-start(f32[256,2048]{1,0:T(8,128)} %shard_map.235) | copy-start | bytes 6291460
  623.7 7.1 %copy-start.6 = (bf16[256,2048]{1,0:T(8,128)(2,1)S(1)}, bf16[256,2048]{1,0:T(8,128)(2,1)}, u32[]{:S(2)}) copy-start(bf16[256,2048]{1,0:T(8,128)(2,1)} %tok_ref.1) | copy-start | bytes 3145732
  623.8 7.5 %copy-start.17 = (f32[64,512]{1,0:T(8,128)}, f32[64,512]{1,0:T(8,128)S(1)}, u32[]{:S(2)}) copy-start(f32[64,512]{1,0:T(8,128)S(1)} %reshape.149) | copy-start | bytes 393220
  628.9 2.5 copy-start.18
  628.9 2.5 copy-start.20
  628.9 2.5 copy-start.22
  628.9 2.6 copy-start.9
  (10 other events, 10.2 us)
Sparse Core Ops, SparseCore 0:
  9.6 35.5 all-gather.6
  47.4 163.7 all-gather.8
  212.7 80.5 all-gather.10
  322.1 74.0 reduce-scatter.4
  398.5 145.7 reduce-scatter.6
  553.9 34.3 reduce-scatter.8
  591.3 26.1 reduce-scatter.10

commit v12 on v11

--- a/solution.py
+++ b/solution.py
@@ -275,11 +275,10 @@
 
 
 class Drift:
-    def __init__(self, pairs, axis):
+    def __init__(self, mine, away, axis):
         self.axis = axis
         self.chip, self.core = place()
-        away = lax.dynamic_index_in_dim(pairs, 1 - self.core, axis + 1, keepdims=False)
-        self.mine = lax.dynamic_index_in_dim(pairs, self.core, axis + 1, keepdims=False)
+        self.mine = mine
         self.twin = lax.ppermute(away, "core", [(0, 1), (1, 0)])
 
     def part(self, step):
@@ -1097,8 +1096,8 @@
 
 
 def entry_kernel(
-    grps, chips, tok_ref, cot_ref, pack_ref, all_tok, all_cot, all_pack,
-    tsend, trecv, tlocal, csend, crecv, clocal, psend, precv, plocal, zsend, zrecv, usend, dsend,
+    grps, chips, tok_ref, cot_ref, pack_ref, tile_ref, all_tok, all_cot, all_pack, all_tile,
+    tsend, trecv, tlocal, csend, crecv, clocal, psend, precv, plocal, zrecv, usend, dsend,
 ):
     grp = lax.axis_index("grp")
     chip, core = place()
@@ -1117,58 +1116,68 @@
 
     tok = Gather(chips, False, tok_ref, all_tok, tsend, trecv, tlocal)
     cot = Gather(chips, False, cot_ref, all_cot, csend, crecv, clocal)
-    packs = []
+    packs, mine = [], []
     for i, (to, c) in enumerate(near):
         copy = remote(
-            pack_ref.at[to * 2 + c], all_pack.at[grp, me], psend.at[i], precv.at[me], to, c
+            pack_ref.at[to * 2 + c], all_pack.at[grp, me], psend.at[0, i], precv.at[0, me], to, c
         )
         copy.start()
         packs.append(copy)
-    mine = pltpu.make_async_copy(pack_ref.at[me], all_pack.at[grp, me], plocal)
-    mine.start()
+        copy = remote(tile_ref, all_tile.at[grp, me], psend.at[1, i], precv.at[1, me], to, c)
+        copy.start()
+        packs.append(copy)
+    for k, (src, dst) in enumerate(((pack_ref.at[me], all_pack), (tile_ref, all_tile))):
+        mine.append(pltpu.make_async_copy(src, dst.at[grp, me], plocal.at[k]))
+        mine[k].start()
     tok.start()
-    cot.start()
     for to, c in near:
         slot = to * 2 + c
-        remote(
-            pack_ref.at[me], all_pack.at[grp, slot], psend.at[0], precv.at[slot], to, c
-        ).wait_recv()
-    mine.wait()
-
-    def z_copy(block, sem, to):
-        return pltpu.make_async_remote_copy(
-            src_ref=all_pack.at[block],
-            dst_ref=all_pack.at[block],
-            send_sem=sem,
-            recv_sem=zrecv.at[block],
-            device_id={"grp": to},
-            device_id_type=MESH,
-        )
+        for k, (src, dst) in enumerate(((pack_ref.at[me], all_pack), (tile_ref, all_tile))):
+            remote(src, dst.at[grp, slot], psend.at[k, 0], precv.at[k, slot], to, c).wait_recv()
+    for copy in mine:
+        copy.wait()
+
+    def z_copies(block, sems, step, to):
+        return [
+            pltpu.make_async_remote_copy(
+                src_ref=whole.at[block],
+                dst_ref=whole.at[block],
+                send_sem=sems.at[k, step],
+                recv_sem=zrecv.at[k, block],
+                device_id={"grp": to},
+                device_id_type=MESH,
+            )
+            for k, whole in enumerate((all_pack, all_tile))
+        ]
 
     has_above, has_below = grp + 1 < grps, grp > 0
 
     def send(step, block, up):
         @pl.when(has_above if up else has_below)
         def _():
-            z_copy(block, (usend if up else dsend).at[step], above if up else below).start()
+            for copy in z_copies(block, usend if up else dsend, step, above if up else below):
+                copy.start()
 
     def relay(step):
         low, high = grp - step, grp + step
 
         @pl.when(low >= 0)
         def _():
-            z_copy(low, zsend, below).wait_recv()
+            for copy in z_copies(low, usend, 0, below):
+                copy.wait_recv()
             send(step, low, True)
 
         @pl.when(high < grps)
         def _():
-            z_copy(high, zsend, above).wait_recv()
+            for copy in z_copies(high, dsend, 0, above):
+                copy.wait_recv()
             send(step, high, False)
 
     send(0, grp, True)
     send(0, grp, False)
     tok.relay(0, 4)
     relay(1)
+    cot.start()
     tok.relay(4, None)
     for step in range(2, grps - 1):
         relay(step)
@@ -1187,10 +1196,12 @@
             @pl.when(held & (has_above if up else has_below))
             def _(step=step, up=up):
                 block = grp - step if up else grp + step
-                z_copy(block, (usend if up else dsend).at[step], above if up else below).wait_send()
-
-
-def entry(tokens, cotangent, packed, grps, chips, call_id):
+                sems, to = (usend, above) if up else (dsend, below)
+                for copy in z_copies(block, sems, step, to):
+                    copy.wait_send()
+
+
+def entry(tokens, cotangent, packed, tile, grps, chips, call_id):
     devs = 2 * chips
     return pl.pallas_call(
         functools.partial(entry_kernel, grps, chips),
@@ -1198,42 +1209,45 @@
             jax.ShapeDtypeStruct((devs,) + tokens.shape, BF16),
             jax.ShapeDtypeStruct((devs,) + cotangent.shape, BF16),
             jax.ShapeDtypeStruct((grps,) + packed.shape, BF16),
+            jax.ShapeDtypeStruct((grps, devs) + tile.shape, BF16),
         ),
-        in_specs=[ANY] * 3,
-        out_specs=(ANY,) * 3,
+        in_specs=[ANY] * 4,
+        out_specs=(ANY,) * 4,
         scratch_shapes=gather_sems(chips)
         + gather_sems(chips)
         + [
-            pltpu.SemaphoreType.DMA((devs,)),
-            pltpu.SemaphoreType.DMA((devs,)),
-            pltpu.SemaphoreType.DMA,
-            pltpu.SemaphoreType.DMA,
-            pltpu.SemaphoreType.DMA((grps,)),
-            pltpu.SemaphoreType.DMA((grps,)),
-            pltpu.SemaphoreType.DMA((grps,)),
+            pltpu.SemaphoreType.DMA((2, devs)),
+            pltpu.SemaphoreType.DMA((2, devs)),
+            pltpu.SemaphoreType.DMA((2,)),
+            pltpu.SemaphoreType.DMA((2, grps)),
+            pltpu.SemaphoreType.DMA((2, grps)),
+            pltpu.SemaphoreType.DMA((2, grps)),
         ],
         cost_estimate=BRIEF,
         compiler_params=pltpu.CompilerParams(collective_id=call_id, has_side_effects=True),
-    )(tokens, cotangent, packed)
-
-
-def project_kernel(used, x_ref, w_ref, n_ref, qkv_ref, gain_ref):
+    )(tokens, cotangent, packed, tile)
+
+
+def project_kernel(width, x_ref, w_ref, tile_ref, n_ref, qkv_ref, gain_ref):
     @pl.when(pl.program_id(0) == 0)
     def _():
-        gain_ref[...] = w_ref[:, used:].astype(F32).T[:8]
+        gain_ref[...] = jnp.zeros_like(gain_ref)
+        for f in range(tile_ref.shape[0]):
+            gain_ref[0:2, f * width : (f + 1) * width] = tile_ref[f, 0:2, :width].astype(F32)
 
     values = x_ref[...].astype(F32)
     factor = lax.rsqrt(jnp.mean(values * values, axis=-1, keepdims=True) + EPSILON)
     normed = (values * factor * gain_ref[0:1]).astype(BF16)
     n_ref[...] = normed
-    qkv_ref[...] = matmul(normed, w_ref[:, :used]).astype(BF16)
-
-
-def project(tokens, packed, used):
+    qkv_ref[...] = matmul(normed, w_ref[...]).astype(BF16)
+
+
+def project(tokens, weights, tiles):
     count, depth = tokens.shape
+    used = weights.shape[1]
     rows = tile_rows(count, 256)
     return pl.pallas_call(
-        functools.partial(project_kernel, used),
+        functools.partial(project_kernel, depth // tiles.shape[0]),
         out_shape=(
             jax.ShapeDtypeStruct((count, depth), BF16),
             jax.ShapeDtypeStruct((count, used), BF16),
@@ -1242,7 +1256,8 @@
         grid=(count // rows,),
         in_specs=[
             pl.BlockSpec((rows, depth), lambda r: (r, 0)),
-            pl.BlockSpec(packed.shape, lambda r: (0, 0)),
+            pl.BlockSpec(weights.shape, lambda r: (0, 0)),
+            pl.BlockSpec(tiles.shape, lambda r: (0, 0, 0)),
         ],
         out_specs=(
             pl.BlockSpec((rows, depth), lambda r: (r, 0)),
@@ -1251,13 +1266,13 @@
         ),
         cost_estimate=BRIEF,
         compiler_params=params(1),
-    )(tokens, packed)
+    )(tokens, weights, tiles)
 
 
 def turn_kernel(
     count, res_ref, dn_ref, cot_ref, gain_ref, branch_ref, own_ref, *refs
 ):
-    came, (att_ref, w_ref, lay_ref, dres_ref, tot_ref, datt_ref, grad_ref, dba) = refs[:count], refs[count:]
+    came, (att_ref, w_ref, lay_ref, dres_ref, tot_ref, datt_ref, *grad_refs, dba) = refs[:count], refs[count:]
 
     @pl.when(pl.program_id(0) == 0)
     def _():
@@ -1291,12 +1306,31 @@
         tot_ref[7:8, :128] = row
 
     datt_ref[...] = dot_nt(dba[...], w_ref[...]).astype(BF16)
-    grad_ref[...] = matmul(att_ref[...].T, dba[...]).astype(BF16)
-
-
-def turn(residual, d_normed, cotangent, gains, branch, own, came, attended, weights):
+    grad = matmul(att_ref[...].T, dba[...])
+    if len(grad_refs) == 1:
+        grad_refs[0][...] = grad.astype(BF16)
+        return
+    mine_ref, away_ref, acc = grad_refs
+    acc[...] = grad
+    core = lax.axis_index("core")
+    width = mine_ref.shape[2]
+    for i in range(mine_ref.shape[1]):
+        for ref, c in ((mine_ref, core), (away_ref, 1 - core)):
+            at = pl.multiple_of((2 * i + c) * width, width)
+            ref[0, i] = acc[pl.ds(at, width)].astype(BF16)
+
+
+def turn(residual, d_normed, cotangent, gains, branch, own, came, attended, weights, width):
     rows = residual.shape[0]
-    cols = 256
+    cols = 4 * width if came else 256
+    scratch = [pltpu.VMEM((rows, D), BF16)]
+    grads = (jax.ShapeDtypeStruct((D, D), BF16),)
+    grad_specs = (pl.BlockSpec((cols, D), lambda j: (j, 0)),)
+    if came:
+        half = (D // (8 * width), 4, width, D)
+        grads = (jax.ShapeDtypeStruct(half, BF16),) * 2
+        grad_specs = (pl.BlockSpec((1, 2, width, D), lambda j: (j // 2, j % 2, 0, 0)),) * 2
+        scratch = [pltpu.VMEM((cols, D), F32)] + scratch
     flat = jax.ShapeDtypeStruct((rows, D), F32)
 
     def held(shape):
@@ -1309,8 +1343,8 @@
             flat,
             jax.ShapeDtypeStruct((8, 3 * D // 16), F32),
             jax.ShapeDtypeStruct((rows, D), BF16),
-            jax.ShapeDtypeStruct((D, D), BF16),
-        ),
+        )
+        + grads,
         grid=(D // cols,),
         in_specs=[held((rows, D))] * 3
         + [held((8, D))]
@@ -1324,9 +1358,9 @@
             held((rows, D)),
             held((8, 3 * D // 16)),
             pl.BlockSpec((rows, cols), lambda j: (0, j)),
-            pl.BlockSpec((cols, D), lambda j: (j, 0)),
-        ),
-        scratch_shapes=[pltpu.VMEM((rows, D), BF16)],
+        )
+        + grad_specs,
+        scratch_shapes=scratch,
         cost_estimate=BRIEF,
         compiler_params=params(1),
     )(residual, d_normed, cotangent, gains, branch, own, *came, attended, weights)
@@ -1384,23 +1418,21 @@
         w = w.reshape(w_rows, devs // kv_copies, kv_cols)
         return jnp.repeat(w, kv_copies, axis=1) if kv_copies > 1 else w
 
-    gains = jnp.stack([attn_gain, mlp_gain], axis=1)
-    cols = D // 4
-    room = cols - q_cols - 2 * kv_cols
-    gains = jnp.pad(gains, ((0, 0), (0, room - 2)))
-    gains = jnp.broadcast_to(gains[:, None, :], (w_rows, devs, room))
     packed = jnp.concatenate(
-        [w_query.reshape(w_rows, devs, q_cols), kv_split(w_key), kv_split(w_value), gains], axis=2
+        [w_query.reshape(w_rows, devs, q_cols), kv_split(w_key), kv_split(w_value)], axis=2
     )
     packed = jnp.swapaxes(packed, 0, 1)
     used = q_cols + 2 * kv_cols
+    tile = jnp.pad(jnp.stack([attn_gain, mlp_gain]), ((0, 14), (0, 128 - w_rows)))
     out_full = gather(w_out[None], "grp")
     upstream = cotangent.astype(F32)
     d_branch_mlp = (RESID_MULT * upstream).astype(BF16)
-    all_tokens, d_branch_mlp, packed = entry(tokens, d_branch_mlp, packed, grps, chips, 2)
-    packed = packed.reshape(D, cols)
-    normed_one, qkv, gains = project(all_tokens.reshape(devs * rows, D), packed, used)
-    gain_one, gain_two, w_qkv = gains[0], gains[1], packed[:, :used]
+    all_tokens, d_branch_mlp, w_qkv, tiles = entry(
+        tokens, d_branch_mlp, packed, tile, grps, chips, 2
+    )
+    w_qkv, tiles = w_qkv.reshape(D, used), tiles.reshape(-1, 16, 128)
+    normed_one, qkv, gains = project(all_tokens.reshape(devs * rows, D), w_qkv, tiles)
+    gain_one, gain_two = gains[0], gains[1]
     d_branch_mlp = d_branch_mlp.reshape(devs * rows, D)
     attended = attend(qkv, order, q_heads)
     attended = plane_exchange(
@@ -1441,7 +1473,7 @@
         branch_mlp = mix(hidden, down_w)
         branch_mlp = plane_reduce(branch_mlp.reshape(devs, rows, D), chips, 5)
 
-    layer_out, d_residual, totals, d_attended, grad_out = turn(
+    layer_out, d_residual, totals, d_attended, grad_out, *away = turn(
         residual,
         d_normed_two,
         cotangent,
@@ -1451,9 +1483,10 @@
         shares if chips == 4 else (),
         attended,
         out_full,
+        w_rows,
     )
     if chips == 4:
-        drift_out = Drift(grad_out.reshape(grps, 4, 2, w_rows, D), 1)
+        drift_out = Drift(grad_out, *away, 1)
     d_attended, totals = exchange_total(
         d_attended, totals, (devs * rows, q_cols), rows, q_cols, grps, chips, 7
     )

time: 651 us -> 615 us (0.945)
  Pallas kernels: 538 us -> 506 us
    pallas_call x1, Pallas kernels: 118 us -> 83.1 us  [entry(): pl.pallas_call(functools.partial(entry_kernel, grps, chips), out_shape=(j...]
where the time goes in v12:
time: 615 us; the launch traced here: 605 us
  Pallas kernels  506 us (82%)
  other arithmetic  30.6 us (5%)
  matrix products  23.7 us (4%)
  between operations  15.1 us (2%)
  local copies, waits for them, and re-layouts  12.3 us (2%)
  waiting for transfers between devices  9.71 us (2%)
  starting transfers between devices  7.35 us (1%)
    pallas_call x1, Pallas kernels, entry(): pl.pallas_call(functools.partial(entry_kernel, grps, chips), out_shape=(j...  83.1 us
    pallas_call x2, Pallas kernels, plane_gather(): pl.pallas_call(functools.partial(gather_kernel, chips, inner), out_shape=...  79.8 us
    pallas_call x1, Pallas kernels, square_reduce(): pl.pallas_call(functools.partial(square_kernel, compute, len(operands)),...  54.3 us
    pallas_call x1, Pallas kernels, attend_back(): pl.pallas_call(functools.partial(attend_back_kernel, heads), out_shape=ja...  42.5 us
    pallas_call x1, Pallas kernels, plane_reduce(): pl.pallas_call(functools.partial(reduce_kernel, chips, inner), out_shape=...  41.4 us
    pallas_call x1, Pallas kernels, widen(): pl.pallas_call(widen_kernel, out_shape=(tall, jax.ShapeDtypeStruct((shard...  30.8 us
    pallas_call x1, Pallas kernels, widen_part(): pl.pallas_call(widen_part_kernel, out_shape=jax.ShapeDtypeStruct((shards,...  23.6 us
    pallas_call x1, Pallas kernels, attend(): pl.pallas_call(functools.partial(attend_kernel, heads), out_shape=jax.Sha...  23.3 us
  transfers between devices with their start and end apart: 14, of which 4 were waited for; matrix products, arithmetic and copies ran while one was open for 8% of the time, Pallas kernels for 84%

profile of v12, /device:TPU:0, one launch (start us, length us, event | category | flops | bytes accessed | tf_op | source)
XLA Modules:
  0.0 605.2 jit_solution(16623829722358866772)
XLA Ops:
  8.0 3.1 pad_maximum_fusion
  14.9 83.1 %shard_map.220 = (bf16[8,256,2048]{2,1,0:T(8,128)(2,1)}, bf16[8,256,2048]{2,1,0:T(8,128)(2,1)}, bf16[4,8,64,384]{3,2,1,0:T(8,128)(2,1)}, bf16[4,8,16,128]{3,2,1,0:T(8,128)(2,1)}) custom-call(bf16[256,2048]{1,0:T(8,128)(2,1)} %tok_ref.1, bf16[256,2048]{1,0:T(8,128)(2,1)} %multiply_convert_fusion.1.cot_ref, bf16[8,64,384]{2,1,0:T(8,128)(2,1)} %maximum_bitcast_fusion.pack_ref, ...), custom_call_target="tpu_custom_call" | custom-call | flops 1000 | bytes 1000 | tf_op jit(solution)/shard_map/pallas_call | solution.py:1206
  98.0 11.5 %shard_map.221 = (bf16[2048,2048]{1,0:T(8,128)(2,1)}, bf16[2048,384]{1,0:T(8,128)(2,1)}, f32[8,2048]{1,0:T(8,128)}) custom-call(bf16[2048,2048]{1,0:T(8,128)(2,1)} %bitcast.81, bf16[2048,384]{1,0:T(8,128)(2,1)} %bitcast.84, bf16[32,16,128]{2,1,0:T(8,128)(2,1)} %bitcast.92), custom_call_target="tpu_custom_call" | custom-call | flops 1000 | bytes 1000 | tf_op jit(solution)/shard_map/pallas_call | solution.py:1249
  109.9 1.4 copy-done
  111.4 23.3 %shard_map.222.x_ref = bf16[2048,256]{1,0:T(8,128)(2,1)S(1)} custom-call(s32[16]{0:T(128)S(1)} %select_reduce_fusion.order_ref, bf16[2048,384]{1,0:T(8,128)(2,1)S(1)} %copy-done), custom_call_target="tpu_custom_call" | custom-call | flops 1000 | bytes 1000 | tf_op jit(solution)/shard_map/pallas_call | solution.py:535
  135.7 15.6 %shard_map.223.refs_3_ = bf16[256,2048]{1,0:T(8,128)(2,1)} custom-call(bf16[2048,256]{1,0:T(8,128)(2,1)} %copy-done.2), custom_call_target="tpu_custom_call" | custom-call | flops 1000 | bytes 1000 | tf_op jit(solution)/shard_map/pallas_call | solution.py:327
  152.2 39.9 %shard_map.224 = bf16[4,8,64,2048]{3,2,1,0:T(8,128)(2,1)} custom-call(bf16[4,64,2048]{2,1,0:T(8,128)(2,1)} %bitcast.86), custom_call_target="tpu_custom_call" | custom-call | flops 1000 | bytes 1000 | tf_op jit(solution)/shard_map/pallas_call | solution.py:160
  192.1 7.5 %multiply_reduce_fusion = (f32[256]{0:T(256)S(1)}, f32[256,2048]{1,0:T(8,128)S(1)}, f32[256,2048]{1,0:T(8,128)}) fusion(bf16[256,2048]{1,0:T(8,128)(2,1)S(1)} %copy-done.5, bf16[256,2048]{1,0:T(8,128)(2,1)} %shard_map.223.refs_3_, bf16[2048,2048]{1,0:T(8,128)(2,1)} %bitcast.73), kind=kOutput, calls=%fused_computation.20 | convolution fusion | flops 2150104832 | bytes 14681088 | tf_op jit(solution)/shard_map/dot_general | solution.py:355
  201.0 40.0 %shard_map.225 = bf16[8,256,2048]{2,1,0:T(8,128)(2,1)} custom-call(bf16[256,2048]{1,0:T(8,128)(2,1)} %multiply_convert_fusion.x_ref), custom_call_target="tpu_custom_call" | custom-call | flops 1000 | bytes 1000 | tf_op jit(solution)/shard_map/pallas_call | solution.py:160
  241.0 30.8 %shard_map.226 = (bf16[4,2048,256]{2,1,0:T(8,128)(2,1)}, bf16[4,256,2048]{2,1,0:T(8,128)(2,1)}, bf16[4,2048,256]{2,1,0:T(8,128)(2,1)}, bf16[4,2048,256]{2,1,0:T(8,128)(2,1)}, bf16[2048,2048]{1,0:T(8,128)(2,1)}) custom-call(bf16[2048,2048]{1,0:T(8,128)(2,1)} %bitcast.77, bf16[4,2,2048,256]{3,2,1,0:T(8,128)(2,1)} %bitcast.71), custom_call_target="tpu_custom_call" | custom-call | flops 1000 | bytes 1000 | tf_op jit(solution)/shard_map/pallas_call | solution.py:697
  271.8 15.9 %shard_map.227 = bf16[4,256,2048]{2,1,0:T(8,128)(2,1)} custom-call(bf16[4,256,2048]{2,1,0:T(8,128)(2,1)} %get-tuple-element.80.ht_ref, bf16[2048,2048]{1,0:T(8,128)(2,1)} %bitcast.75), custom_call_target="tpu_custom_call" | custom-call | flops 1000 | bytes 1000 | tf_op jit(solution)/shard_map/pallas_call | solution.py:731
  287.8 20.8 %shard_map.228 = (f32[256,2048]{1,0:T(8,128)}, bf16[256,2048]{1,0:T(8,128)(2,1)}, bf16[256,2048]{1,0:T(8,128)(2,1)}, bf16[256,2048]{1,0:T(8,128)(2,1)}) custom-call(bf16[4,2048,256]{2,1,0:T(8,128)(2,1)} %get-tuple-element.84.refs_0_, bf16[4,256,2048]{2,1,0:T(8,128)(2,1)} %bitcast.78), custom_call_target="tpu_custom_call" | custom-call | flops 1000 | bytes 1000 | tf_op jit(solution)/shard_map/pallas_call | solution.py:1067
  308.6 1.8 collective-permute-start
  312.1 15.6 %shard_map.229 = (bf16[4,2048,256]{2,1,0:T(8,128)(2,1)}, bf16[4,2048,256]{2,1,0:T(8,128)(2,1)}) custom-call(bf16[4,2048,256]{2,1,0:T(8,128)(2,1)} %get-tuple-element.89.s_ref, bf16[4,2048,256]{2,1,0:T(8,128)(2,1)} %get-tuple-element.90.t_ref, bf16[2048,2048]{1,0:T(8,128)(2,1)} %bitcast.76, bf16[4,256,2048]{2,1,0:T(8,128)(2,1)} %bitcast.79), custom_call_target="tpu_custom_call" | custom-call | flops 1000 | bytes 1000 | tf_op jit(solution)/shard_map/pallas_call | solution.py:789
  327.7 23.6 %shard_map.230 = bf16[4,2,2048,256]{3,2,1,0:T(8,128)(2,1)} custom-call(bf16[2048,2048]{1,0:T(8,128)(2,1)} %get-tuple-element.79.nt_ref, bf16[4,2048,256]{2,1,0:T(8,128)(2,1)} %get-tuple-element.96.dg_ref.refs_0_, bf16[4,2048,256]{2,1,0:T(8,128)(2,1)} %get-tuple-element.97.du_ref.refs_1_), custom_call_target="tpu_custom_call" | custom-call | flops 1000 | bytes 1000 | tf_op jit(solution)/shard_map/pallas_call | solution.py:811
  351.4 5.5 collective-permute-done.1.refs_1_
  358.7 54.3 %shard_map.231.dn_ref = f32[256,2048]{1,0:T(8,128)} custom-call(bf16[4,2048,256]{2,1,0:T(8,128)(2,1)} %get-tuple-element.96.dg_ref.refs_0_, bf16[4,2048,256]{2,1,0:T(8,128)(2,1)} %get-tuple-element.97.du_ref.refs_1_, bf16[4,2,2048,256]{3,2,1,0:T(8,128)(2,1)} %bitcast.72), custom_call_target="tpu_custom_call" | custom-call | flops 1000 | bytes 1000 | tf_op jit(solution)/shard_map/pallas_call | solution.py:973
  413.1 22.1 %shard_map.232 = (bf16[256,2048]{1,0:T(8,128)(2,1)}, f32[256,2048]{1,0:T(8,128)}, f32[8,384]{1,0:T(8,128)}, bf16[256,2048]{1,0:T(8,128)(2,1)}, bf16[4,4,64,2048]...) custom-call(f32[256,2048]{1,0:T(8,128)} %copy-done.7, f32[256,2048]{1,0:T(8,128)} %shard_map.231.dn_ref, ...), custom_call_target="tpu_custom_call" | custom-call | flops 1000 | bytes 1000 | tf_op jit(solution)/shard_map/pallas_call | solution.py:1339
  435.2 18.5 %shard_map.233 = (bf16[2048,256]{1,0:T(8,128)(2,1)}, f32[8,384]{1,0:T(8,128)}) custom-call(bf16[256,2048]{1,0:T(8,128)(2,1)} %get-tuple-element.106.x_ref, f32[8,384]{1,0:T(8,128)} %get-tuple-element.107.t_ref), custom_call_target="tpu_custom_call" | custom-call | flops 1000 | bytes 1000 | tf_op jit(solution)/shard_map/pallas_call | solution.py:639
  453.7 2.9 fusion.10
  456.6 4.5 fusion.9
  461.1 1.5 collective-permute-start.4
  465.9 42.5 %shard_map.234 = bf16[2048,384]{1,0:T(8,128)(2,1)S(1)} custom-call(s32[16]{0:T(128)S(1)} %select_reduce_fusion.order_ref, bf16[2048,384]{1,0:T(8,128)(2,1)S(1)} %copy-done.1, bf16[2048,256]{1,0:T(8,128)(2,1)S(1)} %copy-done.3), custom_call_target="tpu_custom_call" | custom-call | flops 1000 | bytes 1000 | tf_op jit(solution)/shard_map/pallas_call | solution.py:557
  510.2 9.3 %convolution_convert_fusion.1 = bf16[2048,384]{1,0:T(8,128)(2,1)} fusion(bf16[2048,2048]{1,0:T(8,128)(2,1)} %get-tuple-element.118, bf16[2048,384]{1,0:T(8,128)(2,1)S(1)} %shard_map.234), kind=kOutput, calls=%fused_computation.5 | convolution fusion | flops 3222011904 | bytes 11534336 | tf_op jit(solution)/shard_map/dot_general | solution.py:359
  519.7 6.9 %convolution_convert_fusion = bf16[2048,2048]{1,0:T(8,128)(2,1)} fusion(bf16[2048,384]{1,0:T(8,128)(2,1)S(1)} %shard_map.234, bf16[2048,384]{1,0:T(8,128)(2,1)S(1)} %bitcast.85), kind=kOutput, calls=%fused_computation | convolution fusion | flops 3225419776 | bytes 11534336 | tf_op jit(solution)/shard_map/dot_general | solution.py:363
  526.5 4.5 fusion.7
  532.2 1.6 bitcast_convert_fusion
  533.8 41.4 %shard_map.235 = f32[256,2048]{1,0:T(8,128)} custom-call(bf16[8,256,2048]{2,1,0:T(8,128)(2,1)} %bitcast.80), custom_call_target="tpu_custom_call" | custom-call | flops 1000 | bytes 1000 | tf_op jit(solution)/shard_map/pallas_call | solution.py:246
  575.2 2.3 bitcast_convert_fusion.1
  577.6 7.6 %shard_map.236 = bf16[8,64,384]{2,1,0:T(8,128)(2,1)} custom-call(bf16[8,64,384]{2,1,0:T(8,128)(2,1)} %bitcast.91), custom_call_target="tpu_custom_call" | custom-call | flops 1000 | bytes 1000 | tf_op jit(solution)/shard_map/pallas_call | solution.py:327
  593.3 1.9 bitcast_convert_fusion.3
  595.9 1.5 fusion.4
  (119 shorter events, 27.5 us)
Async XLA Ops:
  7.2 145.0 %all-gather.7.cloned.1.call-start = ((), (), s32[]{:S(2)}) async-start(), calls=%async_computation.8 | async-start | bytes 1310720 | tf_op jit(solution)/shard_map/all_gather | solution.py:367
  7.9 233.1 %all-gather.9.cloned.1.call-start = ((), (), s32[]{:S(2)}) async-start(), calls=%async_computation.9 | async-start | bytes 10485760 | tf_op jit(solution)/shard_map/all_gather | solution.py:367
  11.1 2.7 copy-start.8
  11.1 276.7 %all-gather.11.cloned.1.call-start = ((), (), s32[]{:S(2)}) async-start(), calls=%async_computation.10 | async-start | bytes 5242880 | tf_op jit(solution)/shard_map/all_gather | solution.py:367
  11.8 452.8 %reduce-scatter.5.cloned.1.call-start = ((), (), s32[]{:S(2)}) async-start(), calls=%async_computation.4 | async-start | bytes 5242880 | tf_op jit(solution)/shard_map/reduce_scatter | solution.py:371
  98.0 11.5 %copy-start.27 = (s32[64]{0:T(128)S(1)}, s32[64]{0:T(128)}, u32[]{:S(2)}) copy-start(s32[64]{0:T(128)} %param.15) | copy-start | bytes 772
  98.0 11.5 %copy-start.28 = (s32[64]{0:T(128)S(1)}, s32[64]{0:T(128)}, u32[]{:S(2)}) copy-start(s32[64]{0:T(128)} %param.14) | copy-start | bytes 772
  152.2 39.9 %copy-start.5 = (bf16[256,2048]{1,0:T(8,128)(2,1)S(1)}, bf16[256,2048]{1,0:T(8,128)(2,1)}, u32[]{:S(2)}) copy-start(bf16[256,2048]{1,0:T(8,128)(2,1)} %tok_ref.1) | copy-start | bytes 3145732
  199.6 41.4 %copy-start.7 = (f32[256,2048]{1,0:T(8,128)}, f32[256,2048]{1,0:T(8,128)S(1)}, u32[]{:S(2)}) copy-start(f32[256,2048]{1,0:T(8,128)S(1)} %get-tuple-element.139.res_ref) | copy-start | bytes 6291460
  287.7 231.9 %reduce-scatter.7.cloned.1.call-start = ((), (), s32[]{:S(2)}) async-start(), calls=%async_computation.5 | async-start | bytes 10485760 | tf_op jit(solution)/shard_map/reduce_scatter | solution.py:371
  308.6 42.8 %collective-permute-start = (bf16[256,2048]{1,0:T(8,128)(2,1)}, bf16[256,2048]{1,0:T(8,128)(2,1)S(1)}, u32[]{:S(2)}, u32[]{:S(2)}) collective-permute-start(bf16[256,2048]{1,0:T(8,128)(2,1)} %get-tuple-element.93), channel_id=1, source_target_pairs={{0,6},{2,4},{4,2},{6,0},{1,7},{3,5},{5,3},{7,1},{8,14},{10,12},{12... | collective-permute-start | bytes 3145736 | tf_op jit(solution)/shard_map/ppermute | solution.py:274
  310.4 46.4 %collective-permute-start.1 = (bf16[256,2048]{1,0:T(8,128)(2,1)}, bf16[256,2048]{1,0:T(8,128)(2,1)S(1)}, u32[]{:S(2)}, u32[]{:S(2)}) collective-permute-start(bf16[256,2048]{1,0:T(8,128)(2,1)} %get-tuple-element.94), channel_id=1, source_target_pairs={{0,2},{2,0},{4,6},{6,4},{1,3},{3,1},{5,7},{7,5},{8,10},{10,8},{12,... | collective-permute-start | bytes 3145736 | tf_op jit(solution)/shard_map/ppermute | solution.py:274
  310.9 46.8 %collective-permute-start.2 = (bf16[256,2048]{1,0:T(8,128)(2,1)}, bf16[256,2048]{1,0:T(8,128)(2,1)S(1)}, u32[]{:S(2)}, u32[]{:S(2)}) collective-permute-start(bf16[256,2048]{1,0:T(8,128)(2,1)} %get-tuple-element.95), channel_id=1, source_target_pairs={{0,4},{2,6},{4,0},{6,2},{1,5},{3,7},{5,1},{7,3},{8,12},{10,14},{12... | collective-permute-start | bytes 3145736 | tf_op jit(solution)/shard_map/ppermute | solution.py:274
  351.4 6.4 %copy-start.15 = (bf16[256,2048]{1,0:T(8,128)(2,1)}, bf16[256,2048]{1,0:T(8,128)(2,1)S(1)}, u32[]{:S(2)}) copy-start(bf16[256,2048]{1,0:T(8,128)(2,1)S(1)} %collective-permute-done.refs_0_) | copy-start | bytes 3145732
  358.7 218.9 %reduce-scatter.9.cloned.1.call-start = ((), (), s32[]{:S(2)}) async-start(), calls=%async_computation.6 | async-start | bytes 1966080 | tf_op jit(solution)/shard_map/reduce_scatter | solution.py:371
  435.1 18.6 %collective-permute-start.3 = (bf16[4,4,64,2048]{3,2,1,0:T(8,128)(2,1)}, bf16[4,4,64,2048]{3,2,1,0:T(8,128)(2,1)}, u32[]{:S(2)}, u32[]{:S(2)}) collective-permute-start(bf16[4,4,64,2048]{3,2,1,0:T(8,128)(2,1)} %get-tuple-element.105), channel_id=1, source_target_pairs={{0,1},{1,0},{2,3},{3,2},{4,5},{5,4},{6,7},{7,6},{8,9},{9,8},{10,11... | collective-permute-start | bytes 12582920 | tf_op jit(solution)/shard_map/ppermute | solution.py:282
  456.6 8.0 %copy-start.1 = (bf16[2048,384]{1,0:T(8,128)(2,1)S(1)}, bf16[2048,384]{1,0:T(8,128)(2,1)}, u32[]{:S(2)}) copy-start(bf16[2048,384]{1,0:T(8,128)(2,1)} %get-tuple-element.77.qkv_ref) | copy-start | bytes 4718596
  461.1 47.3 %collective-permute-start.4 = (bf16[4,64,2048]{2,1,0:T(8,128)(2,1)}, bf16[4,64,2048]{2,1,0:T(8,128)(2,1)}, u32[]{:S(2)}, u32[]{:S(2)}) collective-permute-start(bf16[4,64,2048]{2,1,0:T(8,128)(2,1)} %fusion.10), channel_id=1, source_target_pairs={{0,6},{2,4},{4,2},{6,0},{1,7},{3,5},{5,3},{7,1},{8,14},{10,12},{12... | collective-permute-start | bytes 3145736 | tf_op jit(solution)/shard_map/ppermute | solution.py:274
  462.7 47.0 %collective-permute-start.5 = (bf16[4,64,2048]{2,1,0:T(8,128)(2,1)}, bf16[4,64,2048]{2,1,0:T(8,128)(2,1)}, u32[]{:S(2)}, u32[]{:S(2)}) collective-permute-start(bf16[4,64,2048]{2,1,0:T(8,128)(2,1)} %get-tuple-element.110), channel_id=1, source_target_pairs={{0,2},{2,0},{4,6},{6,4},{1,3},{3,1},{5,7},{7,5},{8,10},{10,8},{12,... | collective-permute-start | bytes 3145736 | tf_op jit(solution)/shard_map/ppermute | solution.py:274
  463.5 46.8 %collective-permute-start.6 = (bf16[4,64,2048]{2,1,0:T(8,128)(2,1)}, bf16[4,64,2048]{2,1,0:T(8,128)(2,1)}, u32[]{:S(2)}, u32[]{:S(2)}) collective-permute-start(bf16[4,64,2048]{2,1,0:T(8,128)(2,1)} %get-tuple-element.111), channel_id=1, source_target_pairs={{0,4},{2,6},{4,0},{6,2},{1,5},{3,7},{5,1},{7,3},{8,12},{10,14},{12... | collective-permute-start | bytes 3145736 | tf_op jit(solution)/shard_map/ppermute | solution.py:274
  510.2 9.4 %copy-start.12 = (bf16[4,8,64,384]{3,2,1,0:T(8,128)(2,1)S(1)}, bf16[4,8,64,384]{3,2,1,0:T(8,128)(2,1)}, u32[]{:S(2)}) copy-start(bf16[4,8,64,384]{3,2,1,0:T(8,128)(2,1)} %get-tuple-element.75) | copy-start | bytes 4718596
  519.6 65.6 %reduce-scatter.11.cloned.1.call-start = ((), (), s32[]{:S(2)}) async-start(), calls=%async_computation.7 | async-start | bytes 1310720 | tf_op jit(solution)/shard_map/reduce_scatter | solution.py:371
  526.5 4.6 copy-start.24
  526.5 5.7 copy-start.13
  533.8 41.4 %copy-start.10 = (bf16[1,2,2048,256]{3,2,1,0:T(8,128)(2,1)S(1)}, bf16[1,2,2048,256]{3,2,1,0:T(8,128)(2,1)}, u32[]{:S(2)}) copy-start(bf16[1,2,2048,256]{3,2,1,0:T(8,128)(2,1)} %reduce-scatter.7.cloned.1.call-done) | copy-start | bytes 6291460
  588.1 7.1 %copy-start.4 = (f32[256,2048]{1,0:T(8,128)S(1)}, f32[256,2048]{1,0:T(8,128)}, u32[]{:S(2)}) copy-start(f32[256,2048]{1,0:T(8,128)} %shard_map.235) | copy-start | bytes 6291460
  588.1 7.1 %copy-start.6 = (bf16[256,2048]{1,0:T(8,128)(2,1)S(1)}, bf16[256,2048]{1,0:T(8,128)(2,1)}, u32[]{:S(2)}) copy-start(bf16[256,2048]{1,0:T(8,128)(2,1)} %tok_ref.1) | copy-start | bytes 3145732
  588.2 7.5 %copy-start.18 = (f32[64,512]{1,0:T(8,128)}, f32[64,512]{1,0:T(8,128)S(1)}, u32[]{:S(2)}) copy-start(f32[64,512]{1,0:T(8,128)S(1)} %reshape.139) | copy-start | bytes 393220
  593.3 2.5 copy-start.19
  593.3 2.5 copy-start.21
  593.3 2.5 copy-start.23
  593.3 2.6 copy-start.9
  (11 other events, 11.9 us)
Sparse Core Ops, SparseCore 0:
  9.6 36.2 all-gather.6
  48.1 157.4 all-gather.8
  207.1 79.9 all-gather.10
  289.3 75.2 reduce-scatter.4
  366.9 145.7 reduce-scatter.6
  519.7 33.4 reduce-scatter.8
  556.2 26.1 reduce-scatter.10

commit v13 on v12

--- a/solution.py
+++ b/solution.py
@@ -1310,14 +1310,14 @@
     if len(grad_refs) == 1:
         grad_refs[0][...] = grad.astype(BF16)
         return
-    mine_ref, away_ref, acc = grad_refs
-    acc[...] = grad
-    core = lax.axis_index("core")
+    mine_ref, away_ref = grad_refs
+    first = lax.axis_index("core") == 0
     width = mine_ref.shape[2]
     for i in range(mine_ref.shape[1]):
-        for ref, c in ((mine_ref, core), (away_ref, 1 - core)):
-            at = pl.multiple_of((2 * i + c) * width, width)
-            ref[0, i] = acc[pl.ds(at, width)].astype(BF16)
+        even = grad[2 * i * width : (2 * i + 1) * width]
+        odd = grad[(2 * i + 1) * width : (2 * i + 2) * width]
+        mine_ref[0, i] = jnp.where(first, even, odd).astype(BF16)
+        away_ref[0, i] = jnp.where(first, odd, even).astype(BF16)
 
 
 def turn(residual, d_normed, cotangent, gains, branch, own, came, attended, weights, width):
@@ -1330,7 +1330,6 @@
         half = (D // (8 * width), 4, width, D)
         grads = (jax.ShapeDtypeStruct(half, BF16),) * 2
         grad_specs = (pl.BlockSpec((1, 2, width, D), lambda j: (j // 2, j % 2, 0, 0)),) * 2
-        scratch = [pltpu.VMEM((cols, D), F32)] + scratch
     flat = jax.ShapeDtypeStruct((rows, D), F32)
 
     def held(shape):
@@ -1364,6 +1363,42 @@
         cost_estimate=BRIEF,
         compiler_params=params(1),
     )(residual, d_normed, cotangent, gains, branch, own, *came, attended, weights)
+
+
+def split_kernel(copies, q_cols, kv_cols, x_ref, wq_ref, wk_ref, wv_ref, q_ref, k_ref, v_ref, sum_ref):
+    total = jnp.zeros(sum_ref.shape, F32)
+    for s in range(x_ref.shape[0]):
+        block = x_ref[s].astype(F32)
+        at = slice(s * q_cols, (s + 1) * q_cols)
+        q_ref[:, at] = block[:, :q_cols]
+        weight = wq_ref[:, at].astype(F32)
+        total += jnp.sum(block[:, :q_cols] * weight, axis=1, keepdims=True)
+    for h in range(x_ref.shape[0] // copies):
+        at = slice(h * kv_cols, (h + 1) * kv_cols)
+        pair = x_ref[h * copies, :, q_cols:].astype(F32)
+        for c in range(1, copies):
+            pair += x_ref[h * copies + c, :, q_cols:].astype(F32)
+        for ref, w_ref, part in (
+            (k_ref, wk_ref, pair[:, :kv_cols]),
+            (v_ref, wv_ref, pair[:, kv_cols:]),
+        ):
+            ref[:, at] = part
+            total += jnp.sum(part * w_ref[:, at].astype(F32), axis=1, keepdims=True)
+    sum_ref[...] = total
+
+
+def split(sent, w_query, w_key, w_value, copies, q_cols, kv_cols):
+    rows = w_query.shape[0]
+    return pl.pallas_call(
+        functools.partial(split_kernel, copies, q_cols, kv_cols),
+        out_shape=tuple(
+            jax.ShapeDtypeStruct(shape, F32)
+            for shape in (w_query.shape, w_key.shape, w_value.shape, (rows, 1))
+        ),
+        in_specs=[VMEM] * 4,
+        out_specs=(VMEM,) * 4,
+        cost_estimate=BRIEF,
+    )(sent, w_query, w_key, w_value)
 
 
 def norm_parts(values):
@@ -1517,21 +1552,12 @@
     sent = sent.reshape(devs, w_rows, q_cols + 2 * kv_cols)
     sent = plane_exchange(sent, sent.shape, by_slot, by_slot, chips, 9)
     sent, grad_out = lax.optimization_barrier((sent, grad_out))
-    sent, grad_out = sent.astype(F32), grad_out.reshape(w_rows, D).astype(F32)
-
-    def kv_join(g):
-        g = g.reshape(devs // kv_copies, kv_copies, w_rows, kv_cols)
-        g = jnp.sum(g, axis=1) if kv_copies > 1 else g[:, 0]
-        return jnp.swapaxes(g, 0, 1).reshape(w_rows, KV_HEADS * HEAD_DIM)
-
-    grad_query = jnp.swapaxes(sent[:, :, :q_cols], 0, 1).reshape(w_rows, D)
-    grad_key = kv_join(sent[:, :, q_cols : q_cols + kv_cols])
-    grad_value = kv_join(sent[:, :, q_cols + kv_cols : q_cols + 2 * kv_cols])
-
-    gain_one_grad = sum(
-        jnp.sum(weight.astype(F32) * grad, axis=1)
-        for weight, grad in ((w_query, grad_query), (w_key, grad_key), (w_value, grad_value))
-    ) / attn_gain.astype(F32)
+    grad_out = grad_out.reshape(w_rows, D).astype(F32)
+
+    grad_query, grad_key, grad_value, gain_sum = split(
+        sent, w_query, w_key, w_value, kv_copies, q_cols, kv_cols
+    )
+    gain_one_grad = gain_sum[:, 0] / attn_gain.astype(F32)
     rms_stats = jnp.sqrt(totals[7, :3] / (rows * grps * devs * D))
     gain_first = (lax.axis_index("grp") * devs + lax.axis_index(PLANE)) * w_rows
     gain_two_grad = lax.dynamic_slice(totals.reshape(-1), (gain_first,), (w_rows,))

time: 615 us -> 609 us (level)
  no operation moved by 1% of the time
where the time goes in v13:
time: 609 us; the launch traced here: 599 us
  Pallas kernels  508 us (83%)
  other arithmetic  29.2 us (5%)
  matrix products  23.6 us (4%)
  between operations  15 us (2%)
  waiting for transfers between devices  9.54 us (2%)
  starting transfers between devices  7.35 us (1%)
  local copies, waits for them, and re-layouts  6.47 us (1%)
    pallas_call x1, Pallas kernels, entry(): pl.pallas_call(functools.partial(entry_kernel, grps, chips), out_shape=(j...  83.1 us
    pallas_call x2, Pallas kernels, plane_gather(): pl.pallas_call(functools.partial(gather_kernel, chips, inner), out_shape=...  79.8 us
    pallas_call x1, Pallas kernels, square_reduce(): pl.pallas_call(functools.partial(square_kernel, compute, len(operands)),...  54.4 us
    pallas_call x1, Pallas kernels, attend_back(): pl.pallas_call(functools.partial(attend_back_kernel, heads), out_shape=ja...  42.5 us
    pallas_call x1, Pallas kernels, plane_reduce(): pl.pallas_call(functools.partial(reduce_kernel, chips, inner), out_shape=...  41.4 us
    pallas_call x1, Pallas kernels, widen(): pl.pallas_call(widen_kernel, out_shape=(tall, jax.ShapeDtypeStruct((shard...  30.8 us
    pallas_call x1, Pallas kernels, widen_part(): pl.pallas_call(widen_part_kernel, out_shape=jax.ShapeDtypeStruct((shards,...  23.6 us
    pallas_call x1, Pallas kernels, attend(): pl.pallas_call(functools.partial(attend_kernel, heads), out_shape=jax.Sha...  23.3 us
  transfers between devices with their start and end apart: 14, of which 4 were waited for; matrix products, arithmetic and copies ran while one was open for 8% of the time, Pallas kernels for 84%

profile of v13, /device:TPU:0, one launch (start us, length us, event | category | flops | bytes accessed | tf_op | source)
XLA Modules:
  0.0 598.6 jit_solution(18157253451278128741)
XLA Ops:
  8.0 3.1 pad_maximum_fusion
  14.9 83.1 %shard_map.220 = (bf16[8,256,2048]{2,1,0:T(8,128)(2,1)}, bf16[8,256,2048]{2,1,0:T(8,128)(2,1)}, bf16[4,8,64,384]{3,2,1,0:T(8,128)(2,1)}, bf16[4,8,16,128]{3,2,1,0:T(8,128)(2,1)}) custom-call(bf16[256,2048]{1,0:T(8,128)(2,1)} %tok_ref.1, bf16[256,2048]{1,0:T(8,128)(2,1)} %multiply_convert_fusion.1.cot_ref, bf16[8,64,384]{2,1,0:T(8,128)(2,1)} %maximum_bitcast_fusion.pack_ref, ...), custom_call_target="tpu_custom_call" | custom-call | flops 1000 | bytes 1000 | tf_op jit(solution)/shard_map/pallas_call | solution.py:1206
  98.0 11.5 %shard_map.221 = (bf16[2048,2048]{1,0:T(8,128)(2,1)}, bf16[2048,384]{1,0:T(8,128)(2,1)}, f32[8,2048]{1,0:T(8,128)}) custom-call(bf16[2048,2048]{1,0:T(8,128)(2,1)} %bitcast.73, bf16[2048,384]{1,0:T(8,128)(2,1)} %bitcast.74, bf16[32,16,128]{2,1,0:T(8,128)(2,1)} %bitcast.82), custom_call_target="tpu_custom_call" | custom-call | flops 1000 | bytes 1000 | tf_op jit(solution)/shard_map/pallas_call | solution.py:1249
  111.4 23.3 %shard_map.222.x_ref = bf16[2048,256]{1,0:T(8,128)(2,1)S(1)} custom-call(s32[16]{0:T(128)S(1)} %select_reduce_fusion.order_ref, bf16[2048,384]{1,0:T(8,128)(2,1)S(1)} %copy-done), custom_call_target="tpu_custom_call" | custom-call | flops 1000 | bytes 1000 | tf_op jit(solution)/shard_map/pallas_call | solution.py:535
  135.7 15.6 %shard_map.223.refs_3_ = bf16[256,2048]{1,0:T(8,128)(2,1)} custom-call(bf16[2048,256]{1,0:T(8,128)(2,1)} %copy-done.2), custom_call_target="tpu_custom_call" | custom-call | flops 1000 | bytes 1000 | tf_op jit(solution)/shard_map/pallas_call | solution.py:327
  152.2 39.9 %shard_map.224 = bf16[4,8,64,2048]{3,2,1,0:T(8,128)(2,1)} custom-call(bf16[4,64,2048]{2,1,0:T(8,128)(2,1)} %bitcast.76), custom_call_target="tpu_custom_call" | custom-call | flops 1000 | bytes 1000 | tf_op jit(solution)/shard_map/pallas_call | solution.py:160
  192.1 7.5 %multiply_reduce_fusion = (f32[256]{0:T(256)S(1)}, f32[256,2048]{1,0:T(8,128)S(1)}, f32[256,2048]{1,0:T(8,128)}) fusion(bf16[256,2048]{1,0:T(8,128)(2,1)S(1)} %copy-done.5, bf16[256,2048]{1,0:T(8,128)(2,1)} %shard_map.223.refs_3_, bf16[2048,2048]{1,0:T(8,128)(2,1)} %bitcast.65), kind=kOutput, calls=%fused_computation.20 | convolution fusion | flops 2150104832 | bytes 14681088 | tf_op jit(solution)/shard_map/dot_general | solution.py:355
  201.0 40.0 %shard_map.225 = bf16[8,256,2048]{2,1,0:T(8,128)(2,1)} custom-call(bf16[256,2048]{1,0:T(8,128)(2,1)} %multiply_convert_fusion.x_ref), custom_call_target="tpu_custom_call" | custom-call | flops 1000 | bytes 1000 | tf_op jit(solution)/shard_map/pallas_call | solution.py:160
  241.0 30.8 %shard_map.226 = (bf16[4,2048,256]{2,1,0:T(8,128)(2,1)}, bf16[4,256,2048]{2,1,0:T(8,128)(2,1)}, bf16[4,2048,256]{2,1,0:T(8,128)(2,1)}, bf16[4,2048,256]{2,1,0:T(8,128)(2,1)}, bf16[2048,2048]{1,0:T(8,128)(2,1)}) custom-call(bf16[2048,2048]{1,0:T(8,128)(2,1)} %bitcast.69, bf16[4,2,2048,256]{3,2,1,0:T(8,128)(2,1)} %bitcast.63), custom_call_target="tpu_custom_call" | custom-call | flops 1000 | bytes 1000 | tf_op jit(solution)/shard_map/pallas_call | solution.py:697
  271.8 15.9 %shard_map.227 = bf16[4,256,2048]{2,1,0:T(8,128)(2,1)} custom-call(bf16[4,256,2048]{2,1,0:T(8,128)(2,1)} %get-tuple-element.84.ht_ref, bf16[2048,2048]{1,0:T(8,128)(2,1)} %bitcast.67), custom_call_target="tpu_custom_call" | custom-call | flops 1000 | bytes 1000 | tf_op jit(solution)/shard_map/pallas_call | solution.py:731
  287.8 20.8 %shard_map.228 = (f32[256,2048]{1,0:T(8,128)}, bf16[256,2048]{1,0:T(8,128)(2,1)}, bf16[256,2048]{1,0:T(8,128)(2,1)}, bf16[256,2048]{1,0:T(8,128)(2,1)}) custom-call(bf16[4,2048,256]{2,1,0:T(8,128)(2,1)} %get-tuple-element.88.refs_0_, bf16[4,256,2048]{2,1,0:T(8,128)(2,1)} %bitcast.70), custom_call_target="tpu_custom_call" | custom-call | flops 1000 | bytes 1000 | tf_op jit(solution)/shard_map/pallas_call | solution.py:1067
  308.6 1.7 collective-permute-start
  312.2 15.6 %shard_map.229 = (bf16[4,2048,256]{2,1,0:T(8,128)(2,1)}, bf16[4,2048,256]{2,1,0:T(8,128)(2,1)}) custom-call(bf16[4,2048,256]{2,1,0:T(8,128)(2,1)} %get-tuple-element.93.s_ref, bf16[4,2048,256]{2,1,0:T(8,128)(2,1)} %get-tuple-element.94.t_ref, bf16[2048,2048]{1,0:T(8,128)(2,1)} %bitcast.68, bf16[4,256,2048]{2,1,0:T(8,128)(2,1)} %bitcast.71), custom_call_target="tpu_custom_call" | custom-call | flops 1000 | bytes 1000 | tf_op jit(solution)/shard_map/pallas_call | solution.py:789
  327.8 23.6 %shard_map.230 = bf16[4,2,2048,256]{3,2,1,0:T(8,128)(2,1)} custom-call(bf16[2048,2048]{1,0:T(8,128)(2,1)} %get-tuple-element.83.nt_ref, bf16[4,2048,256]{2,1,0:T(8,128)(2,1)} %get-tuple-element.100.dg_ref.refs_0_, bf16[4,2048,256]{2,1,0:T(8,128)(2,1)} %get-tuple-element.101.du_ref.refs_1_), custom_call_target="tpu_custom_call" | custom-call | flops 1000 | bytes 1000 | tf_op jit(solution)/shard_map/pallas_call | solution.py:811
  351.4 5.4 collective-permute-done.1.refs_1_
  358.8 54.4 %shard_map.231.dn_ref = f32[256,2048]{1,0:T(8,128)} custom-call(bf16[4,2048,256]{2,1,0:T(8,128)(2,1)} %get-tuple-element.100.dg_ref.refs_0_, bf16[4,2048,256]{2,1,0:T(8,128)(2,1)} %get-tuple-element.101.du_ref.refs_1_, bf16[4,2,2048,256]{3,2,1,0:T(8,128)(2,1)} %bitcast.64), custom_call_target="tpu_custom_call" | custom-call | flops 1000 | bytes 1000 | tf_op jit(solution)/shard_map/pallas_call | solution.py:973
  413.1 19.7 %shard_map.232 = (bf16[256,2048]{1,0:T(8,128)(2,1)}, f32[256,2048]{1,0:T(8,128)}, f32[8,384]{1,0:T(8,128)}, bf16[256,2048]{1,0:T(8,128)(2,1)}, bf16[4,4,64,2048]...) custom-call(f32[256,2048]{1,0:T(8,128)} %copy-done.7, f32[256,2048]{1,0:T(8,128)} %shard_map.231.dn_ref, ...), custom_call_target="tpu_custom_call" | custom-call | flops 1000 | bytes 1000 | tf_op jit(solution)/shard_map/pallas_call | solution.py:1338
  433.0 18.5 %shard_map.233 = (bf16[2048,256]{1,0:T(8,128)(2,1)}, f32[8,384]{1,0:T(8,128)}) custom-call(bf16[256,2048]{1,0:T(8,128)(2,1)} %get-tuple-element.110.x_ref, f32[8,384]{1,0:T(8,128)} %get-tuple-element.111.t_ref), custom_call_target="tpu_custom_call" | custom-call | flops 1000 | bytes 1000 | tf_op jit(solution)/shard_map/pallas_call | solution.py:639
  451.5 2.9 fusion.10
  454.4 4.5 fusion.9
  459.0 1.4 collective-permute-start.4
  463.7 42.5 %shard_map.234 = bf16[2048,384]{1,0:T(8,128)(2,1)S(1)} custom-call(s32[16]{0:T(128)S(1)} %select_reduce_fusion.order_ref, bf16[2048,384]{1,0:T(8,128)(2,1)S(1)} %copy-done.1, bf16[2048,256]{1,0:T(8,128)(2,1)S(1)} %copy-done.3), custom_call_target="tpu_custom_call" | custom-call | flops 1000 | bytes 1000 | tf_op jit(solution)/shard_map/pallas_call | solution.py:557
  507.9 9.2 %convolution_convert_fusion.1 = bf16[2048,384]{1,0:T(8,128)(2,1)} fusion(bf16[2048,2048]{1,0:T(8,128)(2,1)} %get-tuple-element.122, bf16[2048,384]{1,0:T(8,128)(2,1)S(1)} %shard_map.234), kind=kOutput, calls=%fused_computation.5 | convolution fusion | flops 3222011904 | bytes 11534336 | tf_op jit(solution)/shard_map/dot_general | solution.py:359
  517.2 6.9 %convolution_convert_fusion = bf16[2048,2048]{1,0:T(8,128)(2,1)} fusion(bf16[2048,384]{1,0:T(8,128)(2,1)S(1)} %shard_map.234, bf16[2048,384]{1,0:T(8,128)(2,1)S(1)} %bitcast.75), kind=kOutput, calls=%fused_computation | convolution fusion | flops 3225419776 | bytes 11534336 | tf_op jit(solution)/shard_map/dot_general | solution.py:363
  524.0 4.5 fusion.7
  529.7 1.6 bitcast_convert_fusion
  531.3 41.4 %shard_map.235 = f32[256,2048]{1,0:T(8,128)} custom-call(bf16[8,256,2048]{2,1,0:T(8,128)(2,1)} %bitcast.72), custom_call_target="tpu_custom_call" | custom-call | flops 1000 | bytes 1000 | tf_op jit(solution)/shard_map/pallas_call | solution.py:246
  572.7 2.3 bitcast_convert_fusion.1
  575.1 7.7 %shard_map.236.x_ref = bf16[8,64,384]{2,1,0:T(8,128)(2,1)} custom-call(bf16[8,64,384]{2,1,0:T(8,128)(2,1)} %bitcast.81), custom_call_target="tpu_custom_call" | custom-call | flops 1000 | bytes 1000 | tf_op jit(solution)/shard_map/pallas_call | solution.py:327
  582.8 3.2 shard_map.237
  587.4 1.9 bitcast_convert_fusion.3
  589.8 1.5 fusion.4
  (101 shorter events, 21.6 us)
Async XLA Ops:
  7.2 145.0 %all-gather.7.cloned.1.call-start = ((), (), s32[]{:S(2)}) async-start(), calls=%async_computation.8 | async-start | bytes 1310720 | tf_op jit(solution)/shard_map/all_gather | solution.py:367
  7.9 233.1 %all-gather.9.cloned.1.call-start = ((), (), s32[]{:S(2)}) async-start(), calls=%async_computation.9 | async-start | bytes 10485760 | tf_op jit(solution)/shard_map/all_gather | solution.py:367
  11.0 1.2 copy-start.20
  11.0 1.2 copy-start.21
  11.1 2.7 copy-start.8
  11.1 276.7 %all-gather.11.cloned.1.call-start = ((), (), s32[]{:S(2)}) async-start(), calls=%async_computation.10 | async-start | bytes 5242880 | tf_op jit(solution)/shard_map/all_gather | solution.py:367
  11.8 450.6 %reduce-scatter.5.cloned.1.call-start = ((), (), s32[]{:S(2)}) async-start(), calls=%async_computation.4 | async-start | bytes 5242880 | tf_op jit(solution)/shard_map/reduce_scatter | solution.py:371
  98.0 11.5 %copy-start.22 = (s32[64]{0:T(128)S(1)}, s32[64]{0:T(128)}, u32[]{:S(2)}) copy-start(s32[64]{0:T(128)} %param.15) | copy-start | bytes 772
  98.0 11.5 %copy-start.23 = (s32[64]{0:T(128)S(1)}, s32[64]{0:T(128)}, u32[]{:S(2)}) copy-start(s32[64]{0:T(128)} %param.14) | copy-start | bytes 772
  109.9 1.4 copy-start
  152.2 39.9 %copy-start.5 = (bf16[256,2048]{1,0:T(8,128)(2,1)S(1)}, bf16[256,2048]{1,0:T(8,128)(2,1)}, u32[]{:S(2)}) copy-start(bf16[256,2048]{1,0:T(8,128)(2,1)} %tok_ref.1) | copy-start | bytes 3145732
  199.6 41.4 %copy-start.7 = (f32[256,2048]{1,0:T(8,128)}, f32[256,2048]{1,0:T(8,128)S(1)}, u32[]{:S(2)}) copy-start(f32[256,2048]{1,0:T(8,128)S(1)} %get-tuple-element.147.res_ref) | copy-start | bytes 6291460
  287.7 229.3 %reduce-scatter.7.cloned.1.call-start = ((), (), s32[]{:S(2)}) async-start(), calls=%async_computation.5 | async-start | bytes 10485760 | tf_op jit(solution)/shard_map/reduce_scatter | solution.py:371
  308.6 42.8 %collective-permute-start = (bf16[256,2048]{1,0:T(8,128)(2,1)}, bf16[256,2048]{1,0:T(8,128)(2,1)S(1)}, u32[]{:S(2)}, u32[]{:S(2)}) collective-permute-start(bf16[256,2048]{1,0:T(8,128)(2,1)} %get-tuple-element.97), channel_id=1, source_target_pairs={{0,6},{2,4},{4,2},{6,0},{1,7},{3,5},{5,3},{7,1},{8,14},{10,12},{12... | collective-permute-start | bytes 3145736 | tf_op jit(solution)/shard_map/ppermute | solution.py:274
  310.4 46.5 %collective-permute-start.1 = (bf16[256,2048]{1,0:T(8,128)(2,1)}, bf16[256,2048]{1,0:T(8,128)(2,1)S(1)}, u32[]{:S(2)}, u32[]{:S(2)}) collective-permute-start(bf16[256,2048]{1,0:T(8,128)(2,1)} %get-tuple-element.98), channel_id=1, source_target_pairs={{0,2},{2,0},{4,6},{6,4},{1,3},{3,1},{5,7},{7,5},{8,10},{10,8},{12,... | collective-permute-start | bytes 3145736 | tf_op jit(solution)/shard_map/ppermute | solution.py:274
  310.9 46.9 %collective-permute-start.2 = (bf16[256,2048]{1,0:T(8,128)(2,1)}, bf16[256,2048]{1,0:T(8,128)(2,1)S(1)}, u32[]{:S(2)}, u32[]{:S(2)}) collective-permute-start(bf16[256,2048]{1,0:T(8,128)(2,1)} %get-tuple-element.99), channel_id=1, source_target_pairs={{0,4},{2,6},{4,0},{6,2},{1,5},{3,7},{5,1},{7,3},{8,12},{10,14},{12... | collective-permute-start | bytes 3145736 | tf_op jit(solution)/shard_map/ppermute | solution.py:274
  351.4 6.4 %copy-start.14 = (bf16[256,2048]{1,0:T(8,128)(2,1)}, bf16[256,2048]{1,0:T(8,128)(2,1)S(1)}, u32[]{:S(2)}) copy-start(bf16[256,2048]{1,0:T(8,128)(2,1)S(1)} %collective-permute-done.refs_0_) | copy-start | bytes 3145732
  358.8 216.3 %reduce-scatter.9.cloned.1.call-start = ((), (), s32[]{:S(2)}) async-start(), calls=%async_computation.6 | async-start | bytes 1966080 | tf_op jit(solution)/shard_map/reduce_scatter | solution.py:371
  432.9 18.6 %collective-permute-start.3 = (bf16[4,4,64,2048]{3,2,1,0:T(8,128)(2,1)}, bf16[4,4,64,2048]{3,2,1,0:T(8,128)(2,1)}, u32[]{:S(2)}, u32[]{:S(2)}) collective-permute-start(bf16[4,4,64,2048]{3,2,1,0:T(8,128)(2,1)} %get-tuple-element.109), channel_id=1, source_target_pairs={{0,1},{1,0},{2,3},{3,2},{4,5},{5,4},{6,7},{7,6},{8,9},{9,8},{10,11... | collective-permute-start | bytes 12582920 | tf_op jit(solution)/shard_map/ppermute | solution.py:282
  454.4 8.0 %copy-start.1 = (bf16[2048,384]{1,0:T(8,128)(2,1)S(1)}, bf16[2048,384]{1,0:T(8,128)(2,1)}, u32[]{:S(2)}) copy-start(bf16[2048,384]{1,0:T(8,128)(2,1)} %get-tuple-element.81.qkv_ref) | copy-start | bytes 4718596
  459.0 47.3 %collective-permute-start.4 = (bf16[4,64,2048]{2,1,0:T(8,128)(2,1)}, bf16[4,64,2048]{2,1,0:T(8,128)(2,1)}, u32[]{:S(2)}, u32[]{:S(2)}) collective-permute-start(bf16[4,64,2048]{2,1,0:T(8,128)(2,1)} %fusion.10), channel_id=1, source_target_pairs={{0,6},{2,4},{4,2},{6,0},{1,7},{3,5},{5,3},{7,1},{8,14},{10,12},{12... | collective-permute-start | bytes 3145736 | tf_op jit(solution)/shard_map/ppermute | solution.py:274
  460.4 47.1 %collective-permute-start.5 = (bf16[4,64,2048]{2,1,0:T(8,128)(2,1)}, bf16[4,64,2048]{2,1,0:T(8,128)(2,1)}, u32[]{:S(2)}, u32[]{:S(2)}) collective-permute-start(bf16[4,64,2048]{2,1,0:T(8,128)(2,1)} %get-tuple-element.114), channel_id=1, source_target_pairs={{0,2},{2,0},{4,6},{6,4},{1,3},{3,1},{5,7},{7,5},{8,10},{10,8},{12,... | collective-permute-start | bytes 3145736 | tf_op jit(solution)/shard_map/ppermute | solution.py:274
  461.3 46.6 %collective-permute-start.6 = (bf16[4,64,2048]{2,1,0:T(8,128)(2,1)}, bf16[4,64,2048]{2,1,0:T(8,128)(2,1)}, u32[]{:S(2)}, u32[]{:S(2)}) collective-permute-start(bf16[4,64,2048]{2,1,0:T(8,128)(2,1)} %get-tuple-element.115), channel_id=1, source_target_pairs={{0,4},{2,6},{4,0},{6,2},{1,5},{3,7},{5,1},{7,3},{8,12},{10,14},{12... | collective-permute-start | bytes 3145736 | tf_op jit(solution)/shard_map/ppermute | solution.py:274
  462.5 1.2 copy-start.3
  507.9 9.3 %copy-start.11 = (bf16[4,8,64,384]{3,2,1,0:T(8,128)(2,1)S(1)}, bf16[4,8,64,384]{3,2,1,0:T(8,128)(2,1)}, u32[]{:S(2)}) copy-start(bf16[4,8,64,384]{3,2,1,0:T(8,128)(2,1)} %get-tuple-element.79) | copy-start | bytes 4718596
  517.1 65.7 %reduce-scatter.11.cloned.1.call-start = ((), (), s32[]{:S(2)}) async-start(), calls=%async_computation.7 | async-start | bytes 1310720 | tf_op jit(solution)/shard_map/reduce_scatter | solution.py:371
  524.0 4.6 copy-start.19
  524.0 5.7 copy-start.12
  531.3 41.4 %copy-start.10 = (bf16[1,2,2048,256]{3,2,1,0:T(8,128)(2,1)S(1)}, bf16[1,2,2048,256]{3,2,1,0:T(8,128)(2,1)}, u32[]{:S(2)}) copy-start(bf16[1,2,2048,256]{3,2,1,0:T(8,128)(2,1)} %reduce-scatter.7.cloned.1.call-done) | copy-start | bytes 6291460
  572.7 16.6 %copy-start.6 = (bf16[256,2048]{1,0:T(8,128)(2,1)S(1)}, bf16[256,2048]{1,0:T(8,128)(2,1)}, u32[]{:S(2)}) copy-start(bf16[256,2048]{1,0:T(8,128)(2,1)} %tok_ref.1) | copy-start | bytes 3145732
  575.1 14.2 %copy-start.4 = (f32[256,2048]{1,0:T(8,128)S(1)}, f32[256,2048]{1,0:T(8,128)}, u32[]{:S(2)}) copy-start(f32[256,2048]{1,0:T(8,128)} %shard_map.235) | copy-start | bytes 6291460
  586.9 2.9 copy-start.9
  (6 other events, 6.0 us)
Sparse Core Ops, SparseCore 0:
  9.6 36.2 all-gather.6
  48.1 157.4 all-gather.8
  207.1 79.9 all-gather.10
  289.3 75.2 reduce-scatter.4
  366.9 145.7 reduce-scatter.6
  517.2 33.9 reduce-scatter.8
  554.2 26.1 reduce-scatter.10

commit v14 on v13

--- a/solution.py
+++ b/solution.py
@@ -275,26 +275,35 @@
 
 
 class Drift:
-    def __init__(self, mine, away, axis):
-        self.axis = axis
-        self.chip, self.core = place()
+    def __init__(self, mine, away):
         self.mine = mine
         self.twin = lax.ppermute(away, "core", [(0, 1), (1, 0)])
 
-    def part(self, step):
-        at = jnp.bitwise_xor(self.chip, step)
-        mine = lax.dynamic_index_in_dim(self.mine, at, self.axis, keepdims=False)
-        twin = lax.dynamic_index_in_dim(self.twin, at, self.axis, keepdims=False)
-        return mine.astype(F32) + twin.astype(F32)
-
     def parts(self):
-        return tuple(self.part(step).astype(BF16) for step in (1, 2, 3))
-
-    def finish(self, came):
-        total = self.part(0)
-        for part in came:
-            total = total + part.astype(F32)
-        return total
+        self.own, *others = twin_add(self.mine, self.twin)
+        return others
+
+
+def twin_add_kernel(mine_ref, twin_ref, *refs):
+    chip = lax.axis_index("chip")
+    for step, ref in zip((0, 3, 1, 2), refs):
+        at = jnp.bitwise_xor(chip, step)
+        ref[0] = (mine_ref[0, at].astype(F32) + twin_ref[0, at].astype(F32)).astype(ref.dtype)
+
+
+def twin_add(mine, twin):
+    grps, _, rows, cols = mine.shape
+    spec = pl.BlockSpec((1, 4, rows, cols), lambda g: (g, 0, 0, 0))
+    part_spec = pl.BlockSpec((1, rows, cols), lambda g: (g, 0, 0))
+    part = (grps, rows, cols)
+    return pl.pallas_call(
+        twin_add_kernel,
+        out_shape=(jax.ShapeDtypeStruct(part, F32),) + (jax.ShapeDtypeStruct(part, BF16),) * 3,
+        grid=(grps,),
+        in_specs=[spec, spec],
+        out_specs=(part_spec,) * 4,
+        cost_estimate=BRIEF,
+    )(mine, twin)
 
 
 def exchange_kernel(chips, cut, paste, x_ref, o_ref, send, recv, local):
@@ -1521,13 +1530,13 @@
         w_rows,
     )
     if chips == 4:
-        drift_out = Drift(grad_out, *away, 1)
+        drift_out = Drift(grad_out, *away)
     d_attended, totals = exchange_total(
         d_attended, totals, (devs * rows, q_cols), rows, q_cols, grps, chips, 7
     )
     if chips == 4:
         sent_out, d_attended = lax.optimization_barrier((drift_out.parts(), d_attended))
-        sent_out = swap_others((sent_out[2], sent_out[0], sent_out[1]))
+        sent_out = swap_others(sent_out)
     d_attended, grad_down = lax.optimization_barrier((d_attended, grad_down))
     d_qkv = attend_back(qkv, d_attended, order, q_heads)
     if chips == 4:
@@ -1538,7 +1547,7 @@
     d_normed_one = over_cols(d_qkv, w_qkv).astype(BF16).reshape(devs, rows, D)
     if chips == 4:
         sent_out, d_normed_one = lax.optimization_barrier((sent_out, d_normed_one))
-        grad_out = drift_out.finish(sent_out).astype(BF16)
+        grad_out = join(drift_out.own, sent_out).astype(BF16)
     else:
         grad_out = plane_reduce(
             grad_out.reshape(grps, devs, w_rows, D), chips, 6, dtype=BF16, inner=True

time: 609 us -> 607 us (level)
  other arithmetic: 29.2 us -> 20.9 us
    convert_element_type x3 -> x1, other arithmetic: 12 us -> 3.61 us  [on_device(): grad_out = join(drift_out.own, sent_out).astype(BF16)]
    pallas_call x0 -> x1, Pallas kernels: none -> 6.2 us  [twin_add(): pl.pallas_call(twin_add_kernel, out_shape=(jax.ShapeDtypeStruct(part, F32...]
  transfers between devices with their start and end apart: 14 -> 14, of which waited for: 4 -> 4; matrix products, arithmetic and copies ran while one was open for 8% -> 7% of each run, Pallas kernels for 84% -> 86%
where the time goes in v14:
time: 607 us; the launch traced here: 597 us
  Pallas kernels  514 us (85%)
  matrix products  23.7 us (4%)
  other arithmetic  20.9 us (3%)
  between operations  15 us (2%)
  waiting for transfers between devices  9.32 us (2%)
  starting transfers between devices  7.35 us (1%)
  local copies, waits for them, and re-layouts  6.51 us (1%)
    pallas_call x1, Pallas kernels, entry(): pl.pallas_call(functools.partial(entry_kernel, grps, chips), out_shape=(j...  83.1 us
    pallas_call x2, Pallas kernels, plane_gather(): pl.pallas_call(functools.partial(gather_kernel, chips, inner), out_shape=...  79.8 us
    pallas_call x1, Pallas kernels, square_reduce(): pl.pallas_call(functools.partial(square_kernel, compute, len(operands)),...  54.6 us
    pallas_call x1, Pallas kernels, attend_back(): pl.pallas_call(functools.partial(attend_back_kernel, heads), out_shape=ja...  42.8 us
    pallas_call x1, Pallas kernels, plane_reduce(): pl.pallas_call(functools.partial(reduce_kernel, chips, inner), out_shape=...  41.4 us
    pallas_call x1, Pallas kernels, widen(): pl.pallas_call(widen_kernel, out_shape=(tall, jax.ShapeDtypeStruct((shard...  30.7 us
    pallas_call x1, Pallas kernels, widen_part(): pl.pallas_call(widen_part_kernel, out_shape=jax.ShapeDtypeStruct((shards,...  23.6 us
    pallas_call x1, Pallas kernels, attend(): pl.pallas_call(functools.partial(attend_kernel, heads), out_shape=jax.Sha...  23.3 us
  transfers between devices with their start and end apart: 14, of which 4 were waited for; matrix products, arithmetic and copies ran while one was open for 7% of the time, Pallas kernels for 86%

profile of v14, /device:TPU:0, one launch (start us, length us, event | category | flops | bytes accessed | tf_op | source)
XLA Modules:
  0.0 596.8 jit_solution(392940494932985731)
XLA Ops:
  8.0 3.1 pad_maximum_fusion
  14.9 83.1 %shard_map.220 = (bf16[8,256,2048]{2,1,0:T(8,128)(2,1)}, bf16[8,256,2048]{2,1,0:T(8,128)(2,1)}, bf16[4,8,64,384]{3,2,1,0:T(8,128)(2,1)}, bf16[4,8,16,128]{3,2,1,0:T(8,128)(2,1)}) custom-call(bf16[256,2048]{1,0:T(8,128)(2,1)} %tok_ref.1, bf16[256,2048]{1,0:T(8,128)(2,1)} %multiply_convert_fusion.1.cot_ref, bf16[8,64,384]{2,1,0:T(8,128)(2,1)} %maximum_bitcast_fusion.pack_ref, ...), custom_call_target="tpu_custom_call" | custom-call | flops 1000 | bytes 1000 | tf_op jit(solution)/shard_map/pallas_call | solution.py:1215
  98.0 11.5 %shard_map.221 = (bf16[2048,2048]{1,0:T(8,128)(2,1)}, bf16[2048,384]{1,0:T(8,128)(2,1)}, f32[8,2048]{1,0:T(8,128)}) custom-call(bf16[2048,2048]{1,0:T(8,128)(2,1)} %bitcast.53, bf16[2048,384]{1,0:T(8,128)(2,1)} %bitcast.54, bf16[32,16,128]{2,1,0:T(8,128)(2,1)} %bitcast.62), custom_call_target="tpu_custom_call" | custom-call | flops 1000 | bytes 1000 | tf_op jit(solution)/shard_map/pallas_call | solution.py:1258
  109.9 1.4 copy-done
  111.3 23.3 %shard_map.222.x_ref = bf16[2048,256]{1,0:T(8,128)(2,1)S(1)} custom-call(s32[16]{0:T(128)S(1)} %select_reduce_fusion.order_ref, bf16[2048,384]{1,0:T(8,128)(2,1)S(1)} %copy-done), custom_call_target="tpu_custom_call" | custom-call | flops 1000 | bytes 1000 | tf_op jit(solution)/shard_map/pallas_call | solution.py:544
  135.7 15.6 %shard_map.223.refs_3_ = bf16[256,2048]{1,0:T(8,128)(2,1)} custom-call(bf16[2048,256]{1,0:T(8,128)(2,1)} %copy-done.2), custom_call_target="tpu_custom_call" | custom-call | flops 1000 | bytes 1000 | tf_op jit(solution)/shard_map/pallas_call | solution.py:336
  152.2 39.9 %shard_map.224 = bf16[4,8,64,2048]{3,2,1,0:T(8,128)(2,1)} custom-call(bf16[4,64,2048]{2,1,0:T(8,128)(2,1)} %bitcast.56), custom_call_target="tpu_custom_call" | custom-call | flops 1000 | bytes 1000 | tf_op jit(solution)/shard_map/pallas_call | solution.py:160
  192.1 7.5 %multiply_reduce_fusion = (f32[256]{0:T(256)S(1)}, f32[256,2048]{1,0:T(8,128)S(1)}, f32[256,2048]{1,0:T(8,128)}) fusion(bf16[256,2048]{1,0:T(8,128)(2,1)S(1)} %copy-done.5, bf16[256,2048]{1,0:T(8,128)(2,1)} %shard_map.223.refs_3_, bf16[2048,2048]{1,0:T(8,128)(2,1)} %bitcast.45), kind=kOutput, calls=%fused_computation.14 | convolution fusion | flops 2150104832 | bytes 14681088 | tf_op jit(solution)/shard_map/dot_general | solution.py:364
  199.6 1.4 multiply_convert_fusion.x_ref
  201.0 40.0 %shard_map.225 = bf16[8,256,2048]{2,1,0:T(8,128)(2,1)} custom-call(bf16[256,2048]{1,0:T(8,128)(2,1)} %multiply_convert_fusion.x_ref), custom_call_target="tpu_custom_call" | custom-call | flops 1000 | bytes 1000 | tf_op jit(solution)/shard_map/pallas_call | solution.py:160
  241.0 30.7 %shard_map.226 = (bf16[4,2048,256]{2,1,0:T(8,128)(2,1)}, bf16[4,256,2048]{2,1,0:T(8,128)(2,1)}, bf16[4,2048,256]{2,1,0:T(8,128)(2,1)}, bf16[4,2048,256]{2,1,0:T(8,128)(2,1)}, bf16[2048,2048]{1,0:T(8,128)(2,1)}) custom-call(bf16[2048,2048]{1,0:T(8,128)(2,1)} %bitcast.49, bf16[4,2,2048,256]{3,2,1,0:T(8,128)(2,1)} %bitcast.43), custom_call_target="tpu_custom_call" | custom-call | flops 1000 | bytes 1000 | tf_op jit(solution)/shard_map/pallas_call | solution.py:706
  271.7 15.9 %shard_map.227 = bf16[4,256,2048]{2,1,0:T(8,128)(2,1)} custom-call(bf16[4,256,2048]{2,1,0:T(8,128)(2,1)} %get-tuple-element.88.ht_ref, bf16[2048,2048]{1,0:T(8,128)(2,1)} %bitcast.47), custom_call_target="tpu_custom_call" | custom-call | flops 1000 | bytes 1000 | tf_op jit(solution)/shard_map/pallas_call | solution.py:740
  287.7 21.1 %shard_map.228 = (f32[256,2048]{1,0:T(8,128)}, bf16[256,2048]{1,0:T(8,128)(2,1)}, bf16[256,2048]{1,0:T(8,128)(2,1)}, bf16[256,2048]{1,0:T(8,128)(2,1)}) custom-call(bf16[4,2048,256]{2,1,0:T(8,128)(2,1)} %get-tuple-element.92.refs_0_, bf16[4,256,2048]{2,1,0:T(8,128)(2,1)} %bitcast.50), custom_call_target="tpu_custom_call" | custom-call | flops 1000 | bytes 1000 | tf_op jit(solution)/shard_map/pallas_call | solution.py:1076
  308.8 1.8 collective-permute-start
  312.4 15.6 %shard_map.229 = (bf16[4,2048,256]{2,1,0:T(8,128)(2,1)}, bf16[4,2048,256]{2,1,0:T(8,128)(2,1)}) custom-call(bf16[4,2048,256]{2,1,0:T(8,128)(2,1)} %get-tuple-element.97.s_ref, bf16[4,2048,256]{2,1,0:T(8,128)(2,1)} %get-tuple-element.98.t_ref, bf16[2048,2048]{1,0:T(8,128)(2,1)} %bitcast.48, bf16[4,256,2048]{2,1,0:T(8,128)(2,1)} %bitcast.51), custom_call_target="tpu_custom_call" | custom-call | flops 1000 | bytes 1000 | tf_op jit(solution)/shard_map/pallas_call | solution.py:798
  328.0 23.6 %shard_map.230 = bf16[4,2,2048,256]{3,2,1,0:T(8,128)(2,1)} custom-call(bf16[2048,2048]{1,0:T(8,128)(2,1)} %get-tuple-element.87.nt_ref, bf16[4,2048,256]{2,1,0:T(8,128)(2,1)} %get-tuple-element.104.dg_ref.refs_0_, bf16[4,2048,256]{2,1,0:T(8,128)(2,1)} %get-tuple-element.105.du_ref.refs_1_), custom_call_target="tpu_custom_call" | custom-call | flops 1000 | bytes 1000 | tf_op jit(solution)/shard_map/pallas_call | solution.py:820
  351.6 5.5 collective-permute-done.1.refs_1_
  359.0 54.6 %shard_map.231.dn_ref = f32[256,2048]{1,0:T(8,128)} custom-call(bf16[4,2048,256]{2,1,0:T(8,128)(2,1)} %get-tuple-element.104.dg_ref.refs_0_, bf16[4,2048,256]{2,1,0:T(8,128)(2,1)} %get-tuple-element.105.du_ref.refs_1_, bf16[4,2,2048,256]{3,2,1,0:T(8,128)(2,1)} %bitcast.44), custom_call_target="tpu_custom_call" | custom-call | flops 1000 | bytes 1000 | tf_op jit(solution)/shard_map/pallas_call | solution.py:982
  413.6 19.6 %shard_map.232 = (bf16[256,2048]{1,0:T(8,128)(2,1)}, f32[256,2048]{1,0:T(8,128)}, f32[8,384]{1,0:T(8,128)}, bf16[256,2048]{1,0:T(8,128)(2,1)}, bf16[4,4,64,2048]...) custom-call(f32[256,2048]{1,0:T(8,128)} %copy-done.7, f32[256,2048]{1,0:T(8,128)} %shard_map.231.dn_ref, ...), custom_call_target="tpu_custom_call" | custom-call | flops 1000 | bytes 1000 | tf_op jit(solution)/shard_map/pallas_call | solution.py:1347
  433.2 18.5 %shard_map.234 = (bf16[2048,256]{1,0:T(8,128)(2,1)}, f32[8,384]{1,0:T(8,128)}) custom-call(bf16[256,2048]{1,0:T(8,128)(2,1)} %get-tuple-element.118.x_ref, f32[8,384]{1,0:T(8,128)} %get-tuple-element.119.t_ref), custom_call_target="tpu_custom_call" | custom-call | flops 1000 | bytes 1000 | tf_op jit(solution)/shard_map/pallas_call | solution.py:648
  451.7 6.2 %shard_map.233 = (f32[4,64,2048]{2,1,0:T(8,128)}, bf16[4,64,2048]{2,1,0:T(8,128)(2,1)}, bf16[4,64,2048]{2,1,0:T(8,128)(2,1)}, bf16[4,64,2048]{2,1,0:T(8,128)(2,1)}) custom-call(bf16[4,4,64,2048]{3,2,1,0:T(8,128)(2,1)} %get-tuple-element.112.mine_ref, bf16[4,4,64,2048]{3,2,1,0:T(8,128)(2,1)} %collective-permute-done.3.twin_ref), custom_call_target="tpu_custom_call" | custom-call | flops 1000 | bytes 1000 | tf_op jit(solution)/shard_map/pallas_call | solution.py:299
  462.7 42.8 %shard_map.235 = bf16[2048,384]{1,0:T(8,128)(2,1)S(1)} custom-call(s32[16]{0:T(128)S(1)} %select_reduce_fusion.order_ref, bf16[2048,384]{1,0:T(8,128)(2,1)S(1)} %copy-done.1, bf16[2048,256]{1,0:T(8,128)(2,1)S(1)} %copy-done.3), custom_call_target="tpu_custom_call" | custom-call | flops 1000 | bytes 1000 | tf_op jit(solution)/shard_map/pallas_call | solution.py:566
  506.8 9.2 %convolution_convert_fusion.1 = bf16[2048,384]{1,0:T(8,128)(2,1)} fusion(bf16[2048,2048]{1,0:T(8,128)(2,1)} %get-tuple-element.130, bf16[2048,384]{1,0:T(8,128)(2,1)S(1)} %shard_map.235), kind=kOutput, calls=%fused_computation.5 | convolution fusion | flops 3222011904 | bytes 11534336 | tf_op jit(solution)/shard_map/dot_general | solution.py:368
  516.2 6.9 %convolution_convert_fusion = bf16[2048,2048]{1,0:T(8,128)(2,1)} fusion(bf16[2048,384]{1,0:T(8,128)(2,1)S(1)} %shard_map.235, bf16[2048,384]{1,0:T(8,128)(2,1)S(1)} %bitcast.55), kind=kOutput, calls=%fused_computation | convolution fusion | flops 3225419776 | bytes 11534336 | tf_op jit(solution)/shard_map/dot_general | solution.py:372
  523.1 3.6 add_convert_fusion
  527.9 1.6 bitcast_convert_fusion
  529.4 41.4 %shard_map.236 = f32[256,2048]{1,0:T(8,128)} custom-call(bf16[8,256,2048]{2,1,0:T(8,128)(2,1)} %bitcast.52), custom_call_target="tpu_custom_call" | custom-call | flops 1000 | bytes 1000 | tf_op jit(solution)/shard_map/pallas_call | solution.py:246
  570.8 2.3 bitcast_convert_fusion.1
  573.2 7.7 %shard_map.237.x_ref = bf16[8,64,384]{2,1,0:T(8,128)(2,1)} custom-call(bf16[8,64,384]{2,1,0:T(8,128)(2,1)} %bitcast.61), custom_call_target="tpu_custom_call" | custom-call | flops 1000 | bytes 1000 | tf_op jit(solution)/shard_map/pallas_call | solution.py:336
  580.9 3.2 shard_map.238
  585.5 1.9 bitcast_convert_fusion.3
  588.0 1.5 fusion.4
  (102 shorter events, 20.0 us)
Async XLA Ops:
  7.2 145.0 %all-gather.7.cloned.1.call-start = ((), (), s32[]{:S(2)}) async-start(), calls=%async_computation.8 | async-start | bytes 1310720 | tf_op jit(solution)/shard_map/all_gather | solution.py:376
  7.9 233.1 %all-gather.9.cloned.1.call-start = ((), (), s32[]{:S(2)}) async-start(), calls=%async_computation.9 | async-start | bytes 10485760 | tf_op jit(solution)/shard_map/all_gather | solution.py:376
  11.0 1.2 copy-start.22
  11.1 2.7 copy-start.8
  11.1 276.7 %all-gather.11.cloned.1.call-start = ((), (), s32[]{:S(2)}) async-start(), calls=%async_computation.10 | async-start | bytes 5242880 | tf_op jit(solution)/shard_map/all_gather | solution.py:376
  11.8 449.6 %reduce-scatter.5.cloned.1.call-start = ((), (), s32[]{:S(2)}) async-start(), calls=%async_computation.4 | async-start | bytes 5242880 | tf_op jit(solution)/shard_map/reduce_scatter | solution.py:380
  98.0 11.5 %copy-start.23 = (s32[64]{0:T(128)S(1)}, s32[64]{0:T(128)}, u32[]{:S(2)}) copy-start(s32[64]{0:T(128)} %param.15) | copy-start | bytes 772
  98.0 11.5 %copy-start.24 = (s32[64]{0:T(128)S(1)}, s32[64]{0:T(128)}, u32[]{:S(2)}) copy-start(s32[64]{0:T(128)} %param.14) | copy-start | bytes 772
  109.9 1.4 copy-start
  152.2 39.9 %copy-start.5 = (bf16[256,2048]{1,0:T(8,128)(2,1)S(1)}, bf16[256,2048]{1,0:T(8,128)(2,1)}, u32[]{:S(2)}) copy-start(bf16[256,2048]{1,0:T(8,128)(2,1)} %tok_ref.1) | copy-start | bytes 3145732
  199.6 41.4 %copy-start.7 = (f32[256,2048]{1,0:T(8,128)}, f32[256,2048]{1,0:T(8,128)S(1)}, u32[]{:S(2)}) copy-start(f32[256,2048]{1,0:T(8,128)S(1)} %get-tuple-element.155.res_ref) | copy-start | bytes 6291460
  287.7 228.4 %reduce-scatter.7.cloned.1.call-start = ((), (), s32[]{:S(2)}) async-start(), calls=%async_computation.5 | async-start | bytes 10485760 | tf_op jit(solution)/shard_map/reduce_scatter | solution.py:380
  308.8 42.7 %collective-permute-start = (bf16[256,2048]{1,0:T(8,128)(2,1)}, bf16[256,2048]{1,0:T(8,128)(2,1)S(1)}, u32[]{:S(2)}, u32[]{:S(2)}) collective-permute-start(bf16[256,2048]{1,0:T(8,128)(2,1)} %get-tuple-element.101), channel_id=1, source_target_pairs={{0,6},{2,4},{4,2},{6,0},{1,7},{3,5},{5,3},{7,1},{8,14},{10,12},{12... | collective-permute-start | bytes 3145736 | tf_op jit(solution)/shard_map/ppermute | solution.py:274
  310.6 46.4 %collective-permute-start.1 = (bf16[256,2048]{1,0:T(8,128)(2,1)}, bf16[256,2048]{1,0:T(8,128)(2,1)S(1)}, u32[]{:S(2)}, u32[]{:S(2)}) collective-permute-start(bf16[256,2048]{1,0:T(8,128)(2,1)} %get-tuple-element.102), channel_id=1, source_target_pairs={{0,2},{2,0},{4,6},{6,4},{1,3},{3,1},{5,7},{7,5},{8,10},{10,8},{12,... | collective-permute-start | bytes 3145736 | tf_op jit(solution)/shard_map/ppermute | solution.py:274
  311.2 46.8 %collective-permute-start.2 = (bf16[256,2048]{1,0:T(8,128)(2,1)}, bf16[256,2048]{1,0:T(8,128)(2,1)S(1)}, u32[]{:S(2)}, u32[]{:S(2)}) collective-permute-start(bf16[256,2048]{1,0:T(8,128)(2,1)} %get-tuple-element.103), channel_id=1, source_target_pairs={{0,4},{2,6},{4,0},{6,2},{1,5},{3,7},{5,1},{7,3},{8,12},{10,14},{12... | collective-permute-start | bytes 3145736 | tf_op jit(solution)/shard_map/ppermute | solution.py:274
  351.6 6.4 %copy-start.15 = (bf16[256,2048]{1,0:T(8,128)(2,1)}, bf16[256,2048]{1,0:T(8,128)(2,1)S(1)}, u32[]{:S(2)}) copy-start(bf16[256,2048]{1,0:T(8,128)(2,1)S(1)} %collective-permute-done.refs_0_) | copy-start | bytes 3145732
  359.0 214.2 %reduce-scatter.9.cloned.1.call-start = ((), (), s32[]{:S(2)}) async-start(), calls=%async_computation.6 | async-start | bytes 1966080 | tf_op jit(solution)/shard_map/reduce_scatter | solution.py:380
  433.1 18.6 %collective-permute-start.3 = (bf16[4,4,64,2048]{3,2,1,0:T(8,128)(2,1)}, bf16[4,4,64,2048]{3,2,1,0:T(8,128)(2,1)}, u32[]{:S(2)}, u32[]{:S(2)}) collective-permute-start(bf16[4,4,64,2048]{3,2,1,0:T(8,128)(2,1)} %get-tuple-element.113), channel_id=1, source_target_pairs={{0,1},{1,0},{2,3},{3,2},{4,5},{5,4},{6,7},{7,6},{8,9},{9,8},{10,11... | collective-permute-start | bytes 12582920 | tf_op jit(solution)/shard_map/ppermute | solution.py:280
  451.7 9.7 %copy-start.1 = (bf16[2048,384]{1,0:T(8,128)(2,1)S(1)}, bf16[2048,384]{1,0:T(8,128)(2,1)}, u32[]{:S(2)}) copy-start(bf16[2048,384]{1,0:T(8,128)(2,1)} %get-tuple-element.85.qkv_ref) | copy-start | bytes 4718596
  457.9 47.5 %collective-permute-start.4 = (bf16[4,64,2048]{2,1,0:T(8,128)(2,1)}, bf16[4,64,2048]{2,1,0:T(8,128)(2,1)}, u32[]{:S(2)}, u32[]{:S(2)}) collective-permute-start(bf16[4,64,2048]{2,1,0:T(8,128)(2,1)} %get-tuple-element.121), channel_id=1, source_target_pairs={{0,6},{2,4},{4,2},{6,0},{1,7},{3,5},{5,3},{7,1},{8,14},{10,12},{12... | collective-permute-start | bytes 3145736 | tf_op jit(solution)/shard_map/ppermute | solution.py:274
  459.3 47.1 %collective-permute-start.5 = (bf16[4,64,2048]{2,1,0:T(8,128)(2,1)}, bf16[4,64,2048]{2,1,0:T(8,128)(2,1)}, u32[]{:S(2)}, u32[]{:S(2)}) collective-permute-start(bf16[4,64,2048]{2,1,0:T(8,128)(2,1)} %get-tuple-element.122), channel_id=1, source_target_pairs={{0,2},{2,0},{4,6},{6,4},{1,3},{3,1},{5,7},{7,5},{8,10},{10,8},{12,... | collective-permute-start | bytes 3145736 | tf_op jit(solution)/shard_map/ppermute | solution.py:274
  460.2 46.6 %collective-permute-start.6 = (bf16[4,64,2048]{2,1,0:T(8,128)(2,1)}, bf16[4,64,2048]{2,1,0:T(8,128)(2,1)}, u32[]{:S(2)}, u32[]{:S(2)}) collective-permute-start(bf16[4,64,2048]{2,1,0:T(8,128)(2,1)} %get-tuple-element.123), channel_id=1, source_target_pairs={{0,4},{2,6},{4,0},{6,2},{1,5},{3,7},{5,1},{7,3},{8,12},{10,14},{12... | collective-permute-start | bytes 3145736 | tf_op jit(solution)/shard_map/ppermute | solution.py:274
  461.4 1.3 copy-start.3
  506.8 9.3 %copy-start.12 = (bf16[4,8,64,384]{3,2,1,0:T(8,128)(2,1)S(1)}, bf16[4,8,64,384]{3,2,1,0:T(8,128)(2,1)}, u32[]{:S(2)}) copy-start(bf16[4,8,64,384]{3,2,1,0:T(8,128)(2,1)} %get-tuple-element.83) | copy-start | bytes 4718596
  516.1 64.8 %reduce-scatter.11.cloned.1.call-start = ((), (), s32[]{:S(2)}) async-start(), calls=%async_computation.7 | async-start | bytes 1310720 | tf_op jit(solution)/shard_map/reduce_scatter | solution.py:380
  516.2 6.9 %copy-start.11 = (f32[4,64,2048]{2,1,0:T(8,128)S(1)}, f32[4,64,2048]{2,1,0:T(8,128)}, u32[]{:S(2)}) copy-start(f32[4,64,2048]{2,1,0:T(8,128)} %get-tuple-element.114) | copy-start | bytes 6291460
  523.1 3.7 copy-start.20
  523.1 4.8 copy-start.13
  529.4 41.4 %copy-start.10 = (bf16[1,2,2048,256]{3,2,1,0:T(8,128)(2,1)S(1)}, bf16[1,2,2048,256]{3,2,1,0:T(8,128)(2,1)}, u32[]{:S(2)}) copy-start(bf16[1,2,2048,256]{3,2,1,0:T(8,128)(2,1)} %reduce-scatter.7.cloned.1.call-done) | copy-start | bytes 6291460
  570.8 16.5 %copy-start.6 = (bf16[256,2048]{1,0:T(8,128)(2,1)S(1)}, bf16[256,2048]{1,0:T(8,128)(2,1)}, u32[]{:S(2)}) copy-start(bf16[256,2048]{1,0:T(8,128)(2,1)} %tok_ref.1) | copy-start | bytes 3145732
  573.2 14.2 %copy-start.4 = (f32[256,2048]{1,0:T(8,128)S(1)}, f32[256,2048]{1,0:T(8,128)}, u32[]{:S(2)}) copy-start(f32[256,2048]{1,0:T(8,128)} %shard_map.236) | copy-start | bytes 6291460
  584.9 3.0 copy-start.9
  (7 other events, 7.2 us)
Sparse Core Ops, SparseCore 0:
  9.6 36.2 all-gather.6
  48.1 157.4 all-gather.8
  207.1 79.9 all-gather.10
  289.3 75.2 reduce-scatter.4
  366.9 145.7 reduce-scatter.6
  516.2 34.7 reduce-scatter.8
  554.0 26.1 reduce-scatter.10

commit v15 on v14

--- a/solution.py
+++ b/solution.py
@@ -1138,7 +1138,6 @@
     for k, (src, dst) in enumerate(((pack_ref.at[me], all_pack), (tile_ref, all_tile))):
         mine.append(pltpu.make_async_copy(src, dst.at[grp, me], plocal.at[k]))
         mine[k].start()
-    tok.start()
     for to, c in near:
         slot = to * 2 + c
         for k, (src, dst) in enumerate(((pack_ref.at[me], all_pack), (tile_ref, all_tile))):
@@ -1184,6 +1183,7 @@
 
     send(0, grp, True)
     send(0, grp, False)
+    tok.start()
     tok.relay(0, 4)
     relay(1)
     cot.start()

time: 607 us -> 613 us (level)
    pallas_call x1, Pallas kernels: 83.1 us -> 89.5 us  [entry(): pl.pallas_call(functools.partial(entry_kernel, grps, chips), out_shape=(j...]
where the time goes in v15:
time: 613 us; the launch traced here: 603 us
  Pallas kernels  520 us (85%)
  matrix products  23.7 us (4%)
  other arithmetic  20.9 us (3%)
  between operations  15 us (2%)
  waiting for transfers between devices  9.58 us (2%)
  starting transfers between devices  7.35 us (1%)
  local copies, waits for them, and re-layouts  6.48 us (1%)
    pallas_call x1, Pallas kernels, entry(): pl.pallas_call(functools.partial(entry_kernel, grps, chips), out_shape=(j...  89.5 us
    pallas_call x2, Pallas kernels, plane_gather(): pl.pallas_call(functools.partial(gather_kernel, chips, inner), out_shape=...  79.9 us
    pallas_call x1, Pallas kernels, square_reduce(): pl.pallas_call(functools.partial(square_kernel, compute, len(operands)),...  54.6 us
    pallas_call x1, Pallas kernels, attend_back(): pl.pallas_call(functools.partial(attend_back_kernel, heads), out_shape=ja...  42.8 us
    pallas_call x1, Pallas kernels, plane_reduce(): pl.pallas_call(functools.partial(reduce_kernel, chips, inner), out_shape=...  41.4 us
    pallas_call x1, Pallas kernels, widen(): pl.pallas_call(widen_kernel, out_shape=(tall, jax.ShapeDtypeStruct((shard...  30.6 us
    pallas_call x1, Pallas kernels, widen_part(): pl.pallas_call(widen_part_kernel, out_shape=jax.ShapeDtypeStruct((shards,...  23.5 us
    pallas_call x1, Pallas kernels, attend(): pl.pallas_call(functools.partial(attend_kernel, heads), out_shape=jax.Sha...  23.3 us
  transfers between devices with their start and end apart: 14, of which 4 were waited for; matrix products, arithmetic and copies ran while one was open for 7% of the time, Pallas kernels for 86%

profile of v15, /device:TPU:0, one launch (start us, length us, event | category | flops | bytes accessed | tf_op | source)
XLA Modules:
  0.0 603.1 jit_solution(5309615282219041324)
XLA Ops:
  8.0 3.1 pad_maximum_fusion
  14.9 89.5 %shard_map.220 = (bf16[8,256,2048]{2,1,0:T(8,128)(2,1)}, bf16[8,256,2048]{2,1,0:T(8,128)(2,1)}, bf16[4,8,64,384]{3,2,1,0:T(8,128)(2,1)}, bf16[4,8,16,128]{3,2,1,0:T(8,128)(2,1)}) custom-call(bf16[256,2048]{1,0:T(8,128)(2,1)} %tok_ref.1, bf16[256,2048]{1,0:T(8,128)(2,1)} %multiply_convert_fusion.1.cot_ref, bf16[8,64,384]{2,1,0:T(8,128)(2,1)} %maximum_bitcast_fusion.pack_ref, ...), custom_call_target="tpu_custom_call" | custom-call | flops 1000 | bytes 1000 | tf_op jit(solution)/shard_map/pallas_call | solution.py:1215
  104.4 11.5 %shard_map.221 = (bf16[2048,2048]{1,0:T(8,128)(2,1)}, bf16[2048,384]{1,0:T(8,128)(2,1)}, f32[8,2048]{1,0:T(8,128)}) custom-call(bf16[2048,2048]{1,0:T(8,128)(2,1)} %bitcast.53, bf16[2048,384]{1,0:T(8,128)(2,1)} %bitcast.54, bf16[32,16,128]{2,1,0:T(8,128)(2,1)} %bitcast.62), custom_call_target="tpu_custom_call" | custom-call | flops 1000 | bytes 1000 | tf_op jit(solution)/shard_map/pallas_call | solution.py:1258
  116.3 1.4 copy-done
  117.8 23.3 %shard_map.222.x_ref = bf16[2048,256]{1,0:T(8,128)(2,1)S(1)} custom-call(s32[16]{0:T(128)S(1)} %select_reduce_fusion.order_ref, bf16[2048,384]{1,0:T(8,128)(2,1)S(1)} %copy-done), custom_call_target="tpu_custom_call" | custom-call | flops 1000 | bytes 1000 | tf_op jit(solution)/shard_map/pallas_call | solution.py:544
  142.0 15.3 %shard_map.223.refs_3_ = bf16[256,2048]{1,0:T(8,128)(2,1)} custom-call(bf16[2048,256]{1,0:T(8,128)(2,1)} %copy-done.2), custom_call_target="tpu_custom_call" | custom-call | flops 1000 | bytes 1000 | tf_op jit(solution)/shard_map/pallas_call | solution.py:336
  158.4 40.0 %shard_map.224 = bf16[4,8,64,2048]{3,2,1,0:T(8,128)(2,1)} custom-call(bf16[4,64,2048]{2,1,0:T(8,128)(2,1)} %bitcast.56), custom_call_target="tpu_custom_call" | custom-call | flops 1000 | bytes 1000 | tf_op jit(solution)/shard_map/pallas_call | solution.py:160
  198.4 7.5 %multiply_reduce_fusion = (f32[256]{0:T(256)S(1)}, f32[256,2048]{1,0:T(8,128)S(1)}, f32[256,2048]{1,0:T(8,128)}) fusion(bf16[256,2048]{1,0:T(8,128)(2,1)S(1)} %copy-done.5, bf16[256,2048]{1,0:T(8,128)(2,1)} %shard_map.223.refs_3_, bf16[2048,2048]{1,0:T(8,128)(2,1)} %bitcast.45), kind=kOutput, calls=%fused_computation.14 | convolution fusion | flops 2150104832 | bytes 14681088 | tf_op jit(solution)/shard_map/dot_general | solution.py:364
  207.3 40.0 %shard_map.225 = bf16[8,256,2048]{2,1,0:T(8,128)(2,1)} custom-call(bf16[256,2048]{1,0:T(8,128)(2,1)} %multiply_convert_fusion.x_ref), custom_call_target="tpu_custom_call" | custom-call | flops 1000 | bytes 1000 | tf_op jit(solution)/shard_map/pallas_call | solution.py:160
  247.3 30.6 %shard_map.226 = (bf16[4,2048,256]{2,1,0:T(8,128)(2,1)}, bf16[4,256,2048]{2,1,0:T(8,128)(2,1)}, bf16[4,2048,256]{2,1,0:T(8,128)(2,1)}, bf16[4,2048,256]{2,1,0:T(8,128)(2,1)}, bf16[2048,2048]{1,0:T(8,128)(2,1)}) custom-call(bf16[2048,2048]{1,0:T(8,128)(2,1)} %bitcast.49, bf16[4,2,2048,256]{3,2,1,0:T(8,128)(2,1)} %bitcast.43), custom_call_target="tpu_custom_call" | custom-call | flops 1000 | bytes 1000 | tf_op jit(solution)/shard_map/pallas_call | solution.py:706
  277.9 15.9 %shard_map.227 = bf16[4,256,2048]{2,1,0:T(8,128)(2,1)} custom-call(bf16[4,256,2048]{2,1,0:T(8,128)(2,1)} %get-tuple-element.88.ht_ref, bf16[2048,2048]{1,0:T(8,128)(2,1)} %bitcast.47), custom_call_target="tpu_custom_call" | custom-call | flops 1000 | bytes 1000 | tf_op jit(solution)/shard_map/pallas_call | solution.py:740
  293.9 21.1 %shard_map.228 = (f32[256,2048]{1,0:T(8,128)}, bf16[256,2048]{1,0:T(8,128)(2,1)}, bf16[256,2048]{1,0:T(8,128)(2,1)}, bf16[256,2048]{1,0:T(8,128)(2,1)}) custom-call(bf16[4,2048,256]{2,1,0:T(8,128)(2,1)} %get-tuple-element.92.refs_0_, bf16[4,256,2048]{2,1,0:T(8,128)(2,1)} %bitcast.50), custom_call_target="tpu_custom_call" | custom-call | flops 1000 | bytes 1000 | tf_op jit(solution)/shard_map/pallas_call | solution.py:1076
  315.1 1.6 collective-permute-start
  318.6 15.5 %shard_map.229 = (bf16[4,2048,256]{2,1,0:T(8,128)(2,1)}, bf16[4,2048,256]{2,1,0:T(8,128)(2,1)}) custom-call(bf16[4,2048,256]{2,1,0:T(8,128)(2,1)} %get-tuple-element.97.s_ref, bf16[4,2048,256]{2,1,0:T(8,128)(2,1)} %get-tuple-element.98.t_ref, bf16[2048,2048]{1,0:T(8,128)(2,1)} %bitcast.48, bf16[4,256,2048]{2,1,0:T(8,128)(2,1)} %bitcast.51), custom_call_target="tpu_custom_call" | custom-call | flops 1000 | bytes 1000 | tf_op jit(solution)/shard_map/pallas_call | solution.py:798
  334.1 23.5 %shard_map.230 = bf16[4,2,2048,256]{3,2,1,0:T(8,128)(2,1)} custom-call(bf16[2048,2048]{1,0:T(8,128)(2,1)} %get-tuple-element.87.nt_ref, bf16[4,2048,256]{2,1,0:T(8,128)(2,1)} %get-tuple-element.104.dg_ref.refs_0_, bf16[4,2048,256]{2,1,0:T(8,128)(2,1)} %get-tuple-element.105.du_ref.refs_1_), custom_call_target="tpu_custom_call" | custom-call | flops 1000 | bytes 1000 | tf_op jit(solution)/shard_map/pallas_call | solution.py:820
  357.6 5.8 collective-permute-done.1.refs_1_
  365.1 54.6 %shard_map.231.dn_ref = f32[256,2048]{1,0:T(8,128)} custom-call(bf16[4,2048,256]{2,1,0:T(8,128)(2,1)} %get-tuple-element.104.dg_ref.refs_0_, bf16[4,2048,256]{2,1,0:T(8,128)(2,1)} %get-tuple-element.105.du_ref.refs_1_, bf16[4,2,2048,256]{3,2,1,0:T(8,128)(2,1)} %bitcast.44), custom_call_target="tpu_custom_call" | custom-call | flops 1000 | bytes 1000 | tf_op jit(solution)/shard_map/pallas_call | solution.py:982
  419.8 19.6 %shard_map.232 = (bf16[256,2048]{1,0:T(8,128)(2,1)}, f32[256,2048]{1,0:T(8,128)}, f32[8,384]{1,0:T(8,128)}, bf16[256,2048]{1,0:T(8,128)(2,1)}, bf16[4,4,64,2048]...) custom-call(f32[256,2048]{1,0:T(8,128)} %copy-done.7, f32[256,2048]{1,0:T(8,128)} %shard_map.231.dn_ref, ...), custom_call_target="tpu_custom_call" | custom-call | flops 1000 | bytes 1000 | tf_op jit(solution)/shard_map/pallas_call | solution.py:1347
  439.4 18.4 %shard_map.234 = (bf16[2048,256]{1,0:T(8,128)(2,1)}, f32[8,384]{1,0:T(8,128)}) custom-call(bf16[256,2048]{1,0:T(8,128)(2,1)} %get-tuple-element.118.x_ref, f32[8,384]{1,0:T(8,128)} %get-tuple-element.119.t_ref), custom_call_target="tpu_custom_call" | custom-call | flops 1000 | bytes 1000 | tf_op jit(solution)/shard_map/pallas_call | solution.py:648
  457.9 6.2 %shard_map.233 = (f32[4,64,2048]{2,1,0:T(8,128)}, bf16[4,64,2048]{2,1,0:T(8,128)(2,1)}, bf16[4,64,2048]{2,1,0:T(8,128)(2,1)}, bf16[4,64,2048]{2,1,0:T(8,128)(2,1)}) custom-call(bf16[4,4,64,2048]{3,2,1,0:T(8,128)(2,1)} %get-tuple-element.112.mine_ref, bf16[4,4,64,2048]{3,2,1,0:T(8,128)(2,1)} %collective-permute-done.3.twin_ref), custom_call_target="tpu_custom_call" | custom-call | flops 1000 | bytes 1000 | tf_op jit(solution)/shard_map/pallas_call | solution.py:299
  464.1 1.5 collective-permute-start.4
  468.8 42.8 %shard_map.235 = bf16[2048,384]{1,0:T(8,128)(2,1)S(1)} custom-call(s32[16]{0:T(128)S(1)} %select_reduce_fusion.order_ref, bf16[2048,384]{1,0:T(8,128)(2,1)S(1)} %copy-done.1, bf16[2048,256]{1,0:T(8,128)(2,1)S(1)} %copy-done.3), custom_call_target="tpu_custom_call" | custom-call | flops 1000 | bytes 1000 | tf_op jit(solution)/shard_map/pallas_call | solution.py:566
  513.2 9.2 %convolution_convert_fusion.1 = bf16[2048,384]{1,0:T(8,128)(2,1)} fusion(bf16[2048,2048]{1,0:T(8,128)(2,1)} %get-tuple-element.130, bf16[2048,384]{1,0:T(8,128)(2,1)S(1)} %shard_map.235), kind=kOutput, calls=%fused_computation.5 | convolution fusion | flops 3222011904 | bytes 11534336 | tf_op jit(solution)/shard_map/dot_general | solution.py:368
  522.5 6.9 %convolution_convert_fusion = bf16[2048,2048]{1,0:T(8,128)(2,1)} fusion(bf16[2048,384]{1,0:T(8,128)(2,1)S(1)} %shard_map.235, bf16[2048,384]{1,0:T(8,128)(2,1)S(1)} %bitcast.55), kind=kOutput, calls=%fused_computation | convolution fusion | flops 3225419776 | bytes 11534336 | tf_op jit(solution)/shard_map/dot_general | solution.py:372
  529.4 3.6 add_convert_fusion
  534.2 1.6 bitcast_convert_fusion
  535.7 41.4 %shard_map.236 = f32[256,2048]{1,0:T(8,128)} custom-call(bf16[8,256,2048]{2,1,0:T(8,128)(2,1)} %bitcast.52), custom_call_target="tpu_custom_call" | custom-call | flops 1000 | bytes 1000 | tf_op jit(solution)/shard_map/pallas_call | solution.py:246
  577.1 2.3 bitcast_convert_fusion.1
  579.5 7.7 %shard_map.237.x_ref = bf16[8,64,384]{2,1,0:T(8,128)(2,1)} custom-call(bf16[8,64,384]{2,1,0:T(8,128)(2,1)} %bitcast.61), custom_call_target="tpu_custom_call" | custom-call | flops 1000 | bytes 1000 | tf_op jit(solution)/shard_map/pallas_call | solution.py:336
  587.2 3.2 shard_map.238
  591.7 1.9 bitcast_convert_fusion.3
  594.2 1.5 fusion.4
  (102 shorter events, 20.0 us)
Async XLA Ops:
  7.2 151.2 %all-gather.7.cloned.1.call-start = ((), (), s32[]{:S(2)}) async-start(), calls=%async_computation.8 | async-start | bytes 1310720 | tf_op jit(solution)/shard_map/all_gather | solution.py:376
  7.9 239.4 %all-gather.9.cloned.1.call-start = ((), (), s32[]{:S(2)}) async-start(), calls=%async_computation.9 | async-start | bytes 10485760 | tf_op jit(solution)/shard_map/all_gather | solution.py:376
  11.0 1.2 copy-start.22
  11.1 2.7 copy-start.8
  11.1 282.9 %all-gather.11.cloned.1.call-start = ((), (), s32[]{:S(2)}) async-start(), calls=%async_computation.10 | async-start | bytes 5242880 | tf_op jit(solution)/shard_map/all_gather | solution.py:376
  11.8 455.8 %reduce-scatter.5.cloned.1.call-start = ((), (), s32[]{:S(2)}) async-start(), calls=%async_computation.4 | async-start | bytes 5242880 | tf_op jit(solution)/shard_map/reduce_scatter | solution.py:380
  104.4 11.5 %copy-start.23 = (s32[64]{0:T(128)S(1)}, s32[64]{0:T(128)}, u32[]{:S(2)}) copy-start(s32[64]{0:T(128)} %param.15) | copy-start | bytes 772
  104.4 11.5 %copy-start.24 = (s32[64]{0:T(128)S(1)}, s32[64]{0:T(128)}, u32[]{:S(2)}) copy-start(s32[64]{0:T(128)} %param.14) | copy-start | bytes 772
  116.3 1.4 copy-start
  158.4 40.0 %copy-start.5 = (bf16[256,2048]{1,0:T(8,128)(2,1)S(1)}, bf16[256,2048]{1,0:T(8,128)(2,1)}, u32[]{:S(2)}) copy-start(bf16[256,2048]{1,0:T(8,128)(2,1)} %tok_ref.1) | copy-start | bytes 3145732
  205.9 41.4 %copy-start.7 = (f32[256,2048]{1,0:T(8,128)}, f32[256,2048]{1,0:T(8,128)S(1)}, u32[]{:S(2)}) copy-start(f32[256,2048]{1,0:T(8,128)S(1)} %get-tuple-element.155.res_ref) | copy-start | bytes 6291460
  293.9 228.5 %reduce-scatter.7.cloned.1.call-start = ((), (), s32[]{:S(2)}) async-start(), calls=%async_computation.5 | async-start | bytes 10485760 | tf_op jit(solution)/shard_map/reduce_scatter | solution.py:380
  315.1 42.5 %collective-permute-start = (bf16[256,2048]{1,0:T(8,128)(2,1)}, bf16[256,2048]{1,0:T(8,128)(2,1)S(1)}, u32[]{:S(2)}, u32[]{:S(2)}) collective-permute-start(bf16[256,2048]{1,0:T(8,128)(2,1)} %get-tuple-element.101), channel_id=1, source_target_pairs={{0,6},{2,4},{4,2},{6,0},{1,7},{3,5},{5,3},{7,1},{8,14},{10,12},{12... | collective-permute-start | bytes 3145736 | tf_op jit(solution)/shard_map/ppermute | solution.py:274
  316.6 46.8 %collective-permute-start.1 = (bf16[256,2048]{1,0:T(8,128)(2,1)}, bf16[256,2048]{1,0:T(8,128)(2,1)S(1)}, u32[]{:S(2)}, u32[]{:S(2)}) collective-permute-start(bf16[256,2048]{1,0:T(8,128)(2,1)} %get-tuple-element.102), channel_id=1, source_target_pairs={{0,2},{2,0},{4,6},{6,4},{1,3},{3,1},{5,7},{7,5},{8,10},{10,8},{12,... | collective-permute-start | bytes 3145736 | tf_op jit(solution)/shard_map/ppermute | solution.py:274
  317.3 46.8 %collective-permute-start.2 = (bf16[256,2048]{1,0:T(8,128)(2,1)}, bf16[256,2048]{1,0:T(8,128)(2,1)S(1)}, u32[]{:S(2)}, u32[]{:S(2)}) collective-permute-start(bf16[256,2048]{1,0:T(8,128)(2,1)} %get-tuple-element.103), channel_id=1, source_target_pairs={{0,4},{2,6},{4,0},{6,2},{1,5},{3,7},{5,1},{7,3},{8,12},{10,14},{12... | collective-permute-start | bytes 3145736 | tf_op jit(solution)/shard_map/ppermute | solution.py:274
  357.6 6.6 %copy-start.15 = (bf16[256,2048]{1,0:T(8,128)(2,1)}, bf16[256,2048]{1,0:T(8,128)(2,1)S(1)}, u32[]{:S(2)}) copy-start(bf16[256,2048]{1,0:T(8,128)(2,1)S(1)} %collective-permute-done.refs_0_) | copy-start | bytes 3145732
  365.1 214.4 %reduce-scatter.9.cloned.1.call-start = ((), (), s32[]{:S(2)}) async-start(), calls=%async_computation.6 | async-start | bytes 1966080 | tf_op jit(solution)/shard_map/reduce_scatter | solution.py:380
  439.3 18.5 %collective-permute-start.3 = (bf16[4,4,64,2048]{3,2,1,0:T(8,128)(2,1)}, bf16[4,4,64,2048]{3,2,1,0:T(8,128)(2,1)}, u32[]{:S(2)}, u32[]{:S(2)}) collective-permute-start(bf16[4,4,64,2048]{3,2,1,0:T(8,128)(2,1)} %get-tuple-element.113), channel_id=1, source_target_pairs={{0,1},{1,0},{2,3},{3,2},{4,5},{5,4},{6,7},{7,6},{8,9},{9,8},{10,11... | collective-permute-start | bytes 12582920 | tf_op jit(solution)/shard_map/ppermute | solution.py:280
  457.8 9.7 %copy-start.1 = (bf16[2048,384]{1,0:T(8,128)(2,1)S(1)}, bf16[2048,384]{1,0:T(8,128)(2,1)}, u32[]{:S(2)}) copy-start(bf16[2048,384]{1,0:T(8,128)(2,1)} %get-tuple-element.85.qkv_ref) | copy-start | bytes 4718596
  464.1 47.5 %collective-permute-start.4 = (bf16[4,64,2048]{2,1,0:T(8,128)(2,1)}, bf16[4,64,2048]{2,1,0:T(8,128)(2,1)}, u32[]{:S(2)}, u32[]{:S(2)}) collective-permute-start(bf16[4,64,2048]{2,1,0:T(8,128)(2,1)} %get-tuple-element.121), channel_id=1, source_target_pairs={{0,6},{2,4},{4,2},{6,0},{1,7},{3,5},{5,3},{7,1},{8,14},{10,12},{12... | collective-permute-start | bytes 3145736 | tf_op jit(solution)/shard_map/ppermute | solution.py:274
  465.6 47.0 %collective-permute-start.5 = (bf16[4,64,2048]{2,1,0:T(8,128)(2,1)}, bf16[4,64,2048]{2,1,0:T(8,128)(2,1)}, u32[]{:S(2)}, u32[]{:S(2)}) collective-permute-start(bf16[4,64,2048]{2,1,0:T(8,128)(2,1)} %get-tuple-element.122), channel_id=1, source_target_pairs={{0,2},{2,0},{4,6},{6,4},{1,3},{3,1},{5,7},{7,5},{8,10},{10,8},{12,... | collective-permute-start | bytes 3145736 | tf_op jit(solution)/shard_map/ppermute | solution.py:274
  466.5 46.6 %collective-permute-start.6 = (bf16[4,64,2048]{2,1,0:T(8,128)(2,1)}, bf16[4,64,2048]{2,1,0:T(8,128)(2,1)}, u32[]{:S(2)}, u32[]{:S(2)}) collective-permute-start(bf16[4,64,2048]{2,1,0:T(8,128)(2,1)} %get-tuple-element.123), channel_id=1, source_target_pairs={{0,4},{2,6},{4,0},{6,2},{1,5},{3,7},{5,1},{7,3},{8,12},{10,14},{12... | collective-permute-start | bytes 3145736 | tf_op jit(solution)/shard_map/ppermute | solution.py:274
  467.6 1.2 copy-start.3
  513.1 9.3 %copy-start.12 = (bf16[4,8,64,384]{3,2,1,0:T(8,128)(2,1)S(1)}, bf16[4,8,64,384]{3,2,1,0:T(8,128)(2,1)}, u32[]{:S(2)}) copy-start(bf16[4,8,64,384]{3,2,1,0:T(8,128)(2,1)} %get-tuple-element.83) | copy-start | bytes 4718596
  522.4 64.8 %reduce-scatter.11.cloned.1.call-start = ((), (), s32[]{:S(2)}) async-start(), calls=%async_computation.7 | async-start | bytes 1310720 | tf_op jit(solution)/shard_map/reduce_scatter | solution.py:380
  522.5 6.9 %copy-start.11 = (f32[4,64,2048]{2,1,0:T(8,128)S(1)}, f32[4,64,2048]{2,1,0:T(8,128)}, u32[]{:S(2)}) copy-start(f32[4,64,2048]{2,1,0:T(8,128)} %get-tuple-element.114) | copy-start | bytes 6291460
  529.4 3.7 copy-start.20
  529.4 4.8 copy-start.13
  535.7 41.4 %copy-start.10 = (bf16[1,2,2048,256]{3,2,1,0:T(8,128)(2,1)S(1)}, bf16[1,2,2048,256]{3,2,1,0:T(8,128)(2,1)}, u32[]{:S(2)}) copy-start(bf16[1,2,2048,256]{3,2,1,0:T(8,128)(2,1)} %reduce-scatter.7.cloned.1.call-done) | copy-start | bytes 6291460
  577.1 16.5 %copy-start.6 = (bf16[256,2048]{1,0:T(8,128)(2,1)S(1)}, bf16[256,2048]{1,0:T(8,128)(2,1)}, u32[]{:S(2)}) copy-start(bf16[256,2048]{1,0:T(8,128)(2,1)} %tok_ref.1) | copy-start | bytes 3145732
  579.5 14.1 %copy-start.4 = (f32[256,2048]{1,0:T(8,128)S(1)}, f32[256,2048]{1,0:T(8,128)}, u32[]{:S(2)}) copy-start(f32[256,2048]{1,0:T(8,128)} %shard_map.236) | copy-start | bytes 6291460
  591.2 3.0 copy-start.9
  (7 other events, 7.2 us)
Sparse Core Ops, SparseCore 0:
  9.6 36.5 all-gather.6
  48.3 159.1 all-gather.8
  209.1 80.7 all-gather.10
  294.0 75.4 reduce-scatter.4
  371.9 145.7 reduce-scatter.6
  522.5 33.6 reduce-scatter.8
  559.2 26.0 reduce-scatter.10
